TPU v7x, 32 devices: a whole 2x2x4 slice. The times are simulated.
32 devices in a mesh: fsdp: 4 (over x, core), ctx: 4 (over z), tp: 2 (over y).
Axes of the slice: x: 2, y: 2, z: 4, core: 2. Of those that a mesh axis runs over, the one named last changes fastest.
Arguments:
- layer_input: bfloat16 [4096, 2048], P(('fsdp', 'ctx', 'tp')), may hold values from -6 to 6
- cotangent: bfloat16 [4096, 2048], P(('fsdp', 'ctx', 'tp')), may hold values from -6 to 6
- lengths: int32 [4, 2], P('fsdp'), may hold values from 0 to 1024, as said below
- attn_norm: bfloat16 [2048], replicated, may hold values from 0.5 to 1.5
- query_norm_gain: bfloat16 [128], replicated, may hold values from 0.25 to 1.75
- k_norm: bfloat16 [128], replicated, may hold values from 0.25 to 1.75
- w_query: bfloat16 [2048, 2048], P('fsdp', 'tp'), may hold values from -0.125 to 0.125
- key_weight: bfloat16 [2048, 1024], P('fsdp', 'tp'), may hold values from -0.125 to 0.125
- value_weight: bfloat16 [2048, 1024], P('fsdp', 'tp'), may hold values from -0.125 to 0.125
- w_out_gate: bfloat16 [2048, 2048], P('fsdp', 'tp'), may hold values from -0.125 to 0.125
- w_output: bfloat16 [2048, 2048], P(('tp', 'fsdp')), may hold values from -2 to 2
- ffn_norm: bfloat16 [2048], replicated, may hold values from 0.5 to 1.5
- w_gate: bfloat16 [2048, 6144], P('fsdp', 'tp'), may hold values from -0.125 to 0.125
- w_up: bfloat16 [2048, 6144], P('fsdp', 'tp'), may hold values from -0.125 to 0.125
- w_down: bfloat16 [6144, 2048], P(('tp', 'fsdp')), may hold values from -0.078125 to 0.078125
Outputs:
- layer_output: bfloat16 [4096, 2048], P(('fsdp', 'ctx', 'tp'))
- input_grad: bfloat16 [4096, 2048], P(('fsdp', 'ctx', 'tp'))
- grad_attn_norm: float32 [2048], replicated
- grad_q_norm: float32 [128], replicated
- grad_k_norm: float32 [128], replicated
- grad_w_query: float32 [2048, 2048], P('fsdp', 'tp')
- grad_w_key: float32 [2048, 1024], P('fsdp', 'tp')
- grad_w_value: float32 [2048, 1024], P('fsdp', 'tp')
- grad_w_out_gate: float32 [2048, 2048], P('fsdp', 'tp')
- grad_w_output: float32 [2048, 2048], P(('tp', 'fsdp'))
- grad_ffn_norm: float32 [2048], replicated
- grad_w_gate: float32 [2048, 6144], P('fsdp', 'tp')
- grad_w_up: float32 [2048, 6144], P('fsdp', 'tp')
- grad_w_down: float32 [6144, 2048], P(('tp', 'fsdp'))
Inputs may be any that keep to these rules, and one draw needn't show every extreme that they name: `lengths`: per packed row the first count is at least 512 and the two counts add up to at most 1024; some row holds a single sequence of 1024 tokens.
All inputs are finite; a program needn't handle non-finite values.
Results may differ from a plain program's by a relative error of at most 0.024.
Values may be sent and summed in bfloat16 or wider, within the bound.
No kernel may reach another device: no remote copies, remote signals or barrier semaphores. Data moves between devices by JAX's collectives and lax.ppermute only.
A program may use at most 448 MiB of HBM per device.

v0:
```python
import jax
import jax.numpy as jnp
from jax import lax
from jax.sharding import PartitionSpec as P

HEAD_SIZE = 128


EPSILON = 1e-06
ROPE_BASE = 1000000.0
NEG_FILL = -1e30


def as_sent(value):

    def short(part):
        return part.astype(jnp.bfloat16) if part.dtype == jnp.float32 else part

    return jax.tree.map(short, value)


def apply_rms_norm(values, gain_vec):
    return (
        values * lax.rsqrt(jnp.mean(values * values, axis=-1, keepdims=True) + EPSILON) * gain_vec
    )


def norm_back(values, gain_vec, grad_in):
    row_scale = lax.rsqrt(jnp.mean(values * values, axis=-1, keepdims=True) + EPSILON)
    unit_rows = values * row_scale
    scaled = grad_in * gain_vec
    back_rows = row_scale * (
        scaled - unit_rows * jnp.mean(scaled * unit_rows, axis=-1, keepdims=True)
    )
    gain_grad = jnp.sum((grad_in * unit_rows).reshape(-1, values.shape[-1]), axis=0)
    return (back_rows, gain_grad)


def apply_rotary(values, token_position, direction):
    half_size = values.shape[-1] // 2
    frequency = jnp.power(ROPE_BASE, -jnp.arange(half_size, dtype=jnp.float32) / half_size)
    angle = token_position.astype(jnp.float32)[:, None] * frequency[None, :]
    cosine = jnp.cos(angle)[:, None, :]
    sine = direction * jnp.sin(angle)[:, None, :]
    first_half = values[..., :half_size]
    second_half = values[..., half_size:]
    return jnp.concatenate(
        [first_half * cosine - second_half * sine, second_half * cosine + first_half * sine],
        axis=-1,
    )


def segment_of(slot_ids, lengths):
    first_len = lengths[0, 0]
    second_len = lengths[0, 1]
    return jnp.where(slot_ids < first_len, 0, jnp.where(slot_ids < first_len + second_len, 1, 2))


def position_of(slot_ids, segment, lengths):
    seg_begin = jnp.where(
        segment == 0, 0, jnp.where(segment == 1, lengths[0, 0], lengths[0, 0] + lengths[0, 1])
    )
    return slot_ids - seg_begin


def to_block(local_part):
    return lax.all_gather(local_part, "tp", axis=0, tiled=True)


def to_share(partial_rows):
    return lax.psum_scatter(
        partial_rows.astype(jnp.bfloat16), "tp", scatter_dimension=0, tiled=True
    ).astype(jnp.float32)


def fold_product(left_rows, weight_set):
    pieces = jax.tree.map(
        lambda a: lax.all_gather(a, "fsdp", axis=0, tiled=True), as_sent(weight_set)
    )
    return tuple(
        (
            jnp.dot(left_rows, weight_part, preferred_element_type=jnp.float32)
            for weight_part in pieces
        )
    )


def back_product(grad_rows, weight_set):
    pieces = jax.tree.map(
        lambda a: lax.all_gather(a, "fsdp", axis=0, tiled=True), as_sent(weight_set)
    )
    result = lax.dot_general(
        grad_rows[0], pieces[0], (((1,), (1,)), ((), ())), preferred_element_type=jnp.float32
    )
    for grad_part, weight_part in zip(grad_rows[1:], pieces[1:]):
        result = result + lax.dot_general(
            grad_part, weight_part, (((1,), (1,)), ((), ())), preferred_element_type=jnp.float32
        )
    return result


def weight_grads(left_rows, grad_rows):
    widths = [grad_part.shape[1] for grad_part in grad_rows]
    shared = lax.psum_scatter(
        jnp.concatenate(
            [
                lax.dot_general(
                    left_rows,
                    grad_part,
                    (((0,), (0,)), ((), ())),
                    preferred_element_type=jnp.float32,
                )
                for grad_part in grad_rows
            ],
            axis=1,
        ).astype(jnp.bfloat16),
        "fsdp",
        scatter_dimension=0,
        tiled=True,
    )
    summed = lax.psum(shared, "ctx").astype(jnp.float32)
    pieces = []
    offset = 0
    for column_width in widths:
        pieces.append(summed[:, offset : offset + column_width])
        offset = offset + column_width
    return tuple(pieces)


def body(
    layer_input,
    cotangent,
    lengths,
    attn_norm,
    query_norm_gain,
    k_norm,
    w_query,
    key_weight,
    value_weight,
    w_out_gate,
    w_output,
    ffn_norm,
    w_gate,
    w_up,
    w_down,
):
    local_rows = layer_input.shape[0]
    block_rows = local_rows * lax.axis_size("tp")
    query_heads = w_query.shape[1] // HEAD_SIZE
    kv_heads = key_weight.shape[1] // HEAD_SIZE
    groups = query_heads // kv_heads
    score_scale = HEAD_SIZE ** (-0.5)
    block_first = lax.axis_index("ctx") * block_rows
    own_slots = (
        block_first + lax.axis_index("tp") * local_rows + jnp.arange(local_rows, dtype=jnp.int32)
    )
    own_valid = (segment_of(own_slots, lengths) < 2).astype(jnp.float32)[:, None]
    query_slots = block_first + jnp.arange(block_rows, dtype=jnp.int32)
    query_segment = segment_of(query_slots, lengths)
    query_position = position_of(query_slots, query_segment, lengths)
    inputs = layer_input.astype(jnp.float32)
    gain_one = attn_norm.astype(jnp.float32)
    gain_two = ffn_norm.astype(jnp.float32)
    query_gain = query_norm_gain.astype(jnp.float32)
    key_gain = k_norm.astype(jnp.float32)
    first_normed = to_block(apply_rms_norm(inputs, gain_one).astype(jnp.bfloat16))
    query_rows, key_projected, value_proj, gate_logits = fold_product(
        first_normed, (w_query, key_weight, value_weight, w_out_gate)
    )
    query_heads_raw = query_rows.reshape(block_rows, query_heads, HEAD_SIZE)
    key_heads_raw = key_projected.reshape(block_rows, kv_heads, HEAD_SIZE)
    query_rotated = apply_rotary(
        apply_rms_norm(query_heads_raw, query_gain), query_position, 1.0
    ).astype(jnp.bfloat16)
    key_rot = apply_rotary(apply_rms_norm(key_heads_raw, key_gain), query_position, 1.0).astype(
        jnp.bfloat16
    )
    query_grouped = query_rotated.reshape(block_rows, kv_heads, groups, HEAD_SIZE)
    key_flat = key_rot.reshape(block_rows, kv_heads * HEAD_SIZE)
    value_reduced = value_proj.astype(jnp.bfloat16)

    def key_mask(piece_rows):
        key_slots = jnp.arange(piece_rows, dtype=jnp.int32)
        key_segment = segment_of(key_slots, lengths)
        return (query_segment[:, None] == key_segment[None, :]) & (
            key_slots[None, :] <= query_slots[:, None]
        )

    head_shape = (kv_heads, groups, block_rows)
    running_top = jnp.full(head_shape + (1,), NEG_FILL, jnp.float32)
    key_piece = lax.all_gather(key_flat, "ctx", axis=0, tiled=True)
    value_piece = lax.all_gather(value_reduced, "ctx", axis=0, tiled=True)
    piece_rows = key_piece.shape[0]
    allowed = key_mask(piece_rows)
    raw_scores = jnp.einsum(
        "qhgd,khd->hgqk",
        query_grouped,
        key_piece.reshape(piece_rows, kv_heads, HEAD_SIZE),
        preferred_element_type=jnp.float32,
    )
    scores = jnp.where(allowed, raw_scores * score_scale, NEG_FILL)
    new_top = jnp.maximum(running_top, jnp.max(scores, axis=-1, keepdims=True))
    weights = jnp.where(allowed, jnp.exp(scores - new_top), 0.0)
    running_total = jnp.sum(weights, axis=-1, keepdims=True)
    mixed_sum = jnp.einsum(
        "hgqk,khd->hgqd",
        weights.astype(jnp.bfloat16),
        value_piece.reshape(piece_rows, kv_heads, HEAD_SIZE),
        preferred_element_type=jnp.float32,
    )
    mixed_sum, running_top, running_total = (mixed_sum, new_top, running_total)
    log_total = running_top + jnp.log(running_total)
    attended = jnp.transpose(mixed_sum / running_total, (2, 0, 1, 3))
    attended_rows = attended.reshape(block_rows, query_heads * HEAD_SIZE)
    gate_sig = jax.nn.sigmoid(gate_logits)
    gated_mix = (attended_rows * gate_sig).astype(jnp.bfloat16)
    attn_share = to_share(fold_product(gated_mix, (w_output,))[0])
    hidden_in = inputs + own_valid * attn_share
    normed_two = to_block(apply_rms_norm(hidden_in, gain_two).astype(jnp.bfloat16))
    gate_pre, up_pre = fold_product(normed_two, (w_gate, w_up))
    gate_sigmoid = jax.nn.sigmoid(gate_pre)
    activated = gate_pre * gate_sigmoid
    hidden_act = (activated * up_pre).astype(jnp.bfloat16)
    ffn_share = to_share(fold_product(hidden_act, (w_down,))[0])
    layer_output = (hidden_in + own_valid * ffn_share).astype(jnp.bfloat16)
    out_grad = cotangent.astype(jnp.float32) * own_valid
    ffn_grad = to_block(out_grad.astype(jnp.bfloat16))
    hidden_grad = back_product((ffn_grad,), (w_down,))
    grad_w_down = weight_grads(hidden_act, (ffn_grad,))[0]
    gate_grad = (
        hidden_grad * up_pre * gate_sigmoid * (1.0 + gate_pre * (1.0 - gate_sigmoid))
    ).astype(jnp.bfloat16)
    up_grad = (hidden_grad * activated).astype(jnp.bfloat16)
    normed_two_grad = to_share(back_product((gate_grad, up_grad), (w_gate, w_up)))
    grad_w_gate, grad_w_up = weight_grads(normed_two, (gate_grad, up_grad))
    back_two, gain_two_grad = norm_back(hidden_in, gain_two, normed_two_grad)
    hidden_total_grad = out_grad + back_two
    attn_grad = to_block((own_valid * hidden_total_grad).astype(jnp.bfloat16))
    gated_grad = back_product((attn_grad,), (w_output,))
    grad_w_output = weight_grads(gated_mix, (attn_grad,))[0]
    mixed_grad = (gated_grad * gate_sig).astype(jnp.bfloat16)
    gate_logit_grad = (gated_grad * attended_rows * gate_sig * (1.0 - gate_sig)).astype(
        jnp.bfloat16
    )
    mixed_grad_heads = mixed_grad.reshape(block_rows, kv_heads, groups, HEAD_SIZE)
    delta_rows = jnp.transpose(
        jnp.sum(mixed_grad_heads.astype(jnp.float32) * attended, axis=-1), (1, 2, 0)
    )[..., None]
    key_piece = lax.all_gather(key_flat, "ctx", axis=0, tiled=True)
    value_piece = lax.all_gather(value_reduced, "ctx", axis=0, tiled=True)
    piece_rows = key_piece.shape[0]
    key_view = key_piece.reshape(piece_rows, kv_heads, HEAD_SIZE)
    value_view = value_piece.reshape(piece_rows, kv_heads, HEAD_SIZE)
    allowed = key_mask(piece_rows)
    raw_scores = jnp.einsum(
        "qhgd,khd->hgqk", query_grouped, key_view, preferred_element_type=jnp.float32
    )
    soft_vals = jnp.where(allowed, jnp.exp(raw_scores * score_scale - log_total), 0.0)
    prob_grad = jnp.einsum(
        "qhgd,khd->hgqk", mixed_grad_heads, value_view, preferred_element_type=jnp.float32
    )
    score_grad = (soft_vals * (prob_grad - delta_rows) * score_scale).astype(jnp.bfloat16)
    query_acc = jnp.einsum(
        "hgqk,khd->qhgd", score_grad, key_view, preferred_element_type=jnp.float32
    )
    key_part = jnp.einsum(
        "hgqk,qhgd->khd", score_grad, query_grouped, preferred_element_type=jnp.float32
    ).reshape(piece_rows, kv_heads * HEAD_SIZE)
    value_part = jnp.einsum(
        "hgqk,qhgd->khd",
        soft_vals.astype(jnp.bfloat16),
        mixed_grad_heads,
        preferred_element_type=jnp.float32,
    ).reshape(piece_rows, kv_heads * HEAD_SIZE)
    kv_acc = jnp.concatenate([key_part, value_part], axis=1)
    query_acc, kv_acc = (query_acc, kv_acc)
    kv_own = lax.psum_scatter(
        kv_acc.astype(jnp.bfloat16), "ctx", scatter_dimension=0, tiled=True
    ).astype(jnp.float32)
    key_rot_grad = kv_own[:, : kv_heads * HEAD_SIZE].reshape(block_rows, kv_heads, HEAD_SIZE)
    value_grad = kv_own[:, kv_heads * HEAD_SIZE :].astype(jnp.bfloat16)
    key_back, key_gain_grad = norm_back(
        key_heads_raw, key_gain, apply_rotary(key_rot_grad, query_position, -1.0)
    )
    query_back, query_gain_grad = norm_back(
        query_heads_raw,
        query_gain,
        apply_rotary(query_acc.reshape(block_rows, query_heads, HEAD_SIZE), query_position, -1.0),
    )
    query_grad = query_back.reshape(block_rows, query_heads * HEAD_SIZE).astype(jnp.bfloat16)
    key_grad = key_back.reshape(block_rows, kv_heads * HEAD_SIZE).astype(jnp.bfloat16)
    attn_in_grads = (query_grad, key_grad, value_grad, gate_logit_grad)
    normed_one_grad = to_share(
        back_product(attn_in_grads, (w_query, key_weight, value_weight, w_out_gate))
    )
    grad_w_query, grad_w_key, grad_w_value, grad_w_out_gate = weight_grads(
        first_normed, attn_in_grads
    )
    back_one, gain_one_grad = norm_back(inputs, gain_one, normed_one_grad)
    input_grad = (hidden_total_grad + back_one).astype(jnp.bfloat16)
    gain_totals = lax.psum(
        (gain_one_grad, query_gain_grad, key_gain_grad, gain_two_grad), ("fsdp", "ctx", "tp")
    )
    return (
        layer_output,
        input_grad,
        gain_totals[0],
        gain_totals[1],
        gain_totals[2],
        grad_w_query,
        grad_w_key,
        grad_w_value,
        grad_w_out_gate,
        grad_w_output,
        gain_totals[3],
        grad_w_gate,
        grad_w_up,
        grad_w_down,
    )


def solution(mesh):
    return jax.shard_map(
        body,
        mesh=mesh,
        in_specs=(
            P(("fsdp", "ctx", "tp"), None),
            P(("fsdp", "ctx", "tp"), None),
            P("fsdp", None),
            P(),
            P(),
            P(),
            P("fsdp", "tp"),
            P("fsdp", "tp"),
            P("fsdp", "tp"),
            P("fsdp", "tp"),
            P(("tp", "fsdp"), None),
            P(),
            P("fsdp", "tp"),
            P("fsdp", "tp"),
            P(("tp", "fsdp"), None),
        ),
        out_specs=(
            P(("fsdp", "ctx", "tp"), None),
            P(("fsdp", "ctx", "tp"), None),
            P(),
            P(),
            P(),
            P("fsdp", "tp"),
            P("fsdp", "tp"),
            P("fsdp", "tp"),
            P("fsdp", "tp"),
            P(("tp", "fsdp"), None),
            P(),
            P("fsdp", "tp"),
            P("fsdp", "tp"),
            P(("tp", "fsdp"), None),
        ),
        check_vma=False,
    )
```

profile of v0, /device:TPU:1, one launch (start us, length us, event | category | flops | bytes accessed | tf_op | source)
XLA Modules:
  0.0 1698.8 jit_solution(15141842273888128146)
XLA Ops:
  12.8 21.8 %all-gather.15.cloned.1.call-done = bf16[256,2048]{1,0:T(8,128)(2,1)} async-done(((bf16[128,2048]{1,0:T(8,128)(2,1)}), bf16[256,2048]{1,0:T(8,128)(2,1)}) %all-gather.15.cloned.1.call-update) | async-done | bytes 1048592 | tf_op jit(solution)/shard_map/all_gather | solution.py:67
  34.6 24.7 %all-gather.23.cloned.1.call-done = bf16[2048,512]{1,0:T(8,128)(2,1)} async-done(((bf16[512,512]{1,0:T(8,128)(2,1)}), bf16[2048,512]{1,0:T(8,128)(2,1)}) %all-gather.23.cloned.1.call-update) | async-done | bytes 2097168 | tf_op jit(solution)/shard_map/all_gather | solution.py:78
  59.3 3.3 convolution_convert_fusion.10
  67.1 16.4 all-gather.17.cloned.1.call-done
  92.2 20.4 %all-gather.25.cloned.1.call-done = bf16[1024,512]{1,0:T(8,128)(2,1)} async-done(((bf16[256,512]{1,0:T(8,128)(2,1)}), bf16[1024,512]{1,0:T(8,128)(2,1)}) %all-gather.25.cloned.1.call-update) | async-done | bytes 1048592 | tf_op jit(solution)/shard_map/all_gather | solution.py:192
  114.7 34.0 %all-gather.21.cloned.1.call-done = bf16[2048,1024]{1,0:T(8,128)(2,1)} async-done(((bf16[512,1024]{1,0:T(8,128)(2,1)}), bf16[2048,1024]{1,0:T(8,128)(2,1)}) %all-gather.21.cloned.1.call-update) | async-done | bytes 4194320 | tf_op jit(solution)/shard_map/all_gather | solution.py:78
  148.8 3.4 fusion.82
  154.9 24.1 %all-gather.19.cloned.1.call-done = bf16[1024,512]{0,1:T(8,128)(2,1)} async-done(((bf16[256,512]{0,1:T(8,128)(2,1)}), bf16[1024,512]{0,1:T(8,128)(2,1)}) %all-gather.19.cloned.1.call-update) | async-done | bytes 1048592 | tf_op jit(solution)/shard_map/all_gather | solution.py:191
  191.6 23.4 %all-gather.27.cloned.1.call-done = bf16[2048,1024]{1,0:T(8,128)(2,1)} async-done(((bf16[512,1024]{1,0:T(8,128)(2,1)}), bf16[2048,1024]{1,0:T(8,128)(2,1)}) %all-gather.27.cloned.1.call-update) | async-done | bytes 4194320 | tf_op jit(solution)/shard_map/all_gather | solution.py:78
  215.1 5.0 multiply_convert_fusion.7
  220.0 31.1 %all-gather.29.cloned.1.call-done = bf16[1024,2048]{1,0:T(8,128)(2,1)} async-done(((bf16[256,2048]{1,0:T(8,128)(2,1)}), bf16[1024,2048]{1,0:T(8,128)(2,1)}) %all-gather.29.cloned.1.call-update) | async-done | bytes 4194320 | tf_op jit(solution)/shard_map/all_gather | solution.py:78
  251.1 4.6 convolution_convert_fusion.8
  257.7 18.0 %reduce-scatter.10.cloned.1.call-done = bf16[128,2048]{1,0:T(8,128)(2,1)} async-done(((bf16[256,2048]{1,0:T(8,128)(2,1)}), bf16[128,2048]{1,0:T(8,128)(2,1)}) %reduce-scatter.10.cloned.1.call-update) | async-done | bytes 524304 | tf_op jit(solution)/shard_map/reduce_scatter | solution.py:71
  282.4 18.6 %all-gather.31.cloned.1.call-done = bf16[256,2048]{1,0:T(8,128)(2,1)} async-done(((bf16[128,2048]{1,0:T(8,128)(2,1)}), bf16[256,2048]{1,0:T(8,128)(2,1)}) %all-gather.31.cloned.1.call-update) | async-done | bytes 1048592 | tf_op jit(solution)/shard_map/all_gather | solution.py:67
  301.0 84.3 %all-gather.33.cloned.1.call-done = bf16[2048,3072]{1,0:T(8,128)(2,1)} async-done(((bf16[512,3072]{1,0:T(8,128)(2,1)}), bf16[2048,3072]{1,0:T(8,128)(2,1)}) %all-gather.33.cloned.1.call-update) | async-done | bytes 12582928 | tf_op jit(solution)/shard_map/all_gather | solution.py:78
  385.2 10.0 fusion.83
  395.2 73.5 %all-gather.35.cloned.1.call-done = bf16[2048,3072]{1,0:T(8,128)(2,1)} async-done(((bf16[512,3072]{1,0:T(8,128)(2,1)}), bf16[2048,3072]{1,0:T(8,128)(2,1)}) %all-gather.35.cloned.1.call-update) | async-done | bytes 12582928 | tf_op jit(solution)/shard_map/all_gather | solution.py:78
  468.7 10.0 fusion.84
  478.7 12.9 all-gather.39.cloned.1.call-done
  491.6 84.1 %all-gather.37.cloned.1.call-done = bf16[3072,2048]{1,0:T(8,128)(2,1)} async-done(((bf16[768,2048]{1,0:T(8,128)(2,1)}), bf16[3072,2048]{1,0:T(8,128)(2,1)}) %all-gather.37.cloned.1.call-update) | async-done | bytes 12582928 | tf_op jit(solution)/shard_map/all_gather | solution.py:78
  575.7 13.4 multiply_convert_fusion
  589.1 7.2 fusion.85
  596.3 9.1 fusion.20
  605.5 19.9 %reduce-scatter.14.cloned.1.call-done = bf16[128,2048]{1,0:T(8,128)(2,1)} async-done(((bf16[256,2048]{1,0:T(8,128)(2,1)}), bf16[128,2048]{1,0:T(8,128)(2,1)}) %reduce-scatter.14.cloned.1.call-update) | async-done | bytes 524304 | tf_op jit(solution)/shard_map/reduce_scatter | solution.py:71
  632.1 20.1 %all-gather.41.cloned.1.call-done = bf16[256,2048]{1,0:T(8,128)(2,1)} async-done(((bf16[128,2048]{1,0:T(8,128)(2,1)}), bf16[256,2048]{1,0:T(8,128)(2,1)}) %all-gather.41.cloned.1.call-update) | async-done | bytes 1048592 | tf_op jit(solution)/shard_map/all_gather | solution.py:67
  652.1 5.5 multiply_convert_fusion.4
  661.2 5.6 bitcast_convert_fusion
  666.8 5.7 fusion.2
  677.8 4.7 convolution_convert_fusion.3
  682.5 9.8 convolution_convert_fusion
  707.2 3.3 convolution_convert_fusion.4
  713.9 7.4 reduce-scatter.16.cloned.1.call-done
  733.9 29.4 %pad_maximum_fusion.1 = bf16[2048,3072]{0,1:T(8,128)(2,1)} fusion(bf16[2048,1024]{0,1:T(8,128)(2,1)S(1)} %copy-done.3, bf16[2048,512]{0,1:T(8,128)(2,1)S(1)} %convolution_convert_fusion.6, bf16[2048,512]{0,1:T(8,128)(2,1)S(1)} %convolution_convert_fusion.7, bf16[2048,1024]{0,1:T(8,128)(2,1)S(1)} %copy-done.4), kind=kLoop, calls=%fused_computation.1 | loop fusion | flops 50331648 | bytes 25165824 | tf_op jit(solution)/shard_map/concatenate | solution.py:105
  764.5 8.0 convolution_convert_fusion.1
  772.5 6.9 convolution_convert_fusion.2
  779.4 20.9 %pad_maximum_fusion = bf16[2048,6144]{1,0:T(8,128)(2,1)} fusion(bf16[2048,3072]{1,0:T(8,128)(2,1)} %convolution_convert_fusion.1, bf16[2048,3072]{1,0:T(8,128)(2,1)} %convolution_convert_fusion.2), kind=kLoop, calls=%fused_computation | loop fusion | flops 50331648 | bytes 50331648 | tf_op jit(solution)/shard_map/concatenate | solution.py:105
  801.4 3.6 fusion.88
  810.2 9.8 convolution_convert_fusion.9
  820.1 50.4 %reduce-scatter.26.cloned.1.call-done = bf16[768,2048]{1,0:T(8,128)(2,1)} async-done(((bf16[3072,2048]{1,0:T(8,128)(2,1)}), bf16[768,2048]{1,0:T(8,128)(2,1)}) %reduce-scatter.26.cloned.1.call-update) | async-done | bytes 3145744 | tf_op jit(solution)/shard_map/reduce_scatter | solution.py:104
  870.5 99.6 %reduce-scatter.20.cloned.1.call-done = bf16[512,3072]{0,1:T(8,128)(2,1)} async-done(((bf16[2048,3072]{0,1:T(8,128)(2,1)}), bf16[512,3072]{0,1:T(8,128)(2,1)}) %reduce-scatter.20.cloned.1.call-update) | async-done | bytes 3145744 | tf_op jit(solution)/shard_map/reduce_scatter | solution.py:104
  970.1 184.5 %reduce-scatter.24.cloned.1.call-done = bf16[512,6144]{1,0:T(8,128)(2,1)} async-done(((bf16[2048,6144]{1,0:T(8,128)(2,1)}), bf16[512,6144]{1,0:T(8,128)(2,1)}) %reduce-scatter.24.cloned.1.call-update) | async-done | bytes 6291472 | tf_op jit(solution)/shard_map/reduce_scatter | solution.py:104
  1162.9 15.0 reduce-scatter.18.cloned.1.call-done
  1179.4 41.0 %all-reduce = (f32[2048]{0:T(1024)}, f32[128]{0:T(128)}, f32[128]{0:T(128)}, f32[2048]{0:T(1024)}) all-reduce(f32[2048]{0:T(1024)S(1)} %get-tuple-element.44, f32[128]{0:T(128)S(1)} %fusion.51, f32[128]{0:T(128)S(1)} %fusion.62, f32[2048]{0:T(1024)S(1)} %copy-done.46), channel_id=1, replica_groups=mesh['fsdp'=4,'ctx'=4,'tp'=2] {'fsdp','ctx','tp'}, use_global_device_ids=true, to_apply=%region_17.18 | all-reduce | flops 4352 | bytes 34816 | tf_op jit(solution)/shard_map/psum | solution.py:301
  1220.5 3.4 fusion.39
  1223.9 440.3 %all-reduce.4.cloned.1.call-done = (bf16[512,3072]{0,1:T(8,128)(2,1)}, bf16[512,6144]{1,0:T(8,128)(2,1)}, bf16[256,2048]{1,0:T(8,128)(2,1)}, bf16[768,2048]{1,0:T(8,128)(2,1)}) async-done(((bf16[512,3072]{0,1:T(8,128)(2,1)}, bf16[512,6144]{1,0:T(8,128)(2,1)}, bf16[256,2048]{1,0:T(8,128)(2,1)}, bf16[768,2048]{1,0:T(8,128)(2,1)}), (bf16[512,3072]{0,1:T(8,128)(2,1)}, bf16[512,6144]{1,0:T(8,128)(2,1)}, ...) | async-done | bytes 13631504 | tf_op jit(solution)/shard_map/psum | solution.py:121
  1664.2 4.3 fusion.76
  1678.7 9.4 fusion.75
  1688.1 3.5 convert_element_type.187
  (269 shorter events, 116.5 us)
Async XLA Ops:
  7.2 56.1 %copy-start.63 = (bf16[128]{0:T(256)(128)(2,1)S(1)}, bf16[128]{0:T(256)(128)(2,1)}, u32[]{:S(2)}) copy-start(bf16[128]{0:T(256)(128)(2,1)} %param.20) | copy-start | bytes 772
  7.2 56.1 %copy-start.59 = (s32[1,2]{1,0:T(1,128)S(1)}, s32[1,2]{1,0:T(1,128)}, u32[]{:S(2)}) copy-start(s32[1,2]{1,0:T(1,128)} %param.17) | copy-start | bytes 28
  7.2 27.4 %all-gather.15.cloned.1.call-start = ((), (), s32[]{:S(2)}) async-start(), calls=%async_computation.9 | async-start | bytes 1572864 | tf_op jit(solution)/shard_map/all_gather | solution.py:67
  11.2 48.0 %all-gather.23.cloned.1.call-start = ((), (), s32[]{:S(2)}) async-start(), calls=%async_computation.13 | async-start | bytes 2621440 | tf_op jit(solution)/shard_map/all_gather | solution.py:78
  12.0 71.5 %all-gather.17.cloned.1.call-start = ((), (), s32[]{:S(2)}) async-start(), calls=%async_computation.10 | async-start | bytes 2621440 | tf_op jit(solution)/shard_map/all_gather | solution.py:78
  12.7 99.9 %all-gather.25.cloned.1.call-start = ((), (), s32[]{:S(2)}) async-start(), calls=%async_computation.14 | async-start | bytes 1310720 | tf_op jit(solution)/shard_map/all_gather | solution.py:192
  34.6 48.9 %copy-start.2 = (bf16[256,2048]{1,0:T(8,128)(2,1)S(1)}, bf16[256,2048]{1,0:T(8,128)(2,1)}, u32[]{:S(2)}) copy-start(bf16[256,2048]{1,0:T(8,128)(2,1)} %all-gather.15.cloned.1.call-done) | copy-start | bytes 3145732
  62.6 86.1 %all-gather.21.cloned.1.call-start = ((), (), s32[]{:S(2)}) async-start(), calls=%async_computation.12 | async-start | bytes 5242880 | tf_op jit(solution)/shard_map/all_gather | solution.py:78
  63.2 115.7 %all-gather.19.cloned.1.call-start = ((), (), s32[]{:S(2)}) async-start(), calls=%async_computation.11 | async-start | bytes 1310720 | tf_op jit(solution)/shard_map/all_gather | solution.py:191
  63.3 23.4 %copy-start.54 = (f32[128]{0:T(128)}, f32[128]{0:T(128)S(1)}, u32[]{:S(2)}) copy-start(f32[128]{0:T(128)S(1)} %convert_element_type.150) | copy-start | bytes 1540
  67.1 87.1 %copy-start.27 = (f32[256,64]{1,0:T(8,128)}, f32[256,64]{1,0:T(8,128)S(1)}, u32[]{:S(2)}) copy-start(f32[256,64]{1,0:T(8,128)S(1)} %get-tuple-element.85) | copy-start | bytes 196612
  86.0 28.8 %copy-start.14 = (f32[256,4,128]{2,1,0:T(4,128)}, f32[256,4,128]{2,1,0:T(4,128)S(1)}, u32[]{:S(2)}) copy-start(f32[256,4,128]{2,1,0:T(4,128)S(1)} %reshape.292) | copy-start | bytes 1572868
  88.5 126.6 %all-gather.27.cloned.1.call-start = ((), (), s32[]{:S(2)}) async-start(), calls=%async_computation.15 | async-start | bytes 5242880 | tf_op jit(solution)/shard_map/all_gather | solution.py:78
  89.2 161.9 %all-gather.29.cloned.1.call-start = ((), (), s32[]{:S(2)}) async-start(), calls=%async_computation.16 | async-start | bytes 5242880 | tf_op jit(solution)/shard_map/all_gather | solution.py:78
  90.0 185.7 %reduce-scatter.10.cloned.1.call-start = ((), (), s32[]{:S(2)}) async-start(), calls=%async_computation.17 | async-start | bytes 1572864 | tf_op jit(solution)/shard_map/reduce_scatter | solution.py:71
  90.6 63.2 %copy-start.57 = (f32[128]{0:T(128)}, f32[128]{0:T(128)S(1)}, u32[]{:S(2)}) copy-start(f32[128]{0:T(128)S(1)} %convert_element_type.153) | copy-start | bytes 1540
  154.8 27.5 %copy-start.17 = (bf16[256,8,64]{2,0,1:T(8,128)(2,1)}, bf16[256,8,64]{2,0,1:T(8,128)(2,1)S(1)}, u32[]{:S(2)}) copy-start(bf16[256,8,64]{2,0,1:T(8,128)(2,1)S(1)} %copy.52) | copy-start | bytes 786436
  154.9 27.4 %copy-start.19 = (bf16[256,8,64]{2,0,1:T(8,128)(2,1)}, bf16[256,8,64]{2,0,1:T(8,128)(2,1)S(1)}, u32[]{:S(2)}) copy-start(bf16[256,8,64]{2,0,1:T(8,128)(2,1)S(1)} %copy.51) | copy-start | bytes 786436
  220.0 55.7 %copy-start.1 = (bf16[128,2048]{1,0:T(8,128)(2,1)S(1)}, bf16[128,2048]{1,0:T(8,128)(2,1)}, u32[]{:S(2)}) copy-start(bf16[128,2048]{1,0:T(8,128)(2,1)} %param.15) | copy-start | bytes 1572868
  251.1 26.0 %copy-start.24 = (bf16[128,2048]{1,0:T(8,128)(2,1)S(1)}, bf16[128,2048]{1,0:T(8,128)(2,1)}, u32[]{:S(2)}) copy-start(bf16[128,2048]{1,0:T(8,128)(2,1)} %param.16) | copy-start | bytes 1572868
  255.8 45.2 %all-gather.31.cloned.1.call-start = ((), (), s32[]{:S(2)}) async-start(), calls=%async_computation.18 | async-start | bytes 1572864 | tf_op jit(solution)/shard_map/all_gather | solution.py:67
  279.5 105.7 %all-gather.33.cloned.1.call-start = ((), (), s32[]{:S(2)}) async-start(), calls=%async_computation.19 | async-start | bytes 15728640 | tf_op jit(solution)/shard_map/all_gather | solution.py:78
  280.3 188.5 %all-gather.35.cloned.1.call-start = ((), (), s32[]{:S(2)}) async-start(), calls=%async_computation.20 | async-start | bytes 15728640 | tf_op jit(solution)/shard_map/all_gather | solution.py:78
  280.8 210.8 %all-gather.39.cloned.1.call-start = ((), (), s32[]{:S(2)}) async-start(), calls=%async_computation.23 | async-start | bytes 1572864 | tf_op jit(solution)/shard_map/all_gather | solution.py:67
  281.6 294.2 %all-gather.37.cloned.1.call-start = ((), (), s32[]{:S(2)}) async-start(), calls=%async_computation.21 | async-start | bytes 15728640 | tf_op jit(solution)/shard_map/all_gather | solution.py:78
  282.2 343.2 %reduce-scatter.14.cloned.1.call-start = ((), (), s32[]{:S(2)}) async-start(), calls=%async_computation.24 | async-start | bytes 1572864 | tf_op jit(solution)/shard_map/reduce_scatter | solution.py:71
  596.3 29.1 %copy-start.6 = (bf16[128,2048]{1,0:T(8,128)(2,1)S(1)}, bf16[128,2048]{1,0:T(8,128)(2,1)}, u32[]{:S(2)}) copy-start(bf16[128,2048]{1,0:T(8,128)(2,1)} %reduce-scatter.10.cloned.1.call-done) | copy-start | bytes 1572868
  605.4 46.7 %all-gather.41.cloned.1.call-start = ((), (), s32[]{:S(2)}) async-start(), calls=%async_computation.25 | async-start | bytes 1572864 | tf_op jit(solution)/shard_map/all_gather | solution.py:67
  630.7 90.6 %reduce-scatter.16.cloned.1.call-start = ((), (), s32[]{:S(2)}) async-start(), calls=%async_computation.26 | async-start | bytes 2621440 | tf_op jit(solution)/shard_map/reduce_scatter | solution.py:277
  652.1 9.0 copy-start.49
  666.7 7.7 copy-start.18
  677.7 142.4 %reduce-scatter.22.cloned.1.call-start = ((), (), s32[]{:S(2)}) async-start(), calls=%async_computation.29 | async-start | bytes 5242880 | tf_op jit(solution)/shard_map/reduce_scatter | solution.py:104
  682.5 188.0 %reduce-scatter.26.cloned.1.call-start = ((), (), s32[]{:S(2)}) async-start(), calls=%async_computation.31 | async-start | bytes 15728640 | tf_op jit(solution)/shard_map/reduce_scatter | solution.py:104
  692.3 277.8 %reduce-scatter.20.cloned.1.call-start = ((), (), s32[]{:S(2)}) async-start(), calls=%async_computation.28 | async-start | bytes 15728640 | tf_op jit(solution)/shard_map/reduce_scatter | solution.py:104
  713.9 13.6 copy-start.15
  713.9 13.6 copy-start.56
  763.3 391.4 %reduce-scatter.24.cloned.1.call-start = ((), (), s32[]{:S(2)}) async-start(), calls=%async_computation.30 | async-start | bytes 31457280 | tf_op jit(solution)/shard_map/reduce_scatter | solution.py:104
  764.5 8.0 copy-start.37
  800.3 377.6 %reduce-scatter.18.cloned.1.call-start = ((), (), s32[]{:S(2)}) async-start(), calls=%async_computation.27 | async-start | bytes 1572864 | tf_op jit(solution)/shard_map/reduce_scatter | solution.py:71
  810.1 410.3 %reduce-scatter.12.cloned.1.call-start = ((), (), s32[]{:S(2)}) async-start(), calls=%async_computation.22 | async-start | bytes 1572864 | tf_op jit(solution)/shard_map/reduce_scatter | solution.py:71
  820.0 844.1 %all-reduce.4.cloned.1.call-start = ((), (), s32[]{:S(2)}) async-start(), calls=%async_computation.32 | async-start | bytes 27262976 | tf_op jit(solution)/shard_map/psum | solution.py:121
  1154.7 23.2 %copy-start.45 = (f32[2048]{0:T(1024)S(1)}, f32[2048]{0:T(1024)}, u32[]{:S(2)}) copy-start(f32[2048]{0:T(1024)} %copy-done.44) | copy-start | bytes 24580
  1154.7 23.2 %copy-start.53 = (f32[128]{0:T(128)S(1)}, f32[128]{0:T(128)}, u32[]{:S(2)}) copy-start(f32[128]{0:T(128)} %copy-done.52) | copy-start | bytes 1540
  1156.7 22.7 %copy-start.46 = (f32[2048]{0:T(1024)S(1)}, f32[2048]{0:T(1024)}, u32[]{:S(2)}) copy-start(f32[2048]{0:T(1024)} %get-tuple-element.42) | copy-start | bytes 24580
  1156.7 63.7 %copy-start.48 = (f32[128]{0:T(128)S(1)}, f32[128]{0:T(128)}, u32[]{:S(2)}) copy-start(f32[128]{0:T(128)} %compare_convert_fusion) | copy-start | bytes 1540
  1156.7 63.7 %copy-start.51 = (f32[128]{0:T(128)S(1)}, f32[128]{0:T(128)}, u32[]{:S(2)}) copy-start(f32[128]{0:T(128)} %copy-done.50) | copy-start | bytes 1540
  1156.7 63.7 %copy-start.61 = (f32[128]{0:T(128)S(1)}, f32[128]{0:T(128)}, u32[]{:S(2)}) copy-start(f32[128]{0:T(128)} %copy-done.60) | copy-start | bytes 1540
  1678.7 9.4 copy-start.29
  (41 other events, 141.3 us)
Sparse Core Ops, SparseCore 0:
  11.4 23.1 all-gather.14
  36.1 23.1 all-gather.22
  60.8 22.5 all-gather.16
  85.4 27.1 all-gather.24
  114.0 34.6 all-gather.20
  150.8 28.1 all-gather.18
  180.5 34.4 all-gather.26
  216.6 34.4 all-gather.28
  255.9 19.8 reduce-scatter.9
  279.6 21.2 all-gather.30
  302.5 82.6 all-gather.32
  386.6 82.0 all-gather.34
  470.9 20.6 all-gather.38
  493.0 82.6 all-gather.36
  605.6 19.8 reduce-scatter.13
  630.8 21.2 all-gather.40
  677.8 43.3 reduce-scatter.15
  724.2 44.0 reduce-scatter.21
  770.9 99.6 reduce-scatter.25
  873.0 97.1 reduce-scatter.19
  972.7 181.8 reduce-scatter.23
  1157.5 20.3 reduce-scatter.17
  1180.8 20.7 reduce-scatter.11
  1204.3 459.8 all-reduce.3
where the time goes:
time: 1700 us
  waiting for transfers between devices  1330 us (78%)
  matrix products  151 us (9%)
  other arithmetic  99.3 us (6%)
  local copies, waits for them, and re-layouts  57.9 us (3%)
  blocking collectives  41 us (2%)
  between operations  17 us (1%)
    psum x1, waiting for transfers between devices, weight_grads(): summed = lax.psum(shared, 'ctx').astype(jnp.float32)  440 us
    all_gather x8, waiting for transfers between devices, fold_product(): lax.all_gather(a, 'fsdp', axis=0, tiled=True)  372 us
    reduce_scatter x4, waiting for transfers between devices, weight_grads(): lax.psum_scatter(jnp.concatenate([lax.dot_general(left_rows, grad_part, (...  335 us
    all_gather x4, waiting for transfers between devices, to_block(): return lax.all_gather(local_part, 'tp', axis=0, tiled=True)  73.3 us
    reduce_scatter x4, waiting for transfers between devices, to_share(): lax.psum_scatter(partial_rows.astype(jnp.bfloat16), 'tp', scatter_dimensi...  53 us
    concatenate x2, other arithmetic, weight_grads(): jnp.concatenate([lax.dot_general(left_rows, grad_part, (((0,), (0,)), (()...  50.3 us
    dot_general x8, matrix products, fold_product(): jnp.dot(left_rows, weight_part, preferred_element_type=jnp.float32)  48.5 us
    psum x1, blocking collectives, body(): lax.psum((gain_one_grad, query_gain_grad, key_gain_grad, gain_two_grad),...  41 us
  transfers between devices with their start and end apart: 24, of which 22 were waited for; matrix products, arithmetic and copies ran while one was open for 12% of the time, Pallas kernels for 0%

commit v1 on v0

--- a/solution.py
+++ b/solution.py
@@ -319,9 +319,312 @@
     )
 
 
+def xor_pairs(count, mask):
+    return [(i, i ^ mask) for i in range(count)]
+
+
+def swap_plane(value, fsdp_mask, tp_mask):
+    fsdp_size, tp_size = lax.axis_size("fsdp"), lax.axis_size("tp")
+    if tp_mask == 0:
+        return lax.ppermute(value, "fsdp", xor_pairs(fsdp_size, fsdp_mask))
+    if fsdp_mask == 0:
+        return lax.ppermute(value, "tp", xor_pairs(tp_size, tp_mask))
+    return lax.ppermute(
+        value,
+        ("fsdp", "tp"),
+        xor_pairs(fsdp_size * tp_size, fsdp_mask * tp_size + tp_mask),
+    )
+
+
+def swap_ranks(value):
+    size = lax.axis_size("fsdp")
+    pairs = [(a * size + b, b * size + a) for a in range(size) for b in range(size)]
+    return lax.ppermute(value, ("fsdp", "ctx"), pairs)
+
+
+PIECES = ((0, 0), (0, 1), (2, 0), (2, 1))
+
+
+def plane_gather(own):
+    near = [own if masks == (0, 0) else swap_plane(own, *masks) for masks in PIECES]
+    far = [swap_plane(piece, 1, 0) for piece in near]
+    return jnp.concatenate(near + far, axis=0)
+
+
+def plane_scatter(near_part, far_part):
+    rows = near_part.shape[0] // 4
+    half = near_part + swap_plane(far_part.astype(jnp.bfloat16), 1, 0).astype(jnp.float32)
+    total = half[:rows]
+    for place in range(1, 4):
+        piece = half[place * rows : (place + 1) * rows].astype(jnp.bfloat16)
+        total = total + swap_plane(piece, *PIECES[place]).astype(jnp.float32)
+    return total
+
+
+def dot_nn(a, b):
+    return jnp.dot(a, b, preferred_element_type=jnp.float32)
+
+
+def dot_nt(a, b):
+    return lax.dot_general(a, b, (((1,), (1,)), ((), ())), preferred_element_type=jnp.float32)
+
+
+def dot_tn(a, b):
+    return lax.dot_general(a, b, (((0,), (0,)), ((), ())), preferred_element_type=jnp.float32)
+
+
+def scatter_product(rows, weight, dot):
+    half = rows.shape[0] // 2
+    far_part = dot(rows[half:], weight)
+    near_part = dot(rows[:half], weight)
+    return plane_scatter(near_part, far_part)
+
+
+def chain_sum(part):
+    low = part.astype(jnp.bfloat16)
+    place = lax.axis_index("ctx")
+    inward = lax.ppermute(low, "ctx", [(0, 1), (3, 2)])
+    pair = (low.astype(jnp.float32) + inward.astype(jnp.float32)).astype(jnp.bfloat16)
+    across = lax.ppermute(pair, "ctx", [(1, 2), (2, 1)])
+    total = (pair.astype(jnp.float32) + across.astype(jnp.float32)).astype(jnp.bfloat16)
+    outward = lax.ppermute(total, "ctx", [(1, 0), (2, 3)])
+    inner = (place == 1) | (place == 2)
+    return jnp.where(inner, total, outward).astype(jnp.float32)
+
+
+def all_sum(value):
+    for axis, mask in (("fsdp", 1), ("fsdp", 2), ("tp", 1), ("ctx", 1), ("ctx", 2)):
+        value = value + lax.ppermute(value, axis, xor_pairs(lax.axis_size(axis), mask))
+    return value
+
+
+def weight_columns(weights, owner):
+    parts = []
+    for weight in weights:
+        width = weight.shape[1] // lax.axis_size("fsdp")
+        parts.append(lax.dynamic_slice_in_dim(weight, owner * width, width, 1))
+    return jnp.concatenate(parts, axis=1)
+
+
+def fetch_weights(weights):
+    me, size = lax.axis_index("fsdp"), lax.axis_size("fsdp")
+    rows = weights[0].shape[0]
+    whole = None
+    for mask in range(size):
+        part = weight_columns(weights, me ^ mask)
+        if mask:
+            part = swap_plane(part, mask, 0)
+        if whole is None:
+            whole = jnp.zeros((rows * size, part.shape[1]), part.dtype)
+        whole = lax.dynamic_update_slice_in_dim(whole, part, (me ^ mask) * rows, 0)
+    return whole
+
+
+def return_grads(left, right, widths):
+    me, size = lax.axis_index("fsdp"), lax.axis_size("fsdp")
+    rows = left.shape[1] // size
+    outs = [jnp.zeros((rows, width * size), jnp.float32) for width in widths]
+    for mask in range(size):
+        columns = lax.dynamic_slice_in_dim(left, (me ^ mask) * rows, rows, 1)
+        part = dot_tn(columns, right).astype(jnp.bfloat16)
+        if mask:
+            part = swap_plane(part, mask, 0)
+        summed = chain_sum(part)
+        offset = 0
+        for place, width in enumerate(widths):
+            outs[place] = lax.dynamic_update_slice_in_dim(
+                outs[place], summed[:, offset : offset + width], (me ^ mask) * width, 1
+            )
+            offset += width
+    return outs
+
+
+def plane_body(
+    layer_input,
+    cotangent,
+    lengths,
+    attn_norm,
+    query_norm_gain,
+    k_norm,
+    w_query,
+    key_weight,
+    value_weight,
+    w_out_gate,
+    w_output,
+    ffn_norm,
+    w_gate,
+    w_up,
+    w_down,
+):
+    fsdp_size, tp_size = lax.axis_size("fsdp"), lax.axis_size("tp")
+    fsdp_at, tp_at = lax.axis_index("fsdp"), lax.axis_index("tp")
+    local_rows = layer_input.shape[0]
+    row_slots = local_rows * fsdp_size * tp_size
+    query_heads = w_query.shape[1] // HEAD_SIZE // fsdp_size
+    query_width = query_heads * HEAD_SIZE
+    score_scale = HEAD_SIZE ** (-0.5)
+    gain_one = attn_norm.astype(jnp.float32)
+    gain_two = ffn_norm.astype(jnp.float32)
+    query_gain = query_norm_gain.astype(jnp.float32)
+    key_gain = k_norm.astype(jnp.float32)
+
+    inputs = swap_ranks(layer_input).astype(jnp.float32)
+    lengths = swap_ranks(lengths)
+    cot = swap_ranks(cotangent).astype(jnp.float32)
+
+    def slots_of(fsdp_index, tp_index):
+        return (fsdp_index * tp_size + tp_index) * local_rows + jnp.arange(
+            local_rows, dtype=jnp.int32
+        )
+
+    own_slots = slots_of(fsdp_at, tp_at)
+    own_valid = (segment_of(own_slots, lengths) < 2).astype(jnp.float32)[:, None]
+    slots = jnp.concatenate(
+        [
+            slots_of(fsdp_at ^ fsdp_mask ^ core, tp_at ^ tp_mask)
+            for core in (0, 1)
+            for fsdp_mask, tp_mask in PIECES
+        ]
+    )
+    segment = segment_of(slots, lengths)
+    position = position_of(slots, segment, lengths)
+
+    first_normed = plane_gather(apply_rms_norm(inputs, gain_one).astype(jnp.bfloat16))
+    attn_weights = fetch_weights((w_query, key_weight, value_weight, w_out_gate))
+    out_grad = cot * own_valid
+    ffn_grad = plane_gather(out_grad.astype(jnp.bfloat16))
+    ffn_weights = fetch_weights((w_gate, w_up))
+
+    projected = dot_nn(first_normed, attn_weights)
+    query_raw = projected[:, :query_width].reshape(row_slots, query_heads, HEAD_SIZE)
+    key_raw = projected[:, query_width : query_width + HEAD_SIZE].reshape(row_slots, 1, HEAD_SIZE)
+    value_low = projected[:, query_width + HEAD_SIZE : query_width + 2 * HEAD_SIZE].astype(
+        jnp.bfloat16
+    )
+    gate_logits = projected[:, query_width + 2 * HEAD_SIZE :]
+    query_rot = apply_rotary(apply_rms_norm(query_raw, query_gain), position, 1.0).astype(
+        jnp.bfloat16
+    )
+    key_rot = apply_rotary(apply_rms_norm(key_raw, key_gain), position, 1.0).astype(jnp.bfloat16)[
+        :, 0
+    ]
+
+    allowed = (segment[:, None] == segment[None, :]) & (slots[None, :] <= slots[:, None])
+    raw_scores = jnp.einsum("qgd,kd->gqk", query_rot, key_rot, preferred_element_type=jnp.float32)
+    scores = jnp.where(allowed, raw_scores * score_scale, NEG_FILL)
+    top = jnp.max(scores, axis=-1, keepdims=True)
+    weights = jnp.where(allowed, jnp.exp(scores - top), 0.0)
+    total = jnp.sum(weights, axis=-1, keepdims=True)
+    mixed = jnp.einsum(
+        "gqk,kd->gqd", weights.astype(jnp.bfloat16), value_low, preferred_element_type=jnp.float32
+    )
+    log_total = top + jnp.log(total)
+    attended = jnp.transpose(mixed / total, (1, 0, 2))
+    attended_rows = attended.reshape(row_slots, query_width)
+    gate_sig = jax.nn.sigmoid(gate_logits)
+    gated_mix = (attended_rows * gate_sig).astype(jnp.bfloat16)
+    attn_share = scatter_product(gated_mix, w_output, dot_nn)
+    hidden_in = inputs + own_valid * attn_share
+    normed_two = plane_gather(apply_rms_norm(hidden_in, gain_two).astype(jnp.bfloat16))
+
+    hidden_grad = dot_nt(ffn_grad, w_down)
+    pre = dot_nn(normed_two, ffn_weights)
+    hidden_width = w_down.shape[0]
+    gate_pre, up_pre = pre[:, :hidden_width], pre[:, hidden_width:]
+    gate_sigmoid = jax.nn.sigmoid(gate_pre)
+    activated = gate_pre * gate_sigmoid
+    hidden_act = (activated * up_pre).astype(jnp.bfloat16)
+    grad_w_down = chain_sum(dot_tn(hidden_act, ffn_grad))
+    gate_grad = (
+        hidden_grad * up_pre * gate_sigmoid * (1.0 + gate_pre * (1.0 - gate_sigmoid))
+    ).astype(jnp.bfloat16)
+    up_grad = (hidden_grad * activated).astype(jnp.bfloat16)
+    ffn_in_grads = jnp.concatenate([gate_grad, up_grad], axis=1)
+    normed_two_grad = scatter_product(ffn_in_grads, ffn_weights, dot_nt)
+    grad_w_gate, grad_w_up = return_grads(normed_two, ffn_in_grads, (hidden_width, hidden_width))
+    ffn_share = scatter_product(hidden_act, w_down, dot_nn)
+    layer_output = swap_ranks((hidden_in + own_valid * ffn_share).astype(jnp.bfloat16))
+
+    back_two, gain_two_grad = norm_back(hidden_in, gain_two, normed_two_grad)
+    hidden_total_grad = out_grad + back_two
+    attn_grad = plane_gather((own_valid * hidden_total_grad).astype(jnp.bfloat16))
+    gated_grad = dot_nt(attn_grad, w_output)
+    grad_w_output = chain_sum(dot_tn(gated_mix, attn_grad))
+    mixed_grad = (gated_grad * gate_sig).astype(jnp.bfloat16)
+    gate_logit_grad = (gated_grad * attended_rows * gate_sig * (1.0 - gate_sig)).astype(
+        jnp.bfloat16
+    )
+    mixed_grad_heads = mixed_grad.reshape(row_slots, query_heads, HEAD_SIZE)
+    delta_rows = jnp.transpose(
+        jnp.sum(mixed_grad_heads.astype(jnp.float32) * attended, axis=-1), (1, 0)
+    )[..., None]
+    raw_again = jnp.einsum("qgd,kd->gqk", query_rot, key_rot, preferred_element_type=jnp.float32)
+    soft = jnp.where(allowed, jnp.exp(raw_again * score_scale - log_total), 0.0)
+    prob_grad = jnp.einsum(
+        "qgd,kd->gqk", mixed_grad_heads, value_low, preferred_element_type=jnp.float32
+    )
+    score_grad = (soft * (prob_grad - delta_rows) * score_scale).astype(jnp.bfloat16)
+    query_rot_grad = jnp.einsum(
+        "gqk,kd->qgd", score_grad, key_rot, preferred_element_type=jnp.float32
+    )
+    key_rot_grad = jnp.einsum(
+        "gqk,qgd->kd", score_grad, query_rot, preferred_element_type=jnp.float32
+    )
+    value_grad = jnp.einsum(
+        "gqk,qgd->kd",
+        soft.astype(jnp.bfloat16),
+        mixed_grad_heads,
+        preferred_element_type=jnp.float32,
+    ).astype(jnp.bfloat16)
+    key_back, key_gain_grad = norm_back(
+        key_raw, key_gain, apply_rotary(key_rot_grad[:, None], position, -1.0)
+    )
+    query_back, query_gain_grad = norm_back(
+        query_raw, query_gain, apply_rotary(query_rot_grad, position, -1.0)
+    )
+    attn_in_grads = jnp.concatenate(
+        [
+            query_back.reshape(row_slots, query_width).astype(jnp.bfloat16),
+            key_back[:, 0].astype(jnp.bfloat16),
+            value_grad,
+            gate_logit_grad,
+        ],
+        axis=1,
+    )
+    normed_one_grad = scatter_product(attn_in_grads, attn_weights, dot_nt)
+    grad_w_query, grad_w_key, grad_w_value, grad_w_out_gate = return_grads(
+        first_normed, attn_in_grads, (query_width, HEAD_SIZE, HEAD_SIZE, query_width)
+    )
+    back_one, gain_one_grad = norm_back(inputs, gain_one, normed_one_grad)
+    input_grad = swap_ranks((hidden_total_grad + back_one).astype(jnp.bfloat16))
+    model_width = layer_input.shape[1]
+    gains = all_sum(
+        jnp.concatenate([gain_one_grad, gain_two_grad, query_gain_grad, key_gain_grad])[None]
+    )[0]
+    ends = (model_width, 2 * model_width, 2 * model_width + HEAD_SIZE)
+    return (
+        layer_output,
+        input_grad,
+        gains[: ends[0]],
+        gains[ends[1] : ends[2]],
+        gains[ends[2] :],
+        grad_w_query,
+        grad_w_key,
+        grad_w_value,
+        grad_w_out_gate,
+        grad_w_output,
+        gains[ends[0] : ends[1]],
+        grad_w_gate,
+        grad_w_up,
+        grad_w_down,
+    )
+
+
 def solution(mesh):
+    sizes = dict(mesh.shape)
+    plane = (sizes["fsdp"], sizes["ctx"], sizes["tp"]) == (4, 4, 2)
     return jax.shard_map(
-        body,
+        plane_body if plane else body,
         mesh=mesh,
         in_specs=(
             P(("fsdp", "ctx", "tp"), None),

time: 1700 us -> 1090 us (0.64)
  waiting for transfers between devices: 1330 us -> 609 us
  starting transfers between devices: 2.09 us -> 211 us
  matrix products: 151 us -> 101 us
  blocking collectives: 41 us -> 0 us
    ppermute x0 -> x96, waiting for transfers between devices: none -> 609 us  [the longest x10 195 us: chain_sum(): inward = lax.ppermute(low, 'ctx', [(0, 1), (3, 2)])]
    all_gather x14 -> x0, waiting for transfers between devices: 489 us -> none  [the longest x8 372 us: fold_product(): lax.all_gather(a, 'fsdp', axis=0, tiled=True)]
    psum x1 -> x0, waiting for transfers between devices: 440 us -> none  [weight_grads(): summed = lax.psum(shared, 'ctx').astype(jnp.float32)]
    reduce_scatter x9 -> x0, waiting for transfers between devices: 395 us -> none  [the longest x4 335 us: weight_grads(): lax.psum_scatter(jnp.concatenate([lax.dot_general(left_rows, grad_part, (...]
    ppermute x0 -> x96, starting transfers between devices: none -> 211 us  [the longest x10 70 us: chain_sum(): inward = lax.ppermute(low, 'ctx', [(0, 1), (3, 2)])]
    dot_general x30 -> x28, matrix products: 151 us -> 101 us  [the longest x6 36 us: dot_nt(): lax.dot_general(a, b, (((1,), (1,)), ((), ())), preferred_element_type=jn...]
    concatenate x3 -> x9, other arithmetic: 51.8 us -> 6.77 us  [the longest x6 6.61 us: weight_columns(): return jnp.concatenate(parts, axis=1)]
    psum x1 -> x0, blocking collectives: 41 us -> none  [body(): lax.psum((gain_one_grad, query_gain_grad, key_gain_grad, gain_two_grad),...]
  transfers between devices with their start and end apart: 24 -> 96, of which waited for: 22 -> 37; matrix products, arithmetic and copies ran while one was open for 12% -> 20% of each run, Pallas kernels for 0% -> 0%
where the time goes in v1:
time: 1090 us; the launch traced here: 1080 us
  waiting for transfers between devices  609 us (56%)
  starting transfers between devices  211 us (19%)
  matrix products  101 us (9%)
  other arithmetic  87.7 us (8%)
  local copies, waits for them, and re-layouts  68.7 us (6%)
    ppermute x10, waiting for transfers between devices, chain_sum(): inward = lax.ppermute(low, 'ctx', [(0, 1), (3, 2)])  195 us
    ppermute x40, waiting for transfers between devices, swap_plane(): return lax.ppermute(value, 'fsdp', xor_pairs(fsdp_size, fsdp_mask))  126 us
    ppermute x10, waiting for transfers between devices, chain_sum(): outward = lax.ppermute(total, 'ctx', [(1, 0), (2, 3)])  88 us
    ppermute x5, waiting for transfers between devices, swap_ranks(): return lax.ppermute(value, ('fsdp', 'ctx'), pairs)  81.9 us
    ppermute x10, starting transfers between devices, chain_sum(): inward = lax.ppermute(low, 'ctx', [(0, 1), (3, 2)])  70 us
    ppermute x8, waiting for transfers between devices, swap_plane(): lax.ppermute(value, ('fsdp', 'tp'), xor_pairs(fsdp_size * tp_size, fsdp_m...  66.1 us
    ppermute x5, waiting for transfers between devices, all_sum(): lax.ppermute(value, axis, xor_pairs(lax.axis_size(axis), mask))  48.4 us
    ppermute x40, starting transfers between devices, swap_plane(): return lax.ppermute(value, 'fsdp', xor_pairs(fsdp_size, fsdp_mask))  43.2 us
  transfers between devices with their start and end apart: 96, of which 37 were waited for; matrix products, arithmetic and copies ran while one was open for 20% of the time, Pallas kernels for 0%

profile of v1, /device:TPU:1, one launch (start us, length us, event | category | flops | bytes accessed | tf_op | source)
XLA Modules:
  0.0 1082.1 jit_solution(17900881969944655932)
XLA Ops:
  0.7 4.8 collective-permute-start.1
  20.4 4.7 constant_dynamic-slice_fusion
  52.3 16.2 %collective-permute-done.11 = bf16[512,768]{1,0:T(8,128)(2,1)} collective-permute-done((bf16[512,768]{1,0:T(8,128)(2,1)}, bf16[512,768]{1,0:T(8,128)(2,1)}, u32[]{:S(2)}, u32[]{:S(2)}) %collective-permute-start.11) | collective-permute-done | bytes 786464 | tf_op jit(solution)/shard_map/ppermute | solution.py:329
  68.5 6.5 collective-permute-start.4
  77.1 5.8 collective-permute-done.3
  84.3 9.9 collective-permute-done.4
  97.4 7.0 fusion.143
  148.3 8.7 collective-permute-done.34
  172.8 30.6 %collective-permute-done.15 = bf16[128,2048]{1,0:T(8,128)(2,1)S(1)} collective-permute-done((bf16[128,2048]{1,0:T(8,128)(2,1)S(1)}, bf16[128,2048]{1,0:T(8,128)(2,1)S(1)}, u32[]{:S(2)}, u32[]{:S(2)}) %collective-permute-start.15) | collective-permute-done | bytes 524320 | tf_op jit(solution)/shard_map/ppermute | solution.py:332
  203.4 11.3 %collective-permute-done.14 = bf16[128,2048]{1,0:T(8,128)(2,1)S(1)} collective-permute-done((bf16[128,2048]{1,0:T(8,128)(2,1)S(1)}, bf16[128,2048]{1,0:T(8,128)(2,1)S(1)}, u32[]{:S(2)}, u32[]{:S(2)}) %collective-permute-start.14) | collective-permute-done | bytes 524320 | tf_op jit(solution)/shard_map/ppermute | solution.py:329
  220.4 30.6 %collective-permute-done.25 = bf16[512,1536]{1,0:T(8,128)(2,1)S(1)} collective-permute-done((bf16[512,1536]{1,0:T(8,128)(2,1)S(1)}, bf16[512,1536]{1,0:T(8,128)(2,1)S(1)}, u32[]{:S(2)}, u32[]{:S(2)}) %collective-permute-start.25) | collective-permute-done | bytes 1572896 | tf_op jit(solution)/shard_map/ppermute | solution.py:329
  252.8 6.8 collective-permute-done.17
  263.0 7.8 collective-permute-done.18
  274.3 10.4 fusion.144
  284.7 6.6 multiply_convert_fusion
  294.5 6.6 convolution_convert_fusion.7
  314.5 13.6 %collective-permute-done.78 = bf16[512,1536]{1,0:T(8,128)(2,1)S(1)} collective-permute-done((bf16[512,1536]{1,0:T(8,128)(2,1)S(1)}, bf16[512,1536]{1,0:T(8,128)(2,1)S(1)}, u32[]{:S(2)}, u32[]{:S(2)}) %collective-permute-start.78) | collective-permute-done | bytes 1572896 | tf_op jit(solution)/shard_map/ppermute | solution.py:386
  331.6 8.7 fusion.140
  343.0 3.8 fusion.141
  350.6 33.4 %collective-permute-done.89 = bf16[512,1536]{1,0:T(8,128)(2,1)S(1)} collective-permute-done((bf16[512,1536]{1,0:T(8,128)(2,1)S(1)}, bf16[512,1536]{1,0:T(8,128)(2,1)S(1)}, u32[]{:S(2)}, u32[]{:S(2)}) %collective-permute-start.89) | collective-permute-done | bytes 1572896 | tf_op jit(solution)/shard_map/ppermute | solution.py:329
  386.4 8.8 collective-permute-done.42
  396.4 9.1 collective-permute-done.41
  407.6 5.1 convolution_convert_fusion
  419.3 8.9 collective-permute-done.28
  441.4 72.6 %collective-permute-done.82 = bf16[512,1536]{1,0:T(8,128)(2,1)S(1)} collective-permute-done((bf16[512,1536]{1,0:T(8,128)(2,1)}, bf16[512,1536]{1,0:T(8,128)(2,1)S(1)}, u32[]{:S(2)}, u32[]{:S(2)}) %collective-permute-start.82) | collective-permute-done | bytes 1572896 | tf_op jit(solution)/shard_map/ppermute | solution.py:386
  516.6 31.1 %collective-permute-done.86 = bf16[512,1536]{1,0:T(8,128)(2,1)S(1)} collective-permute-done((bf16[512,1536]{1,0:T(8,128)(2,1)}, bf16[512,1536]{1,0:T(8,128)(2,1)S(1)}, u32[]{:S(2)}, u32[]{:S(2)}) %collective-permute-start.86) | collective-permute-done | bytes 1572896 | tf_op jit(solution)/shard_map/ppermute | solution.py:386
  550.4 5.0 collective-permute-start.46
  555.3 6.1 add_convert_fusion.1
  561.4 20.0 %collective-permute-done.90 = bf16[512,1536]{1,0:T(8,128)(2,1)S(1)} collective-permute-done((bf16[512,1536]{1,0:T(8,128)(2,1)}, bf16[512,1536]{1,0:T(8,128)(2,1)S(1)}, u32[]{:S(2)}, u32[]{:S(2)}) %collective-permute-start.90) | collective-permute-done | bytes 1572896 | tf_op jit(solution)/shard_map/ppermute | solution.py:386
  581.4 6.4 collective-permute-start.30
  591.6 14.5 %collective-permute-done.30 = bf16[128,2048]{1,0:T(8,128)(2,1)S(1)} collective-permute-done((bf16[128,2048]{1,0:T(8,128)(2,1)S(1)}, bf16[128,2048]{1,0:T(8,128)(2,1)S(1)}, u32[]{:S(2)}, u32[]{:S(2)}) %collective-permute-start.30) | collective-permute-done | bytes 524320 | tf_op jit(solution)/shard_map/ppermute | solution.py:342
  619.3 3.7 fusion.2
  642.1 9.8 collective-permute-start.60
  656.1 5.2 convolution_convert_fusion.6
  661.9 6.0 collective-permute-done.60
  676.0 42.5 %collective-permute-start.75 = (bf16[256,2048]{1,0:T(8,128)(2,1)S(1)}, bf16[256,2048]{1,0:T(8,128)(2,1)S(1)}, u32[]{:S(2)}, u32[]{:S(2)}) collective-permute-start(bf16[256,2048]{1,0:T(8,128)(2,1)S(1)} %convolution_convert_fusion.9), channel_id=1, source_target_pairs={{0,2},{6,4},{1,3},{7,5},{8,10},{14,12},{9,11},{15,13},{16,18},{22,... | collective-permute-start | bytes 3145736 | tf_op jit(solution)/shard_map/ppermute | solution.py:386
  728.9 11.5 %collective-permute-done.75 = bf16[256,2048]{1,0:T(8,128)(2,1)S(1)} collective-permute-done((bf16[256,2048]{1,0:T(8,128)(2,1)S(1)}, bf16[256,2048]{1,0:T(8,128)(2,1)S(1)}, u32[]{:S(2)}, u32[]{:S(2)}) %collective-permute-start.75) | collective-permute-done | bytes 1048608 | tf_op jit(solution)/shard_map/ppermute | solution.py:386
  740.4 4.1 collective-permute-start.72
  747.9 9.4 collective-permute-done.64
  758.4 15.8 %collective-permute-done.68 = bf16[512,768]{1,0:T(8,128)(2,1)S(1)} collective-permute-done((bf16[512,768]{1,0:T(8,128)(2,1)S(1)}, bf16[512,768]{1,0:T(8,128)(2,1)S(1)}, u32[]{:S(2)}, u32[]{:S(2)}) %collective-permute-start.68) | collective-permute-done | bytes 786464 | tf_op jit(solution)/shard_map/ppermute | solution.py:386
  775.6 15.4 %collective-permute-done.72 = bf16[512,768]{1,0:T(8,128)(2,1)S(1)} collective-permute-done((bf16[512,768]{1,0:T(8,128)(2,1)S(1)}, bf16[512,768]{1,0:T(8,128)(2,1)S(1)}, u32[]{:S(2)}, u32[]{:S(2)}) %collective-permute-start.72) | collective-permute-done | bytes 786464 | tf_op jit(solution)/shard_map/ppermute | solution.py:386
  795.2 6.4 fusion.142
  802.7 57.8 %collective-permute-done.62 = bf16[512,768]{1,0:T(8,128)(2,1)S(1)} collective-permute-done((bf16[512,768]{1,0:T(8,128)(2,1)S(1)}, bf16[512,768]{1,0:T(8,128)(2,1)S(1)}, u32[]{:S(2)}, u32[]{:S(2)}) %collective-permute-start.62) | collective-permute-done | bytes 786464 | tf_op jit(solution)/shard_map/ppermute | solution.py:390
  876.4 30.2 %collective-permute-done.92 = bf16[512,1536]{1,0:T(8,128)(2,1)} collective-permute-done((bf16[512,1536]{1,0:T(8,128)(2,1)S(1)}, bf16[512,1536]{1,0:T(8,128)(2,1)}, u32[]{:S(2)}, u32[]{:S(2)}) %collective-permute-start.92) | collective-permute-done | bytes 1572896 | tf_op jit(solution)/shard_map/ppermute | solution.py:390
  914.7 15.4 %collective-permute-start.55 = (f32[1,4352]{1,0:T(1,128)S(1)}, f32[1,4352]{1,0:T(1,128)S(1)}, u32[]{:S(2)}, u32[]{:S(2)}) collective-permute-start(f32[1,4352]{1,0:T(1,128)S(1)} %broadcast_in_dim.64), channel_id=1, source_target_pairs={{0,8},{8,0},{16,24},{24,16},{1,9},{9,1},{17,25},{25,17},{2,10},{10... | collective-permute-start | bytes 52232 | tf_op jit(solution)/shard_map/ppermute | solution.py:397
  938.8 41.1 %collective-permute-done.58 = f32[1,4352]{1,0:T(1,128)S(1)} collective-permute-done((f32[1,4352]{1,0:T(1,128)S(1)}, f32[1,4352]{1,0:T(1,128)S(1)}, u32[]{:S(2)}, u32[]{:S(2)}) %collective-permute-start.58) | collective-permute-done | bytes 17440 | tf_op jit(solution)/shard_map/ppermute | solution.py:397
  986.1 16.2 %collective-permute-start.54 = (bf16[128,2048]{1,0:T(8,128)(2,1)S(1)}, bf16[128,2048]{1,0:T(8,128)(2,1)S(1)}, u32[]{:S(2)}, u32[]{:S(2)}) collective-permute-start(bf16[128,2048]{1,0:T(8,128)(2,1)S(1)} %fusion.38), channel_id=1, source_target_pairs={{0,0},{2,8},{4,16},{6,24},{8,2},{10,10},{12,18},{14,26},{16,4},{18... | collective-permute-start | bytes 1572872 | tf_op jit(solution)/shard_map/ppermute | solution.py:342
  1005.1 67.3 %collective-permute-done.54 = bf16[128,2048]{1,0:T(8,128)(2,1)S(1)} collective-permute-done((bf16[128,2048]{1,0:T(8,128)(2,1)S(1)}, bf16[128,2048]{1,0:T(8,128)(2,1)S(1)}, u32[]{:S(2)}, u32[]{:S(2)}) %collective-permute-start.54) | collective-permute-done | bytes 524320 | tf_op jit(solution)/shard_map/ppermute | solution.py:342
  (535 shorter events, 298.3 us)
Async XLA Ops:
  17.5 51.0 %collective-permute-start.11 = (bf16[512,768]{1,0:T(8,128)(2,1)}, bf16[512,768]{1,0:T(8,128)(2,1)}, u32[]{:S(2)}, u32[]{:S(2)}) collective-permute-start(bf16[512,768]{1,0:T(8,128)(2,1)} %pad_maximum_fusion.8), channel_id=1, source_target_pairs={{0,24},{8,16},{16,8},{24,0},{1,25},{9,17},{17,9},{25,1},{2,26},{10... | collective-permute-start | bytes 2359304 | tf_op jit(solution)/shard_map/ppermute | solution.py:329
  30.4 138.4 %collective-permute-start.23 = (bf16[512,1536]{1,0:T(8,128)(2,1)}, bf16[512,1536]{1,0:T(8,128)(2,1)}, u32[]{:S(2)}, u32[]{:S(2)}) collective-permute-start(bf16[512,1536]{1,0:T(8,128)(2,1)} %pad_maximum_fusion.1), channel_id=1, source_target_pairs={{0,8},{8,0},{16,24},{24,16},{1,9},{9,1},{17,25},{25,17},{2,10},{10... | collective-permute-start | bytes 4718600 | tf_op jit(solution)/shard_map/ppermute | solution.py:329
  47.0 80.1 %collective-permute-start.31 = (bf16[128,2048]{1,0:T(8,128)(2,1)}, bf16[128,2048]{1,0:T(8,128)(2,1)}, u32[]{:S(2)}, u32[]{:S(2)}) collective-permute-start(bf16[128,2048]{1,0:T(8,128)(2,1)} %param.16), channel_id=1, source_target_pairs={{0,0},{2,8},{4,16},{6,24},{8,2},{10,10},{12,18},{14,26},{16,4},{18... | collective-permute-start | bytes 1572872 | tf_op jit(solution)/shard_map/ppermute | solution.py:342
  157.1 60.5 %collective-permute-start.24 = (bf16[512,1536]{1,0:T(8,128)(2,1)}, bf16[512,1536]{1,0:T(8,128)(2,1)S(1)}, u32[]{:S(2)}, u32[]{:S(2)}) collective-permute-start(bf16[512,1536]{1,0:T(8,128)(2,1)} %pad_maximum_fusion.2), channel_id=1, source_target_pairs={{0,16},{8,24},{16,0},{24,8},{1,17},{9,25},{17,1},{25,9},{2,18},{10... | collective-permute-start | bytes 4718600 | tf_op jit(solution)/shard_map/ppermute | solution.py:329
  166.1 48.6 %collective-permute-start.14 = (bf16[128,2048]{1,0:T(8,128)(2,1)S(1)}, bf16[128,2048]{1,0:T(8,128)(2,1)S(1)}, u32[]{:S(2)}, u32[]{:S(2)}) collective-permute-start(bf16[128,2048]{1,0:T(8,128)(2,1)S(1)} %get-tuple-element.69), channel_id=1, source_target_pairs={{0,16},{8,24},{16,0},{24,8},{1,17},{9,25},{17,1},{25,9},{2,18},{10... | collective-permute-start | bytes 1572872 | tf_op jit(solution)/shard_map/ppermute | solution.py:329
  167.5 47.3 %collective-permute-start.13 = (bf16[128,2048]{1,0:T(8,128)(2,1)S(1)}, bf16[128,2048]{1,0:T(8,128)(2,1)S(1)}, u32[]{:S(2)}, u32[]{:S(2)}) collective-permute-start(bf16[128,2048]{1,0:T(8,128)(2,1)S(1)} %get-tuple-element.67), channel_id=1, source_target_pairs={{0,1},{1,0},{2,3},{3,2},{4,5},{5,4},{6,7},{7,6},{8,9},{9,8},{10,11... | collective-permute-start | bytes 1572872 | tf_op jit(solution)/shard_map/ppermute | solution.py:331
  168.8 82.2 %collective-permute-start.25 = (bf16[512,1536]{1,0:T(8,128)(2,1)S(1)}, bf16[512,1536]{1,0:T(8,128)(2,1)S(1)}, u32[]{:S(2)}, u32[]{:S(2)}) collective-permute-start(bf16[512,1536]{1,0:T(8,128)(2,1)S(1)} %copy-done.51), channel_id=1, source_target_pairs={{0,24},{8,16},{16,8},{24,0},{1,25},{9,17},{17,9},{25,1},{2,26},{10... | collective-permute-start | bytes 4718600 | tf_op jit(solution)/shard_map/ppermute | solution.py:329
  216.7 42.9 %collective-permute-start.17 = (bf16[128,2048]{1,0:T(8,128)(2,1)S(1)}, bf16[128,2048]{1,0:T(8,128)(2,1)S(1)}, u32[]{:S(2)}, u32[]{:S(2)}) collective-permute-start(bf16[128,2048]{1,0:T(8,128)(2,1)S(1)} %get-tuple-element.32), channel_id=1, source_target_pairs={{0,16},{8,24},{16,0},{24,8},{1,17},{9,25},{17,1},{25,9},{2,18},{10... | collective-permute-start | bytes 1572872 | tf_op jit(solution)/shard_map/ppermute | solution.py:329
  218.9 52.0 %collective-permute-start.18 = (bf16[128,2048]{1,0:T(8,128)(2,1)S(1)}, bf16[128,2048]{1,0:T(8,128)(2,1)S(1)}, u32[]{:S(2)}, u32[]{:S(2)}) collective-permute-start(bf16[128,2048]{1,0:T(8,128)(2,1)S(1)} %get-tuple-element.32), channel_id=1, source_target_pairs={{0,17},{1,16},{8,25},{9,24},{16,1},{17,0},{24,9},{25,8},{2,19},{3,... | collective-permute-start | bytes 1572872 | tf_op jit(solution)/shard_map/ppermute | solution.py:332
  328.1 55.9 %collective-permute-start.89 = (bf16[512,1536]{1,0:T(8,128)(2,1)S(1)}, bf16[512,1536]{1,0:T(8,128)(2,1)S(1)}, u32[]{:S(2)}, u32[]{:S(2)}) collective-permute-start(bf16[512,1536]{1,0:T(8,128)(2,1)S(1)} %convolution_convert_fusion.2), channel_id=1, source_target_pairs={{0,24},{8,16},{16,8},{24,0},{1,25},{9,17},{17,9},{25,1},{2,26},{10... | collective-permute-start | bytes 4718600 | tf_op jit(solution)/shard_map/ppermute | solution.py:329
  340.5 54.7 %collective-permute-start.42 = (bf16[128,2048]{1,0:T(8,128)(2,1)S(1)}, bf16[128,2048]{1,0:T(8,128)(2,1)S(1)}, u32[]{:S(2)}, u32[]{:S(2)}) collective-permute-start(bf16[128,2048]{1,0:T(8,128)(2,1)S(1)} %get-tuple-element.62), channel_id=1, source_target_pairs={{0,17},{1,16},{8,25},{9,24},{16,1},{17,0},{24,9},{25,8},{2,19},{3,... | collective-permute-start | bytes 1572872 | tf_op jit(solution)/shard_map/ppermute | solution.py:332
  341.8 63.7 %collective-permute-start.41 = (bf16[128,2048]{1,0:T(8,128)(2,1)S(1)}, bf16[128,2048]{1,0:T(8,128)(2,1)S(1)}, u32[]{:S(2)}, u32[]{:S(2)}) collective-permute-start(bf16[128,2048]{1,0:T(8,128)(2,1)S(1)} %get-tuple-element.63), channel_id=1, source_target_pairs={{0,16},{8,24},{16,0},{24,8},{1,17},{9,25},{17,1},{25,9},{2,18},{10... | collective-permute-start | bytes 1572872 | tf_op jit(solution)/shard_map/ppermute | solution.py:329
  348.0 88.8 %collective-permute-start.79 = (bf16[512,1536]{1,0:T(8,128)(2,1)}, bf16[512,1536]{1,0:T(8,128)(2,1)}, u32[]{:S(2)}, u32[]{:S(2)}) collective-permute-start(bf16[512,1536]{1,0:T(8,128)(2,1)} %add_convert_fusion.9), channel_id=1, source_target_pairs={{2,4},{4,2},{3,5},{5,3},{10,12},{12,10},{11,13},{13,11},{18,20},{2... | collective-permute-start | bytes 4718600 | tf_op jit(solution)/shard_map/ppermute | solution.py:388
  349.9 62.8 %collective-permute-start.40 = (bf16[128,2048]{1,0:T(8,128)(2,1)S(1)}, bf16[128,2048]{1,0:T(8,128)(2,1)S(1)}, u32[]{:S(2)}, u32[]{:S(2)}) collective-permute-start(bf16[128,2048]{1,0:T(8,128)(2,1)S(1)} %get-tuple-element.61), channel_id=1, source_target_pairs={{0,1},{1,0},{2,3},{3,2},{4,5},{5,4},{6,7},{7,6},{8,9},{9,8},{10,11... | collective-permute-start | bytes 1572872 | tf_op jit(solution)/shard_map/ppermute | solution.py:331
  412.7 137.6 %collective-permute-start.93 = (bf16[768,2048]{1,0:T(8,128)(2,1)}, bf16[768,2048]{1,0:T(8,128)(2,1)}, u32[]{:S(2)}, u32[]{:S(2)}) collective-permute-start(bf16[768,2048]{1,0:T(8,128)(2,1)} %convolution_convert_fusion), channel_id=1, source_target_pairs={{0,2},{6,4},{1,3},{7,5},{8,10},{14,12},{9,11},{15,13},{16,18},{22,... | collective-permute-start | bytes 9437192 | tf_op jit(solution)/shard_map/ppermute | solution.py:386
  417.9 96.1 %collective-permute-start.82 = (bf16[512,1536]{1,0:T(8,128)(2,1)}, bf16[512,1536]{1,0:T(8,128)(2,1)S(1)}, u32[]{:S(2)}, u32[]{:S(2)}) collective-permute-start(bf16[512,1536]{1,0:T(8,128)(2,1)} %copy-done.56), channel_id=1, source_target_pairs={{0,2},{6,4},{1,3},{7,5},{8,10},{14,12},{9,11},{15,13},{16,18},{22,... | collective-permute-start | bytes 4718600 | tf_op jit(solution)/shard_map/ppermute | solution.py:386
  428.2 119.5 %collective-permute-start.86 = (bf16[512,1536]{1,0:T(8,128)(2,1)}, bf16[512,1536]{1,0:T(8,128)(2,1)S(1)}, u32[]{:S(2)}, u32[]{:S(2)}) collective-permute-start(bf16[512,1536]{1,0:T(8,128)(2,1)} %copy-done.54), channel_id=1, source_target_pairs={{0,2},{6,4},{1,3},{7,5},{8,10},{14,12},{9,11},{15,13},{16,18},{22,... | collective-permute-start | bytes 4718600 | tf_op jit(solution)/shard_map/ppermute | solution.py:386
  429.6 151.8 %collective-permute-start.90 = (bf16[512,1536]{1,0:T(8,128)(2,1)}, bf16[512,1536]{1,0:T(8,128)(2,1)S(1)}, u32[]{:S(2)}, u32[]{:S(2)}) collective-permute-start(bf16[512,1536]{1,0:T(8,128)(2,1)} %copy-done.52), channel_id=1, source_target_pairs={{0,2},{6,4},{1,3},{7,5},{8,10},{14,12},{9,11},{15,13},{16,18},{22,... | collective-permute-start | bytes 4718600 | tf_op jit(solution)/shard_map/ppermute | solution.py:386
  436.8 152.5 %collective-permute-start.43 = (bf16[128,2048]{1,0:T(8,128)(2,1)S(1)}, bf16[128,2048]{1,0:T(8,128)(2,1)S(1)}, u32[]{:S(2)}, u32[]{:S(2)}) collective-permute-start(bf16[128,2048]{1,0:T(8,128)(2,1)S(1)} %get-tuple-element.26), channel_id=1, source_target_pairs={{0,1},{1,0},{2,3},{3,2},{4,5},{5,4},{6,7},{7,6},{8,9},{9,8},{10,11... | collective-permute-start | bytes 1572872 | tf_op jit(solution)/shard_map/ppermute | solution.py:331
  514.0 76.7 %collective-permute-start.44 = (bf16[128,2048]{1,0:T(8,128)(2,1)S(1)}, bf16[128,2048]{1,0:T(8,128)(2,1)S(1)}, u32[]{:S(2)}, u32[]{:S(2)}) collective-permute-start(bf16[128,2048]{1,0:T(8,128)(2,1)S(1)} %get-tuple-element.26), channel_id=1, source_target_pairs={{0,16},{8,24},{16,0},{24,8},{1,17},{9,25},{17,1},{25,9},{2,18},{10... | collective-permute-start | bytes 1572872 | tf_op jit(solution)/shard_map/ppermute | solution.py:329
  547.7 43.1 %collective-permute-start.45 = (bf16[128,2048]{1,0:T(8,128)(2,1)S(1)}, bf16[128,2048]{1,0:T(8,128)(2,1)S(1)}, u32[]{:S(2)}, u32[]{:S(2)}) collective-permute-start(bf16[128,2048]{1,0:T(8,128)(2,1)S(1)} %get-tuple-element.26), channel_id=1, source_target_pairs={{0,17},{1,16},{8,25},{9,24},{16,1},{17,0},{24,9},{25,8},{2,19},{3,... | collective-permute-start | bytes 1572872 | tf_op jit(solution)/shard_map/ppermute | solution.py:332
  550.4 41.1 %collective-permute-start.46 = (bf16[128,2048]{1,0:T(8,128)(2,1)S(1)}, bf16[128,2048]{1,0:T(8,128)(2,1)S(1)}, u32[]{:S(2)}, u32[]{:S(2)}) collective-permute-start(bf16[128,2048]{1,0:T(8,128)(2,1)S(1)} %get-tuple-element.26), channel_id=1, source_target_pairs={{0,8},{8,0},{16,24},{24,16},{1,9},{9,1},{17,25},{25,17},{2,10},{10... | collective-permute-start | bytes 1572872 | tf_op jit(solution)/shard_map/ppermute | solution.py:329
  589.3 131.4 %collective-permute-start.80 = (bf16[512,1536]{1,0:T(8,128)(2,1)}, bf16[512,1536]{1,0:T(8,128)(2,1)}, u32[]{:S(2)}, u32[]{:S(2)}) collective-permute-start(bf16[512,1536]{1,0:T(8,128)(2,1)} %add_convert_fusion.8), channel_id=1, source_target_pairs={{2,0},{4,6},{3,1},{5,7},{10,8},{12,14},{11,9},{13,15},{18,16},{20,... | collective-permute-start | bytes 4718600 | tf_op jit(solution)/shard_map/ppermute | solution.py:390
  606.1 63.5 %collective-permute-start.83 = (bf16[512,1536]{1,0:T(8,128)(2,1)}, bf16[512,1536]{1,0:T(8,128)(2,1)}, u32[]{:S(2)}, u32[]{:S(2)}) collective-permute-start(bf16[512,1536]{1,0:T(8,128)(2,1)} %add_convert_fusion.7), channel_id=1, source_target_pairs={{2,4},{4,2},{3,5},{5,3},{10,12},{12,10},{11,13},{13,11},{18,20},{2... | collective-permute-start | bytes 4718600 | tf_op jit(solution)/shard_map/ppermute | solution.py:388
  608.0 64.0 %collective-permute-start.87 = (bf16[512,1536]{1,0:T(8,128)(2,1)}, bf16[512,1536]{1,0:T(8,128)(2,1)}, u32[]{:S(2)}, u32[]{:S(2)}) collective-permute-start(bf16[512,1536]{1,0:T(8,128)(2,1)} %add_convert_fusion.5), channel_id=1, source_target_pairs={{2,4},{4,2},{3,5},{5,3},{10,12},{12,10},{11,13},{13,11},{18,20},{2... | collective-permute-start | bytes 4718600 | tf_op jit(solution)/shard_map/ppermute | solution.py:388
  609.9 66.1 %collective-permute-start.91 = (bf16[512,1536]{1,0:T(8,128)(2,1)}, bf16[512,1536]{1,0:T(8,128)(2,1)}, u32[]{:S(2)}, u32[]{:S(2)}) collective-permute-start(bf16[512,1536]{1,0:T(8,128)(2,1)} %add_convert_fusion.3), channel_id=1, source_target_pairs={{2,4},{4,2},{3,5},{5,3},{10,12},{12,10},{11,13},{13,11},{18,20},{2... | collective-permute-start | bytes 4718600 | tf_op jit(solution)/shard_map/ppermute | solution.py:388
  667.9 55.3 %collective-permute-start.63 = (bf16[512,768]{1,0:T(8,128)(2,1)S(1)}, bf16[512,768]{1,0:T(8,128)(2,1)S(1)}, u32[]{:S(2)}, u32[]{:S(2)}) collective-permute-start(bf16[512,768]{1,0:T(8,128)(2,1)S(1)} %convolution_convert_fusion.12), channel_id=1, source_target_pairs={{0,8},{8,0},{16,24},{24,16},{1,9},{9,1},{17,25},{25,17},{2,10},{10... | collective-permute-start | bytes 2359304 | tf_op jit(solution)/shard_map/ppermute | solution.py:329
  669.7 54.2 %collective-permute-start.67 = (bf16[512,768]{1,0:T(8,128)(2,1)S(1)}, bf16[512,768]{1,0:T(8,128)(2,1)S(1)}, u32[]{:S(2)}, u32[]{:S(2)}) collective-permute-start(bf16[512,768]{1,0:T(8,128)(2,1)S(1)} %convolution_convert_fusion.11), channel_id=1, source_target_pairs={{0,16},{8,24},{16,0},{24,8},{1,17},{9,25},{17,1},{25,9},{2,18},{10... | collective-permute-start | bytes 2359304 | tf_op jit(solution)/shard_map/ppermute | solution.py:329
  672.0 55.5 %collective-permute-start.71 = (bf16[512,768]{1,0:T(8,128)(2,1)S(1)}, bf16[512,768]{1,0:T(8,128)(2,1)S(1)}, u32[]{:S(2)}, u32[]{:S(2)}) collective-permute-start(bf16[512,768]{1,0:T(8,128)(2,1)S(1)} %convolution_convert_fusion.10), channel_id=1, source_target_pairs={{0,24},{8,16},{16,8},{24,0},{1,25},{9,17},{17,9},{25,1},{2,26},{10... | collective-permute-start | bytes 2359304 | tf_op jit(solution)/shard_map/ppermute | solution.py:329
  676.0 64.4 %collective-permute-start.75 = (bf16[256,2048]{1,0:T(8,128)(2,1)S(1)}, bf16[256,2048]{1,0:T(8,128)(2,1)S(1)}, u32[]{:S(2)}, u32[]{:S(2)}) collective-permute-start(bf16[256,2048]{1,0:T(8,128)(2,1)S(1)} %convolution_convert_fusion.9), channel_id=1, source_target_pairs={{0,2},{6,4},{1,3},{7,5},{8,10},{14,12},{9,11},{15,13},{16,18},{22,... | collective-permute-start | bytes 3145736 | tf_op jit(solution)/shard_map/ppermute | solution.py:386
  720.8 73.7 %collective-permute-start.50 = (bf16[512,2048]{1,0:T(8,128)(2,1)}, bf16[512,2048]{1,0:T(8,128)(2,1)}, u32[]{:S(2)}, u32[]{:S(2)}) collective-permute-start(bf16[512,2048]{1,0:T(8,128)(2,1)} %convolution_convert_fusion.6), channel_id=1, source_target_pairs={{0,8},{8,0},{16,24},{24,16},{1,9},{9,1},{17,25},{25,17},{2,10},{10... | collective-permute-start | bytes 6291464 | tf_op jit(solution)/shard_map/ppermute | solution.py:329
  727.6 46.6 %collective-permute-start.68 = (bf16[512,768]{1,0:T(8,128)(2,1)S(1)}, bf16[512,768]{1,0:T(8,128)(2,1)S(1)}, u32[]{:S(2)}, u32[]{:S(2)}) collective-permute-start(bf16[512,768]{1,0:T(8,128)(2,1)S(1)} %collective-permute-done.67), channel_id=1, source_target_pairs={{0,2},{6,4},{1,3},{7,5},{8,10},{14,12},{9,11},{15,13},{16,18},{22,... | collective-permute-start | bytes 2359304 | tf_op jit(solution)/shard_map/ppermute | solution.py:386
  740.4 50.6 %collective-permute-start.72 = (bf16[512,768]{1,0:T(8,128)(2,1)S(1)}, bf16[512,768]{1,0:T(8,128)(2,1)S(1)}, u32[]{:S(2)}, u32[]{:S(2)}) collective-permute-start(bf16[512,768]{1,0:T(8,128)(2,1)S(1)} %collective-permute-done.71), channel_id=1, source_target_pairs={{0,2},{6,4},{1,3},{7,5},{8,10},{14,12},{9,11},{15,13},{16,18},{22,... | collective-permute-start | bytes 2359304 | tf_op jit(solution)/shard_map/ppermute | solution.py:386
  746.8 45.7 %collective-permute-start.76 = (bf16[256,2048]{1,0:T(8,128)(2,1)S(1)}, bf16[256,2048]{1,0:T(8,128)(2,1)S(1)}, u32[]{:S(2)}, u32[]{:S(2)}) collective-permute-start(bf16[256,2048]{1,0:T(8,128)(2,1)S(1)} %add_convert_fusion.11), channel_id=1, source_target_pairs={{2,4},{4,2},{3,5},{5,3},{10,12},{12,10},{11,13},{13,11},{18,20},{2... | collective-permute-start | bytes 3145736 | tf_op jit(solution)/shard_map/ppermute | solution.py:388
  757.3 116.5 %collective-permute-start.94 = (bf16[768,2048]{1,0:T(8,128)(2,1)S(1)}, bf16[768,2048]{1,0:T(8,128)(2,1)S(1)}, u32[]{:S(2)}, u32[]{:S(2)}) collective-permute-start(bf16[768,2048]{1,0:T(8,128)(2,1)S(1)} %copy-done.7), channel_id=1, source_target_pairs={{2,4},{4,2},{3,5},{5,3},{10,12},{12,10},{11,13},{13,11},{18,20},{2... | collective-permute-start | bytes 9437192 | tf_op jit(solution)/shard_map/ppermute | solution.py:388
  774.1 96.0 %collective-permute-start.84 = (bf16[512,1536]{1,0:T(8,128)(2,1)S(1)}, bf16[512,1536]{1,0:T(8,128)(2,1)S(1)}, u32[]{:S(2)}, u32[]{:S(2)}) collective-permute-start(bf16[512,1536]{1,0:T(8,128)(2,1)S(1)} %add_convert_fusion.6), channel_id=1, source_target_pairs={{2,0},{4,6},{3,1},{5,7},{10,8},{12,14},{11,9},{13,15},{18,16},{20,... | collective-permute-start | bytes 4718600 | tf_op jit(solution)/shard_map/ppermute | solution.py:390
  791.0 79.5 %collective-permute-start.88 = (bf16[512,1536]{1,0:T(8,128)(2,1)S(1)}, bf16[512,1536]{1,0:T(8,128)(2,1)}, u32[]{:S(2)}, u32[]{:S(2)}) collective-permute-start(bf16[512,1536]{1,0:T(8,128)(2,1)S(1)} %add_convert_fusion.4), channel_id=1, source_target_pairs={{2,0},{4,6},{3,1},{5,7},{10,8},{12,14},{11,9},{13,15},{18,16},{20,... | collective-permute-start | bytes 4718600 | tf_op jit(solution)/shard_map/ppermute | solution.py:390
  792.5 68.0 %collective-permute-start.62 = (bf16[512,768]{1,0:T(8,128)(2,1)S(1)}, bf16[512,768]{1,0:T(8,128)(2,1)S(1)}, u32[]{:S(2)}, u32[]{:S(2)}) collective-permute-start(bf16[512,768]{1,0:T(8,128)(2,1)S(1)} %add_convert_fusion.18), channel_id=1, source_target_pairs={{2,0},{4,6},{3,1},{5,7},{10,8},{12,14},{11,9},{13,15},{18,16},{20,... | collective-permute-start | bytes 2359304 | tf_op jit(solution)/shard_map/ppermute | solution.py:390
  794.4 69.0 %collective-permute-start.65 = (bf16[512,768]{1,0:T(8,128)(2,1)S(1)}, bf16[512,768]{1,0:T(8,128)(2,1)S(1)}, u32[]{:S(2)}, u32[]{:S(2)}) collective-permute-start(bf16[512,768]{1,0:T(8,128)(2,1)S(1)} %add_convert_fusion.17), channel_id=1, source_target_pairs={{2,4},{4,2},{3,5},{5,3},{10,12},{12,10},{11,13},{13,11},{18,20},{2... | collective-permute-start | bytes 2359304 | tf_op jit(solution)/shard_map/ppermute | solution.py:388
  866.3 40.4 %collective-permute-start.92 = (bf16[512,1536]{1,0:T(8,128)(2,1)S(1)}, bf16[512,1536]{1,0:T(8,128)(2,1)}, u32[]{:S(2)}, u32[]{:S(2)}) collective-permute-start(bf16[512,1536]{1,0:T(8,128)(2,1)S(1)} %add_convert_fusion.2), channel_id=1, source_target_pairs={{2,0},{4,6},{3,1},{5,7},{10,8},{12,14},{11,9},{13,15},{18,16},{20,... | collective-permute-start | bytes 4718600 | tf_op jit(solution)/shard_map/ppermute | solution.py:390
  868.6 117.5 %collective-permute-start.77 = (bf16[256,2048]{1,0:T(8,128)(2,1)S(1)}, bf16[256,2048]{1,0:T(8,128)(2,1)}, u32[]{:S(2)}, u32[]{:S(2)}) collective-permute-start(bf16[256,2048]{1,0:T(8,128)(2,1)S(1)} %add_convert_fusion.10), channel_id=1, source_target_pairs={{2,0},{4,6},{3,1},{5,7},{10,8},{12,14},{11,9},{13,15},{18,16},{20,... | collective-permute-start | bytes 3145736 | tf_op jit(solution)/shard_map/ppermute | solution.py:390
  870.5 40.5 %collective-permute-start.52 = (bf16[128,2048]{1,0:T(8,128)(2,1)}, bf16[128,2048]{1,0:T(8,128)(2,1)}, u32[]{:S(2)}, u32[]{:S(2)}) collective-permute-start(bf16[128,2048]{1,0:T(8,128)(2,1)} %get-tuple-element.58), channel_id=1, source_target_pairs={{0,16},{8,24},{16,0},{24,8},{1,17},{9,25},{17,1},{25,9},{2,18},{10... | collective-permute-start | bytes 1572872 | tf_op jit(solution)/shard_map/ppermute | solution.py:329
  906.7 165.7 %collective-permute-start.66 = (bf16[512,768]{1,0:T(8,128)(2,1)}, bf16[512,768]{1,0:T(8,128)(2,1)S(1)}, u32[]{:S(2)}, u32[]{:S(2)}) collective-permute-start(bf16[512,768]{1,0:T(8,128)(2,1)} %add_convert_fusion.16), channel_id=1, source_target_pairs={{2,0},{4,6},{3,1},{5,7},{10,8},{12,14},{11,9},{13,15},{18,16},{20,... | collective-permute-start | bytes 2359304 | tf_op jit(solution)/shard_map/ppermute | solution.py:390
  909.6 163.0 %collective-permute-start.70 = (bf16[512,768]{1,0:T(8,128)(2,1)S(1)}, bf16[512,768]{1,0:T(8,128)(2,1)S(1)}, u32[]{:S(2)}, u32[]{:S(2)}) collective-permute-start(bf16[512,768]{1,0:T(8,128)(2,1)S(1)} %copy-done.30), channel_id=1, source_target_pairs={{2,0},{4,6},{3,1},{5,7},{10,8},{12,14},{11,9},{13,15},{18,16},{20,... | collective-permute-start | bytes 2359304 | tf_op jit(solution)/shard_map/ppermute | solution.py:390
  910.9 161.9 %collective-permute-start.74 = (bf16[512,768]{1,0:T(8,128)(2,1)S(1)}, bf16[512,768]{1,0:T(8,128)(2,1)S(1)}, u32[]{:S(2)}, u32[]{:S(2)}) collective-permute-start(bf16[512,768]{1,0:T(8,128)(2,1)S(1)} %add_convert_fusion.12), channel_id=1, source_target_pairs={{2,0},{4,6},{3,1},{5,7},{10,8},{12,14},{11,9},{13,15},{18,16},{20,... | collective-permute-start | bytes 2359304 | tf_op jit(solution)/shard_map/ppermute | solution.py:390
  937.1 42.9 %collective-permute-start.58 = (f32[1,4352]{1,0:T(1,128)S(1)}, f32[1,4352]{1,0:T(1,128)S(1)}, u32[]{:S(2)}, u32[]{:S(2)}) collective-permute-start(f32[1,4352]{1,0:T(1,128)S(1)} %add.513), channel_id=1, source_target_pairs={{0,2},{2,0},{4,6},{6,4},{1,3},{3,1},{5,7},{7,5},{8,10},{10,8},{12,... | collective-permute-start | bytes 52232 | tf_op jit(solution)/shard_map/ppermute | solution.py:397
  983.7 92.6 %collective-permute-start.95 = (bf16[768,2048]{1,0:T(8,128)(2,1)S(1)}, bf16[768,2048]{1,0:T(8,128)(2,1)S(1)}, u32[]{:S(2)}, u32[]{:S(2)}) collective-permute-start(bf16[768,2048]{1,0:T(8,128)(2,1)S(1)} %add_convert_fusion), channel_id=1, source_target_pairs={{2,0},{4,6},{3,1},{5,7},{10,8},{12,14},{11,9},{13,15},{18,16},{20,... | collective-permute-start | bytes 9437192 | tf_op jit(solution)/shard_map/ppermute | solution.py:390
  986.1 86.3 %collective-permute-start.54 = (bf16[128,2048]{1,0:T(8,128)(2,1)S(1)}, bf16[128,2048]{1,0:T(8,128)(2,1)S(1)}, u32[]{:S(2)}, u32[]{:S(2)}) collective-permute-start(bf16[128,2048]{1,0:T(8,128)(2,1)S(1)} %fusion.38), channel_id=1, source_target_pairs={{0,0},{2,8},{4,16},{6,24},{8,2},{10,10},{12,18},{14,26},{16,4},{18... | collective-permute-start | bytes 1572872 | tf_op jit(solution)/shard_map/ppermute | solution.py:342
  (141 other events, 2860.7 us)

commit v2 on v1

--- a/solution.py
+++ b/solution.py
@@ -345,10 +345,20 @@
 PIECES = ((0, 0), (0, 1), (2, 0), (2, 1))
 
 
-def plane_gather(own):
-    near = [own if masks == (0, 0) else swap_plane(own, *masks) for masks in PIECES]
+def plane_pieces(own):
+    return [own if masks == (0, 0) else swap_plane(own, *masks) for masks in PIECES]
+
+
+def plane_gather(own, near=None):
+    near = near or plane_pieces(own)
     far = [swap_plane(piece, 1, 0) for piece in near]
     return jnp.concatenate(near + far, axis=0)
+
+
+def plane_gather_slow(own):
+    pair = jnp.stack([own, swap_plane(own, 2, 0)])
+    near = jnp.stack([pair, swap_plane(pair, 0, 1)], axis=1).reshape(-1, own.shape[1])
+    return jnp.concatenate([near, swap_plane(near, 1, 0)], axis=0)
 
 
 def plane_scatter(near_part, far_part):
@@ -380,22 +390,49 @@
     return plane_scatter(near_part, far_part)
 
 
-def chain_sum(part):
-    low = part.astype(jnp.bfloat16)
-    place = lax.axis_index("ctx")
-    inward = lax.ppermute(low, "ctx", [(0, 1), (3, 2)])
-    pair = (low.astype(jnp.float32) + inward.astype(jnp.float32)).astype(jnp.bfloat16)
-    across = lax.ppermute(pair, "ctx", [(1, 2), (2, 1)])
-    total = (pair.astype(jnp.float32) + across.astype(jnp.float32)).astype(jnp.bfloat16)
-    outward = lax.ppermute(total, "ctx", [(1, 0), (2, 3)])
-    inner = (place == 1) | (place == 2)
-    return jnp.where(inner, total, outward).astype(jnp.float32)
+INWARD, ACROSS, OUTWARD = [(0, 1), (3, 2)], [(1, 2), (2, 1)], [(1, 0), (2, 3)]
+
+
+class CtxSums:
+    def __init__(self):
+        self.flight, self.done = [], {}
+
+    def step(self, fresh, kept):
+        old = self.flight.pop(0) if len(self.flight) > 1 else []
+        names = [name for name, _ in fresh]
+        low = [part.astype(jnp.bfloat16) for _, part in fresh]
+        pairs = [entry[2:] for entry in old]
+        pairs, low, kept = lax.optimization_barrier((pairs, low, kept))
+        place = lax.axis_index("ctx")
+        sent = []
+        for (stage, name, _, _), (here, came) in zip(old, pairs):
+            if stage == 2:
+                inner = (place == 1) | (place == 2)
+                self.done[name] = jnp.where(inner, here, came).astype(jnp.float32)
+                continue
+            both = (here.astype(jnp.float32) + came.astype(jnp.float32)).astype(jnp.bfloat16)
+            moved = lax.ppermute(both, "ctx", OUTWARD if stage else ACROSS)
+            sent.append((stage + 1, name, both, moved))
+        for name, part in zip(names, low):
+            sent.append((0, name, part, lax.ppermute(part, "ctx", INWARD)))
+        self.flight.append(sent)
+        return kept
+
+    def drain(self, fresh):
+        fresh = list(fresh)
+        while fresh or any(self.flight):
+            self.step(fresh[:1], ())
+            fresh = fresh[1:]
 
 
 def all_sum(value):
     for axis, mask in (("fsdp", 1), ("fsdp", 2), ("tp", 1), ("ctx", 1), ("ctx", 2)):
         value = value + lax.ppermute(value, axis, xor_pairs(lax.axis_size(axis), mask))
     return value
+
+
+def after(value, *others):
+    return lax.optimization_barrier((value, others))[0]
 
 
 def weight_columns(weights, owner):
@@ -408,35 +445,41 @@
 
 def fetch_weights(weights):
     me, size = lax.axis_index("fsdp"), lax.axis_size("fsdp")
+    side = lax.axis_index("ctx") % 2
     rows = weights[0].shape[0]
-    whole = None
-    for mask in range(size):
-        part = weight_columns(weights, me ^ mask)
-        if mask:
-            part = swap_plane(part, mask, 0)
-        if whole is None:
-            whole = jnp.zeros((rows * size, part.shape[1]), part.dtype)
-        whole = lax.dynamic_update_slice_in_dim(whole, part, (me ^ mask) * rows, 0)
+    half = rows // 2
+    mine = [lax.dynamic_slice_in_dim(weight, side * half, half, 0) for weight in weights]
+    came = [swap_plane(weight_columns(mine, me ^ mask), mask, 0) for mask in (2, 3)]
+    own = weight_columns(weights, me)
+    core = swap_plane(weight_columns(weights, me ^ 1), 1, 0)
+    other = lax.ppermute(jnp.concatenate(came, axis=0), "ctx", xor_pairs(4, 1))
+    whole = jnp.zeros((rows * size, own.shape[1]), own.dtype)
+    for part, start in (
+        (own, me * rows),
+        (core, (me ^ 1) * rows),
+        (came[0], (me ^ 2) * rows + side * half),
+        (came[1], (me ^ 3) * rows + side * half),
+        (other[:half], (me ^ 2) * rows + (1 - side) * half),
+        (other[half:], (me ^ 3) * rows + (1 - side) * half),
+    ):
+        whole = lax.dynamic_update_slice_in_dim(whole, part, start, 0)
     return whole
 
 
-def return_grads(left, right, widths):
+def grad_part(left, right, mask):
+    owner = lax.axis_index("fsdp") ^ mask
+    rows = left.shape[1] // lax.axis_size("fsdp")
+    columns = lax.dynamic_slice_in_dim(left, owner * rows, rows, 1)
+    part = dot_tn(columns, right).astype(jnp.bfloat16)
+    return swap_plane(part, mask, 0) if mask else part
+
+
+def place_columns(parts, width):
     me, size = lax.axis_index("fsdp"), lax.axis_size("fsdp")
-    rows = left.shape[1] // size
-    outs = [jnp.zeros((rows, width * size), jnp.float32) for width in widths]
-    for mask in range(size):
-        columns = lax.dynamic_slice_in_dim(left, (me ^ mask) * rows, rows, 1)
-        part = dot_tn(columns, right).astype(jnp.bfloat16)
-        if mask:
-            part = swap_plane(part, mask, 0)
-        summed = chain_sum(part)
-        offset = 0
-        for place, width in enumerate(widths):
-            outs[place] = lax.dynamic_update_slice_in_dim(
-                outs[place], summed[:, offset : offset + width], (me ^ mask) * width, 1
-            )
-            offset += width
-    return outs
+    whole = jnp.zeros((parts[0].shape[0], width * size), jnp.float32)
+    for mask, part in enumerate(parts):
+        whole = lax.dynamic_update_slice_in_dim(whole, part, (me ^ mask) * width, 1)
+    return whole
 
 
 def plane_body(
@@ -468,9 +511,11 @@
     query_gain = query_norm_gain.astype(jnp.float32)
     key_gain = k_norm.astype(jnp.float32)
 
-    inputs = swap_ranks(layer_input).astype(jnp.float32)
+    input_low = swap_ranks(layer_input)
+    inputs = input_low.astype(jnp.float32)
+    attn_weights = fetch_weights((w_query, key_weight, value_weight, w_out_gate))
+    cot = swap_ranks(after(cotangent, input_low)).astype(jnp.float32)
     lengths = swap_ranks(lengths)
-    cot = swap_ranks(cotangent).astype(jnp.float32)
 
     def slots_of(fsdp_index, tp_index):
         return (fsdp_index * tp_size + tp_index) * local_rows + jnp.arange(
@@ -489,10 +534,11 @@
     segment = segment_of(slots, lengths)
     position = position_of(slots, segment, lengths)
 
-    first_normed = plane_gather(apply_rms_norm(inputs, gain_one).astype(jnp.bfloat16))
-    attn_weights = fetch_weights((w_query, key_weight, value_weight, w_out_gate))
+    first_own = apply_rms_norm(inputs, gain_one).astype(jnp.bfloat16)
+    first_near = plane_pieces(first_own)
+    first_normed = plane_gather(first_own, first_near)
     out_grad = cot * own_valid
-    ffn_grad = plane_gather(out_grad.astype(jnp.bfloat16))
+    w_gate, w_up = after((w_gate, w_up), first_near)
     ffn_weights = fetch_weights((w_gate, w_up))
 
     projected = dot_nn(first_normed, attn_weights)
@@ -510,6 +556,7 @@
     ]
 
     allowed = (segment[:, None] == segment[None, :]) & (slots[None, :] <= slots[:, None])
+    ffn_grad = plane_gather_slow(after(out_grad.astype(jnp.bfloat16), projected))
     raw_scores = jnp.einsum("qgd,kd->gqk", query_rot, key_rot, preferred_element_type=jnp.float32)
     scores = jnp.where(allowed, raw_scores * score_scale, NEG_FILL)
     top = jnp.max(scores, axis=-1, keepdims=True)
@@ -534,25 +581,53 @@
     gate_sigmoid = jax.nn.sigmoid(gate_pre)
     activated = gate_pre * gate_sigmoid
     hidden_act = (activated * up_pre).astype(jnp.bfloat16)
-    grad_w_down = chain_sum(dot_tn(hidden_act, ffn_grad))
     gate_grad = (
         hidden_grad * up_pre * gate_sigmoid * (1.0 + gate_pre * (1.0 - gate_sigmoid))
     ).astype(jnp.bfloat16)
     up_grad = (hidden_grad * activated).astype(jnp.bfloat16)
     ffn_in_grads = jnp.concatenate([gate_grad, up_grad], axis=1)
-    normed_two_grad = scatter_product(ffn_in_grads, ffn_weights, dot_nt)
-    grad_w_gate, grad_w_up = return_grads(normed_two, ffn_in_grads, (hidden_width, hidden_width))
-    ffn_share = scatter_product(hidden_act, w_down, dot_nn)
-    layer_output = swap_ranks((hidden_in + own_valid * ffn_share).astype(jnp.bfloat16))
-
+
+    sums = CtxSums()
+    down_part = dot_tn(hidden_act, ffn_grad).astype(jnp.bfloat16)
+    down_parts = [("down", i) for i in range(4)]
+    down_parts = list(zip(down_parts, jnp.split(down_part, 4, axis=0)))
+    hidden_act, ffn_in_grads, normed_two = sums.step(
+        down_parts[:1], (hidden_act, ffn_in_grads, normed_two)
+    )
+    half = row_slots // 2
+    two_far = dot_nt(ffn_in_grads[half:], ffn_weights)
+    two_near = dot_nt(ffn_in_grads[:half], ffn_weights)
+    two_far, two_near, hidden_act, ffn_in_grads = sums.step(
+        down_parts[1:2], (two_far.astype(jnp.bfloat16), two_near, hidden_act, ffn_in_grads)
+    )
+    normed_two_grad = plane_scatter(two_near, two_far)
+    ffn_parts = {
+        mask: grad_part(normed_two, ffn_in_grads, mask) for mask in (2, 3, 1, 0)
+    }
+    normed_two_grad, ffn_parts[0] = sums.step(
+        down_parts[2:3], (normed_two_grad, ffn_parts[0])
+    )
     back_two, gain_two_grad = norm_back(hidden_in, gain_two, normed_two_grad)
     hidden_total_grad = out_grad + back_two
-    attn_grad = plane_gather((own_valid * hidden_total_grad).astype(jnp.bfloat16))
+    attn_near = plane_pieces((own_valid * hidden_total_grad).astype(jnp.bfloat16))
+    out_far = dot_nn(hidden_act[half:], w_down)
+    out_near = dot_nn(hidden_act[:half], w_down)
+    attn_near, out_far, out_near, ffn_parts[1] = sums.step(
+        down_parts[3:], (attn_near, out_far.astype(jnp.bfloat16), out_near, ffn_parts[1])
+    )
+    ffn_chunks = []
+    for mask in range(4):
+        for i, part in enumerate(jnp.split(ffn_parts[mask], 2, axis=1)):
+            ffn_chunks.append((("ffn", mask, i), part))
+    attn_grad = plane_gather(attn_near[0], attn_near)
     gated_grad = dot_nt(attn_grad, w_output)
-    grad_w_output = chain_sum(dot_tn(gated_mix, attn_grad))
+    output_part = dot_tn(gated_mix, attn_grad).astype(jnp.bfloat16)
     mixed_grad = (gated_grad * gate_sig).astype(jnp.bfloat16)
     gate_logit_grad = (gated_grad * attended_rows * gate_sig * (1.0 - gate_sig)).astype(
         jnp.bfloat16
+    )
+    mixed_grad, gate_logit_grad, output_part = sums.step(
+        ffn_chunks[:1], (mixed_grad, gate_logit_grad, output_part)
     )
     mixed_grad_heads = mixed_grad.reshape(row_slots, query_heads, HEAD_SIZE)
     delta_rows = jnp.transpose(
@@ -576,6 +651,9 @@
         mixed_grad_heads,
         preferred_element_type=jnp.float32,
     ).astype(jnp.bfloat16)
+    query_rot_grad, key_rot_grad, value_grad = sums.step(
+        ffn_chunks[1:2], (query_rot_grad, key_rot_grad, value_grad)
+    )
     key_back, key_gain_grad = norm_back(
         key_raw, key_gain, apply_rotary(key_rot_grad[:, None], position, -1.0)
     )
@@ -591,16 +669,43 @@
         ],
         axis=1,
     )
-    normed_one_grad = scatter_product(attn_in_grads, attn_weights, dot_nt)
-    grad_w_query, grad_w_key, grad_w_value, grad_w_out_gate = return_grads(
-        first_normed, attn_in_grads, (query_width, HEAD_SIZE, HEAD_SIZE, query_width)
+    one_far = dot_nt(attn_in_grads[half:], attn_weights)
+    one_near = dot_nt(attn_in_grads[:half], attn_weights)
+    one_far, one_near, attn_in_grads = sums.step(
+        ffn_chunks[2:3], (one_far.astype(jnp.bfloat16), one_near, attn_in_grads)
+    )
+    normed_one_grad = plane_scatter(one_near, one_far)
+    attn_parts = {mask: grad_part(first_normed, attn_in_grads, mask) for mask in (2, 3, 1, 0)}
+    normed_one_grad, attn_parts[0] = sums.step(
+        ffn_chunks[3:4], (normed_one_grad, attn_parts[0])
     )
     back_one, gain_one_grad = norm_back(inputs, gain_one, normed_one_grad)
     input_grad = swap_ranks((hidden_total_grad + back_one).astype(jnp.bfloat16))
+    ffn_share = plane_scatter(out_near, out_far)
+    layer_output = swap_ranks((hidden_in + own_valid * ffn_share).astype(jnp.bfloat16))
+    gains = jnp.concatenate([gain_one_grad, gain_two_grad, query_gain_grad, key_gain_grad])[None]
+    gains = all_sum(gains)[0]
+    gains, input_grad, layer_output = sums.step(
+        ffn_chunks[4:5], (gains, input_grad, layer_output)
+    )
+    attn_chunks = [(("attn", mask), attn_parts[mask]) for mask in range(4)]
+    sums.drain(ffn_chunks[5:] + [("output", output_part)] + attn_chunks)
+
+    grad_w_down = jnp.concatenate([sums.done["down", i] for i in range(4)], axis=0)
+    grad_w_output = sums.done["output"]
+    grad_w_gate, grad_w_up = (
+        place_columns([sums.done["ffn", mask, i] for mask in range(4)], hidden_width)
+        for i in range(2)
+    )
+    ends = [0, query_width, query_width + HEAD_SIZE, query_width + 2 * HEAD_SIZE]
+    widths = (query_width, HEAD_SIZE, HEAD_SIZE, query_width)
+    grad_w_query, grad_w_key, grad_w_value, grad_w_out_gate = (
+        place_columns(
+            [sums.done["attn", mask][:, start : start + width] for mask in range(4)], width
+        )
+        for start, width in zip(ends, widths)
+    )
     model_width = layer_input.shape[1]
-    gains = all_sum(
-        jnp.concatenate([gain_one_grad, gain_two_grad, query_gain_grad, key_gain_grad])[None]
-    )[0]
     ends = (model_width, 2 * model_width, 2 * model_width + HEAD_SIZE)
     return (
         layer_output,

time: 1090 us -> 878 us (0.81)
  the two profiles are of different devices: /device:TPU:1 before, /device:TPU:2 now
where the time goes in v2:
time: 878 us; the launch traced here: 865 us
  waiting for transfers between devices  370 us (42%)
  starting transfers between devices  235 us (27%)
  matrix products  98.2 us (11%)
  other arithmetic  86.3 us (10%)
  local copies, waits for them, and re-layouts  70.1 us (8%)
    ppermute x17, starting transfers between devices, step(): sent.append((0, name, part, lax.ppermute(part, 'ctx', INWARD)))  125 us
    ppermute x34, waiting for transfers between devices, step(): moved = lax.ppermute(both, 'ctx', OUTWARD if stage else ACROSS)  103 us
    ppermute x37, waiting for transfers between devices, swap_plane(): return lax.ppermute(value, 'fsdp', xor_pairs(fsdp_size, fsdp_mask))  99.3 us
    ppermute x7, waiting for transfers between devices, swap_plane(): lax.ppermute(value, ('fsdp', 'tp'), xor_pairs(fsdp_size * tp_size, fsdp_m...  50.6 us
    ppermute x34, starting transfers between devices, step(): moved = lax.ppermute(both, 'ctx', OUTWARD if stage else ACROSS)  36.2 us
    ppermute x17, waiting for transfers between devices, step(): sent.append((0, name, part, lax.ppermute(part, 'ctx', INWARD)))  30.7 us
    dot_general x6, matrix products, dot_nt(): lax.dot_general(a, b, (((1,), (1,)), ((), ())), preferred_element_type=jn...  30.6 us
    dot_general x6, matrix products, dot_nn(): return jnp.dot(a, b, preferred_element_type=jnp.float32)  30.3 us
  transfers between devices with their start and end apart: 115, of which 41 were waited for; matrix products, arithmetic and copies ran while one was open for 25% of the time, Pallas kernels for 0%

profile of v2, /device:TPU:2, one launch (start us, length us, event | category | flops | bytes accessed | tf_op | source)
XLA Modules:
  0.0 865.2 jit_solution(7656412372699517794)
XLA Ops:
  39.7 5.7 collective-permute-done.1
  70.2 5.6 collective-permute-done.4
  84.4 7.1 fusion.152
  119.6 7.4 collective-permute-start.28
  138.6 7.2 collective-permute-done.25
  145.9 18.1 %collective-permute-done.26 = bf16[256,1536]{1,0:T(8,128)(2,1)} collective-permute-done((bf16[256,1536]{1,0:T(8,128)(2,1)}, bf16[256,1536]{1,0:T(8,128)(2,1)}, u32[]{:S(2)}, u32[]{:S(2)}) %collective-permute-start.26) | collective-permute-done | bytes 786464 | tf_op jit(solution)/shard_map/ppermute | solution.py:329
  182.3 22.2 %collective-permute-done.27 = bf16[512,1536]{1,0:T(8,128)(2,1)S(1)} collective-permute-done((bf16[512,1536]{1,0:T(8,128)(2,1)S(1)}, bf16[512,1536]{1,0:T(8,128)(2,1)S(1)}, u32[]{:S(2)}, u32[]{:S(2)}) %collective-permute-start.27) | collective-permute-done | bytes 1572896 | tf_op jit(solution)/shard_map/ppermute | solution.py:455
  211.9 10.1 %collective-permute-done.29 = bf16[128,2048]{1,0:T(8,128)(2,1)S(1)} collective-permute-done((bf16[128,2048]{1,0:T(8,128)(2,1)S(1)}, bf16[128,2048]{1,0:T(8,128)(2,1)S(1)}, u32[]{:S(2)}, u32[]{:S(2)}) %collective-permute-start.29) | collective-permute-done | bytes 524320 | tf_op jit(solution)/shard_map/ppermute | solution.py:329
  223.8 9.5 %collective-permute-done.18 = bf16[128,2048]{1,0:T(8,128)(2,1)S(1)} collective-permute-done((bf16[128,2048]{1,0:T(8,128)(2,1)S(1)}, bf16[128,2048]{1,0:T(8,128)(2,1)S(1)}, u32[]{:S(2)}, u32[]{:S(2)}) %collective-permute-start.18) | collective-permute-done | bytes 524320 | tf_op jit(solution)/shard_map/ppermute | solution.py:329
  233.3 11.1 %collective-permute-done.19 = bf16[128,2048]{1,0:T(8,128)(2,1)S(1)} collective-permute-done((bf16[128,2048]{1,0:T(8,128)(2,1)S(1)}, bf16[128,2048]{1,0:T(8,128)(2,1)S(1)}, u32[]{:S(2)}, u32[]{:S(2)}) %collective-permute-start.19) | collective-permute-done | bytes 524320 | tf_op jit(solution)/shard_map/ppermute | solution.py:332
  244.6 11.7 %collective-permute-done.30 = bf16[2,128,2048]{2,1,0:T(8,128)(2,1)S(1)} collective-permute-done((bf16[2,128,2048]{2,1,0:T(8,128)(2,1)S(1)}, bf16[2,128,2048]{2,1,0:T(8,128)(2,1)S(1)}, u32[]{:S(2)}, u32[]{:S(2)}) %collective-permute-start.30) | collective-permute-done | bytes 1048608 | tf_op jit(solution)/shard_map/ppermute | solution.py:331
  257.0 11.9 %fusion.153 = f32[1024,1536]{1,0:T(8,128)} fusion(bf16[1024,2048]{1,0:T(8,128)(2,1)S(1)} %constant_dynamic-update-slice_fusion.9, bf16[2048,1536]{1,0:T(8,128)(2,1)} %slice_dynamic-update-slice_fusion), kind=kOutput, calls=%fused_computation.369 | convolution fusion | flops 6442450944 | bytes 16777216 | tf_op jit(solution)/shard_map/dot_general | solution.py:375
  268.8 8.1 multiply_convert_fusion.1
  282.3 5.6 fusion.17
  287.9 6.7 convolution_convert_fusion.8
  320.2 15.5 %collective-permute-done.56 = bf16[512,1536]{1,0:T(8,128)(2,1)S(1)} collective-permute-done((bf16[512,1536]{1,0:T(8,128)(2,1)}, bf16[512,1536]{1,0:T(8,128)(2,1)S(1)}, u32[]{:S(2)}, u32[]{:S(2)}) %collective-permute-start.56) | collective-permute-done | bytes 1572896 | tf_op jit(solution)/shard_map/ppermute | solution.py:329
  338.6 29.0 %collective-permute-done.81 = bf16[512,1536]{1,0:T(8,128)(2,1)S(1)} collective-permute-done((bf16[512,1536]{1,0:T(8,128)(2,1)}, bf16[512,1536]{1,0:T(8,128)(2,1)S(1)}, u32[]{:S(2)}, u32[]{:S(2)}) %collective-permute-start.81) | collective-permute-done | bytes 1572896 | tf_op jit(solution)/shard_map/ppermute | solution.py:329
  373.4 7.3 collective-permute-done.35
  380.7 11.2 %collective-permute-done.36 = bf16[128,2048]{1,0:T(8,128)(2,1)S(1)} collective-permute-done((bf16[128,2048]{1,0:T(8,128)(2,1)S(1)}, bf16[128,2048]{1,0:T(8,128)(2,1)S(1)}, u32[]{:S(2)}, u32[]{:S(2)}) %collective-permute-start.36) | collective-permute-done | bytes 524320 | tf_op jit(solution)/shard_map/ppermute | solution.py:332
  405.5 8.4 collective-permute-start.38
  414.0 6.5 collective-permute-done.42
  424.4 5.6 collective-permute-start.52
  450.6 6.8 collective-permute-start.50
  508.4 10.4 %collective-permute-done.63 = bf16[128,2048]{1,0:T(8,128)(2,1)S(1)} collective-permute-done((bf16[128,2048]{1,0:T(8,128)(2,1)S(1)}, bf16[128,2048]{1,0:T(8,128)(2,1)S(1)}, u32[]{:S(2)}, u32[]{:S(2)}) %collective-permute-start.63) | collective-permute-done | bytes 524320 | tf_op jit(solution)/shard_map/ppermute | solution.py:332
  524.6 5.4 collective-permute-done.71
  534.7 5.8 collective-permute-done.73
  540.9 5.0 collective-permute-start.74
  554.0 9.3 %collective-permute-done.67 = f32[1,4352]{1,0:T(1,128)S(1)} collective-permute-done((f32[1,4352]{1,0:T(1,128)S(1)}, f32[1,4352]{1,0:T(1,128)S(1)}, u32[]{:S(2)}, u32[]{:S(2)}) %collective-permute-start.67) | collective-permute-done | bytes 17440 | tf_op jit(solution)/shard_map/ppermute | solution.py:430
  579.8 16.4 %collective-permute-done.69 = bf16[128,2048]{1,0:T(8,128)(2,1)S(1)} collective-permute-done((bf16[128,2048]{1,0:T(8,128)(2,1)S(1)}, bf16[128,2048]{1,0:T(8,128)(2,1)S(1)}, u32[]{:S(2)}, u32[]{:S(2)}) %collective-permute-start.69) | collective-permute-done | bytes 524320 | tf_op jit(solution)/shard_map/ppermute | solution.py:342
  600.0 15.3 %collective-permute-start.96 = (bf16[512,768]{1,0:T(8,128)(2,1)S(1)}, bf16[512,768]{1,0:T(8,128)(2,1)S(1)}, u32[]{:S(2)}, u32[]{:S(2)}) collective-permute-start(bf16[512,768]{1,0:T(8,128)(2,1)S(1)} %copy-done.31), channel_id=1, source_target_pairs={{0,2},{6,4},{1,3},{7,5},{8,10},{14,12},{9,11},{15,13},{16,18},{22,... | collective-permute-start | bytes 2359304 | tf_op jit(solution)/shard_map/ppermute | solution.py:417
  618.0 14.0 %collective-permute-start.80 = (bf16[512,768]{1,0:T(8,128)(2,1)S(1)}, bf16[512,768]{1,0:T(8,128)(2,1)S(1)}, u32[]{:S(2)}, u32[]{:S(2)}) collective-permute-start(bf16[512,768]{1,0:T(8,128)(2,1)S(1)} %copy-done.30), channel_id=1, source_target_pairs={{0,2},{6,4},{1,3},{7,5},{8,10},{14,12},{9,11},{15,13},{16,18},{22,... | collective-permute-start | bytes 2359304 | tf_op jit(solution)/shard_map/ppermute | solution.py:417
  634.7 14.1 %collective-permute-start.99 = (bf16[512,768]{1,0:T(8,128)(2,1)S(1)}, bf16[512,768]{1,0:T(8,128)(2,1)S(1)}, u32[]{:S(2)}, u32[]{:S(2)}) collective-permute-start(bf16[512,768]{1,0:T(8,128)(2,1)S(1)} %copy-done.28), channel_id=1, source_target_pairs={{0,2},{6,4},{1,3},{7,5},{8,10},{14,12},{9,11},{15,13},{16,18},{22,... | collective-permute-start | bytes 2359304 | tf_op jit(solution)/shard_map/ppermute | solution.py:417
  651.3 14.4 %collective-permute-start.84 = (bf16[512,768]{1,0:T(8,128)(2,1)S(1)}, bf16[512,768]{1,0:T(8,128)(2,1)S(1)}, u32[]{:S(2)}, u32[]{:S(2)}) collective-permute-start(bf16[512,768]{1,0:T(8,128)(2,1)S(1)} %copy-done.29), channel_id=1, source_target_pairs={{0,2},{6,4},{1,3},{7,5},{8,10},{14,12},{9,11},{15,13},{16,18},{22,... | collective-permute-start | bytes 2359304 | tf_op jit(solution)/shard_map/ppermute | solution.py:417
  673.3 6.9 collective-permute-done.84
  682.9 11.1 %collective-permute-start.87 = (bf16[512,768]{1,0:T(8,128)(2,1)S(1)}, bf16[512,768]{1,0:T(8,128)(2,1)S(1)}, u32[]{:S(2)}, u32[]{:S(2)}) collective-permute-start(bf16[512,768]{1,0:T(8,128)(2,1)S(1)} %convolution_convert_fusion.13), channel_id=1, source_target_pairs={{0,2},{6,4},{1,3},{7,5},{8,10},{14,12},{9,11},{15,13},{16,18},{22,... | collective-permute-start | bytes 2359304 | tf_op jit(solution)/shard_map/ppermute | solution.py:417
  695.2 8.0 collective-permute-done.85
  704.7 11.3 %collective-permute-done.87 = bf16[512,768]{1,0:T(8,128)(2,1)S(1)} collective-permute-done((bf16[512,768]{1,0:T(8,128)(2,1)S(1)}, bf16[512,768]{1,0:T(8,128)(2,1)S(1)}, u32[]{:S(2)}, u32[]{:S(2)}) %collective-permute-start.87) | collective-permute-done | bytes 786464 | tf_op jit(solution)/shard_map/ppermute | solution.py:417
  716.0 6.0 collective-permute-start.107
  724.6 5.7 collective-permute-start.91
  733.5 12.7 %collective-permute-done.89 = bf16[512,768]{1,0:T(8,128)(2,1)S(1)} collective-permute-done((bf16[512,768]{1,0:T(8,128)(2,1)S(1)}, bf16[512,768]{1,0:T(8,128)(2,1)S(1)}, u32[]{:S(2)}, u32[]{:S(2)}) %collective-permute-start.89) | collective-permute-done | bytes 786464 | tf_op jit(solution)/shard_map/ppermute | solution.py:414
  753.1 13.6 %collective-permute-done.104 = bf16[512,768]{1,0:T(8,128)(2,1)S(1)} collective-permute-done((bf16[512,768]{1,0:T(8,128)(2,1)S(1)}, bf16[512,768]{1,0:T(8,128)(2,1)S(1)}, u32[]{:S(2)}, u32[]{:S(2)}) %collective-permute-start.104) | collective-permute-done | bytes 786464 | tf_op jit(solution)/shard_map/ppermute | solution.py:414
  770.5 5.7 collective-permute-start.110
  776.5 7.1 collective-permute-done.92
  786.5 6.6 collective-permute-done.110
  793.1 13.0 %collective-permute-done.108 = bf16[256,2048]{1,0:T(8,128)(2,1)S(1)} collective-permute-done((bf16[256,2048]{1,0:T(8,128)(2,1)S(1)}, bf16[256,2048]{1,0:T(8,128)(2,1)S(1)}, u32[]{:S(2)}, u32[]{:S(2)}) %collective-permute-start.108) | collective-permute-done | bytes 1048608 | tf_op jit(solution)/shard_map/ppermute | solution.py:414
  810.0 12.9 %collective-permute-done.113 = bf16[512,768]{1,0:T(8,128)(2,1)S(1)} collective-permute-done((bf16[512,768]{1,0:T(8,128)(2,1)S(1)}, bf16[512,768]{1,0:T(8,128)(2,1)S(1)}, u32[]{:S(2)}, u32[]{:S(2)}) %collective-permute-start.113) | collective-permute-done | bytes 786464 | tf_op jit(solution)/shard_map/ppermute | solution.py:414
  823.1 16.6 %collective-permute-done.111 = bf16[512,768]{1,0:T(8,128)(2,1)S(1)} collective-permute-done((bf16[512,768]{1,0:T(8,128)(2,1)S(1)}, bf16[512,768]{1,0:T(8,128)(2,1)S(1)}, u32[]{:S(2)}, u32[]{:S(2)}) %collective-permute-start.111) | collective-permute-done | bytes 786464 | tf_op jit(solution)/shard_map/ppermute | solution.py:414
  841.6 19.5 %collective-permute-done.114 = bf16[512,768]{1,0:T(8,128)(2,1)S(1)} collective-permute-done((bf16[512,768]{1,0:T(8,128)(2,1)S(1)}, bf16[512,768]{1,0:T(8,128)(2,1)S(1)}, u32[]{:S(2)}, u32[]{:S(2)}) %collective-permute-start.114) | collective-permute-done | bytes 786464 | tf_op jit(solution)/shard_map/ppermute | solution.py:414
  (617 shorter events, 354.6 us)
Async XLA Ops:
  5.8 50.3 %collective-permute-start.10 = (bf16[256,768]{1,0:T(8,128)(2,1)}, bf16[256,768]{1,0:T(8,128)(2,1)S(1)}, u32[]{:S(2)}, u32[]{:S(2)}) collective-permute-start(bf16[256,768]{1,0:T(8,128)(2,1)} %pad_maximum_fusion.16), channel_id=1, source_target_pairs={{0,16},{8,24},{16,0},{24,8},{1,17},{9,25},{17,1},{25,9},{2,18},{10... | collective-permute-start | bytes 1179656 | tf_op jit(solution)/shard_map/ppermute | solution.py:329
  11.8 50.6 %collective-permute-start.9 = (bf16[512,768]{1,0:T(8,128)(2,1)}, bf16[512,768]{1,0:T(8,128)(2,1)}, u32[]{:S(2)}, u32[]{:S(2)}) collective-permute-start(bf16[512,768]{1,0:T(8,128)(2,1)} %pad_maximum_fusion.10), channel_id=1, source_target_pairs={{0,8},{8,0},{16,24},{24,16},{1,9},{9,1},{17,25},{25,17},{2,10},{10... | collective-permute-start | bytes 2359304 | tf_op jit(solution)/shard_map/ppermute | solution.py:329
  13.6 47.6 %collective-permute-start.11 = (bf16[256,768]{1,0:T(8,128)(2,1)}, bf16[256,768]{1,0:T(8,128)(2,1)}, u32[]{:S(2)}, u32[]{:S(2)}) collective-permute-start(bf16[256,768]{1,0:T(8,128)(2,1)} %pad_maximum_fusion.17), channel_id=1, source_target_pairs={{0,24},{8,16},{16,8},{24,0},{1,25},{9,17},{17,9},{25,1},{2,26},{10... | collective-permute-start | bytes 1179656 | tf_op jit(solution)/shard_map/ppermute | solution.py:329
  15.8 36.2 %collective-permute-start = (bf16[128,2048]{1,0:T(8,128)(2,1)}, bf16[128,2048]{1,0:T(8,128)(2,1)}, u32[]{:S(2)}, u32[]{:S(2)}) collective-permute-start(bf16[128,2048]{1,0:T(8,128)(2,1)} %param.15), channel_id=1, source_target_pairs={{0,0},{2,8},{4,16},{6,24},{8,2},{10,10},{12,18},{14,26},{16,4},{18... | collective-permute-start | bytes 1572872 | tf_op jit(solution)/shard_map/ppermute | solution.py:342
  78.5 90.9 %collective-permute-start.24 = (bf16[512,1536]{1,0:T(8,128)(2,1)}, bf16[512,1536]{1,0:T(8,128)(2,1)}, u32[]{:S(2)}, u32[]{:S(2)}) collective-permute-start(bf16[512,1536]{1,0:T(8,128)(2,1)} %pad_maximum_fusion.5), channel_id=1, source_target_pairs={{0,8},{8,0},{16,24},{24,16},{1,9},{9,1},{17,25},{25,17},{2,10},{10... | collective-permute-start | bytes 4718600 | tf_op jit(solution)/shard_map/ppermute | solution.py:329
  115.2 59.0 %collective-permute-start.13 = (bf16[512,2048]{1,0:T(8,128)(2,1)}, bf16[512,2048]{1,0:T(8,128)(2,1)}, u32[]{:S(2)}, u32[]{:S(2)}) collective-permute-start(bf16[512,2048]{1,0:T(8,128)(2,1)} %convolution_convert_fusion.1), channel_id=1, source_target_pairs={{0,8},{8,0},{16,24},{24,16},{1,9},{9,1},{17,25},{25,17},{2,10},{10... | collective-permute-start | bytes 6291464 | tf_op jit(solution)/shard_map/ppermute | solution.py:329
  116.3 29.6 %collective-permute-start.25 = (bf16[256,1536]{1,0:T(8,128)(2,1)}, bf16[256,1536]{1,0:T(8,128)(2,1)}, u32[]{:S(2)}, u32[]{:S(2)}) collective-permute-start(bf16[256,1536]{1,0:T(8,128)(2,1)} %pad_maximum_fusion.12), channel_id=1, source_target_pairs={{0,16},{8,24},{16,0},{24,8},{1,17},{9,25},{17,1},{25,9},{2,18},{10... | collective-permute-start | bytes 2359304 | tf_op jit(solution)/shard_map/ppermute | solution.py:329
  117.5 46.4 %collective-permute-start.26 = (bf16[256,1536]{1,0:T(8,128)(2,1)}, bf16[256,1536]{1,0:T(8,128)(2,1)}, u32[]{:S(2)}, u32[]{:S(2)}) collective-permute-start(bf16[256,1536]{1,0:T(8,128)(2,1)} %pad_maximum_fusion.13), channel_id=1, source_target_pairs={{0,24},{8,16},{16,8},{24,0},{1,25},{9,17},{17,9},{25,1},{2,26},{10... | collective-permute-start | bytes 2359304 | tf_op jit(solution)/shard_map/ppermute | solution.py:329
  119.6 85.7 %collective-permute-start.28 = (bf16[128,2048]{1,0:T(8,128)(2,1)}, bf16[128,2048]{1,0:T(8,128)(2,1)}, u32[]{:S(2)}, u32[]{:S(2)}) collective-permute-start(bf16[128,2048]{1,0:T(8,128)(2,1)} %param.16), channel_id=1, source_target_pairs={{0,0},{2,8},{4,16},{6,24},{8,2},{10,10},{12,18},{14,26},{16,4},{18... | collective-permute-start | bytes 1572872 | tf_op jit(solution)/shard_map/ppermute | solution.py:342
  165.4 39.0 %collective-permute-start.27 = (bf16[512,1536]{1,0:T(8,128)(2,1)S(1)}, bf16[512,1536]{1,0:T(8,128)(2,1)S(1)}, u32[]{:S(2)}, u32[]{:S(2)}) collective-permute-start(bf16[512,1536]{1,0:T(8,128)(2,1)S(1)} %pad_maximum_fusion.6), channel_id=1, source_target_pairs={{0,2},{2,0},{4,6},{6,4},{1,3},{3,1},{5,7},{7,5},{8,10},{10,8},{12,... | collective-permute-start | bytes 4718600 | tf_op jit(solution)/shard_map/ppermute | solution.py:455
  211.9 32.5 %collective-permute-start.19 = (bf16[128,2048]{1,0:T(8,128)(2,1)S(1)}, bf16[128,2048]{1,0:T(8,128)(2,1)S(1)}, u32[]{:S(2)}, u32[]{:S(2)}) collective-permute-start(bf16[128,2048]{1,0:T(8,128)(2,1)S(1)} %get-tuple-element.337), channel_id=1, source_target_pairs={{0,17},{1,16},{8,25},{9,24},{16,1},{17,0},{24,9},{25,8},{2,19},{3,... | collective-permute-start | bytes 1572872 | tf_op jit(solution)/shard_map/ppermute | solution.py:332
  211.9 32.5 %collective-permute-start.20 = (bf16[128,2048]{1,0:T(8,128)(2,1)S(1)}, bf16[128,2048]{1,0:T(8,128)(2,1)S(1)}, u32[]{:S(2)}, u32[]{:S(2)}) collective-permute-start(bf16[128,2048]{1,0:T(8,128)(2,1)S(1)} %get-tuple-element.337), channel_id=1, source_target_pairs={{0,8},{8,0},{16,24},{24,16},{1,9},{9,1},{17,25},{25,17},{2,10},{10... | collective-permute-start | bytes 1572872 | tf_op jit(solution)/shard_map/ppermute | solution.py:329
  222.1 34.2 %collective-permute-start.30 = (bf16[2,128,2048]{2,1,0:T(8,128)(2,1)S(1)}, bf16[2,128,2048]{2,1,0:T(8,128)(2,1)S(1)}, u32[]{:S(2)}, u32[]{:S(2)}) collective-permute-start(bf16[2,128,2048]{2,1,0:T(8,128)(2,1)S(1)} %get-tuple-element.396), channel_id=1, source_target_pairs={{0,1},{1,0},{2,3},{3,2},{4,5},{5,4},{6,7},{7,6},{8,9},{9,8},{10,11... | collective-permute-start | bytes 3145736 | tf_op jit(solution)/shard_map/ppermute | solution.py:331
  298.3 37.5 %collective-permute-start.56 = (bf16[512,1536]{1,0:T(8,128)(2,1)}, bf16[512,1536]{1,0:T(8,128)(2,1)S(1)}, u32[]{:S(2)}, u32[]{:S(2)}) collective-permute-start(bf16[512,1536]{1,0:T(8,128)(2,1)} %convolution_convert_fusion.3), channel_id=1, source_target_pairs={{0,16},{8,24},{16,0},{24,8},{1,17},{9,25},{17,1},{25,9},{2,18},{10... | collective-permute-start | bytes 4718600 | tf_op jit(solution)/shard_map/ppermute | solution.py:329
  303.3 64.3 %collective-permute-start.81 = (bf16[512,1536]{1,0:T(8,128)(2,1)}, bf16[512,1536]{1,0:T(8,128)(2,1)S(1)}, u32[]{:S(2)}, u32[]{:S(2)}) collective-permute-start(bf16[512,1536]{1,0:T(8,128)(2,1)} %convolution_convert_fusion.2), channel_id=1, source_target_pairs={{0,24},{8,16},{16,8},{24,0},{1,25},{9,17},{17,9},{25,1},{2,26},{10... | collective-permute-start | bytes 4718600 | tf_op jit(solution)/shard_map/ppermute | solution.py:329
  315.8 89.7 %collective-permute-start.43 = (bf16[512,1536]{1,0:T(8,128)(2,1)}, bf16[512,1536]{1,0:T(8,128)(2,1)S(1)}, u32[]{:S(2)}, u32[]{:S(2)}) collective-permute-start(bf16[512,1536]{1,0:T(8,128)(2,1)} %convolution_convert_fusion.5), channel_id=1, source_target_pairs={{0,8},{8,0},{16,24},{24,16},{1,9},{9,1},{17,25},{25,17},{2,10},{10... | collective-permute-start | bytes 4718600 | tf_op jit(solution)/shard_map/ppermute | solution.py:329
  317.8 54.2 %collective-permute-start.34 = (bf16[128,2048]{1,0:T(8,128)(2,1)S(1)}, bf16[128,2048]{1,0:T(8,128)(2,1)S(1)}, u32[]{:S(2)}, u32[]{:S(2)}) collective-permute-start(bf16[128,2048]{1,0:T(8,128)(2,1)S(1)} %get-tuple-element.367), channel_id=1, source_target_pairs={{0,1},{1,0},{2,3},{3,2},{4,5},{5,4},{6,7},{7,6},{8,9},{9,8},{10,11... | collective-permute-start | bytes 1572872 | tf_op jit(solution)/shard_map/ppermute | solution.py:331
  319.4 61.3 %collective-permute-start.35 = (bf16[128,2048]{1,0:T(8,128)(2,1)S(1)}, bf16[128,2048]{1,0:T(8,128)(2,1)S(1)}, u32[]{:S(2)}, u32[]{:S(2)}) collective-permute-start(bf16[128,2048]{1,0:T(8,128)(2,1)S(1)} %get-tuple-element.369), channel_id=1, source_target_pairs={{0,16},{8,24},{16,0},{24,8},{1,17},{9,25},{17,1},{25,9},{2,18},{10... | collective-permute-start | bytes 1572872 | tf_op jit(solution)/shard_map/ppermute | solution.py:329
  335.7 56.2 %collective-permute-start.36 = (bf16[128,2048]{1,0:T(8,128)(2,1)S(1)}, bf16[128,2048]{1,0:T(8,128)(2,1)S(1)}, u32[]{:S(2)}, u32[]{:S(2)}) collective-permute-start(bf16[128,2048]{1,0:T(8,128)(2,1)S(1)} %get-tuple-element.368), channel_id=1, source_target_pairs={{0,17},{1,16},{8,25},{9,24},{16,1},{17,0},{24,9},{25,8},{2,19},{3,... | collective-permute-start | bytes 1572872 | tf_op jit(solution)/shard_map/ppermute | solution.py:332
  372.0 32.8 %collective-permute-start.39 = (bf16[192,2048]{1,0:T(8,128)(2,1)S(1)}, bf16[192,2048]{1,0:T(8,128)(2,1)S(1)}, u32[]{:S(2)}, u32[]{:S(2)}) collective-permute-start(bf16[192,2048]{1,0:T(8,128)(2,1)S(1)} %get-tuple-element.195), channel_id=1, source_target_pairs={{0,2},{6,4},{1,3},{7,5},{8,10},{14,12},{9,11},{15,13},{16,18},{22,... | collective-permute-start | bytes 2359304 | tf_op jit(solution)/shard_map/ppermute | solution.py:417
  404.8 30.1 %collective-permute-start.37 = (bf16[192,2048]{1,0:T(8,128)(2,1)S(1)}, bf16[192,2048]{1,0:T(8,128)(2,1)S(1)}, u32[]{:S(2)}, u32[]{:S(2)}) collective-permute-start(bf16[192,2048]{1,0:T(8,128)(2,1)S(1)} %add_convert_fusion.33), channel_id=1, source_target_pairs={{2,4},{4,2},{3,5},{5,3},{10,12},{12,10},{11,13},{13,11},{18,20},{2... | collective-permute-start | bytes 2359304 | tf_op jit(solution)/shard_map/ppermute | solution.py:414
  424.4 33.0 %collective-permute-start.52 = (bf16[192,2048]{1,0:T(8,128)(2,1)S(1)}, bf16[192,2048]{1,0:T(8,128)(2,1)S(1)}, u32[]{:S(2)}, u32[]{:S(2)}) collective-permute-start(bf16[192,2048]{1,0:T(8,128)(2,1)S(1)} %get-tuple-element.210), channel_id=1, source_target_pairs={{0,2},{6,4},{1,3},{7,5},{8,10},{14,12},{9,11},{15,13},{16,18},{22,... | collective-permute-start | bytes 2359304 | tf_op jit(solution)/shard_map/ppermute | solution.py:417
  430.1 63.6 %collective-permute-start.70 = (bf16[512,2048]{1,0:T(8,128)(2,1)}, bf16[512,2048]{1,0:T(8,128)(2,1)}, u32[]{:S(2)}, u32[]{:S(2)}) collective-permute-start(bf16[512,2048]{1,0:T(8,128)(2,1)} %convolution_convert_fusion.6), channel_id=1, source_target_pairs={{0,8},{8,0},{16,24},{24,16},{1,9},{9,1},{17,25},{25,17},{2,10},{10... | collective-permute-start | bytes 6291464 | tf_op jit(solution)/shard_map/ppermute | solution.py:329
  444.0 35.8 %collective-permute-start.49 = (bf16[192,2048]{1,0:T(8,128)(2,1)}, bf16[192,2048]{1,0:T(8,128)(2,1)}, u32[]{:S(2)}, u32[]{:S(2)}) collective-permute-start(bf16[192,2048]{1,0:T(8,128)(2,1)} %add_convert_fusion.31), channel_id=1, source_target_pairs={{2,4},{4,2},{3,5},{5,3},{10,12},{12,10},{11,13},{13,11},{18,20},{2... | collective-permute-start | bytes 2359304 | tf_op jit(solution)/shard_map/ppermute | solution.py:414
  446.7 34.5 %collective-permute-start.48 = (bf16[192,2048]{1,0:T(8,128)(2,1)}, bf16[192,2048]{1,0:T(8,128)(2,1)}, u32[]{:S(2)}, u32[]{:S(2)}) collective-permute-start(bf16[192,2048]{1,0:T(8,128)(2,1)} %add_convert_fusion.32), channel_id=1, source_target_pairs={{2,0},{4,6},{3,1},{5,7},{10,8},{12,14},{11,9},{13,15},{18,16},{20,... | collective-permute-start | bytes 2359304 | tf_op jit(solution)/shard_map/ppermute | solution.py:414
  450.6 30.7 %collective-permute-start.50 = (bf16[512,768]{1,0:T(8,128)(2,1)}, bf16[512,768]{1,0:T(8,128)(2,1)}, u32[]{:S(2)}, u32[]{:S(2)}) collective-permute-start(bf16[512,768]{1,0:T(8,128)(2,1)} %get-tuple-element.205), channel_id=1, source_target_pairs={{0,2},{6,4},{1,3},{7,5},{8,10},{14,12},{9,11},{15,13},{16,18},{22,... | collective-permute-start | bytes 2359304 | tf_op jit(solution)/shard_map/ppermute | solution.py:417
  479.7 41.2 %collective-permute-start.57 = (bf16[192,2048]{1,0:T(8,128)(2,1)S(1)}, bf16[192,2048]{1,0:T(8,128)(2,1)S(1)}, u32[]{:S(2)}, u32[]{:S(2)}) collective-permute-start(bf16[192,2048]{1,0:T(8,128)(2,1)S(1)} %add_convert_fusion.27), channel_id=1, source_target_pairs={{2,0},{4,6},{3,1},{5,7},{10,8},{12,14},{11,9},{13,15},{18,16},{20,... | collective-permute-start | bytes 2359304 | tf_op jit(solution)/shard_map/ppermute | solution.py:414
  520.9 52.2 %collective-permute-start.54 = (bf16[512,768]{1,0:T(8,128)(2,1)S(1)}, bf16[512,768]{1,0:T(8,128)(2,1)S(1)}, u32[]{:S(2)}, u32[]{:S(2)}) collective-permute-start(bf16[512,768]{1,0:T(8,128)(2,1)S(1)} %add_convert_fusion.28), channel_id=1, source_target_pairs={{2,4},{4,2},{3,5},{5,3},{10,12},{12,10},{11,13},{13,11},{18,20},{2... | collective-permute-start | bytes 2359304 | tf_op jit(solution)/shard_map/ppermute | solution.py:414
  521.8 52.0 %collective-permute-start.53 = (bf16[192,2048]{1,0:T(8,128)(2,1)S(1)}, bf16[192,2048]{1,0:T(8,128)(2,1)S(1)}, u32[]{:S(2)}, u32[]{:S(2)}) collective-permute-start(bf16[192,2048]{1,0:T(8,128)(2,1)S(1)} %add_convert_fusion.29), channel_id=1, source_target_pairs={{2,0},{4,6},{3,1},{5,7},{10,8},{12,14},{11,9},{13,15},{18,16},{20,... | collective-permute-start | bytes 2359304 | tf_op jit(solution)/shard_map/ppermute | solution.py:414
  530.0 45.2 %collective-permute-start.55 = (bf16[512,768]{1,0:T(8,128)(2,1)S(1)}, bf16[512,768]{1,0:T(8,128)(2,1)S(1)}, u32[]{:S(2)}, u32[]{:S(2)}) collective-permute-start(bf16[512,768]{1,0:T(8,128)(2,1)S(1)} %copy-done.33), channel_id=1, source_target_pairs={{0,2},{6,4},{1,3},{7,5},{8,10},{14,12},{9,11},{15,13},{16,18},{22,... | collective-permute-start | bytes 2359304 | tf_op jit(solution)/shard_map/ppermute | solution.py:417
  540.9 38.9 %collective-permute-start.74 = (bf16[128,2048]{1,0:T(8,128)(2,1)S(1)}, bf16[128,2048]{1,0:T(8,128)(2,1)S(1)}, u32[]{:S(2)}, u32[]{:S(2)}) collective-permute-start(bf16[128,2048]{1,0:T(8,128)(2,1)S(1)} %fusion.48), channel_id=1, source_target_pairs={{0,0},{2,8},{4,16},{6,24},{8,2},{10,10},{12,18},{14,26},{16,4},{18... | collective-permute-start | bytes 1572872 | tf_op jit(solution)/shard_map/ppermute | solution.py:342
  573.8 41.5 %collective-permute-start.75 = (bf16[192,2048]{1,0:T(8,128)(2,1)S(1)}, bf16[192,2048]{1,0:T(8,128)(2,1)S(1)}, u32[]{:S(2)}, u32[]{:S(2)}) collective-permute-start(bf16[192,2048]{1,0:T(8,128)(2,1)S(1)} %add_convert_fusion.25), channel_id=1, source_target_pairs={{2,0},{4,6},{3,1},{5,7},{10,8},{12,14},{11,9},{13,15},{18,16},{20,... | collective-permute-start | bytes 2359304 | tf_op jit(solution)/shard_map/ppermute | solution.py:414
  575.2 40.2 %collective-permute-start.77 = (bf16[512,768]{1,0:T(8,128)(2,1)S(1)}, bf16[512,768]{1,0:T(8,128)(2,1)S(1)}, u32[]{:S(2)}, u32[]{:S(2)}) collective-permute-start(bf16[512,768]{1,0:T(8,128)(2,1)S(1)} %copy-done.32), channel_id=1, source_target_pairs={{0,2},{6,4},{1,3},{7,5},{8,10},{14,12},{9,11},{15,13},{16,18},{22,... | collective-permute-start | bytes 2359304 | tf_op jit(solution)/shard_map/ppermute | solution.py:417
  597.5 34.6 %collective-permute-start.94 = (bf16[512,768]{1,0:T(8,128)(2,1)S(1)}, bf16[512,768]{1,0:T(8,128)(2,1)S(1)}, u32[]{:S(2)}, u32[]{:S(2)}) collective-permute-start(bf16[512,768]{1,0:T(8,128)(2,1)S(1)} %add_convert_fusion.13), channel_id=1, source_target_pairs={{2,0},{4,6},{3,1},{5,7},{10,8},{12,14},{11,9},{13,15},{18,16},{20,... | collective-permute-start | bytes 2359304 | tf_op jit(solution)/shard_map/ppermute | solution.py:414
  600.0 32.1 %collective-permute-start.96 = (bf16[512,768]{1,0:T(8,128)(2,1)S(1)}, bf16[512,768]{1,0:T(8,128)(2,1)S(1)}, u32[]{:S(2)}, u32[]{:S(2)}) collective-permute-start(bf16[512,768]{1,0:T(8,128)(2,1)S(1)} %copy-done.31), channel_id=1, source_target_pairs={{0,2},{6,4},{1,3},{7,5},{8,10},{14,12},{9,11},{15,13},{16,18},{22,... | collective-permute-start | bytes 2359304 | tf_op jit(solution)/shard_map/ppermute | solution.py:417
  616.5 32.3 %collective-permute-start.78 = (bf16[512,768]{1,0:T(8,128)(2,1)S(1)}, bf16[512,768]{1,0:T(8,128)(2,1)S(1)}, u32[]{:S(2)}, u32[]{:S(2)}) collective-permute-start(bf16[512,768]{1,0:T(8,128)(2,1)S(1)} %add_convert_fusion.23), channel_id=1, source_target_pairs={{2,0},{4,6},{3,1},{5,7},{10,8},{12,14},{11,9},{13,15},{18,16},{20,... | collective-permute-start | bytes 2359304 | tf_op jit(solution)/shard_map/ppermute | solution.py:414
  618.0 30.9 %collective-permute-start.80 = (bf16[512,768]{1,0:T(8,128)(2,1)S(1)}, bf16[512,768]{1,0:T(8,128)(2,1)S(1)}, u32[]{:S(2)}, u32[]{:S(2)}) collective-permute-start(bf16[512,768]{1,0:T(8,128)(2,1)S(1)} %copy-done.30), channel_id=1, source_target_pairs={{0,2},{6,4},{1,3},{7,5},{8,10},{14,12},{9,11},{15,13},{16,18},{22,... | collective-permute-start | bytes 2359304 | tf_op jit(solution)/shard_map/ppermute | solution.py:417
  633.4 37.4 %collective-permute-start.97 = (bf16[512,768]{1,0:T(8,128)(2,1)S(1)}, bf16[512,768]{1,0:T(8,128)(2,1)S(1)}, u32[]{:S(2)}, u32[]{:S(2)}) collective-permute-start(bf16[512,768]{1,0:T(8,128)(2,1)S(1)} %add_convert_fusion.11), channel_id=1, source_target_pairs={{2,0},{4,6},{3,1},{5,7},{10,8},{12,14},{11,9},{13,15},{18,16},{20,... | collective-permute-start | bytes 2359304 | tf_op jit(solution)/shard_map/ppermute | solution.py:414
  634.7 37.2 %collective-permute-start.99 = (bf16[512,768]{1,0:T(8,128)(2,1)S(1)}, bf16[512,768]{1,0:T(8,128)(2,1)S(1)}, u32[]{:S(2)}, u32[]{:S(2)}) collective-permute-start(bf16[512,768]{1,0:T(8,128)(2,1)S(1)} %copy-done.28), channel_id=1, source_target_pairs={{0,2},{6,4},{1,3},{7,5},{8,10},{14,12},{9,11},{15,13},{16,18},{22,... | collective-permute-start | bytes 2359304 | tf_op jit(solution)/shard_map/ppermute | solution.py:417
  671.9 58.3 %collective-permute-start.102 = (bf16[256,2048]{1,0:T(8,128)(2,1)S(1)}, bf16[256,2048]{1,0:T(8,128)(2,1)S(1)}, u32[]{:S(2)}, u32[]{:S(2)}) collective-permute-start(bf16[256,2048]{1,0:T(8,128)(2,1)S(1)} %copy-done.53), channel_id=1, source_target_pairs={{0,2},{6,4},{1,3},{7,5},{8,10},{14,12},{9,11},{15,13},{16,18},{22,... | collective-permute-start | bytes 3145736 | tf_op jit(solution)/shard_map/ppermute | solution.py:417
  682.9 33.1 %collective-permute-start.87 = (bf16[512,768]{1,0:T(8,128)(2,1)S(1)}, bf16[512,768]{1,0:T(8,128)(2,1)S(1)}, u32[]{:S(2)}, u32[]{:S(2)}) collective-permute-start(bf16[512,768]{1,0:T(8,128)(2,1)S(1)} %convolution_convert_fusion.13), channel_id=1, source_target_pairs={{0,2},{6,4},{1,3},{7,5},{8,10},{14,12},{9,11},{15,13},{16,18},{22,... | collective-permute-start | bytes 2359304 | tf_op jit(solution)/shard_map/ppermute | solution.py:417
  716.0 35.8 %collective-permute-start.107 = (bf16[512,768]{1,0:T(8,128)(2,1)S(1)}, bf16[512,768]{1,0:T(8,128)(2,1)S(1)}, u32[]{:S(2)}, u32[]{:S(2)}) collective-permute-start(bf16[512,768]{1,0:T(8,128)(2,1)S(1)} %convolution_convert_fusion.10), channel_id=1, source_target_pairs={{0,24},{8,16},{16,8},{24,0},{1,25},{9,17},{17,9},{25,1},{2,26},{10... | collective-permute-start | bytes 2359304 | tf_op jit(solution)/shard_map/ppermute | solution.py:329
  730.7 37.2 %collective-permute-start.105 = (bf16[256,2048]{1,0:T(8,128)(2,1)S(1)}, bf16[256,2048]{1,0:T(8,128)(2,1)S(1)}, u32[]{:S(2)}, u32[]{:S(2)}) collective-permute-start(bf16[256,2048]{1,0:T(8,128)(2,1)S(1)} %add_convert_fusion.1), channel_id=1, source_target_pairs={{2,4},{4,2},{3,5},{5,3},{10,12},{12,10},{11,13},{13,11},{18,20},{2... | collective-permute-start | bytes 3145736 | tf_op jit(solution)/shard_map/ppermute | solution.py:414
  732.1 34.6 %collective-permute-start.104 = (bf16[512,768]{1,0:T(8,128)(2,1)S(1)}, bf16[512,768]{1,0:T(8,128)(2,1)S(1)}, u32[]{:S(2)}, u32[]{:S(2)}) collective-permute-start(bf16[512,768]{1,0:T(8,128)(2,1)S(1)} %add_convert_fusion.7), channel_id=1, source_target_pairs={{2,0},{4,6},{3,1},{5,7},{10,8},{12,14},{11,9},{13,15},{18,16},{20,... | collective-permute-start | bytes 2359304 | tf_op jit(solution)/shard_map/ppermute | solution.py:414
  751.8 31.8 %collective-permute-start.92 = (bf16[512,768]{1,0:T(8,128)(2,1)S(1)}, bf16[512,768]{1,0:T(8,128)(2,1)S(1)}, u32[]{:S(2)}, u32[]{:S(2)}) collective-permute-start(bf16[512,768]{1,0:T(8,128)(2,1)S(1)} %add_convert_fusion.15), channel_id=1, source_target_pairs={{2,0},{4,6},{3,1},{5,7},{10,8},{12,14},{11,9},{13,15},{18,16},{20,... | collective-permute-start | bytes 2359304 | tf_op jit(solution)/shard_map/ppermute | solution.py:414
  769.2 36.9 %collective-permute-start.108 = (bf16[256,2048]{1,0:T(8,128)(2,1)S(1)}, bf16[256,2048]{1,0:T(8,128)(2,1)S(1)}, u32[]{:S(2)}, u32[]{:S(2)}) collective-permute-start(bf16[256,2048]{1,0:T(8,128)(2,1)S(1)} %add_convert_fusion), channel_id=1, source_target_pairs={{2,0},{4,6},{3,1},{5,7},{10,8},{12,14},{11,9},{13,15},{18,16},{20,... | collective-permute-start | bytes 3145736 | tf_op jit(solution)/shard_map/ppermute | solution.py:414
  783.8 39.1 %collective-permute-start.113 = (bf16[512,768]{1,0:T(8,128)(2,1)S(1)}, bf16[512,768]{1,0:T(8,128)(2,1)S(1)}, u32[]{:S(2)}, u32[]{:S(2)}) collective-permute-start(bf16[512,768]{1,0:T(8,128)(2,1)S(1)} %add_convert_fusion.3), channel_id=1, source_target_pairs={{2,0},{4,6},{3,1},{5,7},{10,8},{12,14},{11,9},{13,15},{18,16},{20,... | collective-permute-start | bytes 2359304 | tf_op jit(solution)/shard_map/ppermute | solution.py:414
  807.2 32.4 %collective-permute-start.111 = (bf16[512,768]{1,0:T(8,128)(2,1)S(1)}, bf16[512,768]{1,0:T(8,128)(2,1)S(1)}, u32[]{:S(2)}, u32[]{:S(2)}) collective-permute-start(bf16[512,768]{1,0:T(8,128)(2,1)S(1)} %add_convert_fusion.5), channel_id=1, source_target_pairs={{2,0},{4,6},{3,1},{5,7},{10,8},{12,14},{11,9},{13,15},{18,16},{20,... | collective-permute-start | bytes 2359304 | tf_op jit(solution)/shard_map/ppermute | solution.py:414
  (164 other events, 2580.6 us)

commit v3 on v1

--- a/solution.py
+++ b/solution.py
@@ -345,20 +345,43 @@
 PIECES = ((0, 0), (0, 1), (2, 0), (2, 1))
 
 
-def plane_gather(own):
-    near = [own if masks == (0, 0) else swap_plane(own, *masks) for masks in PIECES]
-    far = [swap_plane(piece, 1, 0) for piece in near]
-    return jnp.concatenate(near + far, axis=0)
-
-
-def plane_scatter(near_part, far_part):
-    rows = near_part.shape[0] // 4
-    half = near_part + swap_plane(far_part.astype(jnp.bfloat16), 1, 0).astype(jnp.float32)
-    total = half[:rows]
-    for place in range(1, 4):
-        piece = half[place * rows : (place + 1) * rows].astype(jnp.bfloat16)
-        total = total + swap_plane(piece, *PIECES[place]).astype(jnp.float32)
-    return total
+def plane_near(own):
+    rows = own.shape[0] // 2
+    over_tp, over_x = swap_plane(own, 0, 1), swap_plane(own, 2, 0)
+    three = jnp.concatenate([own, over_tp, over_x], axis=0)
+    corner = [swap_plane(over_x[:rows], 0, 1), swap_plane(over_tp[rows:], 2, 0)]
+    return three, swap_plane(three, 1, 0), jnp.concatenate(corner, axis=0)
+
+
+def plane_join(near):
+    three, three_far, corner = near
+    return jnp.concatenate([three, corner, three_far, swap_plane(corner, 1, 0)], axis=0)
+
+
+def scatter_half(near_part, far_part):
+    return near_part + swap_plane(far_part.astype(jnp.bfloat16), 1, 0).astype(jnp.float32)
+
+
+def scatter_plane(half):
+    rows = half.shape[0] // 8
+    piece = [half[at * rows : (at + 1) * rows] for at in range(8)]
+
+    def sent(parts, *masks):
+        low = jnp.concatenate(parts, axis=0).astype(jnp.bfloat16)
+        return swap_plane(low, *masks).astype(jnp.float32)
+
+    by_x = sent([piece[4], piece[6]], 2, 0)
+    by_tp = sent([piece[3], piece[7]], 0, 1)
+    top = sent([piece[2] + by_x[rows:]], 0, 1)
+    bottom = sent([piece[5] + by_tp[rows:]], 2, 0)
+    return jnp.concatenate([piece[0] + by_x[:rows], piece[1] + by_tp[:rows]], axis=0), [
+        top.astype(jnp.bfloat16),
+        bottom.astype(jnp.bfloat16),
+    ]
+
+
+def scatter_total(own, came):
+    return own + jnp.concatenate(came, axis=0).astype(jnp.float32)
 
 
 def dot_nn(a, b):
@@ -373,29 +396,55 @@
     return lax.dot_general(a, b, (((0,), (0,)), ((), ())), preferred_element_type=jnp.float32)
 
 
-def scatter_product(rows, weight, dot):
-    half = rows.shape[0] // 2
-    far_part = dot(rows[half:], weight)
-    near_part = dot(rows[:half], weight)
-    return plane_scatter(near_part, far_part)
-
-
-def chain_sum(part):
-    low = part.astype(jnp.bfloat16)
-    place = lax.axis_index("ctx")
-    inward = lax.ppermute(low, "ctx", [(0, 1), (3, 2)])
-    pair = (low.astype(jnp.float32) + inward.astype(jnp.float32)).astype(jnp.bfloat16)
-    across = lax.ppermute(pair, "ctx", [(1, 2), (2, 1)])
-    total = (pair.astype(jnp.float32) + across.astype(jnp.float32)).astype(jnp.bfloat16)
-    outward = lax.ppermute(total, "ctx", [(1, 0), (2, 3)])
-    inner = (place == 1) | (place == 2)
-    return jnp.where(inner, total, outward).astype(jnp.float32)
-
-
-def all_sum(value):
+INWARD, ACROSS, OUTWARD = [(0, 1), (3, 2)], [(1, 2), (2, 1)], [(1, 0), (2, 3)]
+
+
+class CtxSums:
+    def __init__(self):
+        self.flight, self.arrived, self.done = [], [], {}
+
+    def send(self, *fresh):
+        place = lax.axis_index("ctx")
+        inner = (place == 1) | (place == 2)
+        sent, totals, fresh = [], [], list(fresh)
+        for stage, name, here, came in self.arrived:
+            if stage == 2:
+                self.done[name] = jnp.where(inner, here, came).astype(jnp.float32)
+                continue
+            both = (here.astype(jnp.float32) + came.astype(jnp.float32)).astype(jnp.bfloat16)
+            if stage:
+                totals.append((name, both))
+            else:
+                sent.append(([(1, name, both)], lax.ppermute(both, "ctx", ACROSS)))
+        while totals and fresh and totals[0][1].shape == fresh[0][1].shape:
+            (out, total), (name, part) = totals.pop(0), fresh.pop(0)
+            moved = swap_ctx(jnp.where(inner, total, part))
+            sent.append(([(0, name, part), (2, out, total)], moved))
+        for name, part in fresh:
+            sent.append(([(0, name, part)], lax.ppermute(part, "ctx", INWARD)))
+        for name, total in totals:
+            sent.append(([(2, name, total)], lax.ppermute(total, "ctx", OUTWARD)))
+        self.arrived = []
+        self.flight.append(sent)
+
+    def wait(self, kept, depth=1):
+        old = []
+        while len(self.flight) >= depth:
+            old += self.flight.pop(0)
+        heres = [[here for _, _, here in entry[0]] for entry in old]
+        moved = [entry[1] for entry in old]
+        heres, moved, kept = lax.optimization_barrier((heres, moved, kept))
+        self.arrived = [
+            (stage, name, here, came)
+            for entry, parts, came in zip(old, heres, moved)
+            for (stage, name, _), here in zip(entry[0], parts)
+        ]
+        return kept
+
+
+def sum_hops():
     for axis, mask in (("fsdp", 1), ("fsdp", 2), ("tp", 1), ("ctx", 1), ("ctx", 2)):
-        value = value + lax.ppermute(value, axis, xor_pairs(lax.axis_size(axis), mask))
-    return value
+        yield axis, xor_pairs(lax.axis_size(axis), mask)
 
 
 def weight_columns(weights, owner):
@@ -406,37 +455,57 @@
     return jnp.concatenate(parts, axis=1)
 
 
-def fetch_weights(weights):
+class Fetch:
+    def __init__(self, weights):
+        self.me, self.size = lax.axis_index("fsdp"), lax.axis_size("fsdp")
+        self.side = lax.axis_index("ctx") % 2
+        self.rows = weights[0].shape[0]
+        self.half = self.rows // 2
+        mine = [
+            lax.dynamic_slice_in_dim(weight, self.side * self.half, self.half, 0)
+            for weight in weights
+        ]
+        self.columns = [weight_columns(mine, self.me ^ mask) for mask in (2, 3)]
+        self.own = weight_columns(weights, self.me)
+        self.core = weight_columns(weights, self.me ^ 1)
+
+    def along_x(self, at):
+        return swap_plane(self.columns[at], (2, 3)[at], 0)
+
+    def along_core(self):
+        return swap_plane(self.core, 1, 0)
+
+    def begin(self, core):
+        whole = jnp.zeros((self.rows * self.size, self.own.shape[1]), self.own.dtype)
+        for part, peer in ((self.own, self.me), (core, self.me ^ 1)):
+            whole = lax.dynamic_update_slice_in_dim(whole, part, peer * self.rows, 0)
+        return whole
+
+    def add(self, whole, at, came, other):
+        start = (self.me ^ (2, 3)[at]) * self.rows
+        whole = lax.dynamic_update_slice_in_dim(whole, came, start + self.side * self.half, 0)
+        return lax.dynamic_update_slice_in_dim(
+            whole, other, start + (1 - self.side) * self.half, 0
+        )
+
+
+def swap_ctx(value):
+    return lax.ppermute(value, "ctx", xor_pairs(lax.axis_size("ctx"), 1))
+
+
+def grad_part(left, right, mask):
+    owner = lax.axis_index("fsdp") ^ mask
+    rows = left.shape[1] // lax.axis_size("fsdp")
+    columns = lax.dynamic_slice_in_dim(left, owner * rows, rows, 1)
+    return dot_tn(columns, right).astype(jnp.bfloat16)
+
+
+def place_columns(parts, width):
     me, size = lax.axis_index("fsdp"), lax.axis_size("fsdp")
-    rows = weights[0].shape[0]
-    whole = None
-    for mask in range(size):
-        part = weight_columns(weights, me ^ mask)
-        if mask:
-            part = swap_plane(part, mask, 0)
-        if whole is None:
-            whole = jnp.zeros((rows * size, part.shape[1]), part.dtype)
-        whole = lax.dynamic_update_slice_in_dim(whole, part, (me ^ mask) * rows, 0)
+    whole = jnp.zeros((parts[0].shape[0], width * size), jnp.float32)
+    for mask, part in enumerate(parts):
+        whole = lax.dynamic_update_slice_in_dim(whole, part, (me ^ mask) * width, 1)
     return whole
-
-
-def return_grads(left, right, widths):
-    me, size = lax.axis_index("fsdp"), lax.axis_size("fsdp")
-    rows = left.shape[1] // size
-    outs = [jnp.zeros((rows, width * size), jnp.float32) for width in widths]
-    for mask in range(size):
-        columns = lax.dynamic_slice_in_dim(left, (me ^ mask) * rows, rows, 1)
-        part = dot_tn(columns, right).astype(jnp.bfloat16)
-        if mask:
-            part = swap_plane(part, mask, 0)
-        summed = chain_sum(part)
-        offset = 0
-        for place, width in enumerate(widths):
-            outs[place] = lax.dynamic_update_slice_in_dim(
-                outs[place], summed[:, offset : offset + width], (me ^ mask) * width, 1
-            )
-            offset += width
-    return outs
 
 
 def plane_body(
@@ -468,9 +537,18 @@
     query_gain = query_norm_gain.astype(jnp.float32)
     key_gain = k_norm.astype(jnp.float32)
 
-    inputs = swap_ranks(layer_input).astype(jnp.float32)
+    together = lax.optimization_barrier
+    input_low = swap_ranks(layer_input)
+    attn_fetch = Fetch((w_query, key_weight, value_weight, w_out_gate))
+    attn_came = [attn_fetch.along_x(at) for at in range(2)]
+    attn_core = attn_fetch.along_core()
+    ffn_fetch = Fetch((w_gate, w_up))
+    cot_low = swap_ranks(cotangent)
     lengths = swap_ranks(lengths)
-    cot = swap_ranks(cotangent).astype(jnp.float32)
+    input_low, attn_came, ffn_fetch.columns[0] = together(
+        (input_low, attn_came, ffn_fetch.columns[0])
+    )
+    inputs = input_low.astype(jnp.float32)
 
     def slots_of(fsdp_index, tp_index):
         return (fsdp_index * tp_size + tp_index) * local_rows + jnp.arange(
@@ -489,11 +567,25 @@
     segment = segment_of(slots, lengths)
     position = position_of(slots, segment, lengths)
 
-    first_normed = plane_gather(apply_rms_norm(inputs, gain_one).astype(jnp.bfloat16))
-    attn_weights = fetch_weights((w_query, key_weight, value_weight, w_out_gate))
-    out_grad = cot * own_valid
-    ffn_grad = plane_gather(out_grad.astype(jnp.bfloat16))
-    ffn_weights = fetch_weights((w_gate, w_up))
+    first_own = apply_rms_norm(inputs, gain_one).astype(jnp.bfloat16)
+    first_near = plane_near(first_own)
+    attn_other = [swap_ctx(came) for came in attn_came]
+    attn_weights = attn_fetch.begin(attn_core)
+    ffn_came = [ffn_fetch.along_x(0)]
+    ffn_columns = (ffn_fetch.columns[1], ffn_fetch.core)
+    first_near, attn_other, attn_weights, attn_came, cot_low, ffn_columns, ffn_came = together(
+        (first_near, attn_other, attn_weights, attn_came, cot_low, ffn_columns, ffn_came)
+    )
+    ffn_fetch.columns[1], ffn_fetch.core = ffn_columns
+    out_grad = cot_low.astype(jnp.float32) * own_valid
+    cot_own = out_grad.astype(jnp.bfloat16)
+    cot_across = swap_plane(cot_own, 2, 0)
+    ffn_came.append(ffn_fetch.along_x(1))
+    ffn_other = swap_ctx(ffn_came[0])
+    ffn_core = ffn_fetch.along_core()
+    first_normed = plane_join(first_near)
+    for at in range(2):
+        attn_weights = attn_fetch.add(attn_weights, at, attn_came[at], attn_other[at])
 
     projected = dot_nn(first_normed, attn_weights)
     query_raw = projected[:, :query_width].reshape(row_slots, query_heads, HEAD_SIZE)
@@ -508,6 +600,14 @@
     key_rot = apply_rotary(apply_rms_norm(key_raw, key_gain), position, 1.0).astype(jnp.bfloat16)[
         :, 0
     ]
+
+    query_rot, key_rot, value_low, cot_across = together(
+        (query_rot, key_rot, value_low, cot_across)
+    )
+    cot_pair = jnp.stack([cot_own, cot_across])
+    cot_near = jnp.stack([cot_pair, swap_plane(cot_pair, 0, 1)], axis=1).reshape(
+        -1, cot_own.shape[1]
+    )
 
     allowed = (segment[:, None] == segment[None, :]) & (slots[None, :] <= slots[:, None])
     raw_scores = jnp.einsum("qgd,kd->gqk", query_rot, key_rot, preferred_element_type=jnp.float32)
@@ -523,9 +623,23 @@
     attended_rows = attended.reshape(row_slots, query_width)
     gate_sig = jax.nn.sigmoid(gate_logits)
     gated_mix = (attended_rows * gate_sig).astype(jnp.bfloat16)
-    attn_share = scatter_product(gated_mix, w_output, dot_nn)
-    hidden_in = inputs + own_valid * attn_share
-    normed_two = plane_gather(apply_rms_norm(hidden_in, gain_two).astype(jnp.bfloat16))
+    gated_mix, ffn_other, ffn_came = together((gated_mix, ffn_other, ffn_came))
+    ffn_others = [ffn_other, swap_ctx(ffn_came[1])]
+    half = row_slots // 2
+    far_part = dot_nn(gated_mix[half:], w_output)
+    near_part = dot_nn(gated_mix[:half], w_output)
+    own_part, came_parts = scatter_plane(scatter_half(near_part, far_part))
+    ffn_weights = ffn_fetch.begin(ffn_core)
+    ffn_weights = ffn_fetch.add(ffn_weights, 0, ffn_came[0], ffn_others[0])
+    own_part, came_parts, cot_near, ffn_others, ffn_weights, ffn_came = together(
+        (own_part, came_parts, cot_near, ffn_others, ffn_weights, ffn_came)
+    )
+    ffn_grad = jnp.concatenate([cot_near, swap_plane(cot_near, 1, 0)], axis=0)
+    hidden_in = inputs + own_valid * scatter_total(own_part, came_parts)
+    second_near = plane_near(apply_rms_norm(hidden_in, gain_two).astype(jnp.bfloat16))
+    ffn_weights = ffn_fetch.add(ffn_weights, 1, ffn_came[1], ffn_others[1])
+    second_near, ffn_grad, ffn_weights = together((second_near, ffn_grad, ffn_weights))
+    normed_two = plane_join(second_near)
 
     hidden_grad = dot_nt(ffn_grad, w_down)
     pre = dot_nn(normed_two, ffn_weights)
@@ -534,22 +648,40 @@
     gate_sigmoid = jax.nn.sigmoid(gate_pre)
     activated = gate_pre * gate_sigmoid
     hidden_act = (activated * up_pre).astype(jnp.bfloat16)
-    grad_w_down = chain_sum(dot_tn(hidden_act, ffn_grad))
     gate_grad = (
         hidden_grad * up_pre * gate_sigmoid * (1.0 + gate_pre * (1.0 - gate_sigmoid))
     ).astype(jnp.bfloat16)
     up_grad = (hidden_grad * activated).astype(jnp.bfloat16)
     ffn_in_grads = jnp.concatenate([gate_grad, up_grad], axis=1)
-    normed_two_grad = scatter_product(ffn_in_grads, ffn_weights, dot_nt)
-    grad_w_gate, grad_w_up = return_grads(normed_two, ffn_in_grads, (hidden_width, hidden_width))
-    ffn_share = scatter_product(hidden_act, w_down, dot_nn)
-    layer_output = swap_ranks((hidden_in + own_valid * ffn_share).astype(jnp.bfloat16))
-
+
+    sums = CtxSums()
+    down_part = jnp.split(dot_tn(ffn_grad, hidden_act).astype(jnp.bfloat16), 4, axis=0)
+    down_parts = [jnp.concatenate(down_part[at : at + 2], axis=1) for at in (0, 2)]
+    down_parts, hidden_act, ffn_in_grads, normed_two = together(
+        (down_parts, hidden_act, ffn_in_grads, normed_two)
+    )
+    sums.send((("down", 0), down_parts[0]))
+    two_far = dot_nt(ffn_in_grads[half:], ffn_weights)
+    two_near = dot_nt(ffn_in_grads[:half], ffn_weights)
+    own_part, came_parts = scatter_plane(scatter_half(two_near, two_far))
+    own_part, came_parts, hidden_act, ffn_in_grads, normed_two = sums.wait(
+        (own_part, came_parts, hidden_act, ffn_in_grads, normed_two)
+    )
+    sums.send((("down", 1), down_parts[1]))
+    normed_two_grad = scatter_total(own_part, came_parts)
     back_two, gain_two_grad = norm_back(hidden_in, gain_two, normed_two_grad)
     hidden_total_grad = out_grad + back_two
-    attn_grad = plane_gather((own_valid * hidden_total_grad).astype(jnp.bfloat16))
+    attn_near = plane_near((own_valid * hidden_total_grad).astype(jnp.bfloat16))
+    ffn_parts = {mask: grad_part(normed_two, ffn_in_grads, mask) for mask in (1, 0, 2, 3)}
+    ffn_parts[1] = swap_plane(ffn_parts[1], 1, 0)
+    attn_near, ffn_parts, hidden_act, query_rot = sums.wait(
+        (attn_near, ffn_parts, hidden_act, query_rot)
+    )
+    sums.send((("ffn", 0), ffn_parts[0]))
+    ffn_parts[2] = swap_plane(ffn_parts[2], 2, 0)
+    attn_grad = plane_join(attn_near)
     gated_grad = dot_nt(attn_grad, w_output)
-    grad_w_output = chain_sum(dot_tn(gated_mix, attn_grad))
+    output_part = dot_tn(attn_grad, gated_mix).astype(jnp.bfloat16)
     mixed_grad = (gated_grad * gate_sig).astype(jnp.bfloat16)
     gate_logit_grad = (gated_grad * attended_rows * gate_sig * (1.0 - gate_sig)).astype(
         jnp.bfloat16
@@ -564,6 +696,11 @@
         "qgd,kd->gqk", mixed_grad_heads, value_low, preferred_element_type=jnp.float32
     )
     score_grad = (soft * (prob_grad - delta_rows) * score_scale).astype(jnp.bfloat16)
+    score_grad, soft, ffn_parts, output_part, gate_logit_grad = sums.wait(
+        (score_grad, soft.astype(jnp.bfloat16), ffn_parts, output_part, gate_logit_grad)
+    )
+    sums.send((("ffn", 1), ffn_parts[1]))
+    ffn_parts[3] = swap_plane(ffn_parts[3], 3, 0)
     query_rot_grad = jnp.einsum(
         "gqk,kd->qgd", score_grad, key_rot, preferred_element_type=jnp.float32
     )
@@ -572,7 +709,7 @@
     )
     value_grad = jnp.einsum(
         "gqk,qgd->kd",
-        soft.astype(jnp.bfloat16),
+        soft,
         mixed_grad_heads,
         preferred_element_type=jnp.float32,
     ).astype(jnp.bfloat16)
@@ -591,16 +728,90 @@
         ],
         axis=1,
     )
-    normed_one_grad = scatter_product(attn_in_grads, attn_weights, dot_nt)
-    grad_w_query, grad_w_key, grad_w_value, grad_w_out_gate = return_grads(
-        first_normed, attn_in_grads, (query_width, HEAD_SIZE, HEAD_SIZE, query_width)
-    )
+    attn_in_grads, ffn_parts = sums.wait((attn_in_grads, ffn_parts))
+    sums.send((("ffn", 2), ffn_parts[2]))
+    one_far = dot_nt(attn_in_grads[half:], attn_weights)
+    one_near = dot_nt(attn_in_grads[:half], attn_weights)
+    own_part, came_parts = scatter_plane(scatter_half(one_near, one_far))
+    attn_parts = {mask: grad_part(first_normed, attn_in_grads, mask) for mask in (2, 3, 1, 0)}
+    attn_parts[1] = swap_plane(attn_parts[1], 1, 0)
+    own_part, came_parts, attn_parts, hidden_act = sums.wait(
+        (own_part, came_parts, attn_parts, hidden_act)
+    )
+    output_parts = jnp.split(output_part, 4, axis=0)
+
+    def attn_sum(mask):
+        return (("attn", mask), jnp.concatenate([attn_parts[mask], output_parts[mask]], axis=1))
+
+    hops = sum_hops()
+
+    def hop(value):
+        axis, pairs = next(hops)
+        return value + lax.ppermute(value, axis, pairs)
+
+    sums.send((("ffn", 3), ffn_parts[3]))
+    for mask in (2, 3):
+        attn_parts[mask] = swap_plane(attn_parts[mask], mask, 0)
+    normed_one_grad = scatter_total(own_part, came_parts)
     back_one, gain_one_grad = norm_back(inputs, gain_one, normed_one_grad)
-    input_grad = swap_ranks((hidden_total_grad + back_one).astype(jnp.bfloat16))
+    input_grad = (hidden_total_grad + back_one).astype(jnp.bfloat16)
+    gains = jnp.concatenate([gain_one_grad, gain_two_grad, query_gain_grad, key_gain_grad])[None]
+    out_far = dot_nn(hidden_act[half:], w_down).astype(jnp.bfloat16)
+    out_near = dot_nn(hidden_act[:half], w_down)
+    out_half = scatter_half(out_near, out_far)
+    first_attn, second_attn = attn_sum(0), attn_sum(1)
+    attn_parts, input_grad, gains, out_half, first_attn, second_attn = sums.wait(
+        (
+            attn_parts,
+            input_grad,
+            gains,
+            out_half,
+            dict([first_attn]),
+            dict([second_attn]),
+        )
+    )
+    sums.send(*first_attn.items())
+    input_grad = swap_ranks(input_grad)
+    gains = hop(gains)
+    out_own, out_came = scatter_plane(out_half)
+    sums.send(*second_attn.items())
+    third_attn, fourth_attn = dict([attn_sum(2)]), dict([attn_sum(3)])
+    gains, input_grad, out_own, out_came, third_attn, fourth_attn = sums.wait(
+        (gains, input_grad, out_own, out_came, third_attn, fourth_attn), 2
+    )
+    sums.send(*third_attn.items())
+    layer_output = hidden_in + own_valid * scatter_total(out_own, out_came)
+    layer_output = swap_ranks(layer_output.astype(jnp.bfloat16))
+    gains = sums.wait(hop(gains), 2)
+    sums.send(*fourth_attn.items())
+    gains, layer_output = sums.wait((hop(gains), layer_output), 2)
+    sums.send()
+    gains = sums.wait(hop(gains), 2)
+    sums.send()
+    gains = sums.wait(hop(gains), 2)[0]
+    while any(sums.flight) or sums.arrived:
+        sums.send()
+        sums.wait((), 2)
+
+    down_sums = [sums.done["down", at] for at in range(2)]
+    down_sums = [part for pair in down_sums for part in jnp.split(pair, 2, axis=1)]
+    grad_w_down = jnp.concatenate([part.T for part in down_sums], axis=1)
+    grad_w_output = jnp.concatenate(
+        [sums.done["attn", mask][:, -query_width:].T for mask in range(4)], axis=1
+    )
+    ffn_sums = [jnp.split(sums.done["ffn", mask], 2, axis=1) for mask in range(4)]
+    grad_w_gate, grad_w_up = (
+        place_columns([parts[i] for parts in ffn_sums], hidden_width) for i in range(2)
+    )
+    ends = [0, query_width, query_width + HEAD_SIZE, query_width + 2 * HEAD_SIZE]
+    widths = (query_width, HEAD_SIZE, HEAD_SIZE, query_width)
+    grad_w_query, grad_w_key, grad_w_value, grad_w_out_gate = (
+        place_columns(
+            [sums.done["attn", mask][:, start : start + width] for mask in range(4)], width
+        )
+        for start, width in zip(ends, widths)
+    )
     model_width = layer_input.shape[1]
-    gains = all_sum(
-        jnp.concatenate([gain_one_grad, gain_two_grad, query_gain_grad, key_gain_grad])[None]
-    )[0]
     ends = (model_width, 2 * model_width, 2 * model_width + HEAD_SIZE)
     return (
         layer_output,

time: 1090 us -> 806 us (0.74)
  waiting for transfers between devices: 609 us -> 253 us
  other arithmetic: 87.7 us -> 136 us
  local copies, waits for them, and re-layouts: 68.7 us -> 113 us
  starting transfers between devices: 211 us -> 193 us
    ppermute x43 -> x35, waiting for transfers between devices: 398 us -> 101 us  [the longest x6 45.6 us: send(): sent.append(([(2, name, total)], lax.ppermute(total, 'ctx', OUTWARD)))]
    ppermute x5, waiting for transfers between devices: 81.9 us -> 17.7 us  [swap_ranks(): return lax.ppermute(value, ('fsdp', 'ctx'), pairs)]
    ppermute x8 -> x15, waiting for transfers between devices: 3.72 us -> 46.2 us  [swap_plane(): return lax.ppermute(value, 'tp', xor_pairs(tp_size, tp_mask))]
    ppermute x40 -> x38, waiting for transfers between devices: 126 us -> 88.2 us  [swap_plane(): return lax.ppermute(value, 'fsdp', xor_pairs(fsdp_size, fsdp_mask))]
    split x0 -> x14, local copies, waits for them, and re-layouts: none -> 33.3 us  [the longest x12 32.1 us: plane_body(): jnp.split(sums.done['ffn', mask], 2, axis=1)]
    concatenate x0 -> x28, other arithmetic: none -> 25.1 us  [the longest x4 9.41 us: attn_sum(): jnp.concatenate([attn_parts[mask], output_parts[mask]], axis=1)]
    convert_element_type x31 -> x44, other arithmetic: 41.6 us -> 62.8 us  [the longest x16 37 us: send(): (here.astype(jnp.float32) + came.astype(jnp.float32)).astype(jnp.bfloat16)]
    ppermute x43 -> x35, starting transfers between devices: 126 us -> 109 us  [the longest x6 43.1 us: send(): sent.append(([(0, name, part)], lax.ppermute(part, 'ctx', INWARD)))]
  transfers between devices with their start and end apart: 96 -> 93, of which waited for: 37 -> 35; matrix products, arithmetic and copies ran while one was open for 20% -> 33% of each run, Pallas kernels for 0% -> 0%
where the time goes in v3:
time: 806 us; the launch traced here: 798 us
  waiting for transfers between devices  253 us (31%)
  starting transfers between devices  193 us (24%)
  other arithmetic  136 us (17%)
  local copies, waits for them, and re-layouts  113 us (14%)
  matrix products  97.7 us (12%)
    ppermute x38, waiting for transfers between devices, swap_plane(): return lax.ppermute(value, 'fsdp', xor_pairs(fsdp_size, fsdp_mask))  88.2 us
    ppermute x38, starting transfers between devices, swap_plane(): return lax.ppermute(value, 'fsdp', xor_pairs(fsdp_size, fsdp_mask))  56.6 us
    ppermute x15, waiting for transfers between devices, swap_plane(): return lax.ppermute(value, 'tp', xor_pairs(tp_size, tp_mask))  46.2 us
    ppermute x6, waiting for transfers between devices, send(): sent.append(([(2, name, total)], lax.ppermute(total, 'ctx', OUTWARD)))  45.6 us
    ppermute x6, starting transfers between devices, send(): sent.append(([(0, name, part)], lax.ppermute(part, 'ctx', INWARD)))  43.1 us
    ppermute x8, waiting for transfers between devices, swap_ctx(): return lax.ppermute(value, 'ctx', xor_pairs(lax.axis_size('ctx'), 1))  39.9 us
    convert_element_type x16, other arithmetic, send(): (here.astype(jnp.float32) + came.astype(jnp.float32)).astype(jnp.bfloat16)  37 us
    split x12, local copies, waits for them, and re-layouts, plane_body(): jnp.split(sums.done['ffn', mask], 2, axis=1)  32.1 us
  transfers between devices with their start and end apart: 93, of which 35 were waited for; matrix products, arithmetic and copies ran while one was open for 33% of the time, Pallas kernels for 0%

profile of v3, /device:TPU:1, one launch (start us, length us, event | category | flops | bytes accessed | tf_op | source)
XLA Modules:
  0.0 798.0 jit_solution(427648402786957423)
XLA Ops:
  7.9 3.5 collective-permute-start
  22.9 3.6 constant_dynamic-slice_fusion
  43.3 7.1 collective-permute-done.5
  64.1 5.1 collective-permute-start.12
  71.0 20.8 %collective-permute-done.8 = bf16[64,2048]{1,0:T(8,128)(2,1)S(1)} collective-permute-done((bf16[64,2048]{1,0:T(8,128)(2,1)S(1)}, bf16[64,2048]{1,0:T(8,128)(2,1)S(1)}, u32[]{:S(2)}, u32[]{:S(2)}) %collective-permute-start.8) | collective-permute-done | bytes 262176 | tf_op jit(solution)/shard_map/ppermute | solution.py:329
  97.3 6.2 collective-permute-done.9
  117.1 7.0 fusion.128
  133.9 3.9 collective-permute-done.17
  148.9 16.5 %collective-permute-done.23 = bf16[2,128,2048]{2,1,0:T(8,128)(2,1)S(1)} collective-permute-done((bf16[2,128,2048]{2,1,0:T(8,128)(2,1)S(1)}, bf16[2,128,2048]{2,1,0:T(8,128)(2,1)S(1)}, u32[]{:S(2)}, u32[]{:S(2)}) %collective-permute-start.23) | collective-permute-done | bytes 1048608 | tf_op jit(solution)/shard_map/ppermute | solution.py:331
  165.7 10.9 %collective-permute-done.20 = bf16[128,2048]{1,0:T(8,128)(2,1)S(1)} collective-permute-done((bf16[128,2048]{1,0:T(8,128)(2,1)S(1)}, bf16[128,2048]{1,0:T(8,128)(2,1)S(1)}, u32[]{:S(2)}, u32[]{:S(2)}) %collective-permute-start.20) | collective-permute-done | bytes 524320 | tf_op jit(solution)/shard_map/ppermute | solution.py:331
  180.2 3.5 collective-permute-done.21
  191.5 11.8 %collective-permute-done.27 = bf16[128,2048]{1,0:T(8,128)(2,1)S(1)} collective-permute-done((bf16[128,2048]{1,0:T(8,128)(2,1)S(1)}, bf16[128,2048]{1,0:T(8,128)(2,1)S(1)}, u32[]{:S(2)}, u32[]{:S(2)}) %collective-permute-start.27) | collective-permute-done | bytes 524320 | tf_op jit(solution)/shard_map/ppermute | solution.py:329
  206.5 7.3 collective-permute-done.29
  217.3 8.5 %fusion.129 = f32[1024,1536]{1,0:T(8,128)} fusion(bf16[1024,2048]{1,0:T(8,128)(2,1)S(1)} %constant_dynamic-update-slice_fusion.5, bf16[2048,1536]{1,0:T(8,128)(2,1)S(1)} %constant_dynamic-update-slice_fusion.21), kind=kOutput, calls=%fused_computation.382 | convolution fusion | flops 6442450944 | bytes 16777216 | tf_op jit(solution)/shard_map/dot_general | solution.py:388
  225.8 6.6 multiply_convert_fusion.1
  232.4 3.9 convolution_convert_fusion
  239.6 3.7 convolution_convert_fusion.8
  243.7 4.5 collective-permute-start.33
  248.2 5.0 fusion.126
  256.3 11.2 %collective-permute-done.35 = bf16[128,2048]{1,0:T(8,128)(2,1)} collective-permute-done((bf16[128,2048]{1,0:T(8,128)(2,1)}, bf16[128,2048]{1,0:T(8,128)(2,1)}, u32[]{:S(2)}, u32[]{:S(2)}) %collective-permute-start.35) | collective-permute-done | bytes 524320 | tf_op jit(solution)/shard_map/ppermute | solution.py:329
  306.8 4.5 collective-permute-done.44
  322.8 13.8 %collective-permute-start.48 = (bf16[512,1536]{0,1:T(8,128)(2,1)}, bf16[512,1536]{0,1:T(8,128)(2,1)}, u32[]{:S(2)}, u32[]{:S(2)}) collective-permute-start(bf16[512,1536]{0,1:T(8,128)(2,1)} %get-tuple-element.368), channel_id=1, source_target_pairs={{0,2},{2,0},{4,6},{6,4},{1,3},{3,1},{5,7},{7,5},{8,10},{10,8},{12,... | collective-permute-start | bytes 4718600 | tf_op jit(solution)/shard_map/ppermute | solution.py:493
  341.6 6.0 fusion.6
  356.2 4.8 convolution_convert_fusion.9
  361.0 5.5 fusion.2
  366.5 5.1 collective-permute-done.48
  371.6 4.4 collective-permute-done.50
  392.1 3.8 fusion.22
  411.0 22.6 %collective-permute-done.52 = bf16[512,1536]{0,1:T(8,128)(2,1)S(1)} collective-permute-done((bf16[512,1536]{0,1:T(8,128)(2,1)S(1)}, bf16[512,1536]{0,1:T(8,128)(2,1)S(1)}, u32[]{:S(2)}, u32[]{:S(2)}) %collective-permute-start.52) | collective-permute-done | bytes 1572896 | tf_op jit(solution)/shard_map/ppermute | solution.py:493
  433.6 6.1 collective-permute-done.53
  439.7 4.3 convolution_convert_fusion.3
  454.8 3.8 fusion.127
  465.3 6.7 collective-permute-done.57
  477.3 6.1 collective-permute-done.55
  490.0 4.0 collective-permute-start.63
  529.3 6.2 collective-permute-done.65
  555.5 5.4 collective-permute-start.68
  577.4 11.3 %collective-permute-done.71 = bf16[128,2048]{1,0:T(8,128)(2,1)S(1)} collective-permute-done((bf16[128,2048]{1,0:T(8,128)(2,1)S(1)}, bf16[128,2048]{1,0:T(8,128)(2,1)S(1)}, u32[]{:S(2)}, u32[]{:S(2)}) %collective-permute-start.71) | collective-permute-done | bytes 524320 | tf_op jit(solution)/shard_map/ppermute | solution.py:342
  588.7 9.0 %collective-permute-start.75 = (bf16[64,2048]{1,0:T(8,128)(2,1)S(1)}, bf16[64,2048]{1,0:T(8,128)(2,1)S(1)}, u32[]{:S(2)}, u32[]{:S(2)}) collective-permute-start(bf16[64,2048]{1,0:T(8,128)(2,1)S(1)} %get-tuple-element.377), channel_id=1, source_target_pairs={{0,16},{8,24},{16,0},{24,8},{1,17},{9,25},{17,1},{25,9},{2,18},{10... | collective-permute-start | bytes 786440 | tf_op jit(solution)/shard_map/ppermute | solution.py:329
  600.2 14.8 %collective-permute-start.79 = (bf16[512,1024]{1,0:T(8,128)(2,1)}, bf16[512,1024]{1,0:T(8,128)(2,1)}, u32[]{:S(2)}, u32[]{:S(2)}) collective-permute-start(bf16[512,1024]{1,0:T(8,128)(2,1)} %pad_maximum_fusion.18), channel_id=1, source_target_pairs={{0,2},{6,4},{1,3},{7,5},{8,10},{14,12},{9,11},{15,13},{16,18},{22,... | collective-permute-start | bytes 3145736 | tf_op jit(solution)/shard_map/ppermute | solution.py:424
  615.3 3.6 add_convert_fusion
  624.6 10.8 %collective-permute-start.77 = (bf16[512,1024]{1,0:T(8,128)(2,1)}, bf16[512,1024]{1,0:T(8,128)(2,1)}, u32[]{:S(2)}, u32[]{:S(2)}) collective-permute-start(bf16[512,1024]{1,0:T(8,128)(2,1)} %pad_maximum_fusion.20), channel_id=1, source_target_pairs={{0,2},{6,4},{1,3},{7,5},{8,10},{14,12},{9,11},{15,13},{16,18},{22,... | collective-permute-start | bytes 3145736 | tf_op jit(solution)/shard_map/ppermute | solution.py:424
  657.5 4.7 collective-permute-start.86
  662.2 6.3 collective-permute-done.82
  688.7 13.7 %collective-permute-start.87 = (f32[1,4352]{1,0:T(1,128)S(1)}, f32[1,4352]{1,0:T(1,128)S(1)}, u32[]{:S(2)}, u32[]{:S(2)}) collective-permute-start(f32[1,4352]{1,0:T(1,128)S(1)} %add.631), channel_id=1, source_target_pairs={{0,2},{2,0},{4,6},{6,4},{1,3},{3,1},{5,7},{7,5},{8,10},{10,8},{12,... | collective-permute-start | bytes 52232 | tf_op jit(solution)/shard_map/ppermute | solution.py:750
  715.0 13.2 %collective-permute-done.88 = f32[1,4352]{1,0:T(1,128)S(1)} collective-permute-done((f32[1,4352]{1,0:T(1,128)S(1)}, f32[1,4352]{1,0:T(1,128)S(1)}, u32[]{:S(2)}, u32[]{:S(2)}) %collective-permute-start.88) | collective-permute-done | bytes 17440 | tf_op jit(solution)/shard_map/ppermute | solution.py:750
  740.4 20.3 %collective-permute-done.91 = bf16[512,1024]{1,0:T(8,128)(2,1)S(1)} collective-permute-done((bf16[512,1024]{1,0:T(8,128)(2,1)S(1)}, bf16[512,1024]{1,0:T(8,128)(2,1)S(1)}, u32[]{:S(2)}, u32[]{:S(2)}) %collective-permute-start.91) | collective-permute-done | bytes 1048608 | tf_op jit(solution)/shard_map/ppermute | solution.py:426
  761.2 22.0 %collective-permute-done.92 = bf16[512,1024]{1,0:T(8,128)(2,1)S(1)} collective-permute-done((bf16[512,1024]{1,0:T(8,128)(2,1)S(1)}, bf16[512,1024]{1,0:T(8,128)(2,1)S(1)}, u32[]{:S(2)}, u32[]{:S(2)}) %collective-permute-start.92) | collective-permute-done | bytes 1048608 | tf_op jit(solution)/shard_map/ppermute | solution.py:426
  (583 shorter events, 399.8 us)
Async XLA Ops:
  4.4 29.5 %collective-permute-start.2 = (bf16[256,768]{1,0:T(8,128)(2,1)}, bf16[256,768]{1,0:T(8,128)(2,1)}, u32[]{:S(2)}, u32[]{:S(2)}) collective-permute-start(bf16[256,768]{1,0:T(8,128)(2,1)} %pad_maximum_fusion.39), channel_id=1, source_target_pairs={{0,24},{8,16},{16,8},{24,0},{1,25},{9,17},{17,9},{25,1},{2,26},{10... | collective-permute-start | bytes 1179656 | tf_op jit(solution)/shard_map/ppermute | solution.py:329
  7.9 26.7 %collective-permute-start.1 = (bf16[256,768]{1,0:T(8,128)(2,1)}, bf16[256,768]{1,0:T(8,128)(2,1)}, u32[]{:S(2)}, u32[]{:S(2)}) collective-permute-start(bf16[256,768]{1,0:T(8,128)(2,1)} %pad_maximum_fusion.38), channel_id=1, source_target_pairs={{0,16},{8,24},{16,0},{24,8},{1,17},{9,25},{17,1},{25,9},{2,18},{10... | collective-permute-start | bytes 1179656 | tf_op jit(solution)/shard_map/ppermute | solution.py:329
  7.9 26.7 %collective-permute-start = (bf16[128,2048]{1,0:T(8,128)(2,1)}, bf16[128,2048]{1,0:T(8,128)(2,1)}, u32[]{:S(2)}, u32[]{:S(2)}) collective-permute-start(bf16[128,2048]{1,0:T(8,128)(2,1)} %param.15), channel_id=1, source_target_pairs={{0,0},{2,8},{4,16},{6,24},{8,2},{10,10},{12,18},{14,26},{16,4},{18... | collective-permute-start | bytes 1572872 | tf_op jit(solution)/shard_map/ppermute | solution.py:342
  17.2 46.9 %collective-permute-start.11 = (bf16[512,768]{1,0:T(8,128)(2,1)}, bf16[512,768]{1,0:T(8,128)(2,1)}, u32[]{:S(2)}, u32[]{:S(2)}) collective-permute-start(bf16[512,768]{1,0:T(8,128)(2,1)} %pad_maximum_fusion.23), channel_id=1, source_target_pairs={{0,8},{8,0},{16,24},{24,16},{1,9},{9,1},{17,25},{25,17},{2,10},{10... | collective-permute-start | bytes 2359304 | tf_op jit(solution)/shard_map/ppermute | solution.py:329
  19.5 36.0 %collective-permute-start.3 = (s32[1,2]{1,0:T(1,128)}, s32[1,2]{1,0:T(1,128)S(1)}, u32[]{:S(2)}, u32[]{:S(2)}) collective-permute-start(s32[1,2]{1,0:T(1,128)} %param.17), channel_id=1, source_target_pairs={{0,0},{2,8},{4,16},{6,24},{8,2},{10,10},{12,18},{14,26},{16,4},{18... | collective-permute-start | bytes 32 | tf_op jit(solution)/shard_map/ppermute | solution.py:342
  52.6 50.8 %collective-permute-start.6 = (bf16[384,2048]{1,0:T(8,128)(2,1)}, bf16[384,2048]{1,0:T(8,128)(2,1)}, u32[]{:S(2)}, u32[]{:S(2)}) collective-permute-start(bf16[384,2048]{1,0:T(8,128)(2,1)} %pad_maximum_fusion.5), channel_id=1, source_target_pairs={{0,8},{8,0},{16,24},{24,16},{1,9},{9,1},{17,25},{25,17},{2,10},{10... | collective-permute-start | bytes 4718600 | tf_op jit(solution)/shard_map/ppermute | solution.py:329
  58.1 45.4 %collective-permute-start.13 = (bf16[256,1536]{1,0:T(8,128)(2,1)}, bf16[256,1536]{1,0:T(8,128)(2,1)S(1)}, u32[]{:S(2)}, u32[]{:S(2)}) collective-permute-start(bf16[256,1536]{1,0:T(8,128)(2,1)} %pad_maximum_fusion.22), channel_id=1, source_target_pairs={{0,16},{8,24},{16,0},{24,8},{1,17},{9,25},{17,1},{25,9},{2,18},{10... | collective-permute-start | bytes 2359304 | tf_op jit(solution)/shard_map/ppermute | solution.py:329
  61.5 30.2 %collective-permute-start.8 = (bf16[64,2048]{1,0:T(8,128)(2,1)S(1)}, bf16[64,2048]{1,0:T(8,128)(2,1)S(1)}, u32[]{:S(2)}, u32[]{:S(2)}) collective-permute-start(bf16[64,2048]{1,0:T(8,128)(2,1)S(1)} %slice.447), channel_id=1, source_target_pairs={{0,16},{8,24},{16,0},{24,8},{1,17},{9,25},{17,1},{25,9},{2,18},{10... | collective-permute-start | bytes 786440 | tf_op jit(solution)/shard_map/ppermute | solution.py:329
  64.1 33.2 %collective-permute-start.12 = (bf16[128,2048]{1,0:T(8,128)(2,1)}, bf16[128,2048]{1,0:T(8,128)(2,1)S(1)}, u32[]{:S(2)}, u32[]{:S(2)}) collective-permute-start(bf16[128,2048]{1,0:T(8,128)(2,1)} %param.16), channel_id=1, source_target_pairs={{0,0},{2,8},{4,16},{6,24},{8,2},{10,10},{12,18},{14,26},{16,4},{18... | collective-permute-start | bytes 1572872 | tf_op jit(solution)/shard_map/ppermute | solution.py:342
  71.0 26.3 %collective-permute-start.10 = (bf16[256,768]{1,0:T(8,128)(2,1)}, bf16[256,768]{1,0:T(8,128)(2,1)S(1)}, u32[]{:S(2)}, u32[]{:S(2)}) collective-permute-start(bf16[256,768]{1,0:T(8,128)(2,1)} %collective-permute-done.2), channel_id=1, source_target_pairs={{0,2},{2,0},{4,6},{6,4},{1,3},{3,1},{5,7},{7,5},{8,10},{10,8},{12,... | collective-permute-start | bytes 1179656 | tf_op jit(solution)/shard_map/ppermute | solution.py:493
  110.2 27.7 %collective-permute-start.17 = (bf16[256,1536]{1,0:T(8,128)(2,1)S(1)}, bf16[256,1536]{1,0:T(8,128)(2,1)S(1)}, u32[]{:S(2)}, u32[]{:S(2)}) collective-permute-start(bf16[256,1536]{1,0:T(8,128)(2,1)S(1)} %copy-done.64), channel_id=1, source_target_pairs={{0,24},{8,16},{16,8},{24,0},{1,25},{9,17},{17,9},{25,1},{2,26},{10... | collective-permute-start | bytes 2359304 | tf_op jit(solution)/shard_map/ppermute | solution.py:329
  142.3 37.9 %collective-permute-start.24 = (bf16[256,1536]{1,0:T(8,128)(2,1)S(1)}, bf16[256,1536]{1,0:T(8,128)(2,1)S(1)}, u32[]{:S(2)}, u32[]{:S(2)}) collective-permute-start(bf16[256,1536]{1,0:T(8,128)(2,1)S(1)} %collective-permute-done.17), channel_id=1, source_target_pairs={{0,2},{2,0},{4,6},{6,4},{1,3},{3,1},{5,7},{7,5},{8,10},{10,8},{12,... | collective-permute-start | bytes 2359304 | tf_op jit(solution)/shard_map/ppermute | solution.py:493
  147.6 29.1 %collective-permute-start.20 = (bf16[128,2048]{1,0:T(8,128)(2,1)S(1)}, bf16[128,2048]{1,0:T(8,128)(2,1)S(1)}, u32[]{:S(2)}, u32[]{:S(2)}) collective-permute-start(bf16[128,2048]{1,0:T(8,128)(2,1)S(1)} %pad_maximum_fusion.28), channel_id=1, source_target_pairs={{0,1},{1,0},{2,3},{3,2},{4,5},{5,4},{6,7},{7,6},{8,9},{9,8},{10,11... | collective-permute-start | bytes 1572872 | tf_op jit(solution)/shard_map/ppermute | solution.py:331
  184.9 29.0 %collective-permute-start.31 = (bf16[512,2048]{1,0:T(8,128)(2,1)S(1)}, bf16[512,2048]{1,0:T(8,128)(2,1)S(1)}, u32[]{:S(2)}, u32[]{:S(2)}) collective-permute-start(bf16[512,2048]{1,0:T(8,128)(2,1)S(1)} %bitcast.182), channel_id=1, source_target_pairs={{0,8},{8,0},{16,24},{24,16},{1,9},{9,1},{17,25},{25,17},{2,10},{10... | collective-permute-start | bytes 6291464 | tf_op jit(solution)/shard_map/ppermute | solution.py:329
  243.7 37.6 %collective-permute-start.33 = (bf16[512,1536]{0,1:T(8,128)(2,1)}, bf16[512,1536]{0,1:T(8,128)(2,1)}, u32[]{:S(2)}, u32[]{:S(2)}) collective-permute-start(bf16[512,1536]{0,1:T(8,128)(2,1)} %pad_maximum_fusion.8), channel_id=1, source_target_pairs={{0,2},{6,4},{1,3},{7,5},{8,10},{14,12},{9,11},{15,13},{16,18},{22,... | collective-permute-start | bytes 4718600 | tf_op jit(solution)/shard_map/ppermute | solution.py:424
  277.1 41.2 %collective-permute-start.40 = (bf16[512,1536]{0,1:T(8,128)(2,1)}, bf16[512,1536]{0,1:T(8,128)(2,1)S(1)}, u32[]{:S(2)}, u32[]{:S(2)}) collective-permute-start(bf16[512,1536]{0,1:T(8,128)(2,1)} %pad_maximum_fusion.9), channel_id=1, source_target_pairs={{0,2},{6,4},{1,3},{7,5},{8,10},{14,12},{9,11},{15,13},{16,18},{22,... | collective-permute-start | bytes 4718600 | tf_op jit(solution)/shard_map/ppermute | solution.py:424
  289.0 29.3 %collective-permute-start.46 = (bf16[512,1536]{0,1:T(8,128)(2,1)S(1)}, bf16[512,1536]{0,1:T(8,128)(2,1)S(1)}, u32[]{:S(2)}, u32[]{:S(2)}) collective-permute-start(bf16[512,1536]{0,1:T(8,128)(2,1)S(1)} %convolution_convert_fusion.6), channel_id=1, source_target_pairs={{0,8},{8,0},{16,24},{24,16},{1,9},{9,1},{17,25},{25,17},{2,10},{10... | collective-permute-start | bytes 4718600 | tf_op jit(solution)/shard_map/ppermute | solution.py:329
  318.5 29.1 %collective-permute-start.49 = (bf16[128,2048]{1,0:T(8,128)(2,1)S(1)}, bf16[128,2048]{1,0:T(8,128)(2,1)S(1)}, u32[]{:S(2)}, u32[]{:S(2)}) collective-permute-start(bf16[128,2048]{1,0:T(8,128)(2,1)S(1)} %pad_maximum_fusion.32), channel_id=1, source_target_pairs={{0,8},{8,0},{16,24},{24,16},{1,9},{9,1},{17,25},{25,17},{2,10},{10... | collective-permute-start | bytes 1572872 | tf_op jit(solution)/shard_map/ppermute | solution.py:329
  322.8 48.8 %collective-permute-start.48 = (bf16[512,1536]{0,1:T(8,128)(2,1)}, bf16[512,1536]{0,1:T(8,128)(2,1)}, u32[]{:S(2)}, u32[]{:S(2)}) collective-permute-start(bf16[512,1536]{0,1:T(8,128)(2,1)} %get-tuple-element.368), channel_id=1, source_target_pairs={{0,2},{2,0},{4,6},{6,4},{1,3},{3,1},{5,7},{7,5},{8,10},{10,8},{12,... | collective-permute-start | bytes 4718600 | tf_op jit(solution)/shard_map/ppermute | solution.py:493
  338.1 33.5 %collective-permute-start.47 = (bf16[512,1536]{0,1:T(8,128)(2,1)}, bf16[512,1536]{0,1:T(8,128)(2,1)}, u32[]{:S(2)}, u32[]{:S(2)}) collective-permute-start(bf16[512,1536]{0,1:T(8,128)(2,1)} %add_convert_fusion.10), channel_id=1, source_target_pairs={{2,4},{4,2},{3,5},{5,3},{10,12},{12,10},{11,13},{13,11},{18,20},{2... | collective-permute-start | bytes 4718600 | tf_op jit(solution)/shard_map/ppermute | solution.py:418
  340.0 36.0 %collective-permute-start.50 = (bf16[512,1536]{0,1:T(8,128)(2,1)}, bf16[512,1536]{0,1:T(8,128)(2,1)}, u32[]{:S(2)}, u32[]{:S(2)}) collective-permute-start(bf16[512,1536]{0,1:T(8,128)(2,1)} %convolution_convert_fusion.5), channel_id=1, source_target_pairs={{0,16},{8,24},{16,0},{24,8},{1,17},{9,25},{17,1},{25,9},{2,18},{10... | collective-permute-start | bytes 4718600 | tf_op jit(solution)/shard_map/ppermute | solution.py:329
  398.7 34.9 %collective-permute-start.52 = (bf16[512,1536]{0,1:T(8,128)(2,1)S(1)}, bf16[512,1536]{0,1:T(8,128)(2,1)S(1)}, u32[]{:S(2)}, u32[]{:S(2)}) collective-permute-start(bf16[512,1536]{0,1:T(8,128)(2,1)S(1)} %get-tuple-element.364), channel_id=1, source_target_pairs={{0,2},{2,0},{4,6},{6,4},{1,3},{3,1},{5,7},{7,5},{8,10},{10,8},{12,... | collective-permute-start | bytes 4718600 | tf_op jit(solution)/shard_map/ppermute | solution.py:493
  402.0 31.6 %collective-permute-start.51 = (bf16[512,1536]{0,1:T(8,128)(2,1)S(1)}, bf16[512,1536]{0,1:T(8,128)(2,1)S(1)}, u32[]{:S(2)}, u32[]{:S(2)}) collective-permute-start(bf16[512,1536]{0,1:T(8,128)(2,1)S(1)} %add_convert_fusion.8), channel_id=1, source_target_pairs={{2,4},{4,2},{3,5},{5,3},{10,12},{12,10},{11,13},{13,11},{18,20},{2... | collective-permute-start | bytes 4718600 | tf_op jit(solution)/shard_map/ppermute | solution.py:418
  403.4 36.3 %collective-permute-start.53 = (bf16[512,1536]{0,1:T(8,128)(2,1)S(1)}, bf16[512,1536]{0,1:T(8,128)(2,1)S(1)}, u32[]{:S(2)}, u32[]{:S(2)}) collective-permute-start(bf16[512,1536]{0,1:T(8,128)(2,1)S(1)} %copy-done.82), channel_id=1, source_target_pairs={{0,24},{8,16},{16,8},{24,0},{1,25},{9,17},{17,9},{25,1},{2,26},{10... | collective-permute-start | bytes 4718600 | tf_op jit(solution)/shard_map/ppermute | solution.py:329
  447.4 36.0 %collective-permute-start.55 = (bf16[512,1536]{0,1:T(8,128)(2,1)S(1)}, bf16[512,1536]{0,1:T(8,128)(2,1)S(1)}, u32[]{:S(2)}, u32[]{:S(2)}) collective-permute-start(bf16[512,1536]{0,1:T(8,128)(2,1)S(1)} %get-tuple-element.362), channel_id=1, source_target_pairs={{0,2},{2,0},{4,6},{6,4},{1,3},{3,1},{5,7},{7,5},{8,10},{10,8},{12,... | collective-permute-start | bytes 4718600 | tf_op jit(solution)/shard_map/ppermute | solution.py:493
  449.4 34.0 %collective-permute-start.54 = (bf16[512,1536]{0,1:T(8,128)(2,1)S(1)}, bf16[512,1536]{0,1:T(8,128)(2,1)S(1)}, u32[]{:S(2)}, u32[]{:S(2)}) collective-permute-start(bf16[512,1536]{0,1:T(8,128)(2,1)S(1)} %add_convert_fusion.6), channel_id=1, source_target_pairs={{2,4},{4,2},{3,5},{5,3},{10,12},{12,10},{11,13},{13,11},{18,20},{2... | collective-permute-start | bytes 4718600 | tf_op jit(solution)/shard_map/ppermute | solution.py:418
  486.5 39.3 %collective-permute-start.66 = (bf16[512,2048]{1,0:T(8,128)(2,1)}, bf16[512,2048]{1,0:T(8,128)(2,1)}, u32[]{:S(2)}, u32[]{:S(2)}) collective-permute-start(bf16[512,2048]{1,0:T(8,128)(2,1)} %convolution_convert_fusion.2), channel_id=1, source_target_pairs={{0,8},{8,0},{16,24},{24,16},{1,9},{9,1},{17,25},{25,17},{2,10},{10... | collective-permute-start | bytes 6291464 | tf_op jit(solution)/shard_map/ppermute | solution.py:329
  490.0 45.5 %collective-permute-start.63 = (bf16[512,1536]{0,1:T(8,128)(2,1)}, bf16[512,1536]{0,1:T(8,128)(2,1)}, u32[]{:S(2)}, u32[]{:S(2)}) collective-permute-start(bf16[512,1536]{0,1:T(8,128)(2,1)} %get-tuple-element.360), channel_id=1, source_target_pairs={{0,2},{2,0},{4,6},{6,4},{1,3},{3,1},{5,7},{7,5},{8,10},{10,8},{12,... | collective-permute-start | bytes 4718600 | tf_op jit(solution)/shard_map/ppermute | solution.py:493
  497.0 38.5 %collective-permute-start.62 = (bf16[512,1536]{0,1:T(8,128)(2,1)}, bf16[512,1536]{0,1:T(8,128)(2,1)}, u32[]{:S(2)}, u32[]{:S(2)}) collective-permute-start(bf16[512,1536]{0,1:T(8,128)(2,1)} %add_convert_fusion.4), channel_id=1, source_target_pairs={{2,4},{4,2},{3,5},{5,3},{10,12},{12,10},{11,13},{13,11},{18,20},{2... | collective-permute-start | bytes 4718600 | tf_op jit(solution)/shard_map/ppermute | solution.py:418
  499.0 30.3 %collective-permute-start.64 = (bf16[512,768]{1,0:T(8,128)(2,1)}, bf16[512,768]{1,0:T(8,128)(2,1)}, u32[]{:S(2)}, u32[]{:S(2)}) collective-permute-start(bf16[512,768]{1,0:T(8,128)(2,1)} %convolution_convert_fusion.11), channel_id=1, source_target_pairs={{0,16},{8,24},{16,0},{24,8},{1,17},{9,25},{17,1},{25,9},{2,18},{10... | collective-permute-start | bytes 2359304 | tf_op jit(solution)/shard_map/ppermute | solution.py:329
  500.2 35.3 %collective-permute-start.65 = (bf16[512,768]{1,0:T(8,128)(2,1)}, bf16[512,768]{1,0:T(8,128)(2,1)}, u32[]{:S(2)}, u32[]{:S(2)}) collective-permute-start(bf16[512,768]{1,0:T(8,128)(2,1)} %convolution_convert_fusion.10), channel_id=1, source_target_pairs={{0,24},{8,16},{16,8},{24,0},{1,25},{9,17},{17,9},{25,1},{2,26},{10... | collective-permute-start | bytes 2359304 | tf_op jit(solution)/shard_map/ppermute | solution.py:329
  536.8 33.6 %collective-permute-start.72 = (bf16[128,2048]{1,0:T(8,128)(2,1)}, bf16[128,2048]{1,0:T(8,128)(2,1)}, u32[]{:S(2)}, u32[]{:S(2)}) collective-permute-start(bf16[128,2048]{1,0:T(8,128)(2,1)} %pad_maximum_fusion.36), channel_id=1, source_target_pairs={{0,16},{8,24},{16,0},{24,8},{1,17},{9,25},{17,1},{25,9},{2,18},{10... | collective-permute-start | bytes 1572872 | tf_op jit(solution)/shard_map/ppermute | solution.py:329
  538.7 34.1 %collective-permute-start.73 = (bf16[128,2048]{1,0:T(8,128)(2,1)}, bf16[128,2048]{1,0:T(8,128)(2,1)}, u32[]{:S(2)}, u32[]{:S(2)}) collective-permute-start(bf16[128,2048]{1,0:T(8,128)(2,1)} %pad_maximum_fusion.37), channel_id=1, source_target_pairs={{0,1},{1,0},{2,3},{3,2},{4,5},{5,4},{6,7},{7,6},{8,9},{9,8},{10,11... | collective-permute-start | bytes 1572872 | tf_op jit(solution)/shard_map/ppermute | solution.py:331
  542.4 72.6 %collective-permute-start.69 = (bf16[512,1536]{0,1:T(8,128)(2,1)}, bf16[512,1536]{0,1:T(8,128)(2,1)}, u32[]{:S(2)}, u32[]{:S(2)}) collective-permute-start(bf16[512,1536]{0,1:T(8,128)(2,1)} %add_convert_fusion.1), channel_id=1, source_target_pairs={{2,0},{4,6},{3,1},{5,7},{10,8},{12,14},{11,9},{13,15},{18,16},{20,... | collective-permute-start | bytes 4718600 | tf_op jit(solution)/shard_map/ppermute | solution.py:426
  548.6 66.5 %collective-permute-start.67 = (bf16[512,1536]{0,1:T(8,128)(2,1)}, bf16[512,1536]{0,1:T(8,128)(2,1)}, u32[]{:S(2)}, u32[]{:S(2)}) collective-permute-start(bf16[512,1536]{0,1:T(8,128)(2,1)} %add_convert_fusion.2), channel_id=1, source_target_pairs={{2,4},{4,2},{3,5},{5,3},{10,12},{12,10},{11,13},{13,11},{18,20},{2... | collective-permute-start | bytes 4718600 | tf_op jit(solution)/shard_map/ppermute | solution.py:418
  555.5 59.6 %collective-permute-start.68 = (bf16[512,1024]{1,0:T(8,128)(2,1)}, bf16[512,1024]{1,0:T(8,128)(2,1)}, u32[]{:S(2)}, u32[]{:S(2)}) collective-permute-start(bf16[512,1024]{1,0:T(8,128)(2,1)} %pad_maximum_fusion.17), channel_id=1, source_target_pairs={{0,2},{6,4},{1,3},{7,5},{8,10},{14,12},{9,11},{15,13},{16,18},{22,... | collective-permute-start | bytes 3145736 | tf_op jit(solution)/shard_map/ppermute | solution.py:424
  600.2 53.1 %collective-permute-start.79 = (bf16[512,1024]{1,0:T(8,128)(2,1)}, bf16[512,1024]{1,0:T(8,128)(2,1)}, u32[]{:S(2)}, u32[]{:S(2)}) collective-permute-start(bf16[512,1024]{1,0:T(8,128)(2,1)} %pad_maximum_fusion.18), channel_id=1, source_target_pairs={{0,2},{6,4},{1,3},{7,5},{8,10},{14,12},{9,11},{15,13},{16,18},{22,... | collective-permute-start | bytes 3145736 | tf_op jit(solution)/shard_map/ppermute | solution.py:424
  615.0 28.0 %collective-permute-start.80 = (f32[1,4352]{1,0:T(1,128)S(1)}, f32[1,4352]{1,0:T(1,128)S(1)}, u32[]{:S(2)}, u32[]{:S(2)}) collective-permute-start(f32[1,4352]{1,0:T(1,128)S(1)} %add.623), channel_id=1, source_target_pairs={{0,16},{8,24},{16,0},{24,8},{1,17},{9,25},{17,1},{25,9},{2,18},{10... | collective-permute-start | bytes 52232 | tf_op jit(solution)/shard_map/ppermute | solution.py:750
  618.9 51.4 %collective-permute-start.78 = (bf16[512,1536]{0,1:T(8,128)(2,1)}, bf16[512,1536]{0,1:T(8,128)(2,1)}, u32[]{:S(2)}, u32[]{:S(2)}) collective-permute-start(bf16[512,1536]{0,1:T(8,128)(2,1)} %add_convert_fusion), channel_id=1, source_target_pairs={{2,0},{4,6},{3,1},{5,7},{10,8},{12,14},{11,9},{13,15},{18,16},{20,... | collective-permute-start | bytes 4718600 | tf_op jit(solution)/shard_map/ppermute | solution.py:426
  622.8 47.4 %collective-permute-start.76 = (bf16[512,1024]{1,0:T(8,128)(2,1)}, bf16[512,1024]{1,0:T(8,128)(2,1)}, u32[]{:S(2)}, u32[]{:S(2)}) collective-permute-start(bf16[512,1024]{1,0:T(8,128)(2,1)} %add_convert_fusion.19), channel_id=1, source_target_pairs={{2,4},{4,2},{3,5},{5,3},{10,12},{12,10},{11,13},{13,11},{18,20},{2... | collective-permute-start | bytes 3145736 | tf_op jit(solution)/shard_map/ppermute | solution.py:418
  624.6 45.7 %collective-permute-start.77 = (bf16[512,1024]{1,0:T(8,128)(2,1)}, bf16[512,1024]{1,0:T(8,128)(2,1)}, u32[]{:S(2)}, u32[]{:S(2)}) collective-permute-start(bf16[512,1024]{1,0:T(8,128)(2,1)} %pad_maximum_fusion.20), channel_id=1, source_target_pairs={{0,2},{6,4},{1,3},{7,5},{8,10},{14,12},{9,11},{15,13},{16,18},{22,... | collective-permute-start | bytes 3145736 | tf_op jit(solution)/shard_map/ppermute | solution.py:424
  657.5 51.5 %collective-permute-start.86 = (bf16[512,1024]{1,0:T(8,128)(2,1)}, bf16[512,1024]{1,0:T(8,128)(2,1)}, u32[]{:S(2)}, u32[]{:S(2)}) collective-permute-start(bf16[512,1024]{1,0:T(8,128)(2,1)} %pad_maximum_fusion.21), channel_id=1, source_target_pairs={{0,2},{6,4},{1,3},{7,5},{8,10},{14,12},{9,11},{15,13},{16,18},{22,... | collective-permute-start | bytes 3145736 | tf_op jit(solution)/shard_map/ppermute | solution.py:424
  668.6 40.4 %collective-permute-start.85 = (bf16[512,1024]{1,0:T(8,128)(2,1)}, bf16[512,1024]{1,0:T(8,128)(2,1)}, u32[]{:S(2)}, u32[]{:S(2)}) collective-permute-start(bf16[512,1024]{1,0:T(8,128)(2,1)} %add_convert_fusion.16), channel_id=1, source_target_pairs={{2,4},{4,2},{3,5},{5,3},{10,12},{12,10},{11,13},{13,11},{18,20},{2... | collective-permute-start | bytes 3145736 | tf_op jit(solution)/shard_map/ppermute | solution.py:418
  673.2 55.0 %collective-permute-start.84 = (bf16[512,1024]{1,0:T(8,128)(2,1)}, bf16[512,1024]{1,0:T(8,128)(2,1)}, u32[]{:S(2)}, u32[]{:S(2)}) collective-permute-start(bf16[512,1024]{1,0:T(8,128)(2,1)} %add_convert_fusion.17), channel_id=1, source_target_pairs={{2,0},{4,6},{3,1},{5,7},{10,8},{12,14},{11,9},{13,15},{18,16},{20,... | collective-permute-start | bytes 3145736 | tf_op jit(solution)/shard_map/ppermute | solution.py:426
  677.4 50.8 %collective-permute-start.83 = (bf16[512,1024]{1,0:T(8,128)(2,1)}, bf16[512,1024]{1,0:T(8,128)(2,1)}, u32[]{:S(2)}, u32[]{:S(2)}) collective-permute-start(bf16[512,1024]{1,0:T(8,128)(2,1)} %add_convert_fusion.18), channel_id=1, source_target_pairs={{2,4},{4,2},{3,5},{5,3},{10,12},{12,10},{11,13},{13,11},{18,20},{2... | collective-permute-start | bytes 3145736 | tf_op jit(solution)/shard_map/ppermute | solution.py:418
  711.0 27.2 %collective-permute-start.90 = (bf16[512,1024]{1,0:T(8,128)(2,1)S(1)}, bf16[512,1024]{1,0:T(8,128)(2,1)S(1)}, u32[]{:S(2)}, u32[]{:S(2)}) collective-permute-start(bf16[512,1024]{1,0:T(8,128)(2,1)S(1)} %add_convert_fusion.14), channel_id=1, source_target_pairs={{2,0},{4,6},{3,1},{5,7},{10,8},{12,14},{11,9},{13,15},{18,16},{20,... | collective-permute-start | bytes 3145736 | tf_op jit(solution)/shard_map/ppermute | solution.py:426
  730.2 30.5 %collective-permute-start.91 = (bf16[512,1024]{1,0:T(8,128)(2,1)S(1)}, bf16[512,1024]{1,0:T(8,128)(2,1)S(1)}, u32[]{:S(2)}, u32[]{:S(2)}) collective-permute-start(bf16[512,1024]{1,0:T(8,128)(2,1)S(1)} %add_convert_fusion.13), channel_id=1, source_target_pairs={{2,0},{4,6},{3,1},{5,7},{10,8},{12,14},{11,9},{13,15},{18,16},{20,... | collective-permute-start | bytes 3145736 | tf_op jit(solution)/shard_map/ppermute | solution.py:426
  738.7 44.5 %collective-permute-start.92 = (bf16[512,1024]{1,0:T(8,128)(2,1)S(1)}, bf16[512,1024]{1,0:T(8,128)(2,1)S(1)}, u32[]{:S(2)}, u32[]{:S(2)}) collective-permute-start(bf16[512,1024]{1,0:T(8,128)(2,1)S(1)} %add_convert_fusion.12), channel_id=1, source_target_pairs={{2,0},{4,6},{3,1},{5,7},{10,8},{12,14},{11,9},{13,15},{18,16},{20,... | collective-permute-start | bytes 3145736 | tf_op jit(solution)/shard_map/ppermute | solution.py:426
  (133 other events, 1582.9 us)

commit v4 on v3

--- a/solution.py
+++ b/solution.py
@@ -1,6 +1,8 @@
 import jax
 import jax.numpy as jnp
 from jax import lax
+from jax.experimental import pallas as pl
+from jax.experimental.pallas import tpu as pltpu
 from jax.sharding import PartitionSpec as P
 
 HEAD_SIZE = 128
@@ -336,18 +338,24 @@
     )
 
 
-def swap_ranks(value):
+def swap_ranks(value, by_neighbour=False):
     size = lax.axis_size("fsdp")
-    pairs = [(a * size + b, b * size + a) for a in range(size) for b in range(size)]
-    return lax.ppermute(value, ("fsdp", "ctx"), pairs)
+    mask = 2 if by_neighbour else 0
+    pairs = [(a * size + b, (b ^ mask) * size + a) for a in range(size) for b in range(size)]
+    moved = lax.ppermute(value, ("fsdp", "ctx"), pairs)
+    return swap_plane(moved, mask, 0) if mask else moved
 
 
 PIECES = ((0, 0), (0, 1), (2, 0), (2, 1))
 
 
-def plane_near(own):
+def plane_beside(own):
+    return own, swap_plane(own, 0, 1), swap_plane(own, 2, 0)
+
+
+def plane_near(beside):
+    own, over_tp, over_x = beside
     rows = own.shape[0] // 2
-    over_tp, over_x = swap_plane(own, 0, 1), swap_plane(own, 2, 0)
     three = jnp.concatenate([own, over_tp, over_x], axis=0)
     corner = [swap_plane(over_x[:rows], 0, 1), swap_plane(over_tp[rows:], 2, 0)]
     return three, swap_plane(three, 1, 0), jnp.concatenate(corner, axis=0)
@@ -362,22 +370,21 @@
     return near_part + swap_plane(far_part.astype(jnp.bfloat16), 1, 0).astype(jnp.float32)
 
 
-def scatter_plane(half):
+def scatter_plane(half, beside=()):
     rows = half.shape[0] // 8
     piece = [half[at * rows : (at + 1) * rows] for at in range(8)]
 
     def sent(parts, *masks):
         low = jnp.concatenate(parts, axis=0).astype(jnp.bfloat16)
-        return swap_plane(low, *masks).astype(jnp.float32)
+        return swap_plane(low, *masks)
 
     by_x = sent([piece[4], piece[6]], 2, 0)
     by_tp = sent([piece[3], piece[7]], 0, 1)
+    by_x, by_tp, beside = lax.optimization_barrier((by_x, by_tp, beside))
+    by_x, by_tp = by_x.astype(jnp.float32), by_tp.astype(jnp.float32)
     top = sent([piece[2] + by_x[rows:]], 0, 1)
     bottom = sent([piece[5] + by_tp[rows:]], 2, 0)
-    return jnp.concatenate([piece[0] + by_x[:rows], piece[1] + by_tp[:rows]], axis=0), [
-        top.astype(jnp.bfloat16),
-        bottom.astype(jnp.bfloat16),
-    ]
+    return jnp.concatenate([piece[0] + by_x[:rows], piece[1] + by_tp[:rows]], axis=0), [top, bottom], beside
 
 
 def scatter_total(own, came):
@@ -409,7 +416,7 @@
         sent, totals, fresh = [], [], list(fresh)
         for stage, name, here, came in self.arrived:
             if stage == 2:
-                self.done[name] = jnp.where(inner, here, came).astype(jnp.float32)
+                self.done[name] = here, came
                 continue
             both = (here.astype(jnp.float32) + came.astype(jnp.float32)).astype(jnp.bfloat16)
             if stage:
@@ -443,7 +450,7 @@
 
 
 def sum_hops():
-    for axis, mask in (("fsdp", 1), ("fsdp", 2), ("tp", 1), ("ctx", 1), ("ctx", 2)):
+    for axis, mask in (("fsdp", 1), ("fsdp", 2), ("tp", 1)):
         yield axis, xor_pairs(lax.axis_size(axis), mask)
 
 
@@ -500,12 +507,43 @@
     return dot_tn(columns, right).astype(jnp.bfloat16)
 
 
-def place_columns(parts, width):
-    me, size = lax.axis_index("fsdp"), lax.axis_size("fsdp")
-    whole = jnp.zeros((parts[0].shape[0], width * size), jnp.float32)
-    for mask, part in enumerate(parts):
-        whole = lax.dynamic_update_slice_in_dim(whole, part, (me ^ mask) * width, 1)
-    return whole
+def at_inner():
+    place = lax.axis_index("ctx")
+    return (place == 1) | (place == 2)
+
+
+def chosen(pair):
+    return jnp.where(at_inner(), *pair).astype(jnp.float32)
+
+
+def place_columns(pairs, widths):
+    size, rows, block = lax.axis_size("fsdp"), pairs[0][0].shape[0], 128
+    scalars = jnp.stack([lax.axis_index("fsdp"), at_inner().astype(jnp.int32)])
+
+    def kernel(scalars, *refs):
+        parts, outs = refs[: 2 * size], refs[2 * size :]
+        for mask in range(size):
+            here, came = parts[2 * mask], parts[2 * mask + 1]
+            value = jnp.where(
+                scalars[1] == 1, here[...].astype(jnp.float32), came[...].astype(jnp.float32)
+            )
+            start = 0
+            for out, width in zip(outs, widths):
+                column = pl.multiple_of((scalars[0] ^ mask) * width, 128)
+                out[:, pl.ds(column, width)] = value[:, start : start + width]
+                start += width
+
+    total = sum(widths)
+    return pl.pallas_call(
+        kernel,
+        grid_spec=pltpu.PrefetchScalarGridSpec(
+            num_scalar_prefetch=1,
+            grid=(rows // block,),
+            in_specs=[pl.BlockSpec((block, total), lambda i, _: (i, 0))] * (2 * size),
+            out_specs=[pl.BlockSpec((block, width * size), lambda i, _: (i, 0)) for width in widths],
+        ),
+        out_shape=[jax.ShapeDtypeStruct((rows, width * size), jnp.float32) for width in widths],
+    )(scalars, *(part for pair in pairs for part in pair))
 
 
 def plane_body(
@@ -542,12 +580,8 @@
     attn_fetch = Fetch((w_query, key_weight, value_weight, w_out_gate))
     attn_came = [attn_fetch.along_x(at) for at in range(2)]
     attn_core = attn_fetch.along_core()
-    ffn_fetch = Fetch((w_gate, w_up))
-    cot_low = swap_ranks(cotangent)
     lengths = swap_ranks(lengths)
-    input_low, attn_came, ffn_fetch.columns[0] = together(
-        (input_low, attn_came, ffn_fetch.columns[0])
-    )
+    input_low, attn_came, cotangent = together((input_low, attn_came, cotangent))
     inputs = input_low.astype(jnp.float32)
 
     def slots_of(fsdp_index, tp_index):
@@ -568,24 +602,21 @@
     position = position_of(slots, segment, lengths)
 
     first_own = apply_rms_norm(inputs, gain_one).astype(jnp.bfloat16)
-    first_near = plane_near(first_own)
+    first_beside = plane_beside(first_own)
     attn_other = [swap_ctx(came) for came in attn_came]
+    cot_low = swap_ranks(cotangent)
     attn_weights = attn_fetch.begin(attn_core)
-    ffn_came = [ffn_fetch.along_x(0)]
-    ffn_columns = (ffn_fetch.columns[1], ffn_fetch.core)
-    first_near, attn_other, attn_weights, attn_came, cot_low, ffn_columns, ffn_came = together(
-        (first_near, attn_other, attn_weights, attn_came, cot_low, ffn_columns, ffn_came)
-    )
-    ffn_fetch.columns[1], ffn_fetch.core = ffn_columns
-    out_grad = cot_low.astype(jnp.float32) * own_valid
-    cot_own = out_grad.astype(jnp.bfloat16)
-    cot_across = swap_plane(cot_own, 2, 0)
-    ffn_came.append(ffn_fetch.along_x(1))
-    ffn_other = swap_ctx(ffn_came[0])
+    first_beside, attn_other, attn_weights = together((first_beside, attn_other, attn_weights))
+    first_near = plane_near(first_beside)
+    for at in range(2):
+        attn_weights = attn_fetch.add(attn_weights, at, attn_came[at], attn_other[at])
+    ffn_fetch = Fetch((w_gate, w_up))
+    ffn_columns = (ffn_fetch.columns, ffn_fetch.core)
+    first_near, attn_weights, ffn_columns = together((first_near, attn_weights, ffn_columns))
+    ffn_fetch.columns, ffn_fetch.core = ffn_columns
+    ffn_came = [ffn_fetch.along_x(at) for at in range(2)]
     ffn_core = ffn_fetch.along_core()
     first_normed = plane_join(first_near)
-    for at in range(2):
-        attn_weights = attn_fetch.add(attn_weights, at, attn_came[at], attn_other[at])
 
     projected = dot_nn(first_normed, attn_weights)
     query_raw = projected[:, :query_width].reshape(row_slots, query_heads, HEAD_SIZE)
@@ -601,13 +632,12 @@
         :, 0
     ]
 
-    query_rot, key_rot, value_low, cot_across = together(
-        (query_rot, key_rot, value_low, cot_across)
-    )
-    cot_pair = jnp.stack([cot_own, cot_across])
-    cot_near = jnp.stack([cot_pair, swap_plane(cot_pair, 0, 1)], axis=1).reshape(
-        -1, cot_own.shape[1]
-    )
+    query_rot, key_rot, value_low, ffn_came[0], cot_low = together(
+        (query_rot, key_rot, value_low, ffn_came[0], cot_low)
+    )
+    ffn_other = swap_ctx(ffn_came[0])
+    out_grad = cot_low.astype(jnp.float32) * own_valid
+    cot_beside = plane_beside(out_grad.astype(jnp.bfloat16))
 
     allowed = (segment[:, None] == segment[None, :]) & (slots[None, :] <= slots[:, None])
     raw_scores = jnp.einsum("qgd,kd->gqk", query_rot, key_rot, preferred_element_type=jnp.float32)
@@ -623,20 +653,27 @@
     attended_rows = attended.reshape(row_slots, query_width)
     gate_sig = jax.nn.sigmoid(gate_logits)
     gated_mix = (attended_rows * gate_sig).astype(jnp.bfloat16)
-    gated_mix, ffn_other, ffn_came = together((gated_mix, ffn_other, ffn_came))
+    gated_mix, ffn_came, cot_beside, ffn_other = together(
+        (gated_mix, ffn_came, cot_beside, ffn_other)
+    )
     ffn_others = [ffn_other, swap_ctx(ffn_came[1])]
     half = row_slots // 2
     far_part = dot_nn(gated_mix[half:], w_output)
     near_part = dot_nn(gated_mix[:half], w_output)
-    own_part, came_parts = scatter_plane(scatter_half(near_part, far_part))
+    own_part, came_parts, ffn_others[1] = scatter_plane(
+        scatter_half(near_part, far_part), ffn_others[1]
+    )
     ffn_weights = ffn_fetch.begin(ffn_core)
     ffn_weights = ffn_fetch.add(ffn_weights, 0, ffn_came[0], ffn_others[0])
+    cot_near = plane_near(cot_beside)
     own_part, came_parts, cot_near, ffn_others, ffn_weights, ffn_came = together(
         (own_part, came_parts, cot_near, ffn_others, ffn_weights, ffn_came)
     )
-    ffn_grad = jnp.concatenate([cot_near, swap_plane(cot_near, 1, 0)], axis=0)
+    ffn_grad = plane_join(cot_near)
     hidden_in = inputs + own_valid * scatter_total(own_part, came_parts)
-    second_near = plane_near(apply_rms_norm(hidden_in, gain_two).astype(jnp.bfloat16))
+    second_near = plane_near(
+        plane_beside(apply_rms_norm(hidden_in, gain_two).astype(jnp.bfloat16))
+    )
     ffn_weights = ffn_fetch.add(ffn_weights, 1, ffn_came[1], ffn_others[1])
     second_near, ffn_grad, ffn_weights = together((second_near, ffn_grad, ffn_weights))
     normed_two = plane_join(second_near)
@@ -655,15 +692,14 @@
     ffn_in_grads = jnp.concatenate([gate_grad, up_grad], axis=1)
 
     sums = CtxSums()
-    down_part = jnp.split(dot_tn(ffn_grad, hidden_act).astype(jnp.bfloat16), 4, axis=0)
-    down_parts = [jnp.concatenate(down_part[at : at + 2], axis=1) for at in (0, 2)]
+    down_parts = jnp.split(dot_tn(hidden_act, ffn_grad).astype(jnp.bfloat16), 2, axis=0)
     down_parts, hidden_act, ffn_in_grads, normed_two = together(
         (down_parts, hidden_act, ffn_in_grads, normed_two)
     )
     sums.send((("down", 0), down_parts[0]))
     two_far = dot_nt(ffn_in_grads[half:], ffn_weights)
     two_near = dot_nt(ffn_in_grads[:half], ffn_weights)
-    own_part, came_parts = scatter_plane(scatter_half(two_near, two_far))
+    own_part, came_parts, _ = scatter_plane(scatter_half(two_near, two_far))
     own_part, came_parts, hidden_act, ffn_in_grads, normed_two = sums.wait(
         (own_part, came_parts, hidden_act, ffn_in_grads, normed_two)
     )
@@ -671,7 +707,7 @@
     normed_two_grad = scatter_total(own_part, came_parts)
     back_two, gain_two_grad = norm_back(hidden_in, gain_two, normed_two_grad)
     hidden_total_grad = out_grad + back_two
-    attn_near = plane_near((own_valid * hidden_total_grad).astype(jnp.bfloat16))
+    attn_near = plane_near(plane_beside((own_valid * hidden_total_grad).astype(jnp.bfloat16)))
     ffn_parts = {mask: grad_part(normed_two, ffn_in_grads, mask) for mask in (1, 0, 2, 3)}
     ffn_parts[1] = swap_plane(ffn_parts[1], 1, 0)
     attn_near, ffn_parts, hidden_act, query_rot = sums.wait(
@@ -681,7 +717,7 @@
     ffn_parts[2] = swap_plane(ffn_parts[2], 2, 0)
     attn_grad = plane_join(attn_near)
     gated_grad = dot_nt(attn_grad, w_output)
-    output_part = dot_tn(attn_grad, gated_mix).astype(jnp.bfloat16)
+    output_part = dot_tn(gated_mix, attn_grad).astype(jnp.bfloat16)
     mixed_grad = (gated_grad * gate_sig).astype(jnp.bfloat16)
     gate_logit_grad = (gated_grad * attended_rows * gate_sig * (1.0 - gate_sig)).astype(
         jnp.bfloat16
@@ -728,21 +764,18 @@
         ],
         axis=1,
     )
-    attn_in_grads, ffn_parts = sums.wait((attn_in_grads, ffn_parts))
+    attn_in_grads, ffn_parts, query_gain_grad, key_gain_grad = sums.wait(
+        (attn_in_grads, ffn_parts, query_gain_grad, key_gain_grad)
+    )
     sums.send((("ffn", 2), ffn_parts[2]))
     one_far = dot_nt(attn_in_grads[half:], attn_weights)
     one_near = dot_nt(attn_in_grads[:half], attn_weights)
-    own_part, came_parts = scatter_plane(scatter_half(one_near, one_far))
+    own_part, came_parts, _ = scatter_plane(scatter_half(one_near, one_far))
     attn_parts = {mask: grad_part(first_normed, attn_in_grads, mask) for mask in (2, 3, 1, 0)}
     attn_parts[1] = swap_plane(attn_parts[1], 1, 0)
     own_part, came_parts, attn_parts, hidden_act = sums.wait(
         (own_part, came_parts, attn_parts, hidden_act)
     )
-    output_parts = jnp.split(output_part, 4, axis=0)
-
-    def attn_sum(mask):
-        return (("attn", mask), jnp.concatenate([attn_parts[mask], output_parts[mask]], axis=1))
-
     hops = sum_hops()
 
     def hop(value):
@@ -759,57 +792,42 @@
     out_far = dot_nn(hidden_act[half:], w_down).astype(jnp.bfloat16)
     out_near = dot_nn(hidden_act[:half], w_down)
     out_half = scatter_half(out_near, out_far)
-    first_attn, second_attn = attn_sum(0), attn_sum(1)
-    attn_parts, input_grad, gains, out_half, first_attn, second_attn = sums.wait(
-        (
-            attn_parts,
-            input_grad,
-            gains,
-            out_half,
-            dict([first_attn]),
-            dict([second_attn]),
-        )
-    )
-    sums.send(*first_attn.items())
-    input_grad = swap_ranks(input_grad)
+    input_grad, gains, out_half, attn_parts = sums.wait((input_grad, gains, out_half, attn_parts))
+    sums.send((("output",), output_part))
     gains = hop(gains)
-    out_own, out_came = scatter_plane(out_half)
-    sums.send(*second_attn.items())
-    third_attn, fourth_attn = dict([attn_sum(2)]), dict([attn_sum(3)])
-    gains, input_grad, out_own, out_came, third_attn, fourth_attn = sums.wait(
-        (gains, input_grad, out_own, out_came, third_attn, fourth_attn), 2
-    )
-    sums.send(*third_attn.items())
+    out_own, out_came, _ = scatter_plane(out_half)
+    sums.send((("attn", 0), attn_parts[0]))
+    gains, out_own, out_came = sums.wait((gains, out_own, out_came), 2)
+    sums.send((("attn", 1), attn_parts[1]))
+    gains = sums.wait(hop(gains), 2)
+    sums.send((("attn", 2), attn_parts[2]))
     layer_output = hidden_in + own_valid * scatter_total(out_own, out_came)
-    layer_output = swap_ranks(layer_output.astype(jnp.bfloat16))
-    gains = sums.wait(hop(gains), 2)
-    sums.send(*fourth_attn.items())
-    gains, layer_output = sums.wait((hop(gains), layer_output), 2)
+    gains, layer_output = sums.wait((hop(gains)[0], layer_output.astype(jnp.bfloat16)), 2)
+    gain_rows = jnp.pad(gains, (0, 8 * attn_parts[3].shape[1] - gains.shape[0]))
+    gain_rows = gain_rows.reshape(8, -1).astype(jnp.bfloat16)
+    sums.send((("attn", 3), jnp.concatenate([attn_parts[3], gain_rows], axis=0)))
+    grad_w_gate, grad_w_up = place_columns(
+        [sums.done["ffn", mask] for mask in range(4)], (hidden_width, hidden_width)
+    )
+    grad_w_down = jnp.concatenate([chosen(sums.done["down", at]) for at in range(2)], axis=0)
+    sums.wait((), 2)
     sums.send()
-    gains = sums.wait(hop(gains), 2)
+    grad_w_gate, grad_w_up, grad_w_down, input_grad, layer_output = sums.wait(
+        (grad_w_gate, grad_w_up, grad_w_down, input_grad, layer_output), 2
+    )
     sums.send()
-    gains = sums.wait(hop(gains), 2)[0]
+    input_grad, layer_output = swap_ranks(input_grad), swap_ranks(layer_output, True)
+    grad_w_output = chosen(sums.done["output",])
+    grad_w_output = sums.wait(grad_w_output, 2)
     while any(sums.flight) or sums.arrived:
         sums.send()
         sums.wait((), 2)
-
-    down_sums = [sums.done["down", at] for at in range(2)]
-    down_sums = [part for pair in down_sums for part in jnp.split(pair, 2, axis=1)]
-    grad_w_down = jnp.concatenate([part.T for part in down_sums], axis=1)
-    grad_w_output = jnp.concatenate(
-        [sums.done["attn", mask][:, -query_width:].T for mask in range(4)], axis=1
-    )
-    ffn_sums = [jnp.split(sums.done["ffn", mask], 2, axis=1) for mask in range(4)]
-    grad_w_gate, grad_w_up = (
-        place_columns([parts[i] for parts in ffn_sums], hidden_width) for i in range(2)
-    )
-    ends = [0, query_width, query_width + HEAD_SIZE, query_width + 2 * HEAD_SIZE]
-    widths = (query_width, HEAD_SIZE, HEAD_SIZE, query_width)
-    grad_w_query, grad_w_key, grad_w_value, grad_w_out_gate = (
-        place_columns(
-            [sums.done["attn", mask][:, start : start + width] for mask in range(4)], width
-        )
-        for start, width in zip(ends, widths)
+    last_sum = chosen([part[-8:] for part in sums.done["attn", 3]])
+    sums.done["attn", 3] = [part[:-8] for part in sums.done["attn", 3]]
+    gains = last_sum.reshape(-1)[: gains.shape[0]]
+    grad_w_query, grad_w_key, grad_w_value, grad_w_out_gate = place_columns(
+        [sums.done["attn", mask] for mask in range(4)],
+        (query_width, HEAD_SIZE, HEAD_SIZE, query_width),
     )
     model_width = layer_input.shape[1]
     ends = (model_width, 2 * model_width, 2 * model_width + HEAD_SIZE)

time: 806 us -> 769 us (0.954)
  local copies, waits for them, and re-layouts: 113 us -> 66.2 us
  other arithmetic: 136 us -> 119 us
  Pallas kernels: 0 us -> 16.6 us
  starting transfers between devices: 193 us -> 208 us
    ppermute x6 -> x9, waiting for transfers between devices: 0.02 us -> 34.2 us  [send(): sent.append(([(0, name, part)], lax.ppermute(part, 'ctx', INWARD)))]
    ppermute x5, starting transfers between devices: 15.6 us -> 48.4 us  [swap_ranks(): moved = lax.ppermute(value, ('fsdp', 'ctx'), pairs)]
    split x14 -> x1, local copies, waits for them, and re-layouts: 33.3 us -> 1.88 us  [plane_body(): jnp.split(dot_tn(hidden_act, ffn_grad).astype(jnp.bfloat16), 2, axis=0)]
    ppermute x6 -> x9, waiting for transfers between devices: 45.6 us -> 21.8 us  [send(): sent.append(([(2, name, total)], lax.ppermute(total, 'ctx', OUTWARD)))]
    ppermute x8 -> x6, starting transfers between devices: 26.2 us -> 6.49 us  [swap_ctx(): return lax.ppermute(value, 'ctx', xor_pairs(lax.axis_size('ctx'), 1))]
    ppermute x15 -> x16, waiting for transfers between devices: 46.2 us -> 27.5 us  [swap_plane(): return lax.ppermute(value, 'tp', xor_pairs(tp_size, tp_mask))]
    ppermute x6 -> x9, starting transfers between devices: 43.1 us -> 61.1 us  [send(): sent.append(([(0, name, part)], lax.ppermute(part, 'ctx', INWARD)))]
    ppermute x5, waiting for transfers between devices: 17.7 us -> 34.6 us  [swap_ranks(): moved = lax.ppermute(value, ('fsdp', 'ctx'), pairs)]
  transfers between devices with their start and end apart: 93 -> 100, of which waited for: 35 -> 41; matrix products, arithmetic and copies ran while one was open for 33% -> 28% of each run, Pallas kernels for 0% -> 1%
where the time goes in v4:
time: 769 us; the launch traced here: 758 us
  waiting for transfers between devices  253 us (33%)
  starting transfers between devices  208 us (27%)
  other arithmetic  119 us (15%)
  matrix products  90.2 us (12%)
  local copies, waits for them, and re-layouts  66.2 us (9%)
  Pallas kernels  16.6 us (2%)
    ppermute x41, waiting for transfers between devices, swap_plane(): return lax.ppermute(value, 'fsdp', xor_pairs(fsdp_size, fsdp_mask))  102 us
    ppermute x9, starting transfers between devices, send(): sent.append(([(0, name, part)], lax.ppermute(part, 'ctx', INWARD)))  61.1 us
    ppermute x41, starting transfers between devices, swap_plane(): return lax.ppermute(value, 'fsdp', xor_pairs(fsdp_size, fsdp_mask))  49.4 us
    ppermute x5, starting transfers between devices, swap_ranks(): moved = lax.ppermute(value, ('fsdp', 'ctx'), pairs)  48.4 us
    convert_element_type x20, other arithmetic, send(): (here.astype(jnp.float32) + came.astype(jnp.float32)).astype(jnp.bfloat16)  39.5 us
    ppermute x5, waiting for transfers between devices, swap_ranks(): moved = lax.ppermute(value, ('fsdp', 'ctx'), pairs)  34.6 us
    ppermute x9, waiting for transfers between devices, send(): sent.append(([(0, name, part)], lax.ppermute(part, 'ctx', INWARD)))  34.2 us
    ppermute x6, waiting for transfers between devices, swap_ctx(): return lax.ppermute(value, 'ctx', xor_pairs(lax.axis_size('ctx'), 1))  31.9 us
  transfers between devices with their start and end apart: 100, of which 41 were waited for; matrix products, arithmetic and copies ran while one was open for 28% of the time, Pallas kernels for 1%

profile of v4, /device:TPU:1, one launch (start us, length us, event | category | flops | bytes accessed | tf_op | source)
XLA Modules:
  0.0 758.5 jit_solution(15475817673325421819)
XLA Ops:
  53.5 6.9 collective-permute-done.7
  84.7 3.9 collective-permute-done.11
  92.8 7.0 fusion.123
  102.3 9.6 %collective-permute-done.13 = bf16[256,1536]{1,0:T(8,128)(2,1)S(1)} collective-permute-done((bf16[256,1536]{1,0:T(8,128)(2,1)S(1)}, bf16[256,1536]{1,0:T(8,128)(2,1)S(1)}, u32[]{:S(2)}, u32[]{:S(2)}) %collective-permute-start.13) | collective-permute-done | bytes 786464 | tf_op jit(solution)/shard_map/ppermute | solution.py:331
  122.3 6.4 collective-permute-done.15
  128.8 11.2 %collective-permute-done.17 = bf16[128,2048]{1,0:T(8,128)(2,1)S(1)} collective-permute-done((bf16[128,2048]{1,0:T(8,128)(2,1)S(1)}, bf16[128,2048]{1,0:T(8,128)(2,1)S(1)}, u32[]{:S(2)}, u32[]{:S(2)}) %collective-permute-start.17) | collective-permute-done | bytes 524320 | tf_op jit(solution)/shard_map/ppermute | solution.py:331
  150.4 14.7 %collective-permute-done.22 = bf16[256,1536]{1,0:T(8,128)(2,1)S(1)} collective-permute-done((bf16[256,1536]{1,0:T(8,128)(2,1)S(1)}, bf16[256,1536]{1,0:T(8,128)(2,1)S(1)}, u32[]{:S(2)}, u32[]{:S(2)}) %collective-permute-start.22) | collective-permute-done | bytes 786464 | tf_op jit(solution)/shard_map/ppermute | solution.py:500
  168.6 4.4 collective-permute-done.27
  174.5 4.1 collective-permute-done.24
  183.2 10.1 %collective-permute-done.30 = bf16[128,2048]{1,0:T(8,128)(2,1)S(1)} collective-permute-done((bf16[128,2048]{1,0:T(8,128)(2,1)S(1)}, bf16[128,2048]{1,0:T(8,128)(2,1)S(1)}, u32[]{:S(2)}, u32[]{:S(2)}) %collective-permute-start.30) | collective-permute-done | bytes 524320 | tf_op jit(solution)/shard_map/ppermute | solution.py:331
  210.6 6.7 fusion.124
  217.2 4.4 multiply_convert_fusion.1
  221.7 3.7 convolution_convert_fusion
  227.5 3.7 convolution_convert_fusion.8
  235.4 5.2 fusion.121
  245.7 9.3 %collective-permute-done.39 = bf16[128,2048]{1,0:T(8,128)(2,1)} collective-permute-done((bf16[128,2048]{1,0:T(8,128)(2,1)}, bf16[128,2048]{1,0:T(8,128)(2,1)}, u32[]{:S(2)}, u32[]{:S(2)}) %collective-permute-start.39) | collective-permute-done | bytes 524320 | tf_op jit(solution)/shard_map/ppermute | solution.py:333
  291.5 4.1 collective-permute-done.47
  311.9 19.1 %collective-permute-start.51 = (bf16[512,1536]{1,0:T(8,128)(2,1)}, bf16[512,1536]{1,0:T(8,128)(2,1)}, u32[]{:S(2)}, u32[]{:S(2)}) collective-permute-start(bf16[512,1536]{1,0:T(8,128)(2,1)} %convolution_convert_fusion.7), channel_id=1, source_target_pairs={{0,2},{6,4},{1,3},{7,5},{8,10},{14,12},{9,11},{15,13},{16,18},{22,... | collective-permute-start | bytes 4718600 | tf_op jit(solution)/shard_map/ppermute | solution.py:431
  331.6 5.7 fusion.6
  346.0 4.7 convolution_convert_fusion.9
  350.7 5.5 fusion.2
  356.8 6.7 collective-permute-done.51
  370.1 3.8 add_convert_fusion.7
  380.6 7.2 collective-permute-start.56
  410.7 7.8 %collective-permute-done.56 = bf16[512,1536]{1,0:T(8,128)(2,1)} collective-permute-done((bf16[512,1536]{1,0:T(8,128)(2,1)}, bf16[512,1536]{1,0:T(8,128)(2,1)}, u32[]{:S(2)}, u32[]{:S(2)}) %collective-permute-start.56) | collective-permute-done | bytes 1572896 | tf_op jit(solution)/shard_map/ppermute | solution.py:431
  418.5 8.3 %collective-permute-done.58 = bf16[512,1536]{1,0:T(8,128)(2,1)} collective-permute-done((bf16[512,1536]{1,0:T(8,128)(2,1)}, bf16[512,1536]{1,0:T(8,128)(2,1)}, u32[]{:S(2)}, u32[]{:S(2)}) %collective-permute-start.58) | collective-permute-done | bytes 1572896 | tf_op jit(solution)/shard_map/ppermute | solution.py:331
  426.7 5.1 convolution_convert_fusion.3
  435.2 4.2 broadcast_select_fusion.3
  442.8 4.4 fusion.122
  451.5 8.9 %collective-permute-done.63 = bf16[128,2048]{1,0:T(8,128)(2,1)S(1)} collective-permute-done((bf16[128,2048]{1,0:T(8,128)(2,1)S(1)}, bf16[128,2048]{1,0:T(8,128)(2,1)S(1)}, u32[]{:S(2)}, u32[]{:S(2)}) %collective-permute-start.63) | collective-permute-done | bytes 524320 | tf_op jit(solution)/shard_map/ppermute | solution.py:333
  464.5 10.4 %collective-permute-done.60.refs_1_ = bf16[512,1536]{1,0:T(8,128)(2,1)S(1)} collective-permute-done((bf16[512,1536]{1,0:T(8,128)(2,1)S(1)}, bf16[512,1536]{1,0:T(8,128)(2,1)S(1)}, u32[]{:S(2)}, u32[]{:S(2)}) %collective-permute-start.60) | collective-permute-done | bytes 1572896 | tf_op jit(solution)/shard_map/ppermute | solution.py:500
  481.4 4.2 collective-permute-start.68
  496.1 11.3 %collective-permute-done.70 = bf16[512,768]{1,0:T(8,128)(2,1)} collective-permute-done((bf16[512,768]{1,0:T(8,128)(2,1)S(1)}, bf16[512,768]{1,0:T(8,128)(2,1)}, u32[]{:S(2)}, u32[]{:S(2)}) %collective-permute-start.70) | collective-permute-done | bytes 786464 | tf_op jit(solution)/shard_map/ppermute | solution.py:331
  507.4 17.2 %collective-permute-done.71 = bf16[512,768]{1,0:T(8,128)(2,1)S(1)} collective-permute-done((bf16[512,768]{1,0:T(8,128)(2,1)S(1)}, bf16[512,768]{1,0:T(8,128)(2,1)S(1)}, u32[]{:S(2)}, u32[]{:S(2)}) %collective-permute-start.71) | collective-permute-done | bytes 786464 | tf_op jit(solution)/shard_map/ppermute | solution.py:331
  536.7 6.1 collective-permute-start.73
  552.8 11.7 %collective-permute-done.73 = bf16[256,2048]{1,0:T(8,128)(2,1)S(1)} collective-permute-done((bf16[256,2048]{1,0:T(8,128)(2,1)}, bf16[256,2048]{1,0:T(8,128)(2,1)S(1)}, u32[]{:S(2)}, u32[]{:S(2)}) %collective-permute-start.73) | collective-permute-done | bytes 1048608 | tf_op jit(solution)/shard_map/ppermute | solution.py:431
  564.6 4.1 collective-permute-start.83
  576.4 10.2 %collective-permute-start.81 = (bf16[512,768]{1,0:T(8,128)(2,1)S(1)}, bf16[512,768]{1,0:T(8,128)(2,1)S(1)}, u32[]{:S(2)}, u32[]{:S(2)}) collective-permute-start(bf16[512,768]{1,0:T(8,128)(2,1)S(1)} %copy-done.55), channel_id=1, source_target_pairs={{0,2},{6,4},{1,3},{7,5},{8,10},{14,12},{9,11},{15,13},{16,18},{22,... | collective-permute-start | bytes 2359304 | tf_op jit(solution)/shard_map/ppermute | solution.py:431
  597.3 4.3 collective-permute-done.81
  602.5 9.3 %collective-permute-done.82.refs_7_ = bf16[512,1536]{1,0:T(8,128)(2,1)S(1)} collective-permute-done((bf16[512,1536]{1,0:T(8,128)(2,1)S(1)}, bf16[512,1536]{1,0:T(8,128)(2,1)S(1)}, u32[]{:S(2)}, u32[]{:S(2)}) %collective-permute-start.82) | collective-permute-done | bytes 1572896 | tf_op jit(solution)/shard_map/ppermute | solution.py:433
  615.2 5.9 collective-permute-start.87
  625.0 4.9 maximum_convert_fusion
  637.7 10.0 %shard_map.254 = (f32[512,3072]{1,0:T(8,128)}, f32[512,3072]{1,0:T(8,128)}) custom-call(s32[2]{0:T(128)} %pad_add_fusion.scalars, bf16[512,1536]{1,0:T(8,128)(2,1)} %get-tuple-element.329.refs_0_, bf16[512,1536]{1,0:T(8,128)(2,1)} %copy-done.11, bf16[512,1536]{1,0:T(8,128)(2,1)} %get-tuple-element.330.refs_2_, bf16[512,1536]{1,0:T(8,128)(2,1)} %copy-done.12, ...), custom_call_target="tpu_custom_call" | custom-call | tf_op jit(solution)/shard_map/pallas_call | solution.py:537
  655.7 14.2 %collective-permute-start.89 = (bf16[128,2048]{1,0:T(8,128)(2,1)S(1)}, bf16[128,2048]{1,0:T(8,128)(2,1)S(1)}, u32[]{:S(2)}, u32[]{:S(2)}) collective-permute-start(bf16[128,2048]{1,0:T(8,128)(2,1)S(1)} %copy-done.67), channel_id=1, source_target_pairs={{0,16},{2,24},{4,0},{6,8},{8,18},{10,26},{12,2},{14,10},{16,20},{1... | collective-permute-start | bytes 1572872 | tf_op jit(solution)/shard_map/ppermute | solution.py:345
  669.9 11.3 %collective-permute-done.93.refs_3_ = bf16[512,768]{1,0:T(8,128)(2,1)S(1)} collective-permute-done((bf16[512,768]{1,0:T(8,128)(2,1)S(1)}, bf16[512,768]{1,0:T(8,128)(2,1)S(1)}, u32[]{:S(2)}, u32[]{:S(2)}) %collective-permute-start.93) | collective-permute-done | bytes 786464 | tf_op jit(solution)/shard_map/ppermute | solution.py:433
  685.6 24.2 %collective-permute-start.91 = (bf16[128,2048]{1,0:T(8,128)(2,1)S(1)}, bf16[128,2048]{1,0:T(8,128)(2,1)S(1)}, u32[]{:S(2)}, u32[]{:S(2)}) collective-permute-start(bf16[128,2048]{1,0:T(8,128)(2,1)S(1)} %copy-done.66), channel_id=1, source_target_pairs={{0,0},{2,8},{4,16},{6,24},{8,2},{10,10},{12,18},{14,26},{16,4},{18... | collective-permute-start | bytes 1572872 | tf_op jit(solution)/shard_map/ppermute | solution.py:345
  709.9 34.6 %collective-permute-done.91 = bf16[128,2048]{1,0:T(8,128)(2,1)S(1)} collective-permute-done((bf16[128,2048]{1,0:T(8,128)(2,1)S(1)}, bf16[128,2048]{1,0:T(8,128)(2,1)S(1)}, u32[]{:S(2)}, u32[]{:S(2)}) %collective-permute-start.91) | collective-permute-done | bytes 524320 | tf_op jit(solution)/shard_map/ppermute | solution.py:345
  747.7 6.6 shard_map.255
  (548 shorter events, 346.6 us)
Async XLA Ops:
  4.4 29.6 %collective-permute-start.2 = (bf16[256,768]{1,0:T(8,128)(2,1)}, bf16[256,768]{1,0:T(8,128)(2,1)}, u32[]{:S(2)}, u32[]{:S(2)}) collective-permute-start(bf16[256,768]{1,0:T(8,128)(2,1)} %pad_maximum_fusion.29), channel_id=1, source_target_pairs={{0,24},{8,16},{16,8},{24,0},{1,25},{9,17},{17,9},{25,1},{2,26},{10... | collective-permute-start | bytes 1179656 | tf_op jit(solution)/shard_map/ppermute | solution.py:331
  7.9 26.7 %collective-permute-start.1 = (bf16[256,768]{1,0:T(8,128)(2,1)}, bf16[256,768]{1,0:T(8,128)(2,1)}, u32[]{:S(2)}, u32[]{:S(2)}) collective-permute-start(bf16[256,768]{1,0:T(8,128)(2,1)} %pad_maximum_fusion.28), channel_id=1, source_target_pairs={{0,16},{8,24},{16,0},{24,8},{1,17},{9,25},{17,1},{25,9},{2,18},{10... | collective-permute-start | bytes 1179656 | tf_op jit(solution)/shard_map/ppermute | solution.py:331
  7.9 26.7 %collective-permute-start = (bf16[128,2048]{1,0:T(8,128)(2,1)}, bf16[128,2048]{1,0:T(8,128)(2,1)}, u32[]{:S(2)}, u32[]{:S(2)}) collective-permute-start(bf16[128,2048]{1,0:T(8,128)(2,1)} %param.15), channel_id=1, source_target_pairs={{0,0},{2,8},{4,16},{6,24},{8,2},{10,10},{12,18},{14,26},{16,4},{18... | collective-permute-start | bytes 1572872 | tf_op jit(solution)/shard_map/ppermute | solution.py:345
  17.3 34.1 %collective-permute-start.8 = (bf16[512,768]{1,0:T(8,128)(2,1)}, bf16[512,768]{1,0:T(8,128)(2,1)}, u32[]{:S(2)}, u32[]{:S(2)}) collective-permute-start(bf16[512,768]{1,0:T(8,128)(2,1)} %pad_maximum_fusion.11), channel_id=1, source_target_pairs={{0,8},{8,0},{16,24},{24,16},{1,9},{9,1},{17,25},{25,17},{2,10},{10... | collective-permute-start | bytes 2359304 | tf_op jit(solution)/shard_map/ppermute | solution.py:331
  19.5 24.5 %collective-permute-start.3 = (s32[1,2]{1,0:T(1,128)}, s32[1,2]{1,0:T(1,128)}, u32[]{:S(2)}, u32[]{:S(2)}) collective-permute-start(s32[1,2]{1,0:T(1,128)} %param.17), channel_id=1, source_target_pairs={{0,0},{2,8},{4,16},{6,24},{8,2},{10,10},{12,18},{14,26},{16,4},{18... | collective-permute-start | bytes 32 | tf_op jit(solution)/shard_map/ppermute | solution.py:345
  63.7 25.1 %collective-permute-start.9 = (bf16[384,2048]{1,0:T(8,128)(2,1)S(1)}, bf16[384,2048]{1,0:T(8,128)(2,1)S(1)}, u32[]{:S(2)}, u32[]{:S(2)}) collective-permute-start(bf16[384,2048]{1,0:T(8,128)(2,1)S(1)} %constant_dynamic-update-slice_fusion), channel_id=1, source_target_pairs={{0,8},{8,0},{16,24},{24,16},{1,9},{9,1},{17,25},{25,17},{2,10},{10... | collective-permute-start | bytes 4718600 | tf_op jit(solution)/shard_map/ppermute | solution.py:331
  70.4 31.9 %collective-permute-start.14 = (bf16[128,2048]{1,0:T(8,128)(2,1)S(1)}, bf16[128,2048]{1,0:T(8,128)(2,1)S(1)}, u32[]{:S(2)}, u32[]{:S(2)}) collective-permute-start(bf16[128,2048]{1,0:T(8,128)(2,1)S(1)} %copy-done.78), channel_id=1, source_target_pairs={{0,0},{2,8},{4,16},{6,24},{8,2},{10,10},{12,18},{14,26},{16,4},{18... | collective-permute-start | bytes 1572872 | tf_op jit(solution)/shard_map/ppermute | solution.py:345
  92.5 36.3 %collective-permute-start.15 = (bf16[256,1536]{1,0:T(8,128)(2,1)S(1)}, bf16[256,1536]{1,0:T(8,128)(2,1)S(1)}, u32[]{:S(2)}, u32[]{:S(2)}) collective-permute-start(bf16[256,1536]{1,0:T(8,128)(2,1)S(1)} %copy-done.50), channel_id=1, source_target_pairs={{0,24},{8,16},{16,8},{24,0},{1,25},{9,17},{17,9},{25,1},{2,26},{10... | collective-permute-start | bytes 2359304 | tf_op jit(solution)/shard_map/ppermute | solution.py:331
  112.9 27.1 %collective-permute-start.17 = (bf16[128,2048]{1,0:T(8,128)(2,1)S(1)}, bf16[128,2048]{1,0:T(8,128)(2,1)S(1)}, u32[]{:S(2)}, u32[]{:S(2)}) collective-permute-start(bf16[128,2048]{1,0:T(8,128)(2,1)S(1)} %fusion.50), channel_id=1, source_target_pairs={{0,16},{8,24},{16,0},{24,8},{1,17},{9,25},{17,1},{25,9},{2,18},{10... | collective-permute-start | bytes 1572872 | tf_op jit(solution)/shard_map/ppermute | solution.py:331
  115.1 24.9 %collective-permute-start.18 = (bf16[256,1536]{1,0:T(8,128)(2,1)S(1)}, bf16[256,1536]{1,0:T(8,128)(2,1)S(1)}, u32[]{:S(2)}, u32[]{:S(2)}) collective-permute-start(bf16[256,1536]{1,0:T(8,128)(2,1)S(1)} %collective-permute-done.13), channel_id=1, source_target_pairs={{0,2},{2,0},{4,6},{6,4},{1,3},{3,1},{5,7},{7,5},{8,10},{10,8},{12,... | collective-permute-start | bytes 2359304 | tf_op jit(solution)/shard_map/ppermute | solution.py:500
  145.2 27.9 %collective-permute-start.25 = (bf16[384,2048]{1,0:T(8,128)(2,1)S(1)}, bf16[384,2048]{1,0:T(8,128)(2,1)S(1)}, u32[]{:S(2)}, u32[]{:S(2)}) collective-permute-start(bf16[384,2048]{1,0:T(8,128)(2,1)S(1)} %constant_dynamic-update-slice_fusion.8), channel_id=1, source_target_pairs={{0,8},{8,0},{16,24},{24,16},{1,9},{9,1},{17,25},{25,17},{2,10},{10... | collective-permute-start | bytes 4718600 | tf_op jit(solution)/shard_map/ppermute | solution.py:331
  231.6 36.3 %collective-permute-start.36 = (bf16[384,2048]{1,0:T(8,128)(2,1)}, bf16[384,2048]{1,0:T(8,128)(2,1)}, u32[]{:S(2)}, u32[]{:S(2)}) collective-permute-start(bf16[384,2048]{1,0:T(8,128)(2,1)} %get-tuple-element.248), channel_id=1, source_target_pairs={{0,2},{6,4},{1,3},{7,5},{8,10},{14,12},{9,11},{15,13},{16,18},{22,... | collective-permute-start | bytes 4718600 | tf_op jit(solution)/shard_map/ppermute | solution.py:431
  261.7 40.9 %collective-permute-start.43 = (bf16[384,2048]{1,0:T(8,128)(2,1)S(1)}, bf16[384,2048]{1,0:T(8,128)(2,1)S(1)}, u32[]{:S(2)}, u32[]{:S(2)}) collective-permute-start(bf16[384,2048]{1,0:T(8,128)(2,1)S(1)} %copy-done.14), channel_id=1, source_target_pairs={{0,2},{6,4},{1,3},{7,5},{8,10},{14,12},{9,11},{15,13},{16,18},{22,... | collective-permute-start | bytes 4718600 | tf_op jit(solution)/shard_map/ppermute | solution.py:431
  272.7 29.9 %collective-permute-start.49 = (bf16[512,1536]{1,0:T(8,128)(2,1)S(1)}, bf16[512,1536]{1,0:T(8,128)(2,1)}, u32[]{:S(2)}, u32[]{:S(2)}) collective-permute-start(bf16[512,1536]{1,0:T(8,128)(2,1)S(1)} %convolution_convert_fusion.6), channel_id=1, source_target_pairs={{0,8},{8,0},{16,24},{24,16},{1,9},{9,1},{17,25},{25,17},{2,10},{10... | collective-permute-start | bytes 4718600 | tf_op jit(solution)/shard_map/ppermute | solution.py:331
  277.9 24.8 %collective-permute-start.42 = (bf16[384,2048]{1,0:T(8,128)(2,1)S(1)}, bf16[384,2048]{1,0:T(8,128)(2,1)S(1)}, u32[]{:S(2)}, u32[]{:S(2)}) collective-permute-start(bf16[384,2048]{1,0:T(8,128)(2,1)S(1)} %add_convert_fusion.11), channel_id=1, source_target_pairs={{2,4},{4,2},{3,5},{5,3},{10,12},{12,10},{11,13},{13,11},{18,20},{2... | collective-permute-start | bytes 4718600 | tf_op jit(solution)/shard_map/ppermute | solution.py:425
  302.7 34.6 %collective-permute-start.53 = (bf16[128,2048]{1,0:T(8,128)(2,1)S(1)}, bf16[128,2048]{1,0:T(8,128)(2,1)S(1)}, u32[]{:S(2)}, u32[]{:S(2)}) collective-permute-start(bf16[128,2048]{1,0:T(8,128)(2,1)S(1)} %pad_maximum_fusion.22), channel_id=1, source_target_pairs={{0,8},{8,0},{16,24},{24,16},{1,9},{9,1},{17,25},{25,17},{2,10},{10... | collective-permute-start | bytes 1572872 | tf_op jit(solution)/shard_map/ppermute | solution.py:331
  306.4 50.4 %collective-permute-start.52 = (bf16[384,2048]{1,0:T(8,128)(2,1)}, bf16[384,2048]{1,0:T(8,128)(2,1)}, u32[]{:S(2)}, u32[]{:S(2)}) collective-permute-start(bf16[384,2048]{1,0:T(8,128)(2,1)} %add_convert_fusion.9), channel_id=1, source_target_pairs={{2,0},{4,6},{3,1},{5,7},{10,8},{12,14},{11,9},{13,15},{18,16},{20,... | collective-permute-start | bytes 4718600 | tf_op jit(solution)/shard_map/ppermute | solution.py:433
  310.1 46.8 %collective-permute-start.50 = (bf16[384,2048]{1,0:T(8,128)(2,1)}, bf16[384,2048]{1,0:T(8,128)(2,1)}, u32[]{:S(2)}, u32[]{:S(2)}) collective-permute-start(bf16[384,2048]{1,0:T(8,128)(2,1)} %add_convert_fusion.10), channel_id=1, source_target_pairs={{2,4},{4,2},{3,5},{5,3},{10,12},{12,10},{11,13},{13,11},{18,20},{2... | collective-permute-start | bytes 4718600 | tf_op jit(solution)/shard_map/ppermute | solution.py:425
  311.9 51.7 %collective-permute-start.51 = (bf16[512,1536]{1,0:T(8,128)(2,1)}, bf16[512,1536]{1,0:T(8,128)(2,1)}, u32[]{:S(2)}, u32[]{:S(2)}) collective-permute-start(bf16[512,1536]{1,0:T(8,128)(2,1)} %convolution_convert_fusion.7), channel_id=1, source_target_pairs={{0,2},{6,4},{1,3},{7,5},{8,10},{14,12},{9,11},{15,13},{16,18},{22,... | collective-permute-start | bytes 4718600 | tf_op jit(solution)/shard_map/ppermute | solution.py:431
  331.0 35.7 %collective-permute-start.54 = (bf16[512,1536]{1,0:T(8,128)(2,1)}, bf16[512,1536]{1,0:T(8,128)(2,1)}, u32[]{:S(2)}, u32[]{:S(2)}) collective-permute-start(bf16[512,1536]{1,0:T(8,128)(2,1)} %convolution_convert_fusion.5), channel_id=1, source_target_pairs={{0,16},{8,24},{16,0},{24,8},{1,17},{9,25},{17,1},{25,9},{2,18},{10... | collective-permute-start | bytes 4718600 | tf_op jit(solution)/shard_map/ppermute | solution.py:331
  373.9 36.9 %collective-permute-start.57 = (bf16[384,2048]{1,0:T(8,128)(2,1)}, bf16[384,2048]{1,0:T(8,128)(2,1)}, u32[]{:S(2)}, u32[]{:S(2)}) collective-permute-start(bf16[384,2048]{1,0:T(8,128)(2,1)} %add_convert_fusion.7), channel_id=1, source_target_pairs={{2,0},{4,6},{3,1},{5,7},{10,8},{12,14},{11,9},{13,15},{18,16},{20,... | collective-permute-start | bytes 4718600 | tf_op jit(solution)/shard_map/ppermute | solution.py:433
  378.7 32.0 %collective-permute-start.55 = (bf16[512,1536]{1,0:T(8,128)(2,1)}, bf16[512,1536]{1,0:T(8,128)(2,1)}, u32[]{:S(2)}, u32[]{:S(2)}) collective-permute-start(bf16[512,1536]{1,0:T(8,128)(2,1)} %add_convert_fusion.8), channel_id=1, source_target_pairs={{2,4},{4,2},{3,5},{5,3},{10,12},{12,10},{11,13},{13,11},{18,20},{2... | collective-permute-start | bytes 4718600 | tf_op jit(solution)/shard_map/ppermute | solution.py:425
  380.6 37.9 %collective-permute-start.56 = (bf16[512,1536]{1,0:T(8,128)(2,1)}, bf16[512,1536]{1,0:T(8,128)(2,1)}, u32[]{:S(2)}, u32[]{:S(2)}) collective-permute-start(bf16[512,1536]{1,0:T(8,128)(2,1)} %collective-permute-done.49), channel_id=1, source_target_pairs={{0,2},{6,4},{1,3},{7,5},{8,10},{14,12},{9,11},{15,13},{16,18},{22,... | collective-permute-start | bytes 4718600 | tf_op jit(solution)/shard_map/ppermute | solution.py:431
  387.8 38.9 %collective-permute-start.58 = (bf16[512,1536]{1,0:T(8,128)(2,1)}, bf16[512,1536]{1,0:T(8,128)(2,1)}, u32[]{:S(2)}, u32[]{:S(2)}) collective-permute-start(bf16[512,1536]{1,0:T(8,128)(2,1)} %convolution_convert_fusion.4), channel_id=1, source_target_pairs={{0,24},{8,16},{16,8},{24,0},{1,25},{9,17},{17,9},{25,1},{2,26},{10... | collective-permute-start | bytes 4718600 | tf_op jit(solution)/shard_map/ppermute | solution.py:331
  435.0 29.5 %collective-permute-start.66 = (bf16[512,768]{1,0:T(8,128)(2,1)S(1)}, bf16[512,768]{1,0:T(8,128)(2,1)S(1)}, u32[]{:S(2)}, u32[]{:S(2)}) collective-permute-start(bf16[512,768]{1,0:T(8,128)(2,1)S(1)} %convolution_convert_fusion.12), channel_id=1, source_target_pairs={{0,8},{8,0},{16,24},{24,16},{1,9},{9,1},{17,25},{25,17},{2,10},{10... | collective-permute-start | bytes 2359304 | tf_op jit(solution)/shard_map/ppermute | solution.py:331
  439.4 35.6 %collective-permute-start.60 = (bf16[512,1536]{1,0:T(8,128)(2,1)S(1)}, bf16[512,1536]{1,0:T(8,128)(2,1)S(1)}, u32[]{:S(2)}, u32[]{:S(2)}) collective-permute-start(bf16[512,1536]{1,0:T(8,128)(2,1)S(1)} %get-tuple-element.386), channel_id=1, source_target_pairs={{0,2},{2,0},{4,6},{6,4},{1,3},{3,1},{5,7},{7,5},{8,10},{10,8},{12,... | collective-permute-start | bytes 4718600 | tf_op jit(solution)/shard_map/ppermute | solution.py:500
  441.8 33.2 %collective-permute-start.59 = (bf16[512,1536]{1,0:T(8,128)(2,1)S(1)}, bf16[512,1536]{1,0:T(8,128)(2,1)S(1)}, u32[]{:S(2)}, u32[]{:S(2)}) collective-permute-start(bf16[512,1536]{1,0:T(8,128)(2,1)S(1)} %add_convert_fusion.6), channel_id=1, source_target_pairs={{2,4},{4,2},{3,5},{5,3},{10,12},{12,10},{11,13},{13,11},{18,20},{2... | collective-permute-start | bytes 4718600 | tf_op jit(solution)/shard_map/ppermute | solution.py:425
  481.4 43.2 %collective-permute-start.68 = (bf16[512,1536]{1,0:T(8,128)(2,1)S(1)}, bf16[512,1536]{1,0:T(8,128)(2,1)S(1)}, u32[]{:S(2)}, u32[]{:S(2)}) collective-permute-start(bf16[512,1536]{1,0:T(8,128)(2,1)S(1)} %get-tuple-element.384), channel_id=1, source_target_pairs={{0,2},{2,0},{4,6},{6,4},{1,3},{3,1},{5,7},{7,5},{8,10},{10,8},{12,... | collective-permute-start | bytes 4718600 | tf_op jit(solution)/shard_map/ppermute | solution.py:500
  487.4 37.2 %collective-permute-start.67 = (bf16[512,1536]{1,0:T(8,128)(2,1)S(1)}, bf16[512,1536]{1,0:T(8,128)(2,1)S(1)}, u32[]{:S(2)}, u32[]{:S(2)}) collective-permute-start(bf16[512,1536]{1,0:T(8,128)(2,1)S(1)} %add_convert_fusion.4), channel_id=1, source_target_pairs={{2,4},{4,2},{3,5},{5,3},{10,12},{12,10},{11,13},{13,11},{18,20},{2... | collective-permute-start | bytes 4718600 | tf_op jit(solution)/shard_map/ppermute | solution.py:425
  488.7 35.9 %collective-permute-start.71 = (bf16[512,768]{1,0:T(8,128)(2,1)S(1)}, bf16[512,768]{1,0:T(8,128)(2,1)S(1)}, u32[]{:S(2)}, u32[]{:S(2)}) collective-permute-start(bf16[512,768]{1,0:T(8,128)(2,1)S(1)} %convolution_convert_fusion.10), channel_id=1, source_target_pairs={{0,24},{8,16},{16,8},{24,0},{1,25},{9,17},{17,9},{25,1},{2,26},{10... | collective-permute-start | bytes 2359304 | tf_op jit(solution)/shard_map/ppermute | solution.py:331
  530.1 38.6 %collective-permute-start.74 = (bf16[512,1536]{1,0:T(8,128)(2,1)}, bf16[512,1536]{1,0:T(8,128)(2,1)}, u32[]{:S(2)}, u32[]{:S(2)}) collective-permute-start(bf16[512,1536]{1,0:T(8,128)(2,1)} %add_convert_fusion.1.refs_4_), channel_id=1, source_target_pairs={{2,0},{4,6},{3,1},{5,7},{10,8},{12,14},{11,9},{13,15},{18,16},{20,... | collective-permute-start | bytes 4718600 | tf_op jit(solution)/shard_map/ppermute | solution.py:433
  534.3 34.4 %collective-permute-start.72 = (bf16[512,1536]{1,0:T(8,128)(2,1)}, bf16[512,1536]{1,0:T(8,128)(2,1)}, u32[]{:S(2)}, u32[]{:S(2)}) collective-permute-start(bf16[512,1536]{1,0:T(8,128)(2,1)} %add_convert_fusion.2), channel_id=1, source_target_pairs={{2,4},{4,2},{3,5},{5,3},{10,12},{12,10},{11,13},{13,11},{18,20},{2... | collective-permute-start | bytes 4718600 | tf_op jit(solution)/shard_map/ppermute | solution.py:425
  536.7 27.9 %collective-permute-start.73 = (bf16[256,2048]{1,0:T(8,128)(2,1)}, bf16[256,2048]{1,0:T(8,128)(2,1)S(1)}, u32[]{:S(2)}, u32[]{:S(2)}) collective-permute-start(bf16[256,2048]{1,0:T(8,128)(2,1)} %convolution_convert_fusion.9), channel_id=1, source_target_pairs={{0,2},{6,4},{1,3},{7,5},{8,10},{14,12},{9,11},{15,13},{16,18},{22,... | collective-permute-start | bytes 3145736 | tf_op jit(solution)/shard_map/ppermute | solution.py:431
  564.6 28.1 %collective-permute-start.83 = (bf16[512,768]{1,0:T(8,128)(2,1)S(1)}, bf16[512,768]{1,0:T(8,128)(2,1)S(1)}, u32[]{:S(2)}, u32[]{:S(2)}) collective-permute-start(bf16[512,768]{1,0:T(8,128)(2,1)S(1)} %copy-done.56), channel_id=1, source_target_pairs={{0,2},{6,4},{1,3},{7,5},{8,10},{14,12},{9,11},{15,13},{16,18},{22,... | collective-permute-start | bytes 2359304 | tf_op jit(solution)/shard_map/ppermute | solution.py:431
  571.0 40.7 %collective-permute-start.82 = (bf16[512,1536]{1,0:T(8,128)(2,1)S(1)}, bf16[512,1536]{1,0:T(8,128)(2,1)S(1)}, u32[]{:S(2)}, u32[]{:S(2)}) collective-permute-start(bf16[512,1536]{1,0:T(8,128)(2,1)S(1)} %add_convert_fusion.refs_6_), channel_id=1, source_target_pairs={{2,0},{4,6},{3,1},{5,7},{10,8},{12,14},{11,9},{13,15},{18,16},{20,... | collective-permute-start | bytes 4718600 | tf_op jit(solution)/shard_map/ppermute | solution.py:433
  572.8 28.8 %collective-permute-start.80 = (bf16[256,2048]{1,0:T(8,128)(2,1)S(1)}, bf16[256,2048]{1,0:T(8,128)(2,1)S(1)}, u32[]{:S(2)}, u32[]{:S(2)}) collective-permute-start(bf16[256,2048]{1,0:T(8,128)(2,1)S(1)} %add_convert_fusion.13), channel_id=1, source_target_pairs={{2,4},{4,2},{3,5},{5,3},{10,12},{12,10},{11,13},{13,11},{18,20},{2... | collective-permute-start | bytes 3145736 | tf_op jit(solution)/shard_map/ppermute | solution.py:425
  576.4 25.2 %collective-permute-start.81 = (bf16[512,768]{1,0:T(8,128)(2,1)S(1)}, bf16[512,768]{1,0:T(8,128)(2,1)S(1)}, u32[]{:S(2)}, u32[]{:S(2)}) collective-permute-start(bf16[512,768]{1,0:T(8,128)(2,1)S(1)} %copy-done.55), channel_id=1, source_target_pairs={{0,2},{6,4},{1,3},{7,5},{8,10},{14,12},{9,11},{15,13},{16,18},{22,... | collective-permute-start | bytes 2359304 | tf_op jit(solution)/shard_map/ppermute | solution.py:431
  590.5 39.5 %collective-permute-start.96 = (bf16[512,768]{1,0:T(8,128)(2,1)}, bf16[512,768]{1,0:T(8,128)(2,1)}, u32[]{:S(2)}, u32[]{:S(2)}) collective-permute-start(bf16[512,768]{1,0:T(8,128)(2,1)} %collective-permute-done.70), channel_id=1, source_target_pairs={{0,2},{6,4},{1,3},{7,5},{8,10},{14,12},{9,11},{15,13},{16,18},{22,... | collective-permute-start | bytes 2359304 | tf_op jit(solution)/shard_map/ppermute | solution.py:431
  595.7 34.3 %collective-permute-start.95 = (bf16[512,768]{1,0:T(8,128)(2,1)}, bf16[512,768]{1,0:T(8,128)(2,1)}, u32[]{:S(2)}, u32[]{:S(2)}) collective-permute-start(bf16[512,768]{1,0:T(8,128)(2,1)} %add_convert_fusion.19), channel_id=1, source_target_pairs={{2,4},{4,2},{3,5},{5,3},{10,12},{12,10},{11,13},{13,11},{18,20},{2... | collective-permute-start | bytes 2359304 | tf_op jit(solution)/shard_map/ppermute | solution.py:425
  613.2 34.5 %collective-permute-start.88 = (bf16[256,2048]{1,0:T(8,128)(2,1)}, bf16[256,2048]{1,0:T(8,128)(2,1)}, u32[]{:S(2)}, u32[]{:S(2)}) collective-permute-start(bf16[256,2048]{1,0:T(8,128)(2,1)} %add_convert_fusion.12), channel_id=1, source_target_pairs={{2,0},{4,6},{3,1},{5,7},{10,8},{12,14},{11,9},{13,15},{18,16},{20,... | collective-permute-start | bytes 3145736 | tf_op jit(solution)/shard_map/ppermute | solution.py:433
  615.2 32.5 %collective-permute-start.87 = (bf16[520,768]{1,0:T(8,128)(2,1)}, bf16[520,768]{1,0:T(8,128)(2,1)}, u32[]{:S(2)}, u32[]{:S(2)}) collective-permute-start(bf16[520,768]{1,0:T(8,128)(2,1)} %constant_dynamic-update-slice_fusion.19), channel_id=1, source_target_pairs={{0,2},{6,4},{1,3},{7,5},{8,10},{14,12},{9,11},{15,13},{16,18},{22,... | collective-permute-start | bytes 2396168 | tf_op jit(solution)/shard_map/ppermute | solution.py:431
  649.3 31.9 %collective-permute-start.92 = (bf16[520,768]{1,0:T(8,128)(2,1)S(1)}, bf16[520,768]{1,0:T(8,128)(2,1)S(1)}, u32[]{:S(2)}, u32[]{:S(2)}) collective-permute-start(bf16[520,768]{1,0:T(8,128)(2,1)S(1)} %add_convert_fusion.15), channel_id=1, source_target_pairs={{2,4},{4,2},{3,5},{5,3},{10,12},{12,10},{11,13},{13,11},{18,20},{2... | collective-permute-start | bytes 2396168 | tf_op jit(solution)/shard_map/ppermute | solution.py:425
  651.7 29.5 %collective-permute-start.93 = (bf16[512,768]{1,0:T(8,128)(2,1)S(1)}, bf16[512,768]{1,0:T(8,128)(2,1)S(1)}, u32[]{:S(2)}, u32[]{:S(2)}) collective-permute-start(bf16[512,768]{1,0:T(8,128)(2,1)S(1)} %add_convert_fusion.20.refs_2_), channel_id=1, source_target_pairs={{2,0},{4,6},{3,1},{5,7},{10,8},{12,14},{11,9},{13,15},{18,16},{20,... | collective-permute-start | bytes 2359304 | tf_op jit(solution)/shard_map/ppermute | solution.py:433
  655.7 54.0 %collective-permute-start.89 = (bf16[128,2048]{1,0:T(8,128)(2,1)S(1)}, bf16[128,2048]{1,0:T(8,128)(2,1)S(1)}, u32[]{:S(2)}, u32[]{:S(2)}) collective-permute-start(bf16[128,2048]{1,0:T(8,128)(2,1)S(1)} %copy-done.67), channel_id=1, source_target_pairs={{0,16},{2,24},{4,0},{6,8},{8,18},{10,26},{12,2},{14,10},{16,20},{1... | collective-permute-start | bytes 1572872 | tf_op jit(solution)/shard_map/ppermute | solution.py:345
  681.4 63.1 %collective-permute-start.94 = (bf16[520,768]{1,0:T(8,128)(2,1)S(1)}, bf16[520,768]{1,0:T(8,128)(2,1)S(1)}, u32[]{:S(2)}, u32[]{:S(2)}) collective-permute-start(bf16[520,768]{1,0:T(8,128)(2,1)S(1)} %add_convert_fusion.14), channel_id=1, source_target_pairs={{2,0},{4,6},{3,1},{5,7},{10,8},{12,14},{11,9},{13,15},{18,16},{20,... | collective-permute-start | bytes 2396168 | tf_op jit(solution)/shard_map/ppermute | solution.py:433
  684.3 60.2 %collective-permute-start.99 = (bf16[512,768]{1,0:T(8,128)(2,1)S(1)}, bf16[512,768]{1,0:T(8,128)(2,1)S(1)}, u32[]{:S(2)}, u32[]{:S(2)}) collective-permute-start(bf16[512,768]{1,0:T(8,128)(2,1)S(1)} %add_convert_fusion.16.refs_4_), channel_id=1, source_target_pairs={{2,0},{4,6},{3,1},{5,7},{10,8},{12,14},{11,9},{13,15},{18,16},{20,... | collective-permute-start | bytes 2359304 | tf_op jit(solution)/shard_map/ppermute | solution.py:433
  685.6 58.9 %collective-permute-start.91 = (bf16[128,2048]{1,0:T(8,128)(2,1)S(1)}, bf16[128,2048]{1,0:T(8,128)(2,1)S(1)}, u32[]{:S(2)}, u32[]{:S(2)}) collective-permute-start(bf16[128,2048]{1,0:T(8,128)(2,1)S(1)} %copy-done.66), channel_id=1, source_target_pairs={{0,0},{2,8},{4,16},{6,24},{8,2},{10,10},{12,18},{14,26},{16,4},{18... | collective-permute-start | bytes 1572872 | tf_op jit(solution)/shard_map/ppermute | solution.py:345
  709.8 34.7 %collective-permute-start.90 = (bf16[128,2048]{1,0:T(8,128)(2,1)S(1)}, bf16[128,2048]{1,0:T(8,128)(2,1)S(1)}, u32[]{:S(2)}, u32[]{:S(2)}) collective-permute-start(bf16[128,2048]{1,0:T(8,128)(2,1)S(1)} %collective-permute-done.89), channel_id=1, source_target_pairs={{0,16},{8,24},{16,0},{24,8},{1,17},{9,25},{17,1},{25,9},{2,18},{10... | collective-permute-start | bytes 1572872 | tf_op jit(solution)/shard_map/ppermute | solution.py:331
  (135 other events, 1824.6 us)

commit v5 on v4

--- a/solution.py
+++ b/solution.py
@@ -338,12 +338,10 @@
     )
 
 
-def swap_ranks(value, by_neighbour=False):
+def swap_ranks(value, mask=0):
     size = lax.axis_size("fsdp")
-    mask = 2 if by_neighbour else 0
-    pairs = [(a * size + b, (b ^ mask) * size + a) for a in range(size) for b in range(size)]
-    moved = lax.ppermute(value, ("fsdp", "ctx"), pairs)
-    return swap_plane(moved, mask, 0) if mask else moved
+    pairs = [(a * size + b, b * size + (a ^ mask)) for a in range(size) for b in range(size)]
+    return lax.ppermute(value, ("fsdp", "ctx"), pairs)
 
 
 PIECES = ((0, 0), (0, 1), (2, 0), (2, 1))
@@ -543,6 +541,9 @@
             out_specs=[pl.BlockSpec((block, width * size), lambda i, _: (i, 0)) for width in widths],
         ),
         out_shape=[jax.ShapeDtypeStruct((rows, width * size), jnp.float32) for width in widths],
+        cost_estimate=pl.CostEstimate(
+            flops=0, transcendentals=0, bytes_accessed=8 * rows * total * size
+        ),
     )(scalars, *(part for pair in pairs for part in pair))
 
 
@@ -810,15 +811,17 @@
         [sums.done["ffn", mask] for mask in range(4)], (hidden_width, hidden_width)
     )
     grad_w_down = jnp.concatenate([chosen(sums.done["down", at]) for at in range(2)], axis=0)
-    sums.wait((), 2)
+    layer_output = sums.wait(swap_plane(layer_output, 2, 0), 2)
     sums.send()
     grad_w_gate, grad_w_up, grad_w_down, input_grad, layer_output = sums.wait(
         (grad_w_gate, grad_w_up, grad_w_down, input_grad, layer_output), 2
     )
     sums.send()
-    input_grad, layer_output = swap_ranks(input_grad), swap_ranks(layer_output, True)
+    input_grad, layer_output = swap_ranks(input_grad), swap_ranks(layer_output, 2)
     grad_w_output = chosen(sums.done["output",])
     grad_w_output = sums.wait(grad_w_output, 2)
+    sums.send()
+    input_grad, layer_output = sums.wait((input_grad, layer_output))
     while any(sums.flight) or sums.arrived:
         sums.send()
         sums.wait((), 2)

time: 769 us -> 759 us (0.987)
  starting transfers between devices: 208 us -> 196 us
    ppermute x5, starting transfers between devices: 48.4 us -> 35.8 us  [swap_ranks(): return lax.ppermute(value, ('fsdp', 'ctx'), pairs)]
    ppermute x9, waiting for transfers between devices: 21.8 us -> 30.2 us  [send(): sent.append(([(2, name, total)], lax.ppermute(total, 'ctx', OUTWARD)))]
    unnamed x182 -> x186, local copies, waits for them, and re-layouts: 19.4 us -> 19.2 us
  transfers between devices with their start and end apart: 100 -> 100, of which waited for: 41 -> 43; matrix products, arithmetic and copies ran while one was open for 28% -> 28% of each run, Pallas kernels for 1% -> 1%
where the time goes in v5:
time: 759 us; the launch traced here: 749 us
  waiting for transfers between devices  260 us (34%)
  starting transfers between devices  196 us (26%)
  other arithmetic  116 us (15%)
  matrix products  90.2 us (12%)
  local copies, waits for them, and re-layouts  65.9 us (9%)
  Pallas kernels  16.6 us (2%)
    ppermute x41, waiting for transfers between devices, swap_plane(): return lax.ppermute(value, 'fsdp', xor_pairs(fsdp_size, fsdp_mask))  102 us
    ppermute x9, starting transfers between devices, send(): sent.append(([(0, name, part)], lax.ppermute(part, 'ctx', INWARD)))  60.7 us
    ppermute x41, starting transfers between devices, swap_plane(): return lax.ppermute(value, 'fsdp', xor_pairs(fsdp_size, fsdp_mask))  50.5 us
    convert_element_type x20, other arithmetic, send(): (here.astype(jnp.float32) + came.astype(jnp.float32)).astype(jnp.bfloat16)  36.1 us
    ppermute x5, starting transfers between devices, swap_ranks(): return lax.ppermute(value, ('fsdp', 'ctx'), pairs)  35.8 us
    ppermute x9, waiting for transfers between devices, send(): sent.append(([(0, name, part)], lax.ppermute(part, 'ctx', INWARD)))  34.4 us
    ppermute x5, waiting for transfers between devices, swap_ranks(): return lax.ppermute(value, ('fsdp', 'ctx'), pairs)  32.6 us
    ppermute x6, waiting for transfers between devices, swap_ctx(): return lax.ppermute(value, 'ctx', xor_pairs(lax.axis_size('ctx'), 1))  32 us
  transfers between devices with their start and end apart: 100, of which 43 were waited for; matrix products, arithmetic and copies ran while one was open for 28% of the time, Pallas kernels for 1%

profile of v5, /device:TPU:1, one launch (start us, length us, event | category | flops | bytes accessed | tf_op | source)
XLA Modules:
  0.0 748.8 jit_solution(14945046434170221912)
XLA Ops:
  53.4 7.0 collective-permute-done.7
  84.8 3.9 collective-permute-done.11
  92.8 7.0 fusion.123
  102.3 9.6 %collective-permute-done.13 = bf16[256,1536]{1,0:T(8,128)(2,1)S(1)} collective-permute-done((bf16[256,1536]{1,0:T(8,128)(2,1)S(1)}, bf16[256,1536]{1,0:T(8,128)(2,1)S(1)}, u32[]{:S(2)}, u32[]{:S(2)}) %collective-permute-start.13) | collective-permute-done | bytes 786464 | tf_op jit(solution)/shard_map/ppermute | solution.py:331
  122.3 6.4 collective-permute-done.15
  128.8 11.2 %collective-permute-done.17 = bf16[128,2048]{1,0:T(8,128)(2,1)S(1)} collective-permute-done((bf16[128,2048]{1,0:T(8,128)(2,1)S(1)}, bf16[128,2048]{1,0:T(8,128)(2,1)S(1)}, u32[]{:S(2)}, u32[]{:S(2)}) %collective-permute-start.17) | collective-permute-done | bytes 524320 | tf_op jit(solution)/shard_map/ppermute | solution.py:331
  150.4 14.7 %collective-permute-done.22 = bf16[256,1536]{1,0:T(8,128)(2,1)S(1)} collective-permute-done((bf16[256,1536]{1,0:T(8,128)(2,1)S(1)}, bf16[256,1536]{1,0:T(8,128)(2,1)S(1)}, u32[]{:S(2)}, u32[]{:S(2)}) %collective-permute-start.22) | collective-permute-done | bytes 786464 | tf_op jit(solution)/shard_map/ppermute | solution.py:498
  168.6 4.4 collective-permute-done.27
  174.5 4.1 collective-permute-done.24
  183.2 10.1 %collective-permute-done.30 = bf16[128,2048]{1,0:T(8,128)(2,1)S(1)} collective-permute-done((bf16[128,2048]{1,0:T(8,128)(2,1)S(1)}, bf16[128,2048]{1,0:T(8,128)(2,1)S(1)}, u32[]{:S(2)}, u32[]{:S(2)}) %collective-permute-start.30) | collective-permute-done | bytes 524320 | tf_op jit(solution)/shard_map/ppermute | solution.py:331
  210.6 6.6 fusion.124
  217.2 4.4 multiply_convert_fusion.1
  235.4 5.2 fusion.121
  245.7 9.3 %collective-permute-done.39 = bf16[128,2048]{1,0:T(8,128)(2,1)} collective-permute-done((bf16[128,2048]{1,0:T(8,128)(2,1)}, bf16[128,2048]{1,0:T(8,128)(2,1)}, u32[]{:S(2)}, u32[]{:S(2)}) %collective-permute-start.39) | collective-permute-done | bytes 524320 | tf_op jit(solution)/shard_map/ppermute | solution.py:333
  264.3 3.7 collective-permute-done.36
  291.5 4.1 collective-permute-done.47
  311.9 19.0 %collective-permute-start.51 = (bf16[512,1536]{1,0:T(8,128)(2,1)}, bf16[512,1536]{1,0:T(8,128)(2,1)}, u32[]{:S(2)}, u32[]{:S(2)}) collective-permute-start(bf16[512,1536]{1,0:T(8,128)(2,1)} %convolution_convert_fusion.7), channel_id=1, source_target_pairs={{0,2},{6,4},{1,3},{7,5},{8,10},{14,12},{9,11},{15,13},{16,18},{22,... | collective-permute-start | bytes 4718600 | tf_op jit(solution)/shard_map/ppermute | solution.py:429
  331.6 5.7 fusion.6
  345.9 4.7 convolution_convert_fusion.9
  350.7 5.5 fusion.2
  356.8 6.7 collective-permute-done.51
  370.0 3.8 add_convert_fusion.7
  380.5 7.2 collective-permute-start.56
  410.7 7.8 %collective-permute-done.56 = bf16[512,1536]{1,0:T(8,128)(2,1)} collective-permute-done((bf16[512,1536]{1,0:T(8,128)(2,1)}, bf16[512,1536]{1,0:T(8,128)(2,1)}, u32[]{:S(2)}, u32[]{:S(2)}) %collective-permute-start.56) | collective-permute-done | bytes 1572896 | tf_op jit(solution)/shard_map/ppermute | solution.py:429
  418.5 8.1 %collective-permute-done.58 = bf16[512,1536]{1,0:T(8,128)(2,1)} collective-permute-done((bf16[512,1536]{1,0:T(8,128)(2,1)}, bf16[512,1536]{1,0:T(8,128)(2,1)}, u32[]{:S(2)}, u32[]{:S(2)}) %collective-permute-start.58) | collective-permute-done | bytes 1572896 | tf_op jit(solution)/shard_map/ppermute | solution.py:331
  426.6 5.1 convolution_convert_fusion.3
  435.0 4.1 broadcast_select_fusion.3
  442.6 4.4 fusion.122
  451.4 8.9 %collective-permute-done.63 = bf16[128,2048]{1,0:T(8,128)(2,1)S(1)} collective-permute-done((bf16[128,2048]{1,0:T(8,128)(2,1)S(1)}, bf16[128,2048]{1,0:T(8,128)(2,1)S(1)}, u32[]{:S(2)}, u32[]{:S(2)}) %collective-permute-start.63) | collective-permute-done | bytes 524320 | tf_op jit(solution)/shard_map/ppermute | solution.py:333
  464.4 10.3 %collective-permute-done.60.refs_1_ = bf16[512,1536]{1,0:T(8,128)(2,1)S(1)} collective-permute-done((bf16[512,1536]{1,0:T(8,128)(2,1)S(1)}, bf16[512,1536]{1,0:T(8,128)(2,1)S(1)}, u32[]{:S(2)}, u32[]{:S(2)}) %collective-permute-start.60) | collective-permute-done | bytes 1572896 | tf_op jit(solution)/shard_map/ppermute | solution.py:498
  481.2 4.2 collective-permute-start.68
  495.9 11.3 %collective-permute-done.70 = bf16[512,768]{1,0:T(8,128)(2,1)} collective-permute-done((bf16[512,768]{1,0:T(8,128)(2,1)S(1)}, bf16[512,768]{1,0:T(8,128)(2,1)}, u32[]{:S(2)}, u32[]{:S(2)}) %collective-permute-start.70) | collective-permute-done | bytes 786464 | tf_op jit(solution)/shard_map/ppermute | solution.py:331
  507.2 17.2 %collective-permute-done.71 = bf16[512,768]{1,0:T(8,128)(2,1)S(1)} collective-permute-done((bf16[512,768]{1,0:T(8,128)(2,1)S(1)}, bf16[512,768]{1,0:T(8,128)(2,1)S(1)}, u32[]{:S(2)}, u32[]{:S(2)}) %collective-permute-start.71) | collective-permute-done | bytes 786464 | tf_op jit(solution)/shard_map/ppermute | solution.py:331
  536.7 5.9 collective-permute-start.73
  552.6 11.8 %collective-permute-done.73 = bf16[256,2048]{1,0:T(8,128)(2,1)S(1)} collective-permute-done((bf16[256,2048]{1,0:T(8,128)(2,1)}, bf16[256,2048]{1,0:T(8,128)(2,1)S(1)}, u32[]{:S(2)}, u32[]{:S(2)}) %collective-permute-start.73) | collective-permute-done | bytes 1048608 | tf_op jit(solution)/shard_map/ppermute | solution.py:429
  564.4 4.1 collective-permute-start.83
  576.2 10.2 %collective-permute-start.81 = (bf16[512,768]{1,0:T(8,128)(2,1)S(1)}, bf16[512,768]{1,0:T(8,128)(2,1)S(1)}, u32[]{:S(2)}, u32[]{:S(2)}) collective-permute-start(bf16[512,768]{1,0:T(8,128)(2,1)S(1)} %copy-done.58), channel_id=1, source_target_pairs={{0,2},{6,4},{1,3},{7,5},{8,10},{14,12},{9,11},{15,13},{16,18},{22,... | collective-permute-start | bytes 2359304 | tf_op jit(solution)/shard_map/ppermute | solution.py:429
  597.0 4.3 collective-permute-done.81
  601.4 10.1 %collective-permute-done.82.refs_7_ = bf16[512,1536]{1,0:T(8,128)(2,1)S(1)} collective-permute-done((bf16[512,1536]{1,0:T(8,128)(2,1)S(1)}, bf16[512,1536]{1,0:T(8,128)(2,1)S(1)}, u32[]{:S(2)}, u32[]{:S(2)}) %collective-permute-start.82) | collective-permute-done | bytes 1572896 | tf_op jit(solution)/shard_map/ppermute | solution.py:431
  616.1 5.8 collective-permute-start.87
  625.9 4.9 maximum_convert_fusion
  630.9 10.0 %shard_map.254 = (f32[512,3072]{1,0:T(8,128)}, f32[512,3072]{1,0:T(8,128)}) custom-call(s32[2]{0:T(128)} %pad_add_fusion.scalars, bf16[512,1536]{1,0:T(8,128)(2,1)} %get-tuple-element.332.refs_0_, bf16[512,1536]{1,0:T(8,128)(2,1)} %copy-done.11, bf16[512,1536]{1,0:T(8,128)(2,1)} %get-tuple-element.333.refs_2_, bf16[512,1536]{1,0:T(8,128)(2,1)} %copy-done.12, ...), custom_call_target="tpu_custom_call" | custom-call | bytes 25165824 | tf_op jit(solution)/shard_map/pallas_call | solution.py:535
  653.9 6.5 collective-permute-done.93.refs_1_
  662.0 25.7 %collective-permute-start.97 = (bf16[128,2048]{1,0:T(8,128)(2,1)S(1)}, bf16[128,2048]{1,0:T(8,128)(2,1)S(1)}, u32[]{:S(2)}, u32[]{:S(2)}) collective-permute-start(bf16[128,2048]{1,0:T(8,128)(2,1)S(1)} %copy-done.69), channel_id=1, source_target_pairs={{0,0},{2,8},{4,16},{6,24},{8,2},{10,10},{12,18},{14,26},{16,4},{18... | collective-permute-start | bytes 1572872 | tf_op jit(solution)/shard_map/ppermute | solution.py:344
  687.8 26.4 %collective-permute-done.97 = bf16[128,2048]{1,0:T(8,128)(2,1)S(1)} collective-permute-done((bf16[128,2048]{1,0:T(8,128)(2,1)S(1)}, bf16[128,2048]{1,0:T(8,128)(2,1)S(1)}, u32[]{:S(2)}, u32[]{:S(2)}) %collective-permute-start.97) | collective-permute-done | bytes 524320 | tf_op jit(solution)/shard_map/ppermute | solution.py:344
  714.2 6.1 collective-permute-done.98
  722.7 12.2 %collective-permute-done.99 = bf16[520,768]{1,0:T(8,128)(2,1)S(1)} collective-permute-done((bf16[520,768]{1,0:T(8,128)(2,1)S(1)}, bf16[520,768]{1,0:T(8,128)(2,1)S(1)}, u32[]{:S(2)}, u32[]{:S(2)}) %collective-permute-start.99) | collective-permute-done | bytes 798752 | tf_op jit(solution)/shard_map/ppermute | solution.py:431
  738.0 6.6 shard_map.255
  (552 shorter events, 347.2 us)
Async XLA Ops:
  4.4 29.5 %collective-permute-start.2 = (bf16[256,768]{1,0:T(8,128)(2,1)}, bf16[256,768]{1,0:T(8,128)(2,1)}, u32[]{:S(2)}, u32[]{:S(2)}) collective-permute-start(bf16[256,768]{1,0:T(8,128)(2,1)} %pad_maximum_fusion.29), channel_id=1, source_target_pairs={{0,24},{8,16},{16,8},{24,0},{1,25},{9,17},{17,9},{25,1},{2,26},{10... | collective-permute-start | bytes 1179656 | tf_op jit(solution)/shard_map/ppermute | solution.py:331
  7.9 26.7 %collective-permute-start.1 = (bf16[256,768]{1,0:T(8,128)(2,1)}, bf16[256,768]{1,0:T(8,128)(2,1)}, u32[]{:S(2)}, u32[]{:S(2)}) collective-permute-start(bf16[256,768]{1,0:T(8,128)(2,1)} %pad_maximum_fusion.28), channel_id=1, source_target_pairs={{0,16},{8,24},{16,0},{24,8},{1,17},{9,25},{17,1},{25,9},{2,18},{10... | collective-permute-start | bytes 1179656 | tf_op jit(solution)/shard_map/ppermute | solution.py:331
  7.9 26.7 %collective-permute-start = (bf16[128,2048]{1,0:T(8,128)(2,1)}, bf16[128,2048]{1,0:T(8,128)(2,1)}, u32[]{:S(2)}, u32[]{:S(2)}) collective-permute-start(bf16[128,2048]{1,0:T(8,128)(2,1)} %param.15), channel_id=1, source_target_pairs={{0,0},{2,8},{4,16},{6,24},{8,2},{10,10},{12,18},{14,26},{16,4},{18... | collective-permute-start | bytes 1572872 | tf_op jit(solution)/shard_map/ppermute | solution.py:344
  17.2 34.1 %collective-permute-start.8 = (bf16[512,768]{1,0:T(8,128)(2,1)}, bf16[512,768]{1,0:T(8,128)(2,1)}, u32[]{:S(2)}, u32[]{:S(2)}) collective-permute-start(bf16[512,768]{1,0:T(8,128)(2,1)} %pad_maximum_fusion.11), channel_id=1, source_target_pairs={{0,8},{8,0},{16,24},{24,16},{1,9},{9,1},{17,25},{25,17},{2,10},{10... | collective-permute-start | bytes 2359304 | tf_op jit(solution)/shard_map/ppermute | solution.py:331
  19.5 24.5 %collective-permute-start.3 = (s32[1,2]{1,0:T(1,128)}, s32[1,2]{1,0:T(1,128)}, u32[]{:S(2)}, u32[]{:S(2)}) collective-permute-start(s32[1,2]{1,0:T(1,128)} %param.17), channel_id=1, source_target_pairs={{0,0},{2,8},{4,16},{6,24},{8,2},{10,10},{12,18},{14,26},{16,4},{18... | collective-permute-start | bytes 32 | tf_op jit(solution)/shard_map/ppermute | solution.py:344
  63.7 25.1 %collective-permute-start.9 = (bf16[384,2048]{1,0:T(8,128)(2,1)S(1)}, bf16[384,2048]{1,0:T(8,128)(2,1)S(1)}, u32[]{:S(2)}, u32[]{:S(2)}) collective-permute-start(bf16[384,2048]{1,0:T(8,128)(2,1)S(1)} %constant_dynamic-update-slice_fusion), channel_id=1, source_target_pairs={{0,8},{8,0},{16,24},{24,16},{1,9},{9,1},{17,25},{25,17},{2,10},{10... | collective-permute-start | bytes 4718600 | tf_op jit(solution)/shard_map/ppermute | solution.py:331
  70.4 31.9 %collective-permute-start.14 = (bf16[128,2048]{1,0:T(8,128)(2,1)S(1)}, bf16[128,2048]{1,0:T(8,128)(2,1)S(1)}, u32[]{:S(2)}, u32[]{:S(2)}) collective-permute-start(bf16[128,2048]{1,0:T(8,128)(2,1)S(1)} %copy-done.80), channel_id=1, source_target_pairs={{0,0},{2,8},{4,16},{6,24},{8,2},{10,10},{12,18},{14,26},{16,4},{18... | collective-permute-start | bytes 1572872 | tf_op jit(solution)/shard_map/ppermute | solution.py:344
  92.4 36.3 %collective-permute-start.15 = (bf16[256,1536]{1,0:T(8,128)(2,1)S(1)}, bf16[256,1536]{1,0:T(8,128)(2,1)S(1)}, u32[]{:S(2)}, u32[]{:S(2)}) collective-permute-start(bf16[256,1536]{1,0:T(8,128)(2,1)S(1)} %copy-done.53), channel_id=1, source_target_pairs={{0,24},{8,16},{16,8},{24,0},{1,25},{9,17},{17,9},{25,1},{2,26},{10... | collective-permute-start | bytes 2359304 | tf_op jit(solution)/shard_map/ppermute | solution.py:331
  112.9 27.1 %collective-permute-start.17 = (bf16[128,2048]{1,0:T(8,128)(2,1)S(1)}, bf16[128,2048]{1,0:T(8,128)(2,1)S(1)}, u32[]{:S(2)}, u32[]{:S(2)}) collective-permute-start(bf16[128,2048]{1,0:T(8,128)(2,1)S(1)} %fusion.50), channel_id=1, source_target_pairs={{0,16},{8,24},{16,0},{24,8},{1,17},{9,25},{17,1},{25,9},{2,18},{10... | collective-permute-start | bytes 1572872 | tf_op jit(solution)/shard_map/ppermute | solution.py:331
  115.1 24.9 %collective-permute-start.18 = (bf16[256,1536]{1,0:T(8,128)(2,1)S(1)}, bf16[256,1536]{1,0:T(8,128)(2,1)S(1)}, u32[]{:S(2)}, u32[]{:S(2)}) collective-permute-start(bf16[256,1536]{1,0:T(8,128)(2,1)S(1)} %collective-permute-done.13), channel_id=1, source_target_pairs={{0,2},{2,0},{4,6},{6,4},{1,3},{3,1},{5,7},{7,5},{8,10},{10,8},{12,... | collective-permute-start | bytes 2359304 | tf_op jit(solution)/shard_map/ppermute | solution.py:498
  144.3 24.3 %collective-permute-start.26 = (bf16[64,2048]{1,0:T(8,128)(2,1)S(1)}, bf16[64,2048]{1,0:T(8,128)(2,1)S(1)}, u32[]{:S(2)}, u32[]{:S(2)}) collective-permute-start(bf16[64,2048]{1,0:T(8,128)(2,1)S(1)} %slice.317), channel_id=1, source_target_pairs={{0,1},{1,0},{2,3},{3,2},{4,5},{5,4},{6,7},{7,6},{8,9},{9,8},{10,11... | collective-permute-start | bytes 786440 | tf_op jit(solution)/shard_map/ppermute | solution.py:333
  145.2 27.9 %collective-permute-start.25 = (bf16[384,2048]{1,0:T(8,128)(2,1)S(1)}, bf16[384,2048]{1,0:T(8,128)(2,1)S(1)}, u32[]{:S(2)}, u32[]{:S(2)}) collective-permute-start(bf16[384,2048]{1,0:T(8,128)(2,1)S(1)} %constant_dynamic-update-slice_fusion.8), channel_id=1, source_target_pairs={{0,8},{8,0},{16,24},{24,16},{1,9},{9,1},{17,25},{25,17},{2,10},{10... | collective-permute-start | bytes 4718600 | tf_op jit(solution)/shard_map/ppermute | solution.py:331
  231.7 36.4 %collective-permute-start.36 = (bf16[384,2048]{1,0:T(8,128)(2,1)}, bf16[384,2048]{1,0:T(8,128)(2,1)}, u32[]{:S(2)}, u32[]{:S(2)}) collective-permute-start(bf16[384,2048]{1,0:T(8,128)(2,1)} %get-tuple-element.251), channel_id=1, source_target_pairs={{0,2},{6,4},{1,3},{7,5},{8,10},{14,12},{9,11},{15,13},{16,18},{22,... | collective-permute-start | bytes 4718600 | tf_op jit(solution)/shard_map/ppermute | solution.py:429
  261.6 41.0 %collective-permute-start.43 = (bf16[384,2048]{1,0:T(8,128)(2,1)S(1)}, bf16[384,2048]{1,0:T(8,128)(2,1)S(1)}, u32[]{:S(2)}, u32[]{:S(2)}) collective-permute-start(bf16[384,2048]{1,0:T(8,128)(2,1)S(1)} %copy-done.14), channel_id=1, source_target_pairs={{0,2},{6,4},{1,3},{7,5},{8,10},{14,12},{9,11},{15,13},{16,18},{22,... | collective-permute-start | bytes 4718600 | tf_op jit(solution)/shard_map/ppermute | solution.py:429
  272.7 30.0 %collective-permute-start.49 = (bf16[512,1536]{1,0:T(8,128)(2,1)S(1)}, bf16[512,1536]{1,0:T(8,128)(2,1)}, u32[]{:S(2)}, u32[]{:S(2)}) collective-permute-start(bf16[512,1536]{1,0:T(8,128)(2,1)S(1)} %convolution_convert_fusion.6), channel_id=1, source_target_pairs={{0,8},{8,0},{16,24},{24,16},{1,9},{9,1},{17,25},{25,17},{2,10},{10... | collective-permute-start | bytes 4718600 | tf_op jit(solution)/shard_map/ppermute | solution.py:331
  277.8 24.8 %collective-permute-start.42 = (bf16[384,2048]{1,0:T(8,128)(2,1)S(1)}, bf16[384,2048]{1,0:T(8,128)(2,1)S(1)}, u32[]{:S(2)}, u32[]{:S(2)}) collective-permute-start(bf16[384,2048]{1,0:T(8,128)(2,1)S(1)} %add_convert_fusion.11), channel_id=1, source_target_pairs={{2,4},{4,2},{3,5},{5,3},{10,12},{12,10},{11,13},{13,11},{18,20},{2... | collective-permute-start | bytes 4718600 | tf_op jit(solution)/shard_map/ppermute | solution.py:423
  302.8 34.5 %collective-permute-start.53 = (bf16[128,2048]{1,0:T(8,128)(2,1)S(1)}, bf16[128,2048]{1,0:T(8,128)(2,1)S(1)}, u32[]{:S(2)}, u32[]{:S(2)}) collective-permute-start(bf16[128,2048]{1,0:T(8,128)(2,1)S(1)} %pad_maximum_fusion.22), channel_id=1, source_target_pairs={{0,8},{8,0},{16,24},{24,16},{1,9},{9,1},{17,25},{25,17},{2,10},{10... | collective-permute-start | bytes 1572872 | tf_op jit(solution)/shard_map/ppermute | solution.py:331
  306.4 50.4 %collective-permute-start.52 = (bf16[384,2048]{1,0:T(8,128)(2,1)}, bf16[384,2048]{1,0:T(8,128)(2,1)}, u32[]{:S(2)}, u32[]{:S(2)}) collective-permute-start(bf16[384,2048]{1,0:T(8,128)(2,1)} %add_convert_fusion.9), channel_id=1, source_target_pairs={{2,0},{4,6},{3,1},{5,7},{10,8},{12,14},{11,9},{13,15},{18,16},{20,... | collective-permute-start | bytes 4718600 | tf_op jit(solution)/shard_map/ppermute | solution.py:431
  310.1 46.7 %collective-permute-start.50 = (bf16[384,2048]{1,0:T(8,128)(2,1)}, bf16[384,2048]{1,0:T(8,128)(2,1)}, u32[]{:S(2)}, u32[]{:S(2)}) collective-permute-start(bf16[384,2048]{1,0:T(8,128)(2,1)} %add_convert_fusion.10), channel_id=1, source_target_pairs={{2,4},{4,2},{3,5},{5,3},{10,12},{12,10},{11,13},{13,11},{18,20},{2... | collective-permute-start | bytes 4718600 | tf_op jit(solution)/shard_map/ppermute | solution.py:423
  311.9 51.6 %collective-permute-start.51 = (bf16[512,1536]{1,0:T(8,128)(2,1)}, bf16[512,1536]{1,0:T(8,128)(2,1)}, u32[]{:S(2)}, u32[]{:S(2)}) collective-permute-start(bf16[512,1536]{1,0:T(8,128)(2,1)} %convolution_convert_fusion.7), channel_id=1, source_target_pairs={{0,2},{6,4},{1,3},{7,5},{8,10},{14,12},{9,11},{15,13},{16,18},{22,... | collective-permute-start | bytes 4718600 | tf_op jit(solution)/shard_map/ppermute | solution.py:429
  331.0 35.7 %collective-permute-start.54 = (bf16[512,1536]{1,0:T(8,128)(2,1)}, bf16[512,1536]{1,0:T(8,128)(2,1)}, u32[]{:S(2)}, u32[]{:S(2)}) collective-permute-start(bf16[512,1536]{1,0:T(8,128)(2,1)} %convolution_convert_fusion.5), channel_id=1, source_target_pairs={{0,16},{8,24},{16,0},{24,8},{1,17},{9,25},{17,1},{25,9},{2,18},{10... | collective-permute-start | bytes 4718600 | tf_op jit(solution)/shard_map/ppermute | solution.py:331
  373.8 36.9 %collective-permute-start.57 = (bf16[384,2048]{1,0:T(8,128)(2,1)}, bf16[384,2048]{1,0:T(8,128)(2,1)}, u32[]{:S(2)}, u32[]{:S(2)}) collective-permute-start(bf16[384,2048]{1,0:T(8,128)(2,1)} %add_convert_fusion.7), channel_id=1, source_target_pairs={{2,0},{4,6},{3,1},{5,7},{10,8},{12,14},{11,9},{13,15},{18,16},{20,... | collective-permute-start | bytes 4718600 | tf_op jit(solution)/shard_map/ppermute | solution.py:431
  378.6 32.0 %collective-permute-start.55 = (bf16[512,1536]{1,0:T(8,128)(2,1)}, bf16[512,1536]{1,0:T(8,128)(2,1)}, u32[]{:S(2)}, u32[]{:S(2)}) collective-permute-start(bf16[512,1536]{1,0:T(8,128)(2,1)} %add_convert_fusion.8), channel_id=1, source_target_pairs={{2,4},{4,2},{3,5},{5,3},{10,12},{12,10},{11,13},{13,11},{18,20},{2... | collective-permute-start | bytes 4718600 | tf_op jit(solution)/shard_map/ppermute | solution.py:423
  380.5 37.9 %collective-permute-start.56 = (bf16[512,1536]{1,0:T(8,128)(2,1)}, bf16[512,1536]{1,0:T(8,128)(2,1)}, u32[]{:S(2)}, u32[]{:S(2)}) collective-permute-start(bf16[512,1536]{1,0:T(8,128)(2,1)} %collective-permute-done.49), channel_id=1, source_target_pairs={{0,2},{6,4},{1,3},{7,5},{8,10},{14,12},{9,11},{15,13},{16,18},{22,... | collective-permute-start | bytes 4718600 | tf_op jit(solution)/shard_map/ppermute | solution.py:429
  387.7 38.9 %collective-permute-start.58 = (bf16[512,1536]{1,0:T(8,128)(2,1)}, bf16[512,1536]{1,0:T(8,128)(2,1)}, u32[]{:S(2)}, u32[]{:S(2)}) collective-permute-start(bf16[512,1536]{1,0:T(8,128)(2,1)} %convolution_convert_fusion.4), channel_id=1, source_target_pairs={{0,24},{8,16},{16,8},{24,0},{1,25},{9,17},{17,9},{25,1},{2,26},{10... | collective-permute-start | bytes 4718600 | tf_op jit(solution)/shard_map/ppermute | solution.py:331
  434.9 29.5 %collective-permute-start.66 = (bf16[512,768]{1,0:T(8,128)(2,1)S(1)}, bf16[512,768]{1,0:T(8,128)(2,1)S(1)}, u32[]{:S(2)}, u32[]{:S(2)}) collective-permute-start(bf16[512,768]{1,0:T(8,128)(2,1)S(1)} %convolution_convert_fusion.12), channel_id=1, source_target_pairs={{0,8},{8,0},{16,24},{24,16},{1,9},{9,1},{17,25},{25,17},{2,10},{10... | collective-permute-start | bytes 2359304 | tf_op jit(solution)/shard_map/ppermute | solution.py:331
  439.2 35.6 %collective-permute-start.60 = (bf16[512,1536]{1,0:T(8,128)(2,1)S(1)}, bf16[512,1536]{1,0:T(8,128)(2,1)S(1)}, u32[]{:S(2)}, u32[]{:S(2)}) collective-permute-start(bf16[512,1536]{1,0:T(8,128)(2,1)S(1)} %get-tuple-element.392), channel_id=1, source_target_pairs={{0,2},{2,0},{4,6},{6,4},{1,3},{3,1},{5,7},{7,5},{8,10},{10,8},{12,... | collective-permute-start | bytes 4718600 | tf_op jit(solution)/shard_map/ppermute | solution.py:498
  441.6 33.2 %collective-permute-start.59 = (bf16[512,1536]{1,0:T(8,128)(2,1)S(1)}, bf16[512,1536]{1,0:T(8,128)(2,1)S(1)}, u32[]{:S(2)}, u32[]{:S(2)}) collective-permute-start(bf16[512,1536]{1,0:T(8,128)(2,1)S(1)} %add_convert_fusion.6), channel_id=1, source_target_pairs={{2,4},{4,2},{3,5},{5,3},{10,12},{12,10},{11,13},{13,11},{18,20},{2... | collective-permute-start | bytes 4718600 | tf_op jit(solution)/shard_map/ppermute | solution.py:423
  481.2 43.2 %collective-permute-start.68 = (bf16[512,1536]{1,0:T(8,128)(2,1)S(1)}, bf16[512,1536]{1,0:T(8,128)(2,1)S(1)}, u32[]{:S(2)}, u32[]{:S(2)}) collective-permute-start(bf16[512,1536]{1,0:T(8,128)(2,1)S(1)} %get-tuple-element.390), channel_id=1, source_target_pairs={{0,2},{2,0},{4,6},{6,4},{1,3},{3,1},{5,7},{7,5},{8,10},{10,8},{12,... | collective-permute-start | bytes 4718600 | tf_op jit(solution)/shard_map/ppermute | solution.py:498
  487.2 37.2 %collective-permute-start.67 = (bf16[512,1536]{1,0:T(8,128)(2,1)S(1)}, bf16[512,1536]{1,0:T(8,128)(2,1)S(1)}, u32[]{:S(2)}, u32[]{:S(2)}) collective-permute-start(bf16[512,1536]{1,0:T(8,128)(2,1)S(1)} %add_convert_fusion.4), channel_id=1, source_target_pairs={{2,4},{4,2},{3,5},{5,3},{10,12},{12,10},{11,13},{13,11},{18,20},{2... | collective-permute-start | bytes 4718600 | tf_op jit(solution)/shard_map/ppermute | solution.py:423
  488.6 35.9 %collective-permute-start.71 = (bf16[512,768]{1,0:T(8,128)(2,1)S(1)}, bf16[512,768]{1,0:T(8,128)(2,1)S(1)}, u32[]{:S(2)}, u32[]{:S(2)}) collective-permute-start(bf16[512,768]{1,0:T(8,128)(2,1)S(1)} %convolution_convert_fusion.10), channel_id=1, source_target_pairs={{0,24},{8,16},{16,8},{24,0},{1,25},{9,17},{17,9},{25,1},{2,26},{10... | collective-permute-start | bytes 2359304 | tf_op jit(solution)/shard_map/ppermute | solution.py:331
  530.0 38.6 %collective-permute-start.74 = (bf16[512,1536]{1,0:T(8,128)(2,1)}, bf16[512,1536]{1,0:T(8,128)(2,1)}, u32[]{:S(2)}, u32[]{:S(2)}) collective-permute-start(bf16[512,1536]{1,0:T(8,128)(2,1)} %add_convert_fusion.1.refs_4_), channel_id=1, source_target_pairs={{2,0},{4,6},{3,1},{5,7},{10,8},{12,14},{11,9},{13,15},{18,16},{20,... | collective-permute-start | bytes 4718600 | tf_op jit(solution)/shard_map/ppermute | solution.py:431
  534.2 34.3 %collective-permute-start.72 = (bf16[512,1536]{1,0:T(8,128)(2,1)}, bf16[512,1536]{1,0:T(8,128)(2,1)}, u32[]{:S(2)}, u32[]{:S(2)}) collective-permute-start(bf16[512,1536]{1,0:T(8,128)(2,1)} %add_convert_fusion.2), channel_id=1, source_target_pairs={{2,4},{4,2},{3,5},{5,3},{10,12},{12,10},{11,13},{13,11},{18,20},{2... | collective-permute-start | bytes 4718600 | tf_op jit(solution)/shard_map/ppermute | solution.py:423
  536.7 27.7 %collective-permute-start.73 = (bf16[256,2048]{1,0:T(8,128)(2,1)}, bf16[256,2048]{1,0:T(8,128)(2,1)S(1)}, u32[]{:S(2)}, u32[]{:S(2)}) collective-permute-start(bf16[256,2048]{1,0:T(8,128)(2,1)} %convolution_convert_fusion.9), channel_id=1, source_target_pairs={{0,2},{6,4},{1,3},{7,5},{8,10},{14,12},{9,11},{15,13},{16,18},{22,... | collective-permute-start | bytes 3145736 | tf_op jit(solution)/shard_map/ppermute | solution.py:429
  564.4 28.1 %collective-permute-start.83 = (bf16[512,768]{1,0:T(8,128)(2,1)S(1)}, bf16[512,768]{1,0:T(8,128)(2,1)S(1)}, u32[]{:S(2)}, u32[]{:S(2)}) collective-permute-start(bf16[512,768]{1,0:T(8,128)(2,1)S(1)} %copy-done.59), channel_id=1, source_target_pairs={{0,2},{6,4},{1,3},{7,5},{8,10},{14,12},{9,11},{15,13},{16,18},{22,... | collective-permute-start | bytes 2359304 | tf_op jit(solution)/shard_map/ppermute | solution.py:429
  570.9 40.7 %collective-permute-start.82 = (bf16[512,1536]{1,0:T(8,128)(2,1)S(1)}, bf16[512,1536]{1,0:T(8,128)(2,1)S(1)}, u32[]{:S(2)}, u32[]{:S(2)}) collective-permute-start(bf16[512,1536]{1,0:T(8,128)(2,1)S(1)} %add_convert_fusion.refs_6_), channel_id=1, source_target_pairs={{2,0},{4,6},{3,1},{5,7},{10,8},{12,14},{11,9},{13,15},{18,16},{20,... | collective-permute-start | bytes 4718600 | tf_op jit(solution)/shard_map/ppermute | solution.py:431
  572.6 28.8 %collective-permute-start.80 = (bf16[256,2048]{1,0:T(8,128)(2,1)S(1)}, bf16[256,2048]{1,0:T(8,128)(2,1)S(1)}, u32[]{:S(2)}, u32[]{:S(2)}) collective-permute-start(bf16[256,2048]{1,0:T(8,128)(2,1)S(1)} %add_convert_fusion.13), channel_id=1, source_target_pairs={{2,4},{4,2},{3,5},{5,3},{10,12},{12,10},{11,13},{13,11},{18,20},{2... | collective-permute-start | bytes 3145736 | tf_op jit(solution)/shard_map/ppermute | solution.py:423
  576.2 25.2 %collective-permute-start.81 = (bf16[512,768]{1,0:T(8,128)(2,1)S(1)}, bf16[512,768]{1,0:T(8,128)(2,1)S(1)}, u32[]{:S(2)}, u32[]{:S(2)}) collective-permute-start(bf16[512,768]{1,0:T(8,128)(2,1)S(1)} %copy-done.58), channel_id=1, source_target_pairs={{0,2},{6,4},{1,3},{7,5},{8,10},{14,12},{9,11},{15,13},{16,18},{22,... | collective-permute-start | bytes 2359304 | tf_op jit(solution)/shard_map/ppermute | solution.py:429
  590.3 34.1 %collective-permute-start.90 = (bf16[512,768]{1,0:T(8,128)(2,1)}, bf16[512,768]{1,0:T(8,128)(2,1)}, u32[]{:S(2)}, u32[]{:S(2)}) collective-permute-start(bf16[512,768]{1,0:T(8,128)(2,1)} %collective-permute-done.70), channel_id=1, source_target_pairs={{0,2},{6,4},{1,3},{7,5},{8,10},{14,12},{9,11},{15,13},{16,18},{22,... | collective-permute-start | bytes 2359304 | tf_op jit(solution)/shard_map/ppermute | solution.py:429
  595.4 45.4 %collective-permute-start.89 = (bf16[512,768]{1,0:T(8,128)(2,1)}, bf16[512,768]{1,0:T(8,128)(2,1)}, u32[]{:S(2)}, u32[]{:S(2)}) collective-permute-start(bf16[512,768]{1,0:T(8,128)(2,1)} %add_convert_fusion.20), channel_id=1, source_target_pairs={{2,4},{4,2},{3,5},{5,3},{10,12},{12,10},{11,13},{13,11},{18,20},{2... | collective-permute-start | bytes 2359304 | tf_op jit(solution)/shard_map/ppermute | solution.py:423
  611.5 29.3 %collective-permute-start.91 = (bf16[128,2048]{1,0:T(8,128)(2,1)}, bf16[128,2048]{1,0:T(8,128)(2,1)}, u32[]{:S(2)}, u32[]{:S(2)}) collective-permute-start(bf16[128,2048]{1,0:T(8,128)(2,1)} %add_convert_fusion.22), channel_id=1, source_target_pairs={{0,16},{8,24},{16,0},{24,8},{1,17},{9,25},{17,1},{25,9},{2,18},{10... | collective-permute-start | bytes 1572872 | tf_op jit(solution)/shard_map/ppermute | solution.py:331
  614.1 32.0 %collective-permute-start.88 = (bf16[256,2048]{1,0:T(8,128)(2,1)}, bf16[256,2048]{1,0:T(8,128)(2,1)}, u32[]{:S(2)}, u32[]{:S(2)}) collective-permute-start(bf16[256,2048]{1,0:T(8,128)(2,1)} %add_convert_fusion.12), channel_id=1, source_target_pairs={{2,0},{4,6},{3,1},{5,7},{10,8},{12,14},{11,9},{13,15},{18,16},{20,... | collective-permute-start | bytes 3145736 | tf_op jit(solution)/shard_map/ppermute | solution.py:431
  616.1 30.0 %collective-permute-start.87 = (bf16[520,768]{1,0:T(8,128)(2,1)}, bf16[520,768]{1,0:T(8,128)(2,1)}, u32[]{:S(2)}, u32[]{:S(2)}) collective-permute-start(bf16[520,768]{1,0:T(8,128)(2,1)} %constant_dynamic-update-slice_fusion.19), channel_id=1, source_target_pairs={{0,2},{6,4},{1,3},{7,5},{8,10},{14,12},{9,11},{15,13},{16,18},{22,... | collective-permute-start | bytes 2396168 | tf_op jit(solution)/shard_map/ppermute | solution.py:429
  647.7 72.7 %collective-permute-start.95 = (bf16[512,768]{1,0:T(8,128)(2,1)S(1)}, bf16[512,768]{1,0:T(8,128)(2,1)S(1)}, u32[]{:S(2)}, u32[]{:S(2)}) collective-permute-start(bf16[512,768]{1,0:T(8,128)(2,1)S(1)} %add_convert_fusion.19.refs_2_), channel_id=1, source_target_pairs={{2,0},{4,6},{3,1},{5,7},{10,8},{12,14},{11,9},{13,15},{18,16},{20,... | collective-permute-start | bytes 2359304 | tf_op jit(solution)/shard_map/ppermute | solution.py:431
  650.3 70.0 %collective-permute-start.94 = (bf16[520,768]{1,0:T(8,128)(2,1)S(1)}, bf16[520,768]{1,0:T(8,128)(2,1)S(1)}, u32[]{:S(2)}, u32[]{:S(2)}) collective-permute-start(bf16[520,768]{1,0:T(8,128)(2,1)S(1)} %add_convert_fusion.15), channel_id=1, source_target_pairs={{2,4},{4,2},{3,5},{5,3},{10,12},{12,10},{11,13},{13,11},{18,20},{2... | collective-permute-start | bytes 2396168 | tf_op jit(solution)/shard_map/ppermute | solution.py:423
  660.7 60.4 %collective-permute-start.96 = (bf16[512,768]{1,0:T(8,128)(2,1)S(1)}, bf16[512,768]{1,0:T(8,128)(2,1)S(1)}, u32[]{:S(2)}, u32[]{:S(2)}) collective-permute-start(bf16[512,768]{1,0:T(8,128)(2,1)S(1)} %add_convert_fusion.16.refs_4_), channel_id=1, source_target_pairs={{2,0},{4,6},{3,1},{5,7},{10,8},{12,14},{11,9},{13,15},{18,16},{20,... | collective-permute-start | bytes 2359304 | tf_op jit(solution)/shard_map/ppermute | solution.py:431
  662.0 52.2 %collective-permute-start.97 = (bf16[128,2048]{1,0:T(8,128)(2,1)S(1)}, bf16[128,2048]{1,0:T(8,128)(2,1)S(1)}, u32[]{:S(2)}, u32[]{:S(2)}) collective-permute-start(bf16[128,2048]{1,0:T(8,128)(2,1)S(1)} %copy-done.69), channel_id=1, source_target_pairs={{0,0},{2,8},{4,16},{6,24},{8,2},{10,10},{12,18},{14,26},{16,4},{18... | collective-permute-start | bytes 1572872 | tf_op jit(solution)/shard_map/ppermute | solution.py:344
  687.7 32.6 %collective-permute-start.98 = (bf16[128,2048]{1,0:T(8,128)(2,1)}, bf16[128,2048]{1,0:T(8,128)(2,1)S(1)}, u32[]{:S(2)}, u32[]{:S(2)}) collective-permute-start(bf16[128,2048]{1,0:T(8,128)(2,1)} %collective-permute-done.91), channel_id=1, source_target_pairs={{0,4},{2,12},{4,20},{6,28},{8,6},{10,14},{12,22},{14,30},{16,0},{1... | collective-permute-start | bytes 1572872 | tf_op jit(solution)/shard_map/ppermute | solution.py:344
  (137 other events, 1838.0 us)

commit v6 on v5

--- a/solution.py
+++ b/solution.py
@@ -364,6 +364,19 @@
     return jnp.concatenate([three, corner, three_far, swap_plane(corner, 1, 0)], axis=0)
 
 
+def plane_near_apart(beside):
+    own, over_tp, over_x = beside
+    rows = own.shape[0] // 2
+    corner = [swap_plane(over_x[:rows], 0, 1), swap_plane(over_tp[rows:], 2, 0)]
+    return list(beside), [swap_plane(piece, 1, 0) for piece in beside], corner
+
+
+def plane_join_apart(near):
+    pieces, far, corner = near
+    far_corner = [swap_plane(piece, 1, 0) for piece in corner]
+    return jnp.concatenate(pieces + corner + far + far_corner, axis=0)
+
+
 def scatter_half(near_part, far_part):
     return near_part + swap_plane(far_part.astype(jnp.bfloat16), 1, 0).astype(jnp.float32)
 
@@ -608,7 +621,7 @@
     cot_low = swap_ranks(cotangent)
     attn_weights = attn_fetch.begin(attn_core)
     first_beside, attn_other, attn_weights = together((first_beside, attn_other, attn_weights))
-    first_near = plane_near(first_beside)
+    first_near = plane_near_apart(first_beside)
     for at in range(2):
         attn_weights = attn_fetch.add(attn_weights, at, attn_came[at], attn_other[at])
     ffn_fetch = Fetch((w_gate, w_up))
@@ -617,7 +630,7 @@
     ffn_fetch.columns, ffn_fetch.core = ffn_columns
     ffn_came = [ffn_fetch.along_x(at) for at in range(2)]
     ffn_core = ffn_fetch.along_core()
-    first_normed = plane_join(first_near)
+    first_normed = plane_join_apart(first_near)
 
     projected = dot_nn(first_normed, attn_weights)
     query_raw = projected[:, :query_width].reshape(row_slots, query_heads, HEAD_SIZE)
@@ -654,9 +667,7 @@
     attended_rows = attended.reshape(row_slots, query_width)
     gate_sig = jax.nn.sigmoid(gate_logits)
     gated_mix = (attended_rows * gate_sig).astype(jnp.bfloat16)
-    gated_mix, ffn_came, cot_beside, ffn_other = together(
-        (gated_mix, ffn_came, cot_beside, ffn_other)
-    )
+    gated_mix, ffn_came, ffn_other = together((gated_mix, ffn_came, ffn_other))
     ffn_others = [ffn_other, swap_ctx(ffn_came[1])]
     half = row_slots // 2
     far_part = dot_nn(gated_mix[half:], w_output)
@@ -666,17 +677,17 @@
     )
     ffn_weights = ffn_fetch.begin(ffn_core)
     ffn_weights = ffn_fetch.add(ffn_weights, 0, ffn_came[0], ffn_others[0])
+    own_part, came_parts, cot_beside, ffn_others, ffn_weights, ffn_came = together(
+        (own_part, came_parts, cot_beside, ffn_others, ffn_weights, ffn_came)
+    )
     cot_near = plane_near(cot_beside)
-    own_part, came_parts, cot_near, ffn_others, ffn_weights, ffn_came = together(
-        (own_part, came_parts, cot_near, ffn_others, ffn_weights, ffn_came)
-    )
-    ffn_grad = plane_join(cot_near)
     hidden_in = inputs + own_valid * scatter_total(own_part, came_parts)
     second_near = plane_near(
         plane_beside(apply_rms_norm(hidden_in, gain_two).astype(jnp.bfloat16))
     )
     ffn_weights = ffn_fetch.add(ffn_weights, 1, ffn_came[1], ffn_others[1])
-    second_near, ffn_grad, ffn_weights = together((second_near, ffn_grad, ffn_weights))
+    second_near, cot_near, ffn_weights = together((second_near, cot_near, ffn_weights))
+    ffn_grad = plane_join(cot_near)
     normed_two = plane_join(second_near)
 
     hidden_grad = dot_nt(ffn_grad, w_down)

time: 759 us -> 750 us (0.988)
  local copies, waits for them, and re-layouts: 65.9 us -> 55.1 us
  waiting for transfers between devices: 260 us -> 268 us
    ppermute x41 -> x44, waiting for transfers between devices: 102 us -> 85.5 us  [swap_plane(): return lax.ppermute(value, 'fsdp', xor_pairs(fsdp_size, fsdp_mask))]
    ppermute x16, waiting for transfers between devices: 27.5 us -> 43.6 us  [swap_plane(): return lax.ppermute(value, 'tp', xor_pairs(tp_size, tp_mask))]
    unnamed x186 -> x189, local copies, waits for them, and re-layouts: 19.2 us -> 13.8 us
    ppermute x41 -> x44, starting transfers between devices: 50.5 us -> 53.8 us  [swap_plane(): return lax.ppermute(value, 'fsdp', xor_pairs(fsdp_size, fsdp_mask))]
  transfers between devices with their start and end apart: 100 -> 103, of which waited for: 43 -> 45; matrix products, arithmetic and copies ran while one was open for 28% -> 28% of each run, Pallas kernels for 1% -> 1%
where the time goes in v6:
time: 750 us; the launch traced here: 742 us
  waiting for transfers between devices  268 us (36%)
  starting transfers between devices  195 us (26%)
  other arithmetic  113 us (15%)
  matrix products  90.4 us (12%)
  local copies, waits for them, and re-layouts  55.1 us (7%)
  Pallas kernels  16.6 us (2%)
    ppermute x44, waiting for transfers between devices, swap_plane(): return lax.ppermute(value, 'fsdp', xor_pairs(fsdp_size, fsdp_mask))  85.5 us
    ppermute x9, starting transfers between devices, send(): sent.append(([(0, name, part)], lax.ppermute(part, 'ctx', INWARD)))  59.2 us
    ppermute x44, starting transfers between devices, swap_plane(): return lax.ppermute(value, 'fsdp', xor_pairs(fsdp_size, fsdp_mask))  53.8 us
    ppermute x16, waiting for transfers between devices, swap_plane(): return lax.ppermute(value, 'tp', xor_pairs(tp_size, tp_mask))  43.6 us
    ppermute x6, waiting for transfers between devices, swap_ctx(): return lax.ppermute(value, 'ctx', xor_pairs(lax.axis_size('ctx'), 1))  39.2 us
    convert_element_type x20, other arithmetic, send(): (here.astype(jnp.float32) + came.astype(jnp.float32)).astype(jnp.bfloat16)  36.1 us
    ppermute x5, starting transfers between devices, swap_ranks(): return lax.ppermute(value, ('fsdp', 'ctx'), pairs)  35.9 us
    ppermute x9, waiting for transfers between devices, send(): sent.append(([(0, name, part)], lax.ppermute(part, 'ctx', INWARD)))  35 us
  transfers between devices with their start and end apart: 103, of which 45 were waited for; matrix products, arithmetic and copies ran while one was open for 28% of the time, Pallas kernels for 1%

profile of v6, /device:TPU:1, one launch (start us, length us, event | category | flops | bytes accessed | tf_op | source)
XLA Modules:
  0.0 742.3 jit_solution(6739428559997592899)
XLA Ops:
  50.1 4.7 collective-permute-done.6
  54.8 8.4 %collective-permute-done.7 = bf16[256,768]{1,0:T(8,128)(2,1)S(1)} collective-permute-done((bf16[256,768]{1,0:T(8,128)(2,1)}, bf16[256,768]{1,0:T(8,128)(2,1)S(1)}, u32[]{:S(2)}, u32[]{:S(2)}) %collective-permute-start.7) | collective-permute-done | bytes 393248 | tf_op jit(solution)/shard_map/ppermute | solution.py:511
  83.4 7.0 fusion.123
  92.4 18.0 %collective-permute-done.16 = bf16[256,1536]{1,0:T(8,128)(2,1)S(1)} collective-permute-done((bf16[256,1536]{1,0:T(8,128)(2,1)S(1)}, bf16[256,1536]{1,0:T(8,128)(2,1)S(1)}, u32[]{:S(2)}, u32[]{:S(2)}) %collective-permute-start.16) | collective-permute-done | bytes 786464 | tf_op jit(solution)/shard_map/ppermute | solution.py:331
  117.9 9.4 %collective-permute-done.18 = bf16[256,1536]{1,0:T(8,128)(2,1)S(1)} collective-permute-done((bf16[256,1536]{1,0:T(8,128)(2,1)S(1)}, bf16[256,1536]{1,0:T(8,128)(2,1)S(1)}, u32[]{:S(2)}, u32[]{:S(2)}) %collective-permute-start.18) | collective-permute-done | bytes 786464 | tf_op jit(solution)/shard_map/ppermute | solution.py:331
  139.9 14.9 %collective-permute-done.23 = bf16[256,1536]{1,0:T(8,128)(2,1)S(1)} collective-permute-done((bf16[256,1536]{1,0:T(8,128)(2,1)S(1)}, bf16[256,1536]{1,0:T(8,128)(2,1)S(1)}, u32[]{:S(2)}, u32[]{:S(2)}) %collective-permute-start.23) | collective-permute-done | bytes 786464 | tf_op jit(solution)/shard_map/ppermute | solution.py:511
  162.7 3.9 collective-permute-done.24
  174.9 6.3 collective-permute-done.30
  181.7 3.9 collective-permute-start.31
  188.0 5.6 collective-permute-done.35
  194.3 4.9 collective-permute-done.32
  204.9 6.6 fusion.124
  211.6 4.7 multiply_convert_fusion.1
  230.1 5.0 fusion.121
  240.0 9.4 %collective-permute-done.42 = bf16[128,2048]{1,0:T(8,128)(2,1)} collective-permute-done((bf16[128,2048]{1,0:T(8,128)(2,1)}, bf16[128,2048]{1,0:T(8,128)(2,1)}, u32[]{:S(2)}, u32[]{:S(2)}) %collective-permute-start.42) | collective-permute-done | bytes 524320 | tf_op jit(solution)/shard_map/ppermute | solution.py:333
  285.4 4.6 collective-permute-done.50
  305.9 18.0 %collective-permute-start.54 = (bf16[512,1536]{1,0:T(8,128)(2,1)}, bf16[512,1536]{1,0:T(8,128)(2,1)}, u32[]{:S(2)}, u32[]{:S(2)}) collective-permute-start(bf16[512,1536]{1,0:T(8,128)(2,1)} %convolution_convert_fusion.7), channel_id=1, source_target_pairs={{0,2},{6,4},{1,3},{7,5},{8,10},{14,12},{9,11},{15,13},{16,18},{22,... | collective-permute-start | bytes 4718600 | tf_op jit(solution)/shard_map/ppermute | solution.py:442
  325.1 5.7 fusion.6
  339.4 4.7 convolution_convert_fusion.9
  344.2 5.5 fusion.2
  350.7 5.5 collective-permute-done.54
  363.0 3.8 add_convert_fusion.7
  373.5 8.0 %collective-permute-start.59 = (bf16[512,1536]{1,0:T(8,128)(2,1)}, bf16[512,1536]{1,0:T(8,128)(2,1)}, u32[]{:S(2)}, u32[]{:S(2)}) collective-permute-start(bf16[512,1536]{1,0:T(8,128)(2,1)} %collective-permute-done.52), channel_id=1, source_target_pairs={{0,2},{6,4},{1,3},{7,5},{8,10},{14,12},{9,11},{15,13},{16,18},{22,... | collective-permute-start | bytes 4718600 | tf_op jit(solution)/shard_map/ppermute | solution.py:442
  403.6 8.6 %collective-permute-done.59 = bf16[512,1536]{1,0:T(8,128)(2,1)} collective-permute-done((bf16[512,1536]{1,0:T(8,128)(2,1)}, bf16[512,1536]{1,0:T(8,128)(2,1)}, u32[]{:S(2)}, u32[]{:S(2)}) %collective-permute-start.59) | collective-permute-done | bytes 1572896 | tf_op jit(solution)/shard_map/ppermute | solution.py:442
  412.2 7.8 %collective-permute-done.61 = bf16[512,1536]{1,0:T(8,128)(2,1)} collective-permute-done((bf16[512,1536]{1,0:T(8,128)(2,1)}, bf16[512,1536]{1,0:T(8,128)(2,1)}, u32[]{:S(2)}, u32[]{:S(2)}) %collective-permute-start.61) | collective-permute-done | bytes 1572896 | tf_op jit(solution)/shard_map/ppermute | solution.py:331
  420.0 5.1 convolution_convert_fusion.3
  428.6 4.2 broadcast_select_fusion.3
  436.3 4.4 fusion.122
  445.1 8.8 %collective-permute-done.66 = bf16[128,2048]{1,0:T(8,128)(2,1)S(1)} collective-permute-done((bf16[128,2048]{1,0:T(8,128)(2,1)S(1)}, bf16[128,2048]{1,0:T(8,128)(2,1)S(1)}, u32[]{:S(2)}, u32[]{:S(2)}) %collective-permute-start.66) | collective-permute-done | bytes 524320 | tf_op jit(solution)/shard_map/ppermute | solution.py:333
  458.4 9.8 %collective-permute-done.63.refs_1_ = bf16[512,1536]{1,0:T(8,128)(2,1)S(1)} collective-permute-done((bf16[512,1536]{1,0:T(8,128)(2,1)S(1)}, bf16[512,1536]{1,0:T(8,128)(2,1)S(1)}, u32[]{:S(2)}, u32[]{:S(2)}) %collective-permute-start.63) | collective-permute-done | bytes 1572896 | tf_op jit(solution)/shard_map/ppermute | solution.py:511
  474.7 4.2 collective-permute-start.71
  489.4 11.3 %collective-permute-done.73 = bf16[512,768]{1,0:T(8,128)(2,1)} collective-permute-done((bf16[512,768]{1,0:T(8,128)(2,1)S(1)}, bf16[512,768]{1,0:T(8,128)(2,1)}, u32[]{:S(2)}, u32[]{:S(2)}) %collective-permute-start.73) | collective-permute-done | bytes 786464 | tf_op jit(solution)/shard_map/ppermute | solution.py:331
  500.6 17.2 %collective-permute-done.74 = bf16[512,768]{1,0:T(8,128)(2,1)S(1)} collective-permute-done((bf16[512,768]{1,0:T(8,128)(2,1)S(1)}, bf16[512,768]{1,0:T(8,128)(2,1)S(1)}, u32[]{:S(2)}, u32[]{:S(2)}) %collective-permute-start.74) | collective-permute-done | bytes 786464 | tf_op jit(solution)/shard_map/ppermute | solution.py:331
  530.9 5.8 collective-permute-start.76
  546.0 12.6 %collective-permute-done.76 = bf16[256,2048]{1,0:T(8,128)(2,1)S(1)} collective-permute-done((bf16[256,2048]{1,0:T(8,128)(2,1)}, bf16[256,2048]{1,0:T(8,128)(2,1)S(1)}, u32[]{:S(2)}, u32[]{:S(2)}) %collective-permute-start.76) | collective-permute-done | bytes 1048608 | tf_op jit(solution)/shard_map/ppermute | solution.py:442
  558.7 4.1 collective-permute-start.86
  570.5 10.2 %collective-permute-start.84 = (bf16[512,768]{1,0:T(8,128)(2,1)S(1)}, bf16[512,768]{1,0:T(8,128)(2,1)S(1)}, u32[]{:S(2)}, u32[]{:S(2)}) collective-permute-start(bf16[512,768]{1,0:T(8,128)(2,1)S(1)} %copy-done.58), channel_id=1, source_target_pairs={{0,2},{6,4},{1,3},{7,5},{8,10},{14,12},{9,11},{15,13},{16,18},{22,... | collective-permute-start | bytes 2359304 | tf_op jit(solution)/shard_map/ppermute | solution.py:442
  591.3 4.6 collective-permute-done.84
  595.9 9.7 %collective-permute-done.85.refs_7_ = bf16[512,1536]{1,0:T(8,128)(2,1)S(1)} collective-permute-done((bf16[512,1536]{1,0:T(8,128)(2,1)S(1)}, bf16[512,1536]{1,0:T(8,128)(2,1)S(1)}, u32[]{:S(2)}, u32[]{:S(2)}) %collective-permute-start.85) | collective-permute-done | bytes 1572896 | tf_op jit(solution)/shard_map/ppermute | solution.py:444
  609.9 5.8 collective-permute-start.90
  619.7 4.9 maximum_convert_fusion
  624.6 10.0 %shard_map.254 = (f32[512,3072]{1,0:T(8,128)}, f32[512,3072]{1,0:T(8,128)}) custom-call(s32[2]{0:T(128)} %pad_add_fusion.scalars, bf16[512,1536]{1,0:T(8,128)(2,1)} %get-tuple-element.340.refs_0_, bf16[512,1536]{1,0:T(8,128)(2,1)} %copy-done.11, bf16[512,1536]{1,0:T(8,128)(2,1)} %get-tuple-element.341.refs_2_, bf16[512,1536]{1,0:T(8,128)(2,1)} %copy-done.12, ...), custom_call_target="tpu_custom_call" | custom-call | bytes 25165824 | tf_op jit(solution)/shard_map/pallas_call | solution.py:548
  647.7 6.5 collective-permute-done.96.refs_1_
  655.8 25.7 %collective-permute-start.100 = (bf16[128,2048]{1,0:T(8,128)(2,1)S(1)}, bf16[128,2048]{1,0:T(8,128)(2,1)S(1)}, u32[]{:S(2)}, u32[]{:S(2)}) collective-permute-start(bf16[128,2048]{1,0:T(8,128)(2,1)S(1)} %copy-done.67), channel_id=1, source_target_pairs={{0,0},{2,8},{4,16},{6,24},{8,2},{10,10},{12,18},{14,26},{16,4},{18... | collective-permute-start | bytes 1572872 | tf_op jit(solution)/shard_map/ppermute | solution.py:344
  681.6 26.4 %collective-permute-done.100 = bf16[128,2048]{1,0:T(8,128)(2,1)S(1)} collective-permute-done((bf16[128,2048]{1,0:T(8,128)(2,1)S(1)}, bf16[128,2048]{1,0:T(8,128)(2,1)S(1)}, u32[]{:S(2)}, u32[]{:S(2)}) %collective-permute-start.100) | collective-permute-done | bytes 524320 | tf_op jit(solution)/shard_map/ppermute | solution.py:344
  708.0 6.4 collective-permute-done.101
  716.7 11.9 %collective-permute-done.102 = bf16[520,768]{1,0:T(8,128)(2,1)S(1)} collective-permute-done((bf16[520,768]{1,0:T(8,128)(2,1)S(1)}, bf16[520,768]{1,0:T(8,128)(2,1)S(1)}, u32[]{:S(2)}, u32[]{:S(2)}) %collective-permute-start.102) | collective-permute-done | bytes 798752 | tf_op jit(solution)/shard_map/ppermute | solution.py:444
  731.8 6.6 shard_map.255
  (559 shorter events, 336.2 us)
Async XLA Ops:
  4.4 35.1 %collective-permute-start.2 = (bf16[256,768]{1,0:T(8,128)(2,1)}, bf16[256,768]{1,0:T(8,128)(2,1)}, u32[]{:S(2)}, u32[]{:S(2)}) collective-permute-start(bf16[256,768]{1,0:T(8,128)(2,1)} %pad_maximum_fusion.27), channel_id=1, source_target_pairs={{0,24},{8,16},{16,8},{24,0},{1,25},{9,17},{17,9},{25,1},{2,26},{10... | collective-permute-start | bytes 1179656 | tf_op jit(solution)/shard_map/ppermute | solution.py:331
  7.9 31.6 %collective-permute-start.1 = (bf16[256,768]{1,0:T(8,128)(2,1)}, bf16[256,768]{1,0:T(8,128)(2,1)}, u32[]{:S(2)}, u32[]{:S(2)}) collective-permute-start(bf16[256,768]{1,0:T(8,128)(2,1)} %pad_maximum_fusion.26), channel_id=1, source_target_pairs={{0,16},{8,24},{16,0},{24,8},{1,17},{9,25},{17,1},{25,9},{2,18},{10... | collective-permute-start | bytes 1179656 | tf_op jit(solution)/shard_map/ppermute | solution.py:331
  7.9 31.6 %collective-permute-start = (bf16[128,2048]{1,0:T(8,128)(2,1)}, bf16[128,2048]{1,0:T(8,128)(2,1)}, u32[]{:S(2)}, u32[]{:S(2)}) collective-permute-start(bf16[128,2048]{1,0:T(8,128)(2,1)} %param.15), channel_id=1, source_target_pairs={{0,0},{2,8},{4,16},{6,24},{8,2},{10,10},{12,18},{14,26},{16,4},{18... | collective-permute-start | bytes 1572872 | tf_op jit(solution)/shard_map/ppermute | solution.py:344
  17.3 30.4 %collective-permute-start.8 = (bf16[512,768]{1,0:T(8,128)(2,1)}, bf16[512,768]{1,0:T(8,128)(2,1)}, u32[]{:S(2)}, u32[]{:S(2)}) collective-permute-start(bf16[512,768]{1,0:T(8,128)(2,1)} %pad_maximum_fusion.10), channel_id=1, source_target_pairs={{0,8},{8,0},{16,24},{24,16},{1,9},{9,1},{17,25},{25,17},{2,10},{10... | collective-permute-start | bytes 2359304 | tf_op jit(solution)/shard_map/ppermute | solution.py:331
  42.0 21.2 %collective-permute-start.4 = (bf16[128,2048]{1,0:T(8,128)(2,1)S(1)}, bf16[128,2048]{1,0:T(8,128)(2,1)S(1)}, u32[]{:S(2)}, u32[]{:S(2)}) collective-permute-start(bf16[128,2048]{1,0:T(8,128)(2,1)S(1)} %fusion.23), channel_id=1, source_target_pairs={{0,1},{1,0},{2,3},{3,2},{4,5},{5,4},{6,7},{7,6},{8,9},{9,8},{10,11... | collective-permute-start | bytes 1572872 | tf_op jit(solution)/shard_map/ppermute | solution.py:333
  79.6 30.9 %collective-permute-start.16 = (bf16[256,1536]{1,0:T(8,128)(2,1)S(1)}, bf16[256,1536]{1,0:T(8,128)(2,1)S(1)}, u32[]{:S(2)}, u32[]{:S(2)}) collective-permute-start(bf16[256,1536]{1,0:T(8,128)(2,1)S(1)} %copy-done.54), channel_id=1, source_target_pairs={{0,16},{8,24},{16,0},{24,8},{1,17},{9,25},{17,1},{25,9},{2,18},{10... | collective-permute-start | bytes 2359304 | tf_op jit(solution)/shard_map/ppermute | solution.py:331
  83.1 44.2 %collective-permute-start.18 = (bf16[256,1536]{1,0:T(8,128)(2,1)S(1)}, bf16[256,1536]{1,0:T(8,128)(2,1)S(1)}, u32[]{:S(2)}, u32[]{:S(2)}) collective-permute-start(bf16[256,1536]{1,0:T(8,128)(2,1)S(1)} %copy-done.53), channel_id=1, source_target_pairs={{0,24},{8,16},{16,8},{24,0},{1,25},{9,17},{17,9},{25,1},{2,26},{10... | collective-permute-start | bytes 2359304 | tf_op jit(solution)/shard_map/ppermute | solution.py:331
  134.2 28.4 %collective-permute-start.26 = (bf16[128,2048]{1,0:T(8,128)(2,1)S(1)}, bf16[128,2048]{1,0:T(8,128)(2,1)S(1)}, u32[]{:S(2)}, u32[]{:S(2)}) collective-permute-start(bf16[128,2048]{1,0:T(8,128)(2,1)S(1)} %fusion.50), channel_id=1, source_target_pairs={{0,1},{1,0},{2,3},{3,2},{4,5},{5,4},{6,7},{7,6},{8,9},{9,8},{10,11... | collective-permute-start | bytes 1572872 | tf_op jit(solution)/shard_map/ppermute | solution.py:333
  134.5 28.2 %collective-permute-start.27 = (bf16[128,2048]{1,0:T(8,128)(2,1)S(1)}, bf16[128,2048]{1,0:T(8,128)(2,1)S(1)}, u32[]{:S(2)}, u32[]{:S(2)}) collective-permute-start(bf16[128,2048]{1,0:T(8,128)(2,1)S(1)} %fusion.50), channel_id=1, source_target_pairs={{0,16},{8,24},{16,0},{24,8},{1,17},{9,25},{17,1},{25,9},{2,18},{10... | collective-permute-start | bytes 1572872 | tf_op jit(solution)/shard_map/ppermute | solution.py:331
  171.6 28.6 %collective-permute-start.34 = (bf16[384,2048]{1,0:T(8,128)(2,1)S(1)}, bf16[384,2048]{1,0:T(8,128)(2,1)S(1)}, u32[]{:S(2)}, u32[]{:S(2)}) collective-permute-start(bf16[384,2048]{1,0:T(8,128)(2,1)S(1)} %constant_dynamic-update-slice_fusion.11), channel_id=1, source_target_pairs={{0,8},{8,0},{16,24},{24,16},{1,9},{9,1},{17,25},{25,17},{2,10},{10... | collective-permute-start | bytes 4718600 | tf_op jit(solution)/shard_map/ppermute | solution.py:331
  226.2 35.9 %collective-permute-start.39 = (bf16[384,2048]{1,0:T(8,128)(2,1)}, bf16[384,2048]{1,0:T(8,128)(2,1)}, u32[]{:S(2)}, u32[]{:S(2)}) collective-permute-start(bf16[384,2048]{1,0:T(8,128)(2,1)} %get-tuple-element.259), channel_id=1, source_target_pairs={{0,2},{6,4},{1,3},{7,5},{8,10},{14,12},{9,11},{15,13},{16,18},{22,... | collective-permute-start | bytes 4718600 | tf_op jit(solution)/shard_map/ppermute | solution.py:442
  256.3 40.7 %collective-permute-start.46 = (bf16[384,2048]{1,0:T(8,128)(2,1)S(1)}, bf16[384,2048]{1,0:T(8,128)(2,1)S(1)}, u32[]{:S(2)}, u32[]{:S(2)}) collective-permute-start(bf16[384,2048]{1,0:T(8,128)(2,1)S(1)} %copy-done.14), channel_id=1, source_target_pairs={{0,2},{6,4},{1,3},{7,5},{8,10},{14,12},{9,11},{15,13},{16,18},{22,... | collective-permute-start | bytes 4718600 | tf_op jit(solution)/shard_map/ppermute | solution.py:442
  266.6 30.4 %collective-permute-start.52 = (bf16[512,1536]{1,0:T(8,128)(2,1)S(1)}, bf16[512,1536]{1,0:T(8,128)(2,1)}, u32[]{:S(2)}, u32[]{:S(2)}) collective-permute-start(bf16[512,1536]{1,0:T(8,128)(2,1)S(1)} %convolution_convert_fusion.6), channel_id=1, source_target_pairs={{0,8},{8,0},{16,24},{24,16},{1,9},{9,1},{17,25},{25,17},{2,10},{10... | collective-permute-start | bytes 4718600 | tf_op jit(solution)/shard_map/ppermute | solution.py:331
  272.1 24.9 %collective-permute-start.45 = (bf16[384,2048]{1,0:T(8,128)(2,1)S(1)}, bf16[384,2048]{1,0:T(8,128)(2,1)S(1)}, u32[]{:S(2)}, u32[]{:S(2)}) collective-permute-start(bf16[384,2048]{1,0:T(8,128)(2,1)S(1)} %add_convert_fusion.11), channel_id=1, source_target_pairs={{2,4},{4,2},{3,5},{5,3},{10,12},{12,10},{11,13},{13,11},{18,20},{2... | collective-permute-start | bytes 4718600 | tf_op jit(solution)/shard_map/ppermute | solution.py:436
  275.5 21.5 %collective-permute-start.49 = (bf16[384,2048]{1,0:T(8,128)(2,1)S(1)}, bf16[384,2048]{1,0:T(8,128)(2,1)S(1)}, u32[]{:S(2)}, u32[]{:S(2)}) collective-permute-start(bf16[384,2048]{1,0:T(8,128)(2,1)S(1)} %pad_maximum_fusion.3), channel_id=1, source_target_pairs={{0,8},{8,0},{16,24},{24,16},{1,9},{9,1},{17,25},{25,17},{2,10},{10... | collective-permute-start | bytes 4718600 | tf_op jit(solution)/shard_map/ppermute | solution.py:331
  297.2 33.7 %collective-permute-start.56 = (bf16[128,2048]{1,0:T(8,128)(2,1)S(1)}, bf16[128,2048]{1,0:T(8,128)(2,1)S(1)}, u32[]{:S(2)}, u32[]{:S(2)}) collective-permute-start(bf16[128,2048]{1,0:T(8,128)(2,1)S(1)} %pad_maximum_fusion.20), channel_id=1, source_target_pairs={{0,8},{8,0},{16,24},{24,16},{1,9},{9,1},{17,25},{25,17},{2,10},{10... | collective-permute-start | bytes 1572872 | tf_op jit(solution)/shard_map/ppermute | solution.py:331
  300.8 49.9 %collective-permute-start.55 = (bf16[384,2048]{1,0:T(8,128)(2,1)}, bf16[384,2048]{1,0:T(8,128)(2,1)}, u32[]{:S(2)}, u32[]{:S(2)}) collective-permute-start(bf16[384,2048]{1,0:T(8,128)(2,1)} %add_convert_fusion.9), channel_id=1, source_target_pairs={{2,0},{4,6},{3,1},{5,7},{10,8},{12,14},{11,9},{13,15},{18,16},{20,... | collective-permute-start | bytes 4718600 | tf_op jit(solution)/shard_map/ppermute | solution.py:444
  304.1 46.6 %collective-permute-start.53 = (bf16[384,2048]{1,0:T(8,128)(2,1)}, bf16[384,2048]{1,0:T(8,128)(2,1)}, u32[]{:S(2)}, u32[]{:S(2)}) collective-permute-start(bf16[384,2048]{1,0:T(8,128)(2,1)} %add_convert_fusion.10), channel_id=1, source_target_pairs={{2,4},{4,2},{3,5},{5,3},{10,12},{12,10},{11,13},{13,11},{18,20},{2... | collective-permute-start | bytes 4718600 | tf_op jit(solution)/shard_map/ppermute | solution.py:436
  305.9 50.4 %collective-permute-start.54 = (bf16[512,1536]{1,0:T(8,128)(2,1)}, bf16[512,1536]{1,0:T(8,128)(2,1)}, u32[]{:S(2)}, u32[]{:S(2)}) collective-permute-start(bf16[512,1536]{1,0:T(8,128)(2,1)} %convolution_convert_fusion.7), channel_id=1, source_target_pairs={{0,2},{6,4},{1,3},{7,5},{8,10},{14,12},{9,11},{15,13},{16,18},{22,... | collective-permute-start | bytes 4718600 | tf_op jit(solution)/shard_map/ppermute | solution.py:442
  323.9 35.8 %collective-permute-start.57 = (bf16[512,1536]{1,0:T(8,128)(2,1)}, bf16[512,1536]{1,0:T(8,128)(2,1)}, u32[]{:S(2)}, u32[]{:S(2)}) collective-permute-start(bf16[512,1536]{1,0:T(8,128)(2,1)} %convolution_convert_fusion.5), channel_id=1, source_target_pairs={{0,16},{8,24},{16,0},{24,8},{1,17},{9,25},{17,1},{25,9},{2,18},{10... | collective-permute-start | bytes 4718600 | tf_op jit(solution)/shard_map/ppermute | solution.py:331
  366.8 36.9 %collective-permute-start.60 = (bf16[384,2048]{1,0:T(8,128)(2,1)}, bf16[384,2048]{1,0:T(8,128)(2,1)}, u32[]{:S(2)}, u32[]{:S(2)}) collective-permute-start(bf16[384,2048]{1,0:T(8,128)(2,1)} %add_convert_fusion.7), channel_id=1, source_target_pairs={{2,0},{4,6},{3,1},{5,7},{10,8},{12,14},{11,9},{13,15},{18,16},{20,... | collective-permute-start | bytes 4718600 | tf_op jit(solution)/shard_map/ppermute | solution.py:444
  371.6 32.0 %collective-permute-start.58 = (bf16[512,1536]{1,0:T(8,128)(2,1)}, bf16[512,1536]{1,0:T(8,128)(2,1)}, u32[]{:S(2)}, u32[]{:S(2)}) collective-permute-start(bf16[512,1536]{1,0:T(8,128)(2,1)} %add_convert_fusion.8), channel_id=1, source_target_pairs={{2,4},{4,2},{3,5},{5,3},{10,12},{12,10},{11,13},{13,11},{18,20},{2... | collective-permute-start | bytes 4718600 | tf_op jit(solution)/shard_map/ppermute | solution.py:436
  373.5 38.7 %collective-permute-start.59 = (bf16[512,1536]{1,0:T(8,128)(2,1)}, bf16[512,1536]{1,0:T(8,128)(2,1)}, u32[]{:S(2)}, u32[]{:S(2)}) collective-permute-start(bf16[512,1536]{1,0:T(8,128)(2,1)} %collective-permute-done.52), channel_id=1, source_target_pairs={{0,2},{6,4},{1,3},{7,5},{8,10},{14,12},{9,11},{15,13},{16,18},{22,... | collective-permute-start | bytes 4718600 | tf_op jit(solution)/shard_map/ppermute | solution.py:442
  381.5 38.5 %collective-permute-start.61 = (bf16[512,1536]{1,0:T(8,128)(2,1)}, bf16[512,1536]{1,0:T(8,128)(2,1)}, u32[]{:S(2)}, u32[]{:S(2)}) collective-permute-start(bf16[512,1536]{1,0:T(8,128)(2,1)} %convolution_convert_fusion.4), channel_id=1, source_target_pairs={{0,24},{8,16},{16,8},{24,0},{1,25},{9,17},{17,9},{25,1},{2,26},{10... | collective-permute-start | bytes 4718600 | tf_op jit(solution)/shard_map/ppermute | solution.py:331
  428.5 29.9 %collective-permute-start.69 = (bf16[512,768]{1,0:T(8,128)(2,1)S(1)}, bf16[512,768]{1,0:T(8,128)(2,1)S(1)}, u32[]{:S(2)}, u32[]{:S(2)}) collective-permute-start(bf16[512,768]{1,0:T(8,128)(2,1)S(1)} %convolution_convert_fusion.12), channel_id=1, source_target_pairs={{0,8},{8,0},{16,24},{24,16},{1,9},{9,1},{17,25},{25,17},{2,10},{10... | collective-permute-start | bytes 2359304 | tf_op jit(solution)/shard_map/ppermute | solution.py:331
  432.7 35.5 %collective-permute-start.63 = (bf16[512,1536]{1,0:T(8,128)(2,1)S(1)}, bf16[512,1536]{1,0:T(8,128)(2,1)S(1)}, u32[]{:S(2)}, u32[]{:S(2)}) collective-permute-start(bf16[512,1536]{1,0:T(8,128)(2,1)S(1)} %get-tuple-element.400), channel_id=1, source_target_pairs={{0,2},{2,0},{4,6},{6,4},{1,3},{3,1},{5,7},{7,5},{8,10},{10,8},{12,... | collective-permute-start | bytes 4718600 | tf_op jit(solution)/shard_map/ppermute | solution.py:511
  435.1 33.1 %collective-permute-start.62 = (bf16[512,1536]{1,0:T(8,128)(2,1)S(1)}, bf16[512,1536]{1,0:T(8,128)(2,1)S(1)}, u32[]{:S(2)}, u32[]{:S(2)}) collective-permute-start(bf16[512,1536]{1,0:T(8,128)(2,1)S(1)} %add_convert_fusion.6), channel_id=1, source_target_pairs={{2,4},{4,2},{3,5},{5,3},{10,12},{12,10},{11,13},{13,11},{18,20},{2... | collective-permute-start | bytes 4718600 | tf_op jit(solution)/shard_map/ppermute | solution.py:436
  474.7 43.1 %collective-permute-start.71 = (bf16[512,1536]{1,0:T(8,128)(2,1)S(1)}, bf16[512,1536]{1,0:T(8,128)(2,1)S(1)}, u32[]{:S(2)}, u32[]{:S(2)}) collective-permute-start(bf16[512,1536]{1,0:T(8,128)(2,1)S(1)} %get-tuple-element.398), channel_id=1, source_target_pairs={{0,2},{2,0},{4,6},{6,4},{1,3},{3,1},{5,7},{7,5},{8,10},{10,8},{12,... | collective-permute-start | bytes 4718600 | tf_op jit(solution)/shard_map/ppermute | solution.py:511
  480.7 37.1 %collective-permute-start.70 = (bf16[512,1536]{1,0:T(8,128)(2,1)S(1)}, bf16[512,1536]{1,0:T(8,128)(2,1)S(1)}, u32[]{:S(2)}, u32[]{:S(2)}) collective-permute-start(bf16[512,1536]{1,0:T(8,128)(2,1)S(1)} %add_convert_fusion.4), channel_id=1, source_target_pairs={{2,4},{4,2},{3,5},{5,3},{10,12},{12,10},{11,13},{13,11},{18,20},{2... | collective-permute-start | bytes 4718600 | tf_op jit(solution)/shard_map/ppermute | solution.py:436
  482.3 35.6 %collective-permute-start.74 = (bf16[512,768]{1,0:T(8,128)(2,1)S(1)}, bf16[512,768]{1,0:T(8,128)(2,1)S(1)}, u32[]{:S(2)}, u32[]{:S(2)}) collective-permute-start(bf16[512,768]{1,0:T(8,128)(2,1)S(1)} %convolution_convert_fusion.10), channel_id=1, source_target_pairs={{0,24},{8,16},{16,8},{24,0},{1,25},{9,17},{17,9},{25,1},{2,26},{10... | collective-permute-start | bytes 2359304 | tf_op jit(solution)/shard_map/ppermute | solution.py:331
  524.1 38.8 %collective-permute-start.77 = (bf16[512,1536]{1,0:T(8,128)(2,1)}, bf16[512,1536]{1,0:T(8,128)(2,1)}, u32[]{:S(2)}, u32[]{:S(2)}) collective-permute-start(bf16[512,1536]{1,0:T(8,128)(2,1)} %add_convert_fusion.1.refs_4_), channel_id=1, source_target_pairs={{2,0},{4,6},{3,1},{5,7},{10,8},{12,14},{11,9},{13,15},{18,16},{20,... | collective-permute-start | bytes 4718600 | tf_op jit(solution)/shard_map/ppermute | solution.py:444
  528.3 34.5 %collective-permute-start.75 = (bf16[512,1536]{1,0:T(8,128)(2,1)}, bf16[512,1536]{1,0:T(8,128)(2,1)}, u32[]{:S(2)}, u32[]{:S(2)}) collective-permute-start(bf16[512,1536]{1,0:T(8,128)(2,1)} %add_convert_fusion.2), channel_id=1, source_target_pairs={{2,4},{4,2},{3,5},{5,3},{10,12},{12,10},{11,13},{13,11},{18,20},{2... | collective-permute-start | bytes 4718600 | tf_op jit(solution)/shard_map/ppermute | solution.py:436
  530.9 27.8 %collective-permute-start.76 = (bf16[256,2048]{1,0:T(8,128)(2,1)}, bf16[256,2048]{1,0:T(8,128)(2,1)S(1)}, u32[]{:S(2)}, u32[]{:S(2)}) collective-permute-start(bf16[256,2048]{1,0:T(8,128)(2,1)} %convolution_convert_fusion.9), channel_id=1, source_target_pairs={{0,2},{6,4},{1,3},{7,5},{8,10},{14,12},{9,11},{15,13},{16,18},{22,... | collective-permute-start | bytes 3145736 | tf_op jit(solution)/shard_map/ppermute | solution.py:442
  558.7 28.1 %collective-permute-start.86 = (bf16[512,768]{1,0:T(8,128)(2,1)S(1)}, bf16[512,768]{1,0:T(8,128)(2,1)S(1)}, u32[]{:S(2)}, u32[]{:S(2)}) collective-permute-start(bf16[512,768]{1,0:T(8,128)(2,1)S(1)} %copy-done.59), channel_id=1, source_target_pairs={{0,2},{6,4},{1,3},{7,5},{8,10},{14,12},{9,11},{15,13},{16,18},{22,... | collective-permute-start | bytes 2359304 | tf_op jit(solution)/shard_map/ppermute | solution.py:442
  565.1 40.5 %collective-permute-start.85 = (bf16[512,1536]{1,0:T(8,128)(2,1)S(1)}, bf16[512,1536]{1,0:T(8,128)(2,1)S(1)}, u32[]{:S(2)}, u32[]{:S(2)}) collective-permute-start(bf16[512,1536]{1,0:T(8,128)(2,1)S(1)} %add_convert_fusion.refs_6_), channel_id=1, source_target_pairs={{2,0},{4,6},{3,1},{5,7},{10,8},{12,14},{11,9},{13,15},{18,16},{20,... | collective-permute-start | bytes 4718600 | tf_op jit(solution)/shard_map/ppermute | solution.py:444
  566.9 29.0 %collective-permute-start.83 = (bf16[256,2048]{1,0:T(8,128)(2,1)S(1)}, bf16[256,2048]{1,0:T(8,128)(2,1)S(1)}, u32[]{:S(2)}, u32[]{:S(2)}) collective-permute-start(bf16[256,2048]{1,0:T(8,128)(2,1)S(1)} %add_convert_fusion.13), channel_id=1, source_target_pairs={{2,4},{4,2},{3,5},{5,3},{10,12},{12,10},{11,13},{13,11},{18,20},{2... | collective-permute-start | bytes 3145736 | tf_op jit(solution)/shard_map/ppermute | solution.py:436
  570.5 25.4 %collective-permute-start.84 = (bf16[512,768]{1,0:T(8,128)(2,1)S(1)}, bf16[512,768]{1,0:T(8,128)(2,1)S(1)}, u32[]{:S(2)}, u32[]{:S(2)}) collective-permute-start(bf16[512,768]{1,0:T(8,128)(2,1)S(1)} %copy-done.58), channel_id=1, source_target_pairs={{0,2},{6,4},{1,3},{7,5},{8,10},{14,12},{9,11},{15,13},{16,18},{22,... | collective-permute-start | bytes 2359304 | tf_op jit(solution)/shard_map/ppermute | solution.py:442
  584.5 33.6 %collective-permute-start.93 = (bf16[512,768]{1,0:T(8,128)(2,1)}, bf16[512,768]{1,0:T(8,128)(2,1)}, u32[]{:S(2)}, u32[]{:S(2)}) collective-permute-start(bf16[512,768]{1,0:T(8,128)(2,1)} %collective-permute-done.73), channel_id=1, source_target_pairs={{0,2},{6,4},{1,3},{7,5},{8,10},{14,12},{9,11},{15,13},{16,18},{22,... | collective-permute-start | bytes 2359304 | tf_op jit(solution)/shard_map/ppermute | solution.py:442
  589.7 44.9 %collective-permute-start.92 = (bf16[512,768]{1,0:T(8,128)(2,1)}, bf16[512,768]{1,0:T(8,128)(2,1)}, u32[]{:S(2)}, u32[]{:S(2)}) collective-permute-start(bf16[512,768]{1,0:T(8,128)(2,1)} %add_convert_fusion.20), channel_id=1, source_target_pairs={{2,4},{4,2},{3,5},{5,3},{10,12},{12,10},{11,13},{13,11},{18,20},{2... | collective-permute-start | bytes 2359304 | tf_op jit(solution)/shard_map/ppermute | solution.py:436
  605.6 29.0 %collective-permute-start.94 = (bf16[128,2048]{1,0:T(8,128)(2,1)}, bf16[128,2048]{1,0:T(8,128)(2,1)}, u32[]{:S(2)}, u32[]{:S(2)}) collective-permute-start(bf16[128,2048]{1,0:T(8,128)(2,1)} %add_convert_fusion.22), channel_id=1, source_target_pairs={{0,16},{8,24},{16,0},{24,8},{1,17},{9,25},{17,1},{25,9},{2,18},{10... | collective-permute-start | bytes 1572872 | tf_op jit(solution)/shard_map/ppermute | solution.py:331
  607.9 31.9 %collective-permute-start.91 = (bf16[256,2048]{1,0:T(8,128)(2,1)}, bf16[256,2048]{1,0:T(8,128)(2,1)}, u32[]{:S(2)}, u32[]{:S(2)}) collective-permute-start(bf16[256,2048]{1,0:T(8,128)(2,1)} %add_convert_fusion.12), channel_id=1, source_target_pairs={{2,0},{4,6},{3,1},{5,7},{10,8},{12,14},{11,9},{13,15},{18,16},{20,... | collective-permute-start | bytes 3145736 | tf_op jit(solution)/shard_map/ppermute | solution.py:444
  609.9 30.0 %collective-permute-start.90 = (bf16[520,768]{1,0:T(8,128)(2,1)}, bf16[520,768]{1,0:T(8,128)(2,1)}, u32[]{:S(2)}, u32[]{:S(2)}) collective-permute-start(bf16[520,768]{1,0:T(8,128)(2,1)} %constant_dynamic-update-slice_fusion.26), channel_id=1, source_target_pairs={{0,2},{6,4},{1,3},{7,5},{8,10},{14,12},{9,11},{15,13},{16,18},{22,... | collective-permute-start | bytes 2396168 | tf_op jit(solution)/shard_map/ppermute | solution.py:442
  618.2 21.7 %collective-permute-start.89 = (bf16[512,768]{1,0:T(8,128)(2,1)}, bf16[512,768]{1,0:T(8,128)(2,1)}, u32[]{:S(2)}, u32[]{:S(2)}) collective-permute-start(bf16[512,768]{1,0:T(8,128)(2,1)} %add_convert_fusion.21), channel_id=1, source_target_pairs={{2,4},{4,2},{3,5},{5,3},{10,12},{12,10},{11,13},{13,11},{18,20},{2... | collective-permute-start | bytes 2359304 | tf_op jit(solution)/shard_map/ppermute | solution.py:436
  641.4 73.0 %collective-permute-start.98 = (bf16[512,768]{1,0:T(8,128)(2,1)S(1)}, bf16[512,768]{1,0:T(8,128)(2,1)S(1)}, u32[]{:S(2)}, u32[]{:S(2)}) collective-permute-start(bf16[512,768]{1,0:T(8,128)(2,1)S(1)} %add_convert_fusion.19.refs_2_), channel_id=1, source_target_pairs={{2,0},{4,6},{3,1},{5,7},{10,8},{12,14},{11,9},{13,15},{18,16},{20,... | collective-permute-start | bytes 2359304 | tf_op jit(solution)/shard_map/ppermute | solution.py:444
  644.1 70.3 %collective-permute-start.97 = (bf16[520,768]{1,0:T(8,128)(2,1)S(1)}, bf16[520,768]{1,0:T(8,128)(2,1)S(1)}, u32[]{:S(2)}, u32[]{:S(2)}) collective-permute-start(bf16[520,768]{1,0:T(8,128)(2,1)S(1)} %add_convert_fusion.15), channel_id=1, source_target_pairs={{2,4},{4,2},{3,5},{5,3},{10,12},{12,10},{11,13},{13,11},{18,20},{2... | collective-permute-start | bytes 2396168 | tf_op jit(solution)/shard_map/ppermute | solution.py:436
  654.5 60.8 %collective-permute-start.99 = (bf16[512,768]{1,0:T(8,128)(2,1)S(1)}, bf16[512,768]{1,0:T(8,128)(2,1)S(1)}, u32[]{:S(2)}, u32[]{:S(2)}) collective-permute-start(bf16[512,768]{1,0:T(8,128)(2,1)S(1)} %add_convert_fusion.16.refs_4_), channel_id=1, source_target_pairs={{2,0},{4,6},{3,1},{5,7},{10,8},{12,14},{11,9},{13,15},{18,16},{20,... | collective-permute-start | bytes 2359304 | tf_op jit(solution)/shard_map/ppermute | solution.py:444
  655.8 52.2 %collective-permute-start.100 = (bf16[128,2048]{1,0:T(8,128)(2,1)S(1)}, bf16[128,2048]{1,0:T(8,128)(2,1)S(1)}, u32[]{:S(2)}, u32[]{:S(2)}) collective-permute-start(bf16[128,2048]{1,0:T(8,128)(2,1)S(1)} %copy-done.67), channel_id=1, source_target_pairs={{0,0},{2,8},{4,16},{6,24},{8,2},{10,10},{12,18},{14,26},{16,4},{18... | collective-permute-start | bytes 1572872 | tf_op jit(solution)/shard_map/ppermute | solution.py:344
  681.5 32.9 %collective-permute-start.101 = (bf16[128,2048]{1,0:T(8,128)(2,1)}, bf16[128,2048]{1,0:T(8,128)(2,1)S(1)}, u32[]{:S(2)}, u32[]{:S(2)}) collective-permute-start(bf16[128,2048]{1,0:T(8,128)(2,1)} %collective-permute-done.94), channel_id=1, source_target_pairs={{0,4},{2,12},{4,20},{6,28},{8,6},{10,14},{12,22},{14,30},{16,0},{1... | collective-permute-start | bytes 1572872 | tf_op jit(solution)/shard_map/ppermute | solution.py:344
  (138 other events, 1890.6 us)

commit v7 on v6

--- a/solution.py
+++ b/solution.py
@@ -528,7 +528,7 @@
 
 
 def place_columns(pairs, widths):
-    size, rows, block = lax.axis_size("fsdp"), pairs[0][0].shape[0], 128
+    size, rows, block = lax.axis_size("fsdp"), pairs[0][0].shape[0], 256
     scalars = jnp.stack([lax.axis_index("fsdp"), at_inner().astype(jnp.int32)])
 
     def kernel(scalars, *refs):

time: 750 us -> 748 us (level)
  no operation moved by 1% of the time
where the time goes in v7:
time: 748 us; the launch traced here: 740 us
  waiting for transfers between devices  268 us (36%)
  starting transfers between devices  195 us (26%)
  other arithmetic  113 us (15%)
  matrix products  90.4 us (12%)
  local copies, waits for them, and re-layouts  55.1 us (7%)
  Pallas kernels  14.7 us (2%)
    ppermute x44, waiting for transfers between devices, swap_plane(): return lax.ppermute(value, 'fsdp', xor_pairs(fsdp_size, fsdp_mask))  85.5 us
    ppermute x9, starting transfers between devices, send(): sent.append(([(0, name, part)], lax.ppermute(part, 'ctx', INWARD)))  59.2 us
    ppermute x44, starting transfers between devices, swap_plane(): return lax.ppermute(value, 'fsdp', xor_pairs(fsdp_size, fsdp_mask))  53.8 us
    ppermute x16, waiting for transfers between devices, swap_plane(): return lax.ppermute(value, 'tp', xor_pairs(tp_size, tp_mask))  43.6 us
    ppermute x6, waiting for transfers between devices, swap_ctx(): return lax.ppermute(value, 'ctx', xor_pairs(lax.axis_size('ctx'), 1))  39.2 us
    convert_element_type x20, other arithmetic, send(): (here.astype(jnp.float32) + came.astype(jnp.float32)).astype(jnp.bfloat16)  36.1 us
    ppermute x5, starting transfers between devices, swap_ranks(): return lax.ppermute(value, ('fsdp', 'ctx'), pairs)  35.9 us
    ppermute x9, waiting for transfers between devices, send(): sent.append(([(0, name, part)], lax.ppermute(part, 'ctx', INWARD)))  35 us
  transfers between devices with their start and end apart: 103, of which 45 were waited for; matrix products, arithmetic and copies ran while one was open for 28% of the time, Pallas kernels for 1%

profile of v7, /device:TPU:1, one launch (start us, length us, event | category | flops | bytes accessed | tf_op | source)
XLA Modules:
  0.0 740.5 jit_solution(15525543797898067137)
XLA Ops:
  50.1 4.7 collective-permute-done.6
  54.8 8.4 %collective-permute-done.7 = bf16[256,768]{1,0:T(8,128)(2,1)S(1)} collective-permute-done((bf16[256,768]{1,0:T(8,128)(2,1)}, bf16[256,768]{1,0:T(8,128)(2,1)S(1)}, u32[]{:S(2)}, u32[]{:S(2)}) %collective-permute-start.7) | collective-permute-done | bytes 393248 | tf_op jit(solution)/shard_map/ppermute | solution.py:511
  83.4 7.0 fusion.123
  92.4 18.0 %collective-permute-done.16 = bf16[256,1536]{1,0:T(8,128)(2,1)S(1)} collective-permute-done((bf16[256,1536]{1,0:T(8,128)(2,1)S(1)}, bf16[256,1536]{1,0:T(8,128)(2,1)S(1)}, u32[]{:S(2)}, u32[]{:S(2)}) %collective-permute-start.16) | collective-permute-done | bytes 786464 | tf_op jit(solution)/shard_map/ppermute | solution.py:331
  117.9 9.4 %collective-permute-done.18 = bf16[256,1536]{1,0:T(8,128)(2,1)S(1)} collective-permute-done((bf16[256,1536]{1,0:T(8,128)(2,1)S(1)}, bf16[256,1536]{1,0:T(8,128)(2,1)S(1)}, u32[]{:S(2)}, u32[]{:S(2)}) %collective-permute-start.18) | collective-permute-done | bytes 786464 | tf_op jit(solution)/shard_map/ppermute | solution.py:331
  139.9 14.9 %collective-permute-done.23 = bf16[256,1536]{1,0:T(8,128)(2,1)S(1)} collective-permute-done((bf16[256,1536]{1,0:T(8,128)(2,1)S(1)}, bf16[256,1536]{1,0:T(8,128)(2,1)S(1)}, u32[]{:S(2)}, u32[]{:S(2)}) %collective-permute-start.23) | collective-permute-done | bytes 786464 | tf_op jit(solution)/shard_map/ppermute | solution.py:511
  162.7 3.9 collective-permute-done.24
  174.9 6.3 collective-permute-done.30
  181.7 3.9 collective-permute-start.31
  188.0 5.6 collective-permute-done.35
  194.3 4.9 collective-permute-done.32
  204.9 6.6 fusion.124
  211.6 4.7 multiply_convert_fusion.1
  230.1 5.0 fusion.121
  240.0 9.4 %collective-permute-done.42 = bf16[128,2048]{1,0:T(8,128)(2,1)} collective-permute-done((bf16[128,2048]{1,0:T(8,128)(2,1)}, bf16[128,2048]{1,0:T(8,128)(2,1)}, u32[]{:S(2)}, u32[]{:S(2)}) %collective-permute-start.42) | collective-permute-done | bytes 524320 | tf_op jit(solution)/shard_map/ppermute | solution.py:333
  285.4 4.6 collective-permute-done.50
  305.9 18.0 %collective-permute-start.54 = (bf16[512,1536]{1,0:T(8,128)(2,1)}, bf16[512,1536]{1,0:T(8,128)(2,1)}, u32[]{:S(2)}, u32[]{:S(2)}) collective-permute-start(bf16[512,1536]{1,0:T(8,128)(2,1)} %convolution_convert_fusion.7), channel_id=1, source_target_pairs={{0,2},{6,4},{1,3},{7,5},{8,10},{14,12},{9,11},{15,13},{16,18},{22,... | collective-permute-start | bytes 4718600 | tf_op jit(solution)/shard_map/ppermute | solution.py:442
  325.1 5.7 fusion.6
  339.4 4.7 convolution_convert_fusion.9
  344.2 5.5 fusion.2
  350.7 5.5 collective-permute-done.54
  363.0 3.8 add_convert_fusion.7
  373.5 8.0 %collective-permute-start.59 = (bf16[512,1536]{1,0:T(8,128)(2,1)}, bf16[512,1536]{1,0:T(8,128)(2,1)}, u32[]{:S(2)}, u32[]{:S(2)}) collective-permute-start(bf16[512,1536]{1,0:T(8,128)(2,1)} %collective-permute-done.52), channel_id=1, source_target_pairs={{0,2},{6,4},{1,3},{7,5},{8,10},{14,12},{9,11},{15,13},{16,18},{22,... | collective-permute-start | bytes 4718600 | tf_op jit(solution)/shard_map/ppermute | solution.py:442
  403.6 8.6 %collective-permute-done.59 = bf16[512,1536]{1,0:T(8,128)(2,1)} collective-permute-done((bf16[512,1536]{1,0:T(8,128)(2,1)}, bf16[512,1536]{1,0:T(8,128)(2,1)}, u32[]{:S(2)}, u32[]{:S(2)}) %collective-permute-start.59) | collective-permute-done | bytes 1572896 | tf_op jit(solution)/shard_map/ppermute | solution.py:442
  412.2 7.8 %collective-permute-done.61 = bf16[512,1536]{1,0:T(8,128)(2,1)} collective-permute-done((bf16[512,1536]{1,0:T(8,128)(2,1)}, bf16[512,1536]{1,0:T(8,128)(2,1)}, u32[]{:S(2)}, u32[]{:S(2)}) %collective-permute-start.61) | collective-permute-done | bytes 1572896 | tf_op jit(solution)/shard_map/ppermute | solution.py:331
  420.0 5.1 convolution_convert_fusion.3
  428.6 4.2 broadcast_select_fusion.3
  436.3 4.4 fusion.122
  445.1 8.8 %collective-permute-done.66 = bf16[128,2048]{1,0:T(8,128)(2,1)S(1)} collective-permute-done((bf16[128,2048]{1,0:T(8,128)(2,1)S(1)}, bf16[128,2048]{1,0:T(8,128)(2,1)S(1)}, u32[]{:S(2)}, u32[]{:S(2)}) %collective-permute-start.66) | collective-permute-done | bytes 524320 | tf_op jit(solution)/shard_map/ppermute | solution.py:333
  458.4 9.8 %collective-permute-done.63.refs_1_ = bf16[512,1536]{1,0:T(8,128)(2,1)S(1)} collective-permute-done((bf16[512,1536]{1,0:T(8,128)(2,1)S(1)}, bf16[512,1536]{1,0:T(8,128)(2,1)S(1)}, u32[]{:S(2)}, u32[]{:S(2)}) %collective-permute-start.63) | collective-permute-done | bytes 1572896 | tf_op jit(solution)/shard_map/ppermute | solution.py:511
  474.7 4.2 collective-permute-start.71
  489.4 11.3 %collective-permute-done.73 = bf16[512,768]{1,0:T(8,128)(2,1)} collective-permute-done((bf16[512,768]{1,0:T(8,128)(2,1)S(1)}, bf16[512,768]{1,0:T(8,128)(2,1)}, u32[]{:S(2)}, u32[]{:S(2)}) %collective-permute-start.73) | collective-permute-done | bytes 786464 | tf_op jit(solution)/shard_map/ppermute | solution.py:331
  500.6 17.2 %collective-permute-done.74 = bf16[512,768]{1,0:T(8,128)(2,1)S(1)} collective-permute-done((bf16[512,768]{1,0:T(8,128)(2,1)S(1)}, bf16[512,768]{1,0:T(8,128)(2,1)S(1)}, u32[]{:S(2)}, u32[]{:S(2)}) %collective-permute-start.74) | collective-permute-done | bytes 786464 | tf_op jit(solution)/shard_map/ppermute | solution.py:331
  530.9 5.8 collective-permute-start.76
  546.0 12.6 %collective-permute-done.76 = bf16[256,2048]{1,0:T(8,128)(2,1)S(1)} collective-permute-done((bf16[256,2048]{1,0:T(8,128)(2,1)}, bf16[256,2048]{1,0:T(8,128)(2,1)S(1)}, u32[]{:S(2)}, u32[]{:S(2)}) %collective-permute-start.76) | collective-permute-done | bytes 1048608 | tf_op jit(solution)/shard_map/ppermute | solution.py:442
  558.7 4.1 collective-permute-start.86
  570.5 10.2 %collective-permute-start.84 = (bf16[512,768]{1,0:T(8,128)(2,1)S(1)}, bf16[512,768]{1,0:T(8,128)(2,1)S(1)}, u32[]{:S(2)}, u32[]{:S(2)}) collective-permute-start(bf16[512,768]{1,0:T(8,128)(2,1)S(1)} %copy-done.58), channel_id=1, source_target_pairs={{0,2},{6,4},{1,3},{7,5},{8,10},{14,12},{9,11},{15,13},{16,18},{22,... | collective-permute-start | bytes 2359304 | tf_op jit(solution)/shard_map/ppermute | solution.py:442
  591.3 4.6 collective-permute-done.84
  595.9 9.7 %collective-permute-done.85.refs_7_ = bf16[512,1536]{1,0:T(8,128)(2,1)S(1)} collective-permute-done((bf16[512,1536]{1,0:T(8,128)(2,1)S(1)}, bf16[512,1536]{1,0:T(8,128)(2,1)S(1)}, u32[]{:S(2)}, u32[]{:S(2)}) %collective-permute-start.85) | collective-permute-done | bytes 1572896 | tf_op jit(solution)/shard_map/ppermute | solution.py:444
  609.9 5.8 collective-permute-start.90
  619.7 4.9 maximum_convert_fusion
  624.6 9.2 %shard_map.254 = (f32[512,3072]{1,0:T(8,128)}, f32[512,3072]{1,0:T(8,128)}) custom-call(s32[2]{0:T(128)} %pad_add_fusion.scalars, bf16[512,1536]{1,0:T(8,128)(2,1)} %get-tuple-element.340.refs_0_, bf16[512,1536]{1,0:T(8,128)(2,1)} %copy-done.11, bf16[512,1536]{1,0:T(8,128)(2,1)} %get-tuple-element.341.refs_2_, bf16[512,1536]{1,0:T(8,128)(2,1)} %copy-done.12, ...), custom_call_target="tpu_custom_call" | custom-call | bytes 25165824 | tf_op jit(solution)/shard_map/pallas_call | solution.py:548
  646.9 6.5 collective-permute-done.96.refs_1_
  655.0 25.7 %collective-permute-start.100 = (bf16[128,2048]{1,0:T(8,128)(2,1)S(1)}, bf16[128,2048]{1,0:T(8,128)(2,1)S(1)}, u32[]{:S(2)}, u32[]{:S(2)}) collective-permute-start(bf16[128,2048]{1,0:T(8,128)(2,1)S(1)} %copy-done.67), channel_id=1, source_target_pairs={{0,0},{2,8},{4,16},{6,24},{8,2},{10,10},{12,18},{14,26},{16,4},{18... | collective-permute-start | bytes 1572872 | tf_op jit(solution)/shard_map/ppermute | solution.py:344
  680.8 26.4 %collective-permute-done.100 = bf16[128,2048]{1,0:T(8,128)(2,1)S(1)} collective-permute-done((bf16[128,2048]{1,0:T(8,128)(2,1)S(1)}, bf16[128,2048]{1,0:T(8,128)(2,1)S(1)}, u32[]{:S(2)}, u32[]{:S(2)}) %collective-permute-start.100) | collective-permute-done | bytes 524320 | tf_op jit(solution)/shard_map/ppermute | solution.py:344
  707.3 6.4 collective-permute-done.101
  716.0 11.9 %collective-permute-done.102 = bf16[520,768]{1,0:T(8,128)(2,1)S(1)} collective-permute-done((bf16[520,768]{1,0:T(8,128)(2,1)S(1)}, bf16[520,768]{1,0:T(8,128)(2,1)S(1)}, u32[]{:S(2)}, u32[]{:S(2)}) %collective-permute-start.102) | collective-permute-done | bytes 798752 | tf_op jit(solution)/shard_map/ppermute | solution.py:444
  731.0 5.5 shard_map.255
  (559 shorter events, 336.2 us)
Async XLA Ops:
  4.4 35.1 %collective-permute-start.2 = (bf16[256,768]{1,0:T(8,128)(2,1)}, bf16[256,768]{1,0:T(8,128)(2,1)}, u32[]{:S(2)}, u32[]{:S(2)}) collective-permute-start(bf16[256,768]{1,0:T(8,128)(2,1)} %pad_maximum_fusion.27), channel_id=1, source_target_pairs={{0,24},{8,16},{16,8},{24,0},{1,25},{9,17},{17,9},{25,1},{2,26},{10... | collective-permute-start | bytes 1179656 | tf_op jit(solution)/shard_map/ppermute | solution.py:331
  7.9 31.6 %collective-permute-start.1 = (bf16[256,768]{1,0:T(8,128)(2,1)}, bf16[256,768]{1,0:T(8,128)(2,1)}, u32[]{:S(2)}, u32[]{:S(2)}) collective-permute-start(bf16[256,768]{1,0:T(8,128)(2,1)} %pad_maximum_fusion.26), channel_id=1, source_target_pairs={{0,16},{8,24},{16,0},{24,8},{1,17},{9,25},{17,1},{25,9},{2,18},{10... | collective-permute-start | bytes 1179656 | tf_op jit(solution)/shard_map/ppermute | solution.py:331
  7.9 31.6 %collective-permute-start = (bf16[128,2048]{1,0:T(8,128)(2,1)}, bf16[128,2048]{1,0:T(8,128)(2,1)}, u32[]{:S(2)}, u32[]{:S(2)}) collective-permute-start(bf16[128,2048]{1,0:T(8,128)(2,1)} %param.15), channel_id=1, source_target_pairs={{0,0},{2,8},{4,16},{6,24},{8,2},{10,10},{12,18},{14,26},{16,4},{18... | collective-permute-start | bytes 1572872 | tf_op jit(solution)/shard_map/ppermute | solution.py:344
  17.3 30.4 %collective-permute-start.8 = (bf16[512,768]{1,0:T(8,128)(2,1)}, bf16[512,768]{1,0:T(8,128)(2,1)}, u32[]{:S(2)}, u32[]{:S(2)}) collective-permute-start(bf16[512,768]{1,0:T(8,128)(2,1)} %pad_maximum_fusion.10), channel_id=1, source_target_pairs={{0,8},{8,0},{16,24},{24,16},{1,9},{9,1},{17,25},{25,17},{2,10},{10... | collective-permute-start | bytes 2359304 | tf_op jit(solution)/shard_map/ppermute | solution.py:331
  42.0 21.2 %collective-permute-start.4 = (bf16[128,2048]{1,0:T(8,128)(2,1)S(1)}, bf16[128,2048]{1,0:T(8,128)(2,1)S(1)}, u32[]{:S(2)}, u32[]{:S(2)}) collective-permute-start(bf16[128,2048]{1,0:T(8,128)(2,1)S(1)} %fusion.23), channel_id=1, source_target_pairs={{0,1},{1,0},{2,3},{3,2},{4,5},{5,4},{6,7},{7,6},{8,9},{9,8},{10,11... | collective-permute-start | bytes 1572872 | tf_op jit(solution)/shard_map/ppermute | solution.py:333
  79.6 30.9 %collective-permute-start.16 = (bf16[256,1536]{1,0:T(8,128)(2,1)S(1)}, bf16[256,1536]{1,0:T(8,128)(2,1)S(1)}, u32[]{:S(2)}, u32[]{:S(2)}) collective-permute-start(bf16[256,1536]{1,0:T(8,128)(2,1)S(1)} %copy-done.54), channel_id=1, source_target_pairs={{0,16},{8,24},{16,0},{24,8},{1,17},{9,25},{17,1},{25,9},{2,18},{10... | collective-permute-start | bytes 2359304 | tf_op jit(solution)/shard_map/ppermute | solution.py:331
  83.1 44.2 %collective-permute-start.18 = (bf16[256,1536]{1,0:T(8,128)(2,1)S(1)}, bf16[256,1536]{1,0:T(8,128)(2,1)S(1)}, u32[]{:S(2)}, u32[]{:S(2)}) collective-permute-start(bf16[256,1536]{1,0:T(8,128)(2,1)S(1)} %copy-done.53), channel_id=1, source_target_pairs={{0,24},{8,16},{16,8},{24,0},{1,25},{9,17},{17,9},{25,1},{2,26},{10... | collective-permute-start | bytes 2359304 | tf_op jit(solution)/shard_map/ppermute | solution.py:331
  134.2 28.4 %collective-permute-start.26 = (bf16[128,2048]{1,0:T(8,128)(2,1)S(1)}, bf16[128,2048]{1,0:T(8,128)(2,1)S(1)}, u32[]{:S(2)}, u32[]{:S(2)}) collective-permute-start(bf16[128,2048]{1,0:T(8,128)(2,1)S(1)} %fusion.50), channel_id=1, source_target_pairs={{0,1},{1,0},{2,3},{3,2},{4,5},{5,4},{6,7},{7,6},{8,9},{9,8},{10,11... | collective-permute-start | bytes 1572872 | tf_op jit(solution)/shard_map/ppermute | solution.py:333
  134.5 28.2 %collective-permute-start.27 = (bf16[128,2048]{1,0:T(8,128)(2,1)S(1)}, bf16[128,2048]{1,0:T(8,128)(2,1)S(1)}, u32[]{:S(2)}, u32[]{:S(2)}) collective-permute-start(bf16[128,2048]{1,0:T(8,128)(2,1)S(1)} %fusion.50), channel_id=1, source_target_pairs={{0,16},{8,24},{16,0},{24,8},{1,17},{9,25},{17,1},{25,9},{2,18},{10... | collective-permute-start | bytes 1572872 | tf_op jit(solution)/shard_map/ppermute | solution.py:331
  171.6 28.6 %collective-permute-start.34 = (bf16[384,2048]{1,0:T(8,128)(2,1)S(1)}, bf16[384,2048]{1,0:T(8,128)(2,1)S(1)}, u32[]{:S(2)}, u32[]{:S(2)}) collective-permute-start(bf16[384,2048]{1,0:T(8,128)(2,1)S(1)} %constant_dynamic-update-slice_fusion.11), channel_id=1, source_target_pairs={{0,8},{8,0},{16,24},{24,16},{1,9},{9,1},{17,25},{25,17},{2,10},{10... | collective-permute-start | bytes 4718600 | tf_op jit(solution)/shard_map/ppermute | solution.py:331
  226.2 35.9 %collective-permute-start.39 = (bf16[384,2048]{1,0:T(8,128)(2,1)}, bf16[384,2048]{1,0:T(8,128)(2,1)}, u32[]{:S(2)}, u32[]{:S(2)}) collective-permute-start(bf16[384,2048]{1,0:T(8,128)(2,1)} %get-tuple-element.259), channel_id=1, source_target_pairs={{0,2},{6,4},{1,3},{7,5},{8,10},{14,12},{9,11},{15,13},{16,18},{22,... | collective-permute-start | bytes 4718600 | tf_op jit(solution)/shard_map/ppermute | solution.py:442
  256.3 40.7 %collective-permute-start.46 = (bf16[384,2048]{1,0:T(8,128)(2,1)S(1)}, bf16[384,2048]{1,0:T(8,128)(2,1)S(1)}, u32[]{:S(2)}, u32[]{:S(2)}) collective-permute-start(bf16[384,2048]{1,0:T(8,128)(2,1)S(1)} %copy-done.14), channel_id=1, source_target_pairs={{0,2},{6,4},{1,3},{7,5},{8,10},{14,12},{9,11},{15,13},{16,18},{22,... | collective-permute-start | bytes 4718600 | tf_op jit(solution)/shard_map/ppermute | solution.py:442
  266.6 30.4 %collective-permute-start.52 = (bf16[512,1536]{1,0:T(8,128)(2,1)S(1)}, bf16[512,1536]{1,0:T(8,128)(2,1)}, u32[]{:S(2)}, u32[]{:S(2)}) collective-permute-start(bf16[512,1536]{1,0:T(8,128)(2,1)S(1)} %convolution_convert_fusion.6), channel_id=1, source_target_pairs={{0,8},{8,0},{16,24},{24,16},{1,9},{9,1},{17,25},{25,17},{2,10},{10... | collective-permute-start | bytes 4718600 | tf_op jit(solution)/shard_map/ppermute | solution.py:331
  272.1 24.9 %collective-permute-start.45 = (bf16[384,2048]{1,0:T(8,128)(2,1)S(1)}, bf16[384,2048]{1,0:T(8,128)(2,1)S(1)}, u32[]{:S(2)}, u32[]{:S(2)}) collective-permute-start(bf16[384,2048]{1,0:T(8,128)(2,1)S(1)} %add_convert_fusion.11), channel_id=1, source_target_pairs={{2,4},{4,2},{3,5},{5,3},{10,12},{12,10},{11,13},{13,11},{18,20},{2... | collective-permute-start | bytes 4718600 | tf_op jit(solution)/shard_map/ppermute | solution.py:436
  275.5 21.5 %collective-permute-start.49 = (bf16[384,2048]{1,0:T(8,128)(2,1)S(1)}, bf16[384,2048]{1,0:T(8,128)(2,1)S(1)}, u32[]{:S(2)}, u32[]{:S(2)}) collective-permute-start(bf16[384,2048]{1,0:T(8,128)(2,1)S(1)} %pad_maximum_fusion.3), channel_id=1, source_target_pairs={{0,8},{8,0},{16,24},{24,16},{1,9},{9,1},{17,25},{25,17},{2,10},{10... | collective-permute-start | bytes 4718600 | tf_op jit(solution)/shard_map/ppermute | solution.py:331
  297.2 33.7 %collective-permute-start.56 = (bf16[128,2048]{1,0:T(8,128)(2,1)S(1)}, bf16[128,2048]{1,0:T(8,128)(2,1)S(1)}, u32[]{:S(2)}, u32[]{:S(2)}) collective-permute-start(bf16[128,2048]{1,0:T(8,128)(2,1)S(1)} %pad_maximum_fusion.20), channel_id=1, source_target_pairs={{0,8},{8,0},{16,24},{24,16},{1,9},{9,1},{17,25},{25,17},{2,10},{10... | collective-permute-start | bytes 1572872 | tf_op jit(solution)/shard_map/ppermute | solution.py:331
  300.8 49.9 %collective-permute-start.55 = (bf16[384,2048]{1,0:T(8,128)(2,1)}, bf16[384,2048]{1,0:T(8,128)(2,1)}, u32[]{:S(2)}, u32[]{:S(2)}) collective-permute-start(bf16[384,2048]{1,0:T(8,128)(2,1)} %add_convert_fusion.9), channel_id=1, source_target_pairs={{2,0},{4,6},{3,1},{5,7},{10,8},{12,14},{11,9},{13,15},{18,16},{20,... | collective-permute-start | bytes 4718600 | tf_op jit(solution)/shard_map/ppermute | solution.py:444
  304.1 46.6 %collective-permute-start.53 = (bf16[384,2048]{1,0:T(8,128)(2,1)}, bf16[384,2048]{1,0:T(8,128)(2,1)}, u32[]{:S(2)}, u32[]{:S(2)}) collective-permute-start(bf16[384,2048]{1,0:T(8,128)(2,1)} %add_convert_fusion.10), channel_id=1, source_target_pairs={{2,4},{4,2},{3,5},{5,3},{10,12},{12,10},{11,13},{13,11},{18,20},{2... | collective-permute-start | bytes 4718600 | tf_op jit(solution)/shard_map/ppermute | solution.py:436
  305.9 50.4 %collective-permute-start.54 = (bf16[512,1536]{1,0:T(8,128)(2,1)}, bf16[512,1536]{1,0:T(8,128)(2,1)}, u32[]{:S(2)}, u32[]{:S(2)}) collective-permute-start(bf16[512,1536]{1,0:T(8,128)(2,1)} %convolution_convert_fusion.7), channel_id=1, source_target_pairs={{0,2},{6,4},{1,3},{7,5},{8,10},{14,12},{9,11},{15,13},{16,18},{22,... | collective-permute-start | bytes 4718600 | tf_op jit(solution)/shard_map/ppermute | solution.py:442
  323.9 35.8 %collective-permute-start.57 = (bf16[512,1536]{1,0:T(8,128)(2,1)}, bf16[512,1536]{1,0:T(8,128)(2,1)}, u32[]{:S(2)}, u32[]{:S(2)}) collective-permute-start(bf16[512,1536]{1,0:T(8,128)(2,1)} %convolution_convert_fusion.5), channel_id=1, source_target_pairs={{0,16},{8,24},{16,0},{24,8},{1,17},{9,25},{17,1},{25,9},{2,18},{10... | collective-permute-start | bytes 4718600 | tf_op jit(solution)/shard_map/ppermute | solution.py:331
  366.8 36.9 %collective-permute-start.60 = (bf16[384,2048]{1,0:T(8,128)(2,1)}, bf16[384,2048]{1,0:T(8,128)(2,1)}, u32[]{:S(2)}, u32[]{:S(2)}) collective-permute-start(bf16[384,2048]{1,0:T(8,128)(2,1)} %add_convert_fusion.7), channel_id=1, source_target_pairs={{2,0},{4,6},{3,1},{5,7},{10,8},{12,14},{11,9},{13,15},{18,16},{20,... | collective-permute-start | bytes 4718600 | tf_op jit(solution)/shard_map/ppermute | solution.py:444
  371.6 32.0 %collective-permute-start.58 = (bf16[512,1536]{1,0:T(8,128)(2,1)}, bf16[512,1536]{1,0:T(8,128)(2,1)}, u32[]{:S(2)}, u32[]{:S(2)}) collective-permute-start(bf16[512,1536]{1,0:T(8,128)(2,1)} %add_convert_fusion.8), channel_id=1, source_target_pairs={{2,4},{4,2},{3,5},{5,3},{10,12},{12,10},{11,13},{13,11},{18,20},{2... | collective-permute-start | bytes 4718600 | tf_op jit(solution)/shard_map/ppermute | solution.py:436
  373.5 38.7 %collective-permute-start.59 = (bf16[512,1536]{1,0:T(8,128)(2,1)}, bf16[512,1536]{1,0:T(8,128)(2,1)}, u32[]{:S(2)}, u32[]{:S(2)}) collective-permute-start(bf16[512,1536]{1,0:T(8,128)(2,1)} %collective-permute-done.52), channel_id=1, source_target_pairs={{0,2},{6,4},{1,3},{7,5},{8,10},{14,12},{9,11},{15,13},{16,18},{22,... | collective-permute-start | bytes 4718600 | tf_op jit(solution)/shard_map/ppermute | solution.py:442
  381.5 38.5 %collective-permute-start.61 = (bf16[512,1536]{1,0:T(8,128)(2,1)}, bf16[512,1536]{1,0:T(8,128)(2,1)}, u32[]{:S(2)}, u32[]{:S(2)}) collective-permute-start(bf16[512,1536]{1,0:T(8,128)(2,1)} %convolution_convert_fusion.4), channel_id=1, source_target_pairs={{0,24},{8,16},{16,8},{24,0},{1,25},{9,17},{17,9},{25,1},{2,26},{10... | collective-permute-start | bytes 4718600 | tf_op jit(solution)/shard_map/ppermute | solution.py:331
  428.5 29.9 %collective-permute-start.69 = (bf16[512,768]{1,0:T(8,128)(2,1)S(1)}, bf16[512,768]{1,0:T(8,128)(2,1)S(1)}, u32[]{:S(2)}, u32[]{:S(2)}) collective-permute-start(bf16[512,768]{1,0:T(8,128)(2,1)S(1)} %convolution_convert_fusion.12), channel_id=1, source_target_pairs={{0,8},{8,0},{16,24},{24,16},{1,9},{9,1},{17,25},{25,17},{2,10},{10... | collective-permute-start | bytes 2359304 | tf_op jit(solution)/shard_map/ppermute | solution.py:331
  432.7 35.5 %collective-permute-start.63 = (bf16[512,1536]{1,0:T(8,128)(2,1)S(1)}, bf16[512,1536]{1,0:T(8,128)(2,1)S(1)}, u32[]{:S(2)}, u32[]{:S(2)}) collective-permute-start(bf16[512,1536]{1,0:T(8,128)(2,1)S(1)} %get-tuple-element.400), channel_id=1, source_target_pairs={{0,2},{2,0},{4,6},{6,4},{1,3},{3,1},{5,7},{7,5},{8,10},{10,8},{12,... | collective-permute-start | bytes 4718600 | tf_op jit(solution)/shard_map/ppermute | solution.py:511
  435.1 33.1 %collective-permute-start.62 = (bf16[512,1536]{1,0:T(8,128)(2,1)S(1)}, bf16[512,1536]{1,0:T(8,128)(2,1)S(1)}, u32[]{:S(2)}, u32[]{:S(2)}) collective-permute-start(bf16[512,1536]{1,0:T(8,128)(2,1)S(1)} %add_convert_fusion.6), channel_id=1, source_target_pairs={{2,4},{4,2},{3,5},{5,3},{10,12},{12,10},{11,13},{13,11},{18,20},{2... | collective-permute-start | bytes 4718600 | tf_op jit(solution)/shard_map/ppermute | solution.py:436
  474.7 43.1 %collective-permute-start.71 = (bf16[512,1536]{1,0:T(8,128)(2,1)S(1)}, bf16[512,1536]{1,0:T(8,128)(2,1)S(1)}, u32[]{:S(2)}, u32[]{:S(2)}) collective-permute-start(bf16[512,1536]{1,0:T(8,128)(2,1)S(1)} %get-tuple-element.398), channel_id=1, source_target_pairs={{0,2},{2,0},{4,6},{6,4},{1,3},{3,1},{5,7},{7,5},{8,10},{10,8},{12,... | collective-permute-start | bytes 4718600 | tf_op jit(solution)/shard_map/ppermute | solution.py:511
  480.7 37.1 %collective-permute-start.70 = (bf16[512,1536]{1,0:T(8,128)(2,1)S(1)}, bf16[512,1536]{1,0:T(8,128)(2,1)S(1)}, u32[]{:S(2)}, u32[]{:S(2)}) collective-permute-start(bf16[512,1536]{1,0:T(8,128)(2,1)S(1)} %add_convert_fusion.4), channel_id=1, source_target_pairs={{2,4},{4,2},{3,5},{5,3},{10,12},{12,10},{11,13},{13,11},{18,20},{2... | collective-permute-start | bytes 4718600 | tf_op jit(solution)/shard_map/ppermute | solution.py:436
  482.3 35.6 %collective-permute-start.74 = (bf16[512,768]{1,0:T(8,128)(2,1)S(1)}, bf16[512,768]{1,0:T(8,128)(2,1)S(1)}, u32[]{:S(2)}, u32[]{:S(2)}) collective-permute-start(bf16[512,768]{1,0:T(8,128)(2,1)S(1)} %convolution_convert_fusion.10), channel_id=1, source_target_pairs={{0,24},{8,16},{16,8},{24,0},{1,25},{9,17},{17,9},{25,1},{2,26},{10... | collective-permute-start | bytes 2359304 | tf_op jit(solution)/shard_map/ppermute | solution.py:331
  524.1 38.8 %collective-permute-start.77 = (bf16[512,1536]{1,0:T(8,128)(2,1)}, bf16[512,1536]{1,0:T(8,128)(2,1)}, u32[]{:S(2)}, u32[]{:S(2)}) collective-permute-start(bf16[512,1536]{1,0:T(8,128)(2,1)} %add_convert_fusion.1.refs_4_), channel_id=1, source_target_pairs={{2,0},{4,6},{3,1},{5,7},{10,8},{12,14},{11,9},{13,15},{18,16},{20,... | collective-permute-start | bytes 4718600 | tf_op jit(solution)/shard_map/ppermute | solution.py:444
  528.3 34.5 %collective-permute-start.75 = (bf16[512,1536]{1,0:T(8,128)(2,1)}, bf16[512,1536]{1,0:T(8,128)(2,1)}, u32[]{:S(2)}, u32[]{:S(2)}) collective-permute-start(bf16[512,1536]{1,0:T(8,128)(2,1)} %add_convert_fusion.2), channel_id=1, source_target_pairs={{2,4},{4,2},{3,5},{5,3},{10,12},{12,10},{11,13},{13,11},{18,20},{2... | collective-permute-start | bytes 4718600 | tf_op jit(solution)/shard_map/ppermute | solution.py:436
  530.9 27.8 %collective-permute-start.76 = (bf16[256,2048]{1,0:T(8,128)(2,1)}, bf16[256,2048]{1,0:T(8,128)(2,1)S(1)}, u32[]{:S(2)}, u32[]{:S(2)}) collective-permute-start(bf16[256,2048]{1,0:T(8,128)(2,1)} %convolution_convert_fusion.9), channel_id=1, source_target_pairs={{0,2},{6,4},{1,3},{7,5},{8,10},{14,12},{9,11},{15,13},{16,18},{22,... | collective-permute-start | bytes 3145736 | tf_op jit(solution)/shard_map/ppermute | solution.py:442
  558.7 28.1 %collective-permute-start.86 = (bf16[512,768]{1,0:T(8,128)(2,1)S(1)}, bf16[512,768]{1,0:T(8,128)(2,1)S(1)}, u32[]{:S(2)}, u32[]{:S(2)}) collective-permute-start(bf16[512,768]{1,0:T(8,128)(2,1)S(1)} %copy-done.59), channel_id=1, source_target_pairs={{0,2},{6,4},{1,3},{7,5},{8,10},{14,12},{9,11},{15,13},{16,18},{22,... | collective-permute-start | bytes 2359304 | tf_op jit(solution)/shard_map/ppermute | solution.py:442
  565.1 40.5 %collective-permute-start.85 = (bf16[512,1536]{1,0:T(8,128)(2,1)S(1)}, bf16[512,1536]{1,0:T(8,128)(2,1)S(1)}, u32[]{:S(2)}, u32[]{:S(2)}) collective-permute-start(bf16[512,1536]{1,0:T(8,128)(2,1)S(1)} %add_convert_fusion.refs_6_), channel_id=1, source_target_pairs={{2,0},{4,6},{3,1},{5,7},{10,8},{12,14},{11,9},{13,15},{18,16},{20,... | collective-permute-start | bytes 4718600 | tf_op jit(solution)/shard_map/ppermute | solution.py:444
  566.9 29.0 %collective-permute-start.83 = (bf16[256,2048]{1,0:T(8,128)(2,1)S(1)}, bf16[256,2048]{1,0:T(8,128)(2,1)S(1)}, u32[]{:S(2)}, u32[]{:S(2)}) collective-permute-start(bf16[256,2048]{1,0:T(8,128)(2,1)S(1)} %add_convert_fusion.13), channel_id=1, source_target_pairs={{2,4},{4,2},{3,5},{5,3},{10,12},{12,10},{11,13},{13,11},{18,20},{2... | collective-permute-start | bytes 3145736 | tf_op jit(solution)/shard_map/ppermute | solution.py:436
  570.5 25.4 %collective-permute-start.84 = (bf16[512,768]{1,0:T(8,128)(2,1)S(1)}, bf16[512,768]{1,0:T(8,128)(2,1)S(1)}, u32[]{:S(2)}, u32[]{:S(2)}) collective-permute-start(bf16[512,768]{1,0:T(8,128)(2,1)S(1)} %copy-done.58), channel_id=1, source_target_pairs={{0,2},{6,4},{1,3},{7,5},{8,10},{14,12},{9,11},{15,13},{16,18},{22,... | collective-permute-start | bytes 2359304 | tf_op jit(solution)/shard_map/ppermute | solution.py:442
  584.5 33.6 %collective-permute-start.93 = (bf16[512,768]{1,0:T(8,128)(2,1)}, bf16[512,768]{1,0:T(8,128)(2,1)}, u32[]{:S(2)}, u32[]{:S(2)}) collective-permute-start(bf16[512,768]{1,0:T(8,128)(2,1)} %collective-permute-done.73), channel_id=1, source_target_pairs={{0,2},{6,4},{1,3},{7,5},{8,10},{14,12},{9,11},{15,13},{16,18},{22,... | collective-permute-start | bytes 2359304 | tf_op jit(solution)/shard_map/ppermute | solution.py:442
  589.7 44.2 %collective-permute-start.92 = (bf16[512,768]{1,0:T(8,128)(2,1)}, bf16[512,768]{1,0:T(8,128)(2,1)}, u32[]{:S(2)}, u32[]{:S(2)}) collective-permute-start(bf16[512,768]{1,0:T(8,128)(2,1)} %add_convert_fusion.20), channel_id=1, source_target_pairs={{2,4},{4,2},{3,5},{5,3},{10,12},{12,10},{11,13},{13,11},{18,20},{2... | collective-permute-start | bytes 2359304 | tf_op jit(solution)/shard_map/ppermute | solution.py:436
  605.6 28.3 %collective-permute-start.94 = (bf16[128,2048]{1,0:T(8,128)(2,1)}, bf16[128,2048]{1,0:T(8,128)(2,1)}, u32[]{:S(2)}, u32[]{:S(2)}) collective-permute-start(bf16[128,2048]{1,0:T(8,128)(2,1)} %add_convert_fusion.22), channel_id=1, source_target_pairs={{0,16},{8,24},{16,0},{24,8},{1,17},{9,25},{17,1},{25,9},{2,18},{10... | collective-permute-start | bytes 1572872 | tf_op jit(solution)/shard_map/ppermute | solution.py:331
  607.9 31.2 %collective-permute-start.91 = (bf16[256,2048]{1,0:T(8,128)(2,1)}, bf16[256,2048]{1,0:T(8,128)(2,1)}, u32[]{:S(2)}, u32[]{:S(2)}) collective-permute-start(bf16[256,2048]{1,0:T(8,128)(2,1)} %add_convert_fusion.12), channel_id=1, source_target_pairs={{2,0},{4,6},{3,1},{5,7},{10,8},{12,14},{11,9},{13,15},{18,16},{20,... | collective-permute-start | bytes 3145736 | tf_op jit(solution)/shard_map/ppermute | solution.py:444
  609.9 29.3 %collective-permute-start.90 = (bf16[520,768]{1,0:T(8,128)(2,1)}, bf16[520,768]{1,0:T(8,128)(2,1)}, u32[]{:S(2)}, u32[]{:S(2)}) collective-permute-start(bf16[520,768]{1,0:T(8,128)(2,1)} %constant_dynamic-update-slice_fusion.26), channel_id=1, source_target_pairs={{0,2},{6,4},{1,3},{7,5},{8,10},{14,12},{9,11},{15,13},{16,18},{22,... | collective-permute-start | bytes 2396168 | tf_op jit(solution)/shard_map/ppermute | solution.py:442
  618.2 21.0 %collective-permute-start.89 = (bf16[512,768]{1,0:T(8,128)(2,1)}, bf16[512,768]{1,0:T(8,128)(2,1)}, u32[]{:S(2)}, u32[]{:S(2)}) collective-permute-start(bf16[512,768]{1,0:T(8,128)(2,1)} %add_convert_fusion.21), channel_id=1, source_target_pairs={{2,4},{4,2},{3,5},{5,3},{10,12},{12,10},{11,13},{13,11},{18,20},{2... | collective-permute-start | bytes 2359304 | tf_op jit(solution)/shard_map/ppermute | solution.py:436
  640.7 73.0 %collective-permute-start.98 = (bf16[512,768]{1,0:T(8,128)(2,1)S(1)}, bf16[512,768]{1,0:T(8,128)(2,1)S(1)}, u32[]{:S(2)}, u32[]{:S(2)}) collective-permute-start(bf16[512,768]{1,0:T(8,128)(2,1)S(1)} %add_convert_fusion.19.refs_2_), channel_id=1, source_target_pairs={{2,0},{4,6},{3,1},{5,7},{10,8},{12,14},{11,9},{13,15},{18,16},{20,... | collective-permute-start | bytes 2359304 | tf_op jit(solution)/shard_map/ppermute | solution.py:444
  643.4 70.3 %collective-permute-start.97 = (bf16[520,768]{1,0:T(8,128)(2,1)S(1)}, bf16[520,768]{1,0:T(8,128)(2,1)S(1)}, u32[]{:S(2)}, u32[]{:S(2)}) collective-permute-start(bf16[520,768]{1,0:T(8,128)(2,1)S(1)} %add_convert_fusion.15), channel_id=1, source_target_pairs={{2,4},{4,2},{3,5},{5,3},{10,12},{12,10},{11,13},{13,11},{18,20},{2... | collective-permute-start | bytes 2396168 | tf_op jit(solution)/shard_map/ppermute | solution.py:436
  653.7 60.8 %collective-permute-start.99 = (bf16[512,768]{1,0:T(8,128)(2,1)S(1)}, bf16[512,768]{1,0:T(8,128)(2,1)S(1)}, u32[]{:S(2)}, u32[]{:S(2)}) collective-permute-start(bf16[512,768]{1,0:T(8,128)(2,1)S(1)} %add_convert_fusion.16.refs_4_), channel_id=1, source_target_pairs={{2,0},{4,6},{3,1},{5,7},{10,8},{12,14},{11,9},{13,15},{18,16},{20,... | collective-permute-start | bytes 2359304 | tf_op jit(solution)/shard_map/ppermute | solution.py:444
  655.0 52.2 %collective-permute-start.100 = (bf16[128,2048]{1,0:T(8,128)(2,1)S(1)}, bf16[128,2048]{1,0:T(8,128)(2,1)S(1)}, u32[]{:S(2)}, u32[]{:S(2)}) collective-permute-start(bf16[128,2048]{1,0:T(8,128)(2,1)S(1)} %copy-done.67), channel_id=1, source_target_pairs={{0,0},{2,8},{4,16},{6,24},{8,2},{10,10},{12,18},{14,26},{16,4},{18... | collective-permute-start | bytes 1572872 | tf_op jit(solution)/shard_map/ppermute | solution.py:344
  680.8 32.9 %collective-permute-start.101 = (bf16[128,2048]{1,0:T(8,128)(2,1)}, bf16[128,2048]{1,0:T(8,128)(2,1)S(1)}, u32[]{:S(2)}, u32[]{:S(2)}) collective-permute-start(bf16[128,2048]{1,0:T(8,128)(2,1)} %collective-permute-done.94), channel_id=1, source_target_pairs={{0,4},{2,12},{4,20},{6,28},{8,6},{10,14},{12,22},{14,30},{16,0},{1... | collective-permute-start | bytes 1572872 | tf_op jit(solution)/shard_map/ppermute | solution.py:344
  (138 other events, 1890.6 us)
